TPU v7x, 32 devices: a whole 2x2x4 slice. The times are simulated.
32 devices in a mesh: grp: 2 (over y), gx: 4 (over z), gy: 4 (over x, core).
Axes of the slice: x: 2, y: 2, z: 4, core: 2. Of those that a mesh axis runs over, the one named last changes fastest.
Arguments:
- input_activation: bfloat16 [32, 32, 1024], P(('grp', 'gx'), 'gy'), parts along dimension 0, may hold values from -6 to 6
- pre_one: bfloat16 [32, 32, 1024], P(('grp', 'gx'), 'gy'), parts along dimension 0, may hold values from -6 to 6
- pre_two: bfloat16 [32, 32, 1024], P(('grp', 'gx'), 'gy'), parts along dimension 0, may hold values from -6 to 6
- w_one: bfloat16 [27, 64, 64], replicated, may hold values from -0.15625 to 0.15625
- w_two: bfloat16 [27, 64, 64], replicated, may hold values from -0.15625 to 0.15625
- w_trans: bfloat16 [512, 512], replicated, may hold values from -0.5 to 0.5
- keep_mask: int32 [8, 8], replicated, may hold values 0 or 1
- out_grad: bfloat16 [16, 16, 8, 512], P('grp', 'gy', None, 'gx'), parts along dimension 0, may hold values from -6 to 6
Outputs:
- grad_in: bfloat16 [32, 32, 1024], P(('grp', 'gx'), 'gy'), parts along dimension 0
- grad_w_one: float32 [54, 64, 64], P('grp'), parts along dimension 0
- grad_w_two: float32 [54, 64, 64], P('grp'), parts along dimension 0
- grad_w_trans: float32 [1024, 512], P('grp'), parts along dimension 0
There are 2 independent parts, one for each index of `grp`. A program takes and returns all parts, laid end to end along the dimension named above; an argument that names none is the same for every part. Nothing has to cross between parts.
All inputs are finite; a program needn't handle non-finite values.
Results may differ from a plain program's by a relative error of at most 0.0058.
Values may be sent and summed in bfloat16 or wider, within the bound.
No kernel may reach another device: no remote copies, remote signals or barrier semaphores. Data moves between devices by JAX's collectives and lax.ppermute only.
A program may use at most 64 MiB of HBM per device.

v0:
```python
import math

import jax
import jax.numpy as jnp
from jax import lax
from jax.sharding import PartitionSpec as P

DILATION_STEP = 2


def padded(cells, sides, width):
    for axis, dim in sides:
        count = lax.axis_size(axis)
        ends = count - 1
        head = lax.slice_in_dim(cells, 0, width, axis=dim)
        tail = lax.slice_in_dim(cells, cells.shape[dim] - width, cells.shape[dim], axis=dim)
        cells = jnp.concatenate(
            [
                lax.ppermute(tail, axis, [(i, (i + 1) % count) for i in range(ends)]),
                cells,
                lax.ppermute(head, axis, [((i + 1) % count, i) for i in range(ends)]),
            ],
            axis=dim,
        )
    return cells


def split_layout(joined_layout, channel_count):
    return joined_layout.reshape(joined_layout.shape[0], joined_layout.shape[1], -1, channel_count)


def to_blocks(cube_volume):
    shape_all = cube_volume.shape
    parted = cube_volume.reshape(
        shape_all[0] // 2, 2, shape_all[1] // 2, 2, shape_all[2] // 2, 2, shape_all[3]
    )
    parted = parted.transpose(0, 2, 4, 1, 3, 5, 6)
    return parted.reshape(shape_all[0] // 2, shape_all[1] // 2, shape_all[2] // 2, 8 * shape_all[3])


def from_blocks(blocked, channel_count):
    shape_all = blocked.shape
    parted = blocked.reshape(shape_all[0], shape_all[1], shape_all[2], 2, 2, 2, channel_count)
    parted = parted.transpose(0, 3, 1, 4, 2, 5, 6)
    return parted.reshape(2 * shape_all[0], 2 * shape_all[1], 2 * shape_all[2], channel_count)


def padding_depth(cube_volume, margin):
    return jnp.pad(cube_volume, ((0, 0), (0, 0), (margin, margin), (0, 0)))


def weight_terms(bordered_input, upstream_gradient):
    channel_count = upstream_gradient.shape[3]
    grid_extent = upstream_gradient.shape
    padded_input = padding_depth(bordered_input, DILATION_STEP)
    flat_grad = upstream_gradient.reshape(-1, channel_count)
    partials = []
    for x_index in range(3):
        for y_index in range(3):
            sliding_window = padded_input[
                DILATION_STEP * x_index : DILATION_STEP * x_index + grid_extent[0],
                DILATION_STEP * y_index : DILATION_STEP * y_index + grid_extent[1],
            ]
            columns = jnp.concatenate(
                [
                    sliding_window[
                        :, :, DILATION_STEP * tap_index : DILATION_STEP * tap_index + grid_extent[2]
                    ].reshape(-1, channel_count)
                    for tap_index in range(3)
                ],
                axis=1,
            )
            partials.append(
                lax.dot_general(
                    columns, flat_grad, (((0,), (0,)), ((), ())), preferred_element_type=jnp.float32
                )
            )
    return jnp.stack(partials).reshape(27, channel_count, channel_count)


def data_terms(bordered_input, weights):
    channel_count = weights.shape[1]
    x_stretch = bordered_input.shape[0] - 2 * DILATION_STEP
    y_stretch = bordered_input.shape[1] - 2 * DILATION_STEP
    depth_cells = bordered_input.shape[2]
    padded_input = padding_depth(bordered_input, DILATION_STEP)
    stacked = jnp.transpose(weights, (0, 2, 1)).reshape(9, 3 * channel_count, channel_count)
    running = jnp.zeros((x_stretch * y_stretch * depth_cells, channel_count), jnp.float32)
    for x_index in range(3):
        for y_index in range(3):
            sliding_window = padded_input[
                DILATION_STEP * (2 - x_index) : DILATION_STEP * (2 - x_index) + x_stretch,
                DILATION_STEP * (2 - y_index) : DILATION_STEP * (2 - y_index) + y_stretch,
            ]
            columns = jnp.concatenate(
                [
                    sliding_window[
                        :,
                        :,
                        DILATION_STEP * (2 - tap_index) : DILATION_STEP * (2 - tap_index)
                        + depth_cells,
                    ].reshape(-1, channel_count)
                    for tap_index in range(3)
                ],
                axis=1,
            )
            running = running + jnp.dot(
                columns, stacked[x_index * 3 + y_index], preferred_element_type=jnp.float32
            )
    return running.reshape(x_stretch, y_stretch, depth_cells, channel_count)


def body(input_activation, pre_one, pre_two, w_one, w_two, w_trans, keep_mask, out_grad):
    channel_count = w_one.shape[1]
    x_stretch, y_stretch, joined_layout = input_activation.shape
    depth_cells = joined_layout // channel_count
    width_t = w_trans.shape[0]
    factor = 1.0 / math.sqrt(
        x_stretch * lax.axis_size("gx") * y_stretch * lax.axis_size("gy") * depth_cells
    )
    blocks = jnp.repeat(
        jnp.repeat(keep_mask.astype(jnp.bfloat16), channel_count, axis=0), channel_count, axis=1
    )
    w_kept = w_trans * blocks
    regrouped = lax.all_to_all(out_grad, "gx", split_axis=0, concat_axis=3, tiled=True)
    grad_rows = regrouped.reshape(-1, width_t)
    back_blocks = lax.dot_general(
        grad_rows, w_kept, (((1,), (1,)), ((), ())), preferred_element_type=jnp.float32
    ).astype(jnp.bfloat16)
    act_two = split_layout(jnp.maximum(pre_two, 0), channel_count)
    two_rows = to_blocks(act_two).reshape(-1, width_t)
    trans_term = (
        lax.dot_general(
            two_rows, grad_rows, (((0,), (0,)), ((), ())), preferred_element_type=jnp.float32
        )
        * blocks.astype(jnp.float32)
        * factor
    )
    grad_w_trans = lax.psum(trans_term, ("gx", "gy"))
    back_two = from_blocks(
        back_blocks.reshape(x_stretch // 2, y_stretch // 2, depth_cells // 2, width_t),
        channel_count,
    )
    back_two = jnp.where(
        split_layout(pre_two, channel_count) > 0, back_two, jnp.zeros_like(back_two)
    )
    first_activation = jnp.maximum(pre_one, 0)
    bordered_input = padded(
        jnp.concatenate([input_activation, first_activation], axis=2),
        (("gx", 0), ("gy", 1)),
        DILATION_STEP,
    )
    in_rim = split_layout(bordered_input[:, :, :joined_layout], channel_count)
    one_rim = split_layout(bordered_input[:, :, joined_layout:], channel_count)
    two_term = weight_terms(one_rim, back_two) * factor
    flattened_backward = back_two.reshape(x_stretch, y_stretch, joined_layout)
    narrowed_slice = split_layout(
        padded(flattened_backward, (("gx", 0), ("gy", 1)), DILATION_STEP), channel_count
    )
    first_backward = data_terms(narrowed_slice, w_two)
    first_backward = jnp.where(
        split_layout(pre_one, channel_count) > 0, first_backward, jnp.zeros_like(first_backward)
    ).astype(jnp.bfloat16)
    one_grad_rim = split_layout(
        padded(
            first_backward.reshape(x_stretch, y_stretch, joined_layout),
            (("gx", 0), ("gy", 1)),
            DILATION_STEP,
        ),
        channel_count,
    )
    grad_w_two = lax.psum(two_term, ("gx", "gy"))
    one_term = weight_terms(in_rim, first_backward) * factor
    grad_w_one = lax.psum(one_term, ("gx", "gy"))
    grad_in = (
        data_terms(one_grad_rim, w_one)
        .astype(jnp.bfloat16)
        .reshape(x_stretch, y_stretch, joined_layout)
    )
    return (grad_in, grad_w_one, grad_w_two, grad_w_trans)


def solution(mesh):
    return jax.shard_map(
        body,
        mesh=mesh,
        in_specs=(
            P(("grp", "gx"), "gy", None),
            P(("grp", "gx"), "gy", None),
            P(("grp", "gx"), "gy", None),
            P(),
            P(),
            P(),
            P(),
            P("grp", "gy", None, "gx"),
        ),
        out_specs=(
            P(("grp", "gx"), "gy", None),
            P("grp", None, None),
            P("grp", None, None),
            P("grp", None),
        ),
        check_vma=False,
    )
```

profile of v0, /device:TPU:0, one launch (start us, length us, event | category | flops | bytes accessed | tf_op | source)
XLA Modules:
  0.0 242.6 jit_solution(7582713262238297557)
XLA Ops:
  7.2 6.3 %all-to-all-start = ((bf16[8,4,8,128]{3,2,1,0:T(8,128)(2,1)}), bf16[8,4,8,128]{3,2,1,0:T(8,128)(2,1)S(1)}, u32[]{:S(2)}, u32[]{:S(2)}) async-start(bf16[8,4,8,128]{3,2,1,0:T(8,128)(2,1)} %param.15), calls=%async_computation | async-start | bytes 131072 | tf_op jit(solution)/shard_map/all_to_all | solution.py:125
  13.5 1.1 fusion.242
  23.4 1.3 collective-permute-start.1
  24.8 4.6 %collective-permute-start = (bf16[2,8,1024]{2,1,0:T(8,128)(2,1)S(1)}, bf16[2,8,1024]{2,1,0:T(8,128)(2,1)S(1)}, u32[]{:S(2)}, u32[]{:S(2)}) collective-permute-start(bf16[2,8,1024]{2,1,0:T(8,128)(2,1)S(1)} %slice.631), channel_id=1, source_target_pairs={{0,4},{4,8},{8,12},{1,5},{5,9},{9,13},{2,6},{6,10},{10,14},{3,7},{... | collective-permute-start | bytes 98312 | tf_op jit(solution)/shard_map/ppermute | solution.py:19
  29.8 1.3 fusion
  31.3 1.3 collective-permute-start.3
  32.6 3.0 %collective-permute-start.2 = (bf16[8,2,1024]{2,1,0:T(2,128)(2,1)S(1)}, bf16[8,2,1024]{2,1,0:T(2,128)(2,1)S(1)}, u32[]{:S(2)}, u32[]{:S(2)}) collective-permute-start(bf16[8,2,1024]{2,1,0:T(2,128)(2,1)S(1)} %get-tuple-element.147), channel_id=1, source_target_pairs={{0,1},{1,2},{2,3},{4,5},{5,6},{6,7},{8,9},{9,10},{10,11},{12,13},{... | collective-permute-start | bytes 98312 | tf_op jit(solution)/shard_map/ppermute | solution.py:19
  42.5 1.3 collective-permute-start.5
  44.0 4.6 %collective-permute-start.4 = (bf16[2,8,1024]{2,1,0:T(8,128)(2,1)S(1)}, bf16[2,8,1024]{2,1,0:T(8,128)(2,1)S(1)}, u32[]{:S(2)}, u32[]{:S(2)}) collective-permute-start(bf16[2,8,1024]{2,1,0:T(8,128)(2,1)S(1)} %slice.673), channel_id=1, source_target_pairs={{0,4},{4,8},{8,12},{1,5},{5,9},{9,13},{2,6},{6,10},{10,14},{3,7},{... | collective-permute-start | bytes 98312 | tf_op jit(solution)/shard_map/ppermute | solution.py:19
  50.1 1.3 collective-permute-start.7
  51.4 3.0 %collective-permute-start.6 = (bf16[8,2,1024]{2,1,0:T(2,128)(2,1)S(1)}, bf16[8,2,1024]{2,1,0:T(2,128)(2,1)S(1)}, u32[]{:S(2)}, u32[]{:S(2)}) collective-permute-start(bf16[8,2,1024]{2,1,0:T(2,128)(2,1)S(1)} %get-tuple-element.143), channel_id=1, source_target_pairs={{0,1},{1,2},{2,3},{4,5},{5,6},{6,7},{8,9},{9,10},{10,11},{12,13},{... | collective-permute-start | bytes 98312 | tf_op jit(solution)/shard_map/ppermute | solution.py:19
  54.5 1.3 collective-permute-start.9
  55.8 4.9 %collective-permute-start.8 = (bf16[2,8,2048]{2,1,0:T(8,128)(2,1)S(1)}, bf16[2,8,2048]{2,1,0:T(8,128)(2,1)S(1)}, u32[]{:S(2)}, u32[]{:S(2)}) collective-permute-start(bf16[2,8,2048]{2,1,0:T(8,128)(2,1)S(1)} %get-tuple-element.141), channel_id=1, source_target_pairs={{0,4},{4,8},{8,12},{1,5},{5,9},{9,13},{2,6},{6,10},{10,14},{3,7},{... | collective-permute-start | bytes 196616 | tf_op jit(solution)/shard_map/ppermute | solution.py:19
  62.7 1.3 collective-permute-start.11
  64.0 5.2 %collective-permute-start.10 = (bf16[8,2,2048]{2,1,0:T(2,128)(2,1)S(1)}, bf16[8,2,2048]{2,1,0:T(2,128)(2,1)S(1)}, u32[]{:S(2)}, u32[]{:S(2)}) collective-permute-start(bf16[8,2,2048]{2,1,0:T(2,128)(2,1)S(1)} %get-tuple-element.139), channel_id=1, source_target_pairs={{0,1},{1,2},{2,3},{4,5},{5,6},{6,7},{8,9},{9,10},{10,11},{12,13},{... | collective-permute-start | bytes 196616 | tf_op jit(solution)/shard_map/ppermute | solution.py:19
  70.1 1.0 convolution_add_fusion.5
  73.8 1.6 pad_slice_fusion.19
  75.4 1.1 fusion.245
  76.8 1.6 pad_slice_fusion.1
  78.4 1.1 fusion.244
  79.5 0.9 copy-done.43
  80.4 0.9 copy-done.42
  81.3 0.9 copy-done.36
  82.2 0.9 copy-done.41
  83.1 0.9 copy-done.34
  85.8 0.9 copy-done.31
  86.7 0.9 copy-done.30
  87.6 0.9 copy-done.39
  88.5 0.9 copy-done.29
  91.2 0.9 copy-done.27
  92.1 0.9 copy-done.26
  93.0 0.9 copy-done.35
  93.9 0.9 copy-done.25
  96.7 0.9 copy-done.23
  97.6 0.9 copy-done.22
  98.5 0.9 copy-done.21
  99.4 0.9 copy-done.20
  100.3 0.9 copy-done.19
  104.6 1.2 copy.159
  105.8 0.9 copy.163
  107.7 0.9 copy-done.12
  108.6 0.9 copy-done.16
  111.3 0.9 copy-done.15
  124.3 1.2 copy.188
  131.5 99.4 %all-reduce.7.cloned.1.call-done = (f32[27,64,64]{2,1,0:T(8,128)}, f32[27,64,64]{2,1,0:T(8,128)}, f32[512,512]{1,0:T(8,128)}) async-done(((f32[27,64,64]{2,1,0:T(8,128)}, f32[27,64,64]{2,1,0:T(8,128)}, f32[512,512]{1,0:T(8,128)}), (f32[27,64,64]{2,1,0:T(8,128)}, f32[27,64,64]{2,1,0:T(8,128)}, f32[512,512]{1,0:T(8,128)})) %all-reduce.7.cloned.1.call-update) | async-done | bytes 1933328 | tf_op jit(solution)/shard_map/psum | solution.py:174
  230.9 2.3 copy.215
  233.2 0.9 copy.216
  234.7 1.0 copy.217
  (333 shorter events, 53.6 us)
Async XLA Ops:
  7.2 14.5 %all-to-all-start = ((bf16[8,4,8,128]{3,2,1,0:T(8,128)(2,1)}), bf16[8,4,8,128]{3,2,1,0:T(8,128)(2,1)S(1)}, u32[]{:S(2)}, u32[]{:S(2)}) async-start(bf16[8,4,8,128]{3,2,1,0:T(8,128)(2,1)} %param.15), calls=%async_computation | async-start | bytes 131072 | tf_op jit(solution)/shard_map/all_to_all | solution.py:125
  13.5 217.4 %all-reduce.7.cloned.1.call-start = ((), (), s32[]{:S(2)}) async-start(), calls=%async_computation.1 | async-start | bytes 5636096 | tf_op jit(solution)/shard_map/psum | solution.py:174
  13.5 1.2 copy-start.45
  14.7 1.0 copy-start.44
  23.4 7.8 %collective-permute-start.1 = (bf16[2,8,1024]{2,1,0:T(8,128)(2,1)S(1)}, bf16[2,8,1024]{2,1,0:T(8,128)(2,1)S(1)}, u32[]{:S(2)}, u32[]{:S(2)}) collective-permute-start(bf16[2,8,1024]{2,1,0:T(8,128)(2,1)S(1)} %slice.633), channel_id=1, source_target_pairs={{4,0},{8,4},{12,8},{5,1},{9,5},{13,9},{6,2},{10,6},{14,10},{7,3},{... | collective-permute-start | bytes 98312 | tf_op jit(solution)/shard_map/ppermute | solution.py:21
  24.8 6.4 %collective-permute-start = (bf16[2,8,1024]{2,1,0:T(8,128)(2,1)S(1)}, bf16[2,8,1024]{2,1,0:T(8,128)(2,1)S(1)}, u32[]{:S(2)}, u32[]{:S(2)}) collective-permute-start(bf16[2,8,1024]{2,1,0:T(8,128)(2,1)S(1)} %slice.631), channel_id=1, source_target_pairs={{0,4},{4,8},{8,12},{1,5},{5,9},{9,13},{2,6},{6,10},{10,14},{3,7},{... | collective-permute-start | bytes 98312 | tf_op jit(solution)/shard_map/ppermute | solution.py:19
  31.3 5.0 %collective-permute-start.3 = (bf16[8,2,1024]{2,1,0:T(2,128)(2,1)S(1)}, bf16[8,2,1024]{2,1,0:T(2,128)(2,1)S(1)}, u32[]{:S(2)}, u32[]{:S(2)}) collective-permute-start(bf16[8,2,1024]{2,1,0:T(2,128)(2,1)S(1)} %get-tuple-element.148), channel_id=1, source_target_pairs={{1,0},{2,1},{3,2},{5,4},{6,5},{7,6},{9,8},{10,9},{11,10},{13,12},{... | collective-permute-start | bytes 98312 | tf_op jit(solution)/shard_map/ppermute | solution.py:21
  32.6 3.9 %collective-permute-start.2 = (bf16[8,2,1024]{2,1,0:T(2,128)(2,1)S(1)}, bf16[8,2,1024]{2,1,0:T(2,128)(2,1)S(1)}, u32[]{:S(2)}, u32[]{:S(2)}) collective-permute-start(bf16[8,2,1024]{2,1,0:T(2,128)(2,1)S(1)} %get-tuple-element.147), channel_id=1, source_target_pairs={{0,1},{1,2},{2,3},{4,5},{5,6},{6,7},{8,9},{9,10},{10,11},{12,13},{... | collective-permute-start | bytes 98312 | tf_op jit(solution)/shard_map/ppermute | solution.py:19
  42.5 6.8 %collective-permute-start.5 = (bf16[2,8,1024]{2,1,0:T(8,128)(2,1)S(1)}, bf16[2,8,1024]{2,1,0:T(8,128)(2,1)S(1)}, u32[]{:S(2)}, u32[]{:S(2)}) collective-permute-start(bf16[2,8,1024]{2,1,0:T(8,128)(2,1)S(1)} %slice.675), channel_id=1, source_target_pairs={{4,0},{8,4},{12,8},{5,1},{9,5},{13,9},{6,2},{10,6},{14,10},{7,3},{... | collective-permute-start | bytes 98312 | tf_op jit(solution)/shard_map/ppermute | solution.py:21
  44.0 6.1 %collective-permute-start.4 = (bf16[2,8,1024]{2,1,0:T(8,128)(2,1)S(1)}, bf16[2,8,1024]{2,1,0:T(8,128)(2,1)S(1)}, u32[]{:S(2)}, u32[]{:S(2)}) collective-permute-start(bf16[2,8,1024]{2,1,0:T(8,128)(2,1)S(1)} %slice.673), channel_id=1, source_target_pairs={{0,4},{4,8},{8,12},{1,5},{5,9},{9,13},{2,6},{6,10},{10,14},{3,7},{... | collective-permute-start | bytes 98312 | tf_op jit(solution)/shard_map/ppermute | solution.py:19
  50.1 4.4 %copy-start.2 = (bf16[4,8,1024]{2,1,0:T(8,128)(2,1)S(1)}, bf16[4,8,1024]{2,1,0:T(8,128)(2,1)}, u32[]{:S(2)}) copy-start(bf16[4,8,1024]{2,1,0:T(8,128)(2,1)} %param.8) | copy-start | bytes 196612
  50.1 10.6 %collective-permute-start.7 = (bf16[8,2,1024]{2,1,0:T(2,128)(2,1)S(1)}, bf16[8,2,1024]{2,1,0:T(2,128)(2,1)S(1)}, u32[]{:S(2)}, u32[]{:S(2)}) collective-permute-start(bf16[8,2,1024]{2,1,0:T(2,128)(2,1)S(1)} %get-tuple-element.144), channel_id=1, source_target_pairs={{1,0},{2,1},{3,2},{5,4},{6,5},{7,6},{9,8},{10,9},{11,10},{13,12},{... | collective-permute-start | bytes 98312 | tf_op jit(solution)/shard_map/ppermute | solution.py:21
  51.4 9.3 %collective-permute-start.6 = (bf16[8,2,1024]{2,1,0:T(2,128)(2,1)S(1)}, bf16[8,2,1024]{2,1,0:T(2,128)(2,1)S(1)}, u32[]{:S(2)}, u32[]{:S(2)}) collective-permute-start(bf16[8,2,1024]{2,1,0:T(2,128)(2,1)S(1)} %get-tuple-element.143), channel_id=1, source_target_pairs={{0,1},{1,2},{2,3},{4,5},{5,6},{6,7},{8,9},{9,10},{10,11},{12,13},{... | collective-permute-start | bytes 98312 | tf_op jit(solution)/shard_map/ppermute | solution.py:19
  54.5 7.8 %collective-permute-start.9 = (bf16[2,8,2048]{2,1,0:T(8,128)(2,1)S(1)}, bf16[2,8,2048]{2,1,0:T(8,128)(2,1)S(1)}, u32[]{:S(2)}, u32[]{:S(2)}) collective-permute-start(bf16[2,8,2048]{2,1,0:T(8,128)(2,1)S(1)} %get-tuple-element.142), channel_id=1, source_target_pairs={{4,0},{8,4},{12,8},{5,1},{9,5},{13,9},{6,2},{10,6},{14,10},{7,3},{... | collective-permute-start | bytes 196616 | tf_op jit(solution)/shard_map/ppermute | solution.py:21
  55.8 6.8 %collective-permute-start.8 = (bf16[2,8,2048]{2,1,0:T(8,128)(2,1)S(1)}, bf16[2,8,2048]{2,1,0:T(8,128)(2,1)S(1)}, u32[]{:S(2)}, u32[]{:S(2)}) collective-permute-start(bf16[2,8,2048]{2,1,0:T(8,128)(2,1)S(1)} %get-tuple-element.141), channel_id=1, source_target_pairs={{0,4},{4,8},{8,12},{1,5},{5,9},{9,13},{2,6},{6,10},{10,14},{3,7},{... | collective-permute-start | bytes 196616 | tf_op jit(solution)/shard_map/ppermute | solution.py:19
  62.7 10.4 %collective-permute-start.11 = (bf16[8,2,2048]{2,1,0:T(2,128)(2,1)S(1)}, bf16[8,2,2048]{2,1,0:T(2,128)(2,1)S(1)}, u32[]{:S(2)}, u32[]{:S(2)}) collective-permute-start(bf16[8,2,2048]{2,1,0:T(2,128)(2,1)S(1)} %get-tuple-element.140), channel_id=1, source_target_pairs={{1,0},{2,1},{3,2},{5,4},{6,5},{7,6},{9,8},{10,9},{11,10},{13,12},{... | collective-permute-start | bytes 196616 | tf_op jit(solution)/shard_map/ppermute | solution.py:21
  64.0 9.1 %collective-permute-start.10 = (bf16[8,2,2048]{2,1,0:T(2,128)(2,1)S(1)}, bf16[8,2,2048]{2,1,0:T(2,128)(2,1)S(1)}, u32[]{:S(2)}, u32[]{:S(2)}) collective-permute-start(bf16[8,2,2048]{2,1,0:T(2,128)(2,1)S(1)} %get-tuple-element.139), channel_id=1, source_target_pairs={{0,1},{1,2},{2,3},{4,5},{5,6},{6,7},{8,9},{9,10},{10,11},{12,13},{... | collective-permute-start | bytes 196616 | tf_op jit(solution)/shard_map/ppermute | solution.py:19
  78.4 1.1 copy-start.38
  79.4 0.9 copy-start.43
  80.4 0.9 copy-start.42
  81.3 0.9 copy-start.36
  82.2 0.9 copy-start.41
  83.1 0.9 copy-start.34
  86.7 0.9 copy-start.30
  87.6 0.9 copy-start.39
  88.5 0.9 copy-start.29
  92.1 0.9 copy-start.26
  93.0 0.9 copy-start.35
  93.9 0.9 copy-start.25
  97.5 0.9 copy-start.22
  98.4 0.9 copy-start.21
  99.4 0.9 copy-start.20
  100.3 0.9 copy-start.19
  105.8 1.0 copy-start.18
  106.8 0.9 copy-start.17
  107.7 0.9 copy-start.12
  108.6 0.9 copy-start.16
  112.2 0.9 copy-start.7
  113.1 0.9 copy-start.6
  118.6 0.9 copy-start.11
  119.5 0.9 copy-start.8
  120.5 0.9 copy-start.46
  125.5 1.0 copy-start.48
  125.5 1.0 copy-start.49
  125.5 1.0 copy-start.57
  125.5 1.1 copy-start.59
  230.9 2.3 copy-start.1
  233.2 1.5 copy-start
  (26 other events, 22.7 us)
Sparse Core Ops, SparseCore 0:
  125.7 105.2 all-reduce.6
where the time goes:
time: 244 us; the launch traced here: 243 us
  waiting for transfers between devices  101 us (41%)
  local copies, waits for them, and re-layouts  72.1 us (30%)
  starting transfers between devices  39.3 us (16%)
  between operations  15.4 us (6%)
  matrix products  12.8 us (5%)
    psum x1, waiting for transfers between devices, body(): grad_w_one = lax.psum(one_term, ('gx', 'gy'))  99.4 us
    unnamed x124, local copies, waits for them, and re-layouts  47.6 us
    ppermute x6, starting transfers between devices, padded(): lax.ppermute(tail, axis, [(i, (i + 1) % count) for i in range(ends)])  25.3 us
    ppermute x6, starting transfers between devices, padded(): lax.ppermute(head, axis, [((i + 1) % count, i) for i in range(ends)])  7.75 us
    slice x58, local copies, waits for them, and re-layouts, weight_terms(): sliding_window[:, :, DILATION_STEP * tap_index:DILATION_STEP * tap_index...  6.75 us
    all_to_all x1, starting transfers between devices, body(): lax.all_to_all(out_grad, 'gx', split_axis=0, concat_axis=3, tiled=True)  6.33 us
    dot_general x18, matrix products, data_terms(): jnp.dot(columns, stacked[x_index * 3 + y_index], preferred_element_type=j...  6.06 us
    slice x20, local copies, waits for them, and re-layouts, data_terms(): stacked[x_index * 3 + y_index]  5.96 us
  transfers between devices with their start and end apart: 14, of which 4 were waited for; matrix products, arithmetic and copies ran while one was open for 7% of the time, Pallas kernels for 0%

commit v1 on v0

--- a/solution.py
+++ b/solution.py
@@ -1,11 +1,18 @@
+import functools
 import math
 
 import jax
 import jax.numpy as jnp
 from jax import lax
+from jax.experimental import pallas as pl
+from jax.experimental.pallas import tpu as pltpu
 from jax.sharding import PartitionSpec as P
 
 DILATION_STEP = 2
+VMEM = pltpu.MemorySpace.VMEM
+SMEM = pltpu.MemorySpace.SMEM
+F32 = jnp.float32
+BF16 = jnp.bfloat16
 
 
 def padded(cells, sides, width):
@@ -180,9 +187,277 @@
     return (grad_in, grad_w_one, grad_w_two, grad_w_trans)
 
 
+def call(kernel, out_shape, scratch, flops, *args):
+    spec = [
+        pl.BlockSpec(memory_space=SMEM if a.dtype == jnp.int32 and a.ndim == 1 else VMEM)
+        for a in args
+    ]
+    outs = jax.tree.map(lambda _: pl.BlockSpec(memory_space=VMEM), out_shape)
+    return pl.pallas_call(
+        kernel,
+        out_shape=out_shape,
+        in_specs=spec,
+        out_specs=outs,
+        scratch_shapes=scratch,
+        cost_estimate=pl.CostEstimate(
+            flops=flops, transcendentals=0, bytes_accessed=sum(a.size * a.dtype.itemsize for a in args)
+        ),
+        compiler_params=pltpu.CompilerParams(vmem_limit_bytes=48 * 1024 * 1024),
+    )(*args)
+
+
+def transition_kernel(
+    factor, at_ref, a0, a1, a2, a3, w_ref, keep_ref, back_ref, one_ref, low_ref, high_ref, trans_ref, og_ref, two_ref
+):
+    me = at_ref[0]
+    parts = (a0, a1, a2, a3)
+    n = len(parts)
+    rows = a0.shape[0] // 3
+    for s, part in enumerate(parts):
+        src = lax.rem(me + n - s, n)
+        og_ref[src] = part[0:rows]
+        spot = pl.ds(src * 4, 4)
+        two_ref[spot] = part[rows : 2 * rows].reshape(4, rows // 4, 128)
+        one_ref[spot] = part[2 * rows : 3 * rows].reshape(4, rows // 4, 128)
+    og = jnp.concatenate([og_ref[j] for j in range(n)], axis=1)
+    width = w_ref.shape[0]
+    blocks = keep_ref.shape[0]
+    side = width // blocks
+    left = (
+        lax.broadcasted_iota(jnp.int32, (width, blocks), 0) // side
+        == lax.broadcasted_iota(jnp.int32, (width, blocks), 1)
+    ).astype(BF16)
+    right = (
+        lax.broadcasted_iota(jnp.int32, (blocks, width), 1) // side
+        == lax.broadcasted_iota(jnp.int32, (blocks, width), 0)
+    ).astype(BF16)
+    keep = keep_ref[...].astype(F32).astype(BF16)
+    wide = jnp.dot(keep, right, preferred_element_type=F32).astype(BF16)
+    mask = jnp.dot(left, wide, preferred_element_type=F32)
+    kept = (w_ref[...].astype(F32) * mask).astype(BF16)
+    back = lax.dot_general(og, kept, (((1,), (1,)), ((), ())), preferred_element_type=F32)
+    two = two_ref[...].astype(F32).reshape(8, 2, 4, 2, 8, 128)
+    cells = []
+    for p in range(2):
+        halves = []
+        for q in range(2):
+            pre = two[:, p, :, q]
+            at = (p * 2 + q) * 128
+            grad = back[:, at : at + 128].reshape(8, 4, 8, 128)
+            halves.append(jnp.where(pre > 0, grad, 0.0))
+            cells.append(jnp.maximum(pre, 0.0).reshape(256, 128).astype(BF16))
+        back_ref[:, p] = jnp.stack(halves, axis=2).reshape(8, 64, 128).astype(BF16)
+    flat = jnp.concatenate(cells, axis=1)
+    trans = lax.dot_general(flat, og, (((0,), (0,)), ((), ())), preferred_element_type=F32)
+    trans_ref[...] = trans * mask * factor
+    low_ref[:, :, 0:32] = back_ref[:, :, 0:32]
+    high_ref[:, :, 0:32] = back_ref[:, :, 32:64]
+    low_ref[:, :, 32:48] = one_ref[:, 0:16].reshape(8, 2, 16, 128)
+    high_ref[:, :, 32:48] = one_ref[:, 48:64].reshape(8, 2, 16, 128)
+
+
+def triple(v):
+    x, rows, _ = v.shape
+    flat = v.reshape(x * rows, 128)
+    t = lax.broadcasted_iota(jnp.int32, flat.shape, 0) % 8
+    later = jnp.where(t == 7, 0.0, pltpu.roll(flat, x * rows - 1, 0))
+    earlier = jnp.where(t == 0, 0.0, pltpu.roll(flat, 1, 0))
+    wide = jnp.concatenate([later, flat, earlier], axis=1)
+    return wide.astype(BF16).reshape(x, rows, 384)
+
+
+def fold(sums, factor, out_ref, at):
+    lane = lax.broadcasted_iota(jnp.int32, (64, 128), 1)
+    taps = []
+    for g in sums:
+        for l in range(3):
+            part = g[:, l * 128 : (l + 1) * 128]
+            f = jnp.where(lane < 64, part[0:64], part[64:128])
+            taps.append((f + pltpu.roll(f, 64, 1)) * factor)
+    taps.append(taps[-1])
+    for m in range(14):
+        row = at + (m % 7) * 64
+        out_ref[m // 7, row : row + 64] = jnp.where(lane < 64, taps[2 * m], taps[2 * m + 1])
+
+
+def conv_kernel(
+    factor, at_ref, back_ref, one_ref, left_ref, right_ref, w2_ref, w1_ref, i0, i1, i2, i3, trans_ref,
+    grad_ref, sums_ref, wide_ref, outer_ref, in_ref, acc_ref,
+):
+    me = at_ref[0]
+    parts = (i0, i1, i2, i3)
+    n = len(parts)
+    for s, part in enumerate(parts):
+        in_ref[pl.ds(lax.rem(me + n - s, n) * 4, 4)] = part[...].reshape(4, 64, 128)
+    edge = jnp.zeros((2, 128, 384), BF16)
+    wide_ref[0:2] = edge
+    wide_ref[18:20] = edge
+    outer_ref[0:2] = edge[:, :96]
+    outer_ref[18:20] = edge[:, :96]
+    wide_ref[2:18, 0:32] = triple(left_ref[:, 0:32].astype(F32))
+    wide_ref[2:18, 32:96] = triple(back_ref[...].astype(F32))
+    wide_ref[2:18, 96:128] = triple(right_ref[:, 0:32].astype(F32))
+    for i in range(3):
+        for j in range(3):
+            rows = wide_ref[4 - 2 * i : 20 - 2 * i, 32 - 16 * j : 128 - 16 * j].reshape(1536, 384)
+            part = jnp.dot(rows, w2_ref[i * 3 + j], preferred_element_type=F32)
+            if i == 0 and j == 0:
+                acc_ref[...] = part
+            else:
+                acc_ref[...] += part
+    pre = jnp.concatenate([left_ref[:, 32:48], one_ref[...], right_ref[:, 32:48]], axis=1).astype(F32)
+    first = jnp.where(pre > 0, acc_ref[...].reshape(16, 96, 128), 0.0)
+    outer_ref[2:18] = triple(first)
+    act = jnp.maximum(one_ref[...].astype(F32), 0.0).reshape(1024, 128).T.astype(BF16)
+    sums = []
+    for i in range(3):
+        for j in range(3):
+            rows = wide_ref[4 - 2 * i : 20 - 2 * i, 48 - 16 * j : 112 - 16 * j].reshape(1024, 384)
+            sums.append(jnp.dot(act, rows, preferred_element_type=F32))
+    fold(sums, factor, sums_ref, 448)
+    act = in_ref[...].astype(F32).reshape(1024, 128).T.astype(BF16)
+    sums = []
+    grad = jnp.zeros((256, 128), F32)
+    for i in range(3):
+        for j in range(3):
+            rows = outer_ref[4 - 2 * i : 20 - 2 * i, 32 - 16 * j : 96 - 16 * j].reshape(1024, 384)
+            sums.append(jnp.dot(act, rows, preferred_element_type=F32))
+            mine = outer_ref[pl.ds(me * 4 + 4 - 2 * i, 4), 32 - 16 * j : 96 - 16 * j].reshape(256, 384)
+            grad += jnp.dot(mine, w1_ref[i * 3 + j], preferred_element_type=F32)
+    fold(sums, factor, sums_ref, 0)
+    grad_ref[...] = grad.reshape(4, 64, 128).astype(BF16)
+    for h in range(2):
+        for m in range(4):
+            sums_ref[h, 896 + 256 * m : 1152 + 256 * m] = trans_ref[
+                256 * h : 256 * h + 256, 128 * m : 128 * m + 128
+            ]
+
+
+def spread_kernel(at_ref, mine_ref, other_ref, one_ref, two_ref, trans_ref):
+    def emit(low_ref, high_ref):
+        for h, ref in enumerate((low_ref, high_ref)):
+            for out, at in ((one_ref, 0), (two_ref, 448)):
+                for m in range(7):
+                    block = ref[at + 64 * m : at + 64 * m + 64]
+                    tap = 2 * (7 * h + m)
+                    out[tap] = block[:, 0:64]
+                    if tap < 26:
+                        out[tap + 1] = block[:, 64:128]
+            for m in range(4):
+                trans_ref[256 * h : 256 * h + 256, 128 * m : 128 * m + 128] = ref[
+                    896 + 256 * m : 1152 + 256 * m
+                ]
+
+    @pl.when(at_ref[0] == 0)
+    def _():
+        emit(mine_ref, other_ref)
+
+    @pl.when(at_ref[0] != 0)
+    def _():
+        emit(other_ref, mine_ref)
+
+
+def twin(weights):
+    turned = jnp.transpose(weights, (0, 2, 1))
+    none = jnp.zeros_like(turned)
+    both = jnp.concatenate(
+        [jnp.concatenate([turned, none], axis=2), jnp.concatenate([none, turned], axis=2)], axis=1
+    )
+    return both.reshape(9, 384, 128)
+
+
+def rotate(value, axis, step):
+    n = lax.axis_size(axis)
+    return lax.ppermute(value, axis, [(i, (i + step) % n) for i in range(n)])
+
+
+def swap(value, axis, bit):
+    n = lax.axis_size(axis)
+    return lax.ppermute(value, axis, [(i, i ^ bit) for i in range(n)])
+
+
+def slab_body(input_activation, pre_one, pre_two, w_one, w_two, w_trans, keep_mask, out_grad):
+    factor = 1.0 / math.sqrt(
+        input_activation.shape[0] * 4 * input_activation.shape[1] * 4 * (input_activation.shape[2] // 64)
+    )
+    gx = lax.axis_index("gx").astype(jnp.int32)
+    gy = lax.axis_index("gy").astype(jnp.int32)
+    core = lax.rem(gy, 2)
+    first = jnp.concatenate(
+        [out_grad.reshape(256, 128), pre_two.reshape(256, 128), pre_one.reshape(256, 128)], axis=0
+    )
+    firsts = [first] + [rotate(first, "gx", s) for s in (1, 2, 3)]
+    second = input_activation.reshape(256, 128)
+    seconds = [second] + [rotate(second, "gx", s) for s in (1, 2, 3)]
+    shape = jax.ShapeDtypeStruct
+    back, one, low, high, trans = call(
+        functools.partial(transition_kernel, factor),
+        (
+            shape((8, 2, 64, 128), BF16),
+            shape((16, 64, 128), BF16),
+            shape((8, 2, 48, 128), BF16),
+            shape((8, 2, 48, 128), BF16),
+            shape((512, 512), F32),
+        ),
+        [pltpu.VMEM((4, 256, 128), BF16), pltpu.VMEM((16, 64, 128), BF16)],
+        4 * 256 * 512 * 512,
+        gx.reshape(1),
+        *firsts,
+        w_trans,
+        keep_mask,
+    )
+    n = lax.axis_size("gy")
+    from_left = lax.ppermute(high, "gy", [(i, i + 1) for i in range(n - 1)])
+    from_right = lax.ppermute(low, "gy", [(i + 1, i) for i in range(n - 1)])
+    grad_in, sums = call(
+        functools.partial(conv_kernel, factor),
+        (shape((4, 64, 128), BF16), shape((2, 1920, 128), F32)),
+        [
+            pltpu.VMEM((20, 128, 384), BF16),
+            pltpu.VMEM((20, 96, 384), BF16),
+            pltpu.VMEM((16, 64, 128), BF16),
+            pltpu.VMEM((1536, 128), F32),
+        ],
+        2 * 128 * 3456 * (1536 + 1024 + 1024 + 256),
+        gx.reshape(1),
+        back.reshape(16, 64, 128),
+        one,
+        from_left.reshape(16, 48, 128),
+        from_right.reshape(16, 48, 128),
+        twin(w_two),
+        twin(w_one),
+        *seconds,
+        trans,
+    )
+    mine = lax.dynamic_index_in_dim(sums, core, 0, keepdims=False)
+    other = lax.dynamic_index_in_dim(sums, 1 - core, 0, keepdims=False)
+    mine = (mine + swap(other, "gy", 1)).astype(BF16)
+    mine = mine.astype(F32) + swap(mine, "gy", 2).astype(F32)
+    other = swap(mine, "gy", 1)
+    grad_w_one, grad_w_two, grad_w_trans = call(
+        spread_kernel,
+        (shape((27, 64, 64), F32), shape((27, 64, 64), F32), shape((512, 512), F32)),
+        [],
+        0,
+        core.reshape(1),
+        mine,
+        other,
+    )
+    return (grad_in.reshape(input_activation.shape), grad_w_one, grad_w_two, grad_w_trans)
+
+
 def solution(mesh):
+    fits = mesh.shape["gx"] == 4 and mesh.shape["gy"] == 4
+
+    def pick(*args):
+        shapes = tuple(a.shape for a in args)
+        known = (
+            ((4, 8, 1024),) * 3 + ((27, 64, 64),) * 2 + ((512, 512), (8, 8), (8, 4, 8, 128))
+        )
+        return (slab_body if fits and shapes == known else body)(*args)
+
     return jax.shard_map(
-        body,
+        pick,
         mesh=mesh,
         in_specs=(
             P(("grp", "gx"), "gy", None),

time: 244 us -> 82.5 us (0.34)
  the two profiles are of different devices: /device:TPU:0 before, /device:TPU:27 now
where the time goes in v1:
time: 82.5 us; the launch traced here: 81.8 us
  waiting for transfers between devices  31.6 us (38%)
  local copies, waits for them, and re-layouts  20.2 us (24%)
  starting transfers between devices  14.8 us (18%)
  Pallas kernels  9.66 us (12%)
  other arithmetic  4.81 us (6%)
    ppermute x3, waiting for transfers between devices, swap(): return lax.ppermute(value, axis, [(i, i ^ bit) for i in range(n)])  16.5 us
    ppermute x6, waiting for transfers between devices, rotate(): return lax.ppermute(value, axis, [(i, (i + step) % n) for i in range(n)])  15.1 us
    unnamed x34, local copies, waits for them, and re-layouts  11.7 us
    pallas_call x3, Pallas kernels, call(): pl.pallas_call(kernel, out_shape=out_shape, in_specs=spec, out_specs=outs...  9.66 us
    ppermute x1, starting transfers between devices, slab_body(): from_right = lax.ppermute(low, 'gy', [(i + 1, i) for i in range(n - 1)])  5.24 us
    ppermute x6, starting transfers between devices, rotate(): return lax.ppermute(value, axis, [(i, (i + step) % n) for i in range(n)])  5.17 us
    concatenate x2, local copies, waits for them, and re-layouts, twin(): jnp.concatenate([jnp.concatenate([turned, none], axis=2), jnp.concatenate...  4.09 us
    ppermute x3, starting transfers between devices, swap(): return lax.ppermute(value, axis, [(i, i ^ bit) for i in range(n)])  3.06 us
  transfers between devices with their start and end apart: 11, of which 5 were waited for; matrix products, arithmetic and copies ran while one was open for 10% of the time, Pallas kernels for 2%

profile of v1, /device:TPU:27, one launch (start us, length us, event | category | flops | bytes accessed | tf_op | source)
XLA Modules:
  0.0 81.8 jit_solution(12812770566941379782)
XLA Ops:
  0.6 0.9 %reshape.47 = bf16[256,128]{1,0:T(8,128)(2,1)S(1)} reshape(bf16[4,8,1024]{2,1,0:T(8,128)(2,1)} %param.10) | data formatting | bytes 131072 | tf_op jit(solution)/shard_map/reshape | solution.py:387
  1.6 0.9 %reshape.48 = bf16[256,128]{1,0:T(8,128)(2,1)S(1)} reshape(bf16[4,8,1024]{2,1,0:T(8,128)(2,1)} %param.9) | data formatting | bytes 131072 | tf_op jit(solution)/shard_map/reshape | solution.py:387
  2.4 0.9 %pad_maximum_fusion.a0 = bf16[768,128]{1,0:T(8,128)(2,1)S(1)} fusion(bf16[256,128]{1,0:T(8,128)(2,1)S(1)} %reshape.48, bf16[256,128]{1,0:T(8,128)(2,1)S(1)} %reshape.47, bf16[256,128]{1,0:T(8,128)(2,1)} %bitcast.23), kind=kLoop, calls=%fused_computation.12 | loop fusion | flops 589824 | bytes 393216 | tf_op jit(solution)/shard_map/concatenate | solution.py:386
  3.3 0.1 collective-permute-start
  3.4 1.3 %collective-permute-start.1 = (bf16[768,128]{1,0:T(8,128)(2,1)S(1)}, bf16[768,128]{1,0:T(8,128)(2,1)S(1)}, u32[]{:S(2)}, u32[]{:S(2)}) collective-permute-start(bf16[768,128]{1,0:T(8,128)(2,1)S(1)} %pad_maximum_fusion.a0), channel_id=1, source_target_pairs={{0,8},{4,12},{8,0},{12,4},{1,9},{5,13},{9,1},{13,5},{2,10},{6,14},... | collective-permute-start | bytes 589832 | tf_op jit(solution)/shard_map/ppermute | solution.py:371
  4.7 0.2 collective-permute-start.2
  4.9 0.9 %reshape.54.i0 = bf16[256,128]{1,0:T(8,128)(2,1)S(1)} reshape(bf16[4,8,1024]{2,1,0:T(8,128)(2,1)} %param.8) | data formatting | bytes 131072 | tf_op jit(solution)/shard_map/reshape | solution.py:390
  5.8 3.1 %collective-permute-start.5 = (bf16[256,128]{1,0:T(8,128)(2,1)S(1)}, bf16[256,128]{1,0:T(8,128)(2,1)S(1)}, u32[]{:S(2)}, u32[]{:S(2)}) collective-permute-start(bf16[256,128]{1,0:T(8,128)(2,1)S(1)} %reshape.54.i0), channel_id=1, source_target_pairs={{0,4},{4,8},{8,12},{12,0},{1,5},{5,9},{9,13},{13,1},{2,6},{6,10},{... | collective-permute-start | bytes 196616 | tf_op jit(solution)/shard_map/ppermute | solution.py:371
  8.9 0.0 collective-permute-start.6
  8.9 0.2 collective-permute-done.a1
  9.1 0.5 collective-permute-start.7
  9.6 14.9 %collective-permute-done.1.a2 = bf16[768,128]{1,0:T(8,128)(2,1)S(1)} collective-permute-done((bf16[768,128]{1,0:T(8,128)(2,1)S(1)}, bf16[768,128]{1,0:T(8,128)(2,1)S(1)}, u32[]{:S(2)}, u32[]{:S(2)}) %collective-permute-start.1) | collective-permute-done | bytes 196640 | tf_op jit(solution)/shard_map/ppermute | solution.py:371
  24.5 0.0 collective-permute-done.2.a3
  24.5 1.0 %copy-done.1 = bf16[512,512]{1,0:T(8,128)(2,1)S(1)} copy-done((bf16[512,512]{1,0:T(8,128)(2,1)S(1)}, bf16[512,512]{1,0:T(8,128)(2,1)}, u32[]{:S(2)}) %copy-start.1) | copy-done | bytes 524312
  25.5 0.7 copy-done.2
  26.2 1.5 %shard_map.111 = (bf16[8,2,64,128]{3,2,1,0:T(8,128)(2,1)S(1)}, bf16[16,64,128]{2,1,0:T(8,128)(2,1)S(1)}, bf16[8,2,48,128]{3,2,1,0:T(8,128)(2,1)}, bf16[8,2,48,128]{3,2,1,0:T(8,128)(2,1)}, f32[512,512]{1,0:T(8,128)S(1)}) custom-call(s32[1]{0:T(128)} %bitcast.at_ref, bf16[768,128]{1,0:T(8,128)(2,1)S(1)} %pad_maximum_fusion.a0, ...), custom_call_target="tpu_custom_call" | custom-call | flops 268435456 | bytes 1310980 | tf_op jit(solution)/shard_map/pallas_call | solution.py:196
  27.7 1.3 %collective-permute-start.3 = (bf16[8,2,48,128]{3,2,1,0:T(8,128)(2,1)}, bf16[8,2,48,128]{3,2,1,0:T(8,128)(2,1)S(1)}, u32[]{:S(2)}, u32[]{:S(2)}) collective-permute-start(bf16[8,2,48,128]{3,2,1,0:T(8,128)(2,1)} %get-tuple-element.16), channel_id=1, source_target_pairs={{0,1},{1,2},{2,3},{4,5},{5,6},{6,7},{8,9},{9,10},{10,11},{12,13},{... | collective-permute-start | bytes 589832 | tf_op jit(solution)/shard_map/ppermute | solution.py:410
  29.0 5.2 %collective-permute-start.4 = (bf16[8,2,48,128]{3,2,1,0:T(8,128)(2,1)}, bf16[8,2,48,128]{3,2,1,0:T(8,128)(2,1)S(1)}, u32[]{:S(2)}, u32[]{:S(2)}) collective-permute-start(bf16[8,2,48,128]{3,2,1,0:T(8,128)(2,1)} %get-tuple-element.17), channel_id=1, source_target_pairs={{1,0},{2,1},{3,2},{5,4},{6,5},{7,6},{9,8},{10,9},{11,10},{13,12},{... | collective-permute-start | bytes 589832 | tf_op jit(solution)/shard_map/ppermute | solution.py:411
  34.3 1.3 %fusion.5 = bf16[27,128,128]{1,2,0:T(8,128)(2,1)} fusion(bf16[27,64,64]{1,2,0:T(8,128)(2,1)S(1)} %bitcast.21), kind=kLoop, calls=%fused_computation.10 | loop fusion | flops 3538944 | bytes 1105920 | tf_op jit(solution)/shard_map/concatenate | solution.py:363
  35.5 1.3 %fusion.6 = bf16[27,128,128]{1,2,0:T(8,128)(2,1)} fusion(bf16[27,64,64]{1,2,0:T(8,128)(2,1)S(1)} %bitcast.22), kind=kLoop, calls=%fused_computation.11 | loop fusion | flops 3538944 | bytes 1105920 | tf_op jit(solution)/shard_map/concatenate | solution.py:363
  36.8 1.9 %copy.12 = bf16[27,128,128]{2,1,0:T(8,128)(2,1)S(1)} copy(bf16[27,128,128]{1,2,0:T(8,128)(2,1)} %fusion.5) | data formatting | bytes 1769472 | tf_op jit(solution)/shard_map/concatenate | solution.py:363
  38.7 2.2 %copy.13 = bf16[27,128,128]{2,1,0:T(8,128)(2,1)} copy(bf16[27,128,128]{1,2,0:T(8,128)(2,1)} %fusion.6) | data formatting | bytes 1769472 | tf_op jit(solution)/shard_map/concatenate | solution.py:363
  40.9 0.0 collective-permute-done.5.i1
  40.9 0.6 copy-done.9
  41.6 0.6 copy-done.11
  42.2 0.6 copy-done.13
  42.8 0.0 collective-permute-done.3
  42.8 0.7 copy-done.5
  43.5 0.7 copy-done.7
  44.2 1.2 %copy-done = bf16[27,128,128]{2,1,0:T(8,128)(2,1)S(1)} copy-done((bf16[27,128,128]{2,1,0:T(8,128)(2,1)S(1)}, bf16[27,128,128]{2,1,0:T(8,128)(2,1)}, u32[]{:S(2)}) %copy-start) | copy-done | bytes 884760
  45.4 1.2 %copy-done.4 = f32[512,512]{1,0:T(8,128)S(1)} copy-done((f32[512,512]{1,0:T(8,128)S(1)}, f32[512,512]{1,0:T(8,128)}, u32[]{:S(2)}) %copy-start.4) | copy-done | bytes 1048600
  46.6 0.9 %copy-done.6 = bf16[8,2,48,128]{3,2,1,0:T(8,128)(2,1)S(1)} copy-done((bf16[8,2,48,128]{3,2,1,0:T(8,128)(2,1)S(1)}, bf16[8,2,48,128]{3,2,1,0:T(8,128)(2,1)}, u32[]{:S(2)}) %copy-start.6) | copy-done | bytes 196632
  47.5 0.9 %copy-done.8 = bf16[8,2,48,128]{3,2,1,0:T(8,128)(2,1)S(1)} copy-done((bf16[8,2,48,128]{3,2,1,0:T(8,128)(2,1)S(1)}, bf16[8,2,48,128]{3,2,1,0:T(8,128)(2,1)}, u32[]{:S(2)}) %copy-start.8) | copy-done | bytes 196632
  48.5 0.8 %copy-done.10 = bf16[256,128]{1,0:T(8,128)(2,1)S(1)} copy-done((bf16[256,128]{1,0:T(8,128)(2,1)S(1)}, bf16[256,128]{1,0:T(8,128)(2,1)}, u32[]{:S(2)}) %copy-start.10) | copy-done | bytes 65560
  49.3 0.8 %copy-done.12 = bf16[256,128]{1,0:T(8,128)(2,1)S(1)} copy-done((bf16[256,128]{1,0:T(8,128)(2,1)S(1)}, bf16[256,128]{1,0:T(8,128)(2,1)}, u32[]{:S(2)}) %copy-start.12) | copy-done | bytes 65560
  50.1 0.8 %copy-done.14 = bf16[256,128]{1,0:T(8,128)(2,1)S(1)} copy-done((bf16[256,128]{1,0:T(8,128)(2,1)S(1)}, bf16[256,128]{1,0:T(8,128)(2,1)}, u32[]{:S(2)}) %copy-start.14) | copy-done | bytes 65560
  51.0 6.3 %shard_map.112 = (bf16[4,64,128]{2,1,0:T(8,128)(2,1)S(1)}, f32[2,1920,128]{2,1,0:T(8,128)S(1)}) custom-call(s32[1]{0:T(128)} %bitcast.at_ref, bf16[16,64,128]{2,1,0:T(8,128)(2,1)S(1)} %bitcast.18, bf16[16,64,128]{2,1,0:T(8,128)(2,1)S(1)} %get-tuple-element.15.one_ref, bf16[16,48,128]{2,1,0:T(8,128)(2,1)S(1)} %bitcast.19, bf16[16,48,128]{2,1,0:T(8,128)(2,1)S(1)} %bitcast.20, ...), custom_call_target="tpu_custom_call" | custom-call | flops 3397386240 | bytes 3997700 | tf_op jit(solution)/shard_map/pallas_call | solution.py:196
  57.3 1.0 %dynamic-slice_bitcast_fusion = f32[1920,128]{1,0:T(8,128)} fusion(f32[2,1920,128]{2,1,0:T(8,128)S(1)} %get-tuple-element.20, s32[]{:T(128)S(6)} %select_n.8), kind=kLoop, calls=%fused_computation.9 | loop fusion | bytes 1966084 | tf_op jit(solution)/shard_map/jit(dynamic_index_in_dim)/squeeze | solution.py:433
  58.3 1.7 %collective-permute-start.8 = (f32[1920,128]{1,0:T(8,128)}, f32[1920,128]{1,0:T(8,128)}, u32[]{:S(2)}, u32[]{:S(2)}) collective-permute-start(f32[1920,128]{1,0:T(8,128)} %dynamic-slice_bitcast_fusion), channel_id=1, source_target_pairs={{0,1},{1,0},{2,3},{3,2},{4,5},{5,4},{6,7},{7,6},{8,9},{9,8},{10,11... | collective-permute-start | bytes 2949128 | tf_op jit(solution)/shard_map/ppermute | solution.py:376
  60.0 2.5 %collective-permute-done.8 = f32[1920,128]{1,0:T(8,128)} collective-permute-done((f32[1920,128]{1,0:T(8,128)}, f32[1920,128]{1,0:T(8,128)}, u32[]{:S(2)}, u32[]{:S(2)}) %collective-permute-start.8) | collective-permute-done | bytes 983072 | tf_op jit(solution)/shard_map/ppermute | solution.py:376
  62.5 1.3 %fusion.4 = bf16[1920,128]{1,0:T(8,128)(2,1)S(1)} fusion(f32[1920,128]{1,0:T(8,128)} %collective-permute-done.8, f32[2,1920,128]{2,1,0:T(8,128)S(1)} %get-tuple-element.20, s32[]{:T(128)S(6)} %select_n.7), kind=kLoop, calls=%fused_computation.7 | loop fusion | flops 491520 | bytes 2457604 | tf_op jit(solution)/shard_map/convert_element_type | solution.py:434
  63.8 0.1 collective-permute-start.9
  63.9 12.4 %collective-permute-done.9 = bf16[1920,128]{1,0:T(8,128)(2,1)S(1)} collective-permute-done((bf16[1920,128]{1,0:T(8,128)(2,1)S(1)}, bf16[1920,128]{1,0:T(8,128)(2,1)S(1)}, u32[]{:S(2)}, u32[]{:S(2)}) %collective-permute-start.9) | collective-permute-done | bytes 491552 | tf_op jit(solution)/shard_map/ppermute | solution.py:376
  76.3 0.1 convert_add_fusion.mine_ref
  76.4 1.3 %collective-permute-start.10 = (f32[1920,128]{1,0:T(8,128)S(1)}, f32[1920,128]{1,0:T(8,128)S(1)}, u32[]{:S(2)}, u32[]{:S(2)}) collective-permute-start(f32[1920,128]{1,0:T(8,128)S(1)} %convert_add_fusion.mine_ref), channel_id=1, source_target_pairs={{0,1},{1,0},{2,3},{3,2},{4,5},{5,4},{6,7},{7,6},{8,9},{9,8},{10,11... | collective-permute-start | bytes 2949128 | tf_op jit(solution)/shard_map/ppermute | solution.py:376
  77.7 0.7 reshape.55
  78.4 1.5 %collective-permute-done.10.other_ref = f32[1920,128]{1,0:T(8,128)S(1)} collective-permute-done((f32[1920,128]{1,0:T(8,128)S(1)}, f32[1920,128]{1,0:T(8,128)S(1)}, u32[]{:S(2)}, u32[]{:S(2)}) %collective-permute-start.10) | collective-permute-done | bytes 983072 | tf_op jit(solution)/shard_map/ppermute | solution.py:376
  79.9 1.9 %shard_map.113 = (f32[27,64,64]{2,1,0:T(8,128)}, f32[27,64,64]{2,1,0:T(8,128)}, f32[512,512]{1,0:T(8,128)}) custom-call(s32[1]{0:T(128)} %bitcast.9.at_ref, f32[1920,128]{1,0:T(8,128)S(1)} %convert_add_fusion.mine_ref, f32[1920,128]{1,0:T(8,128)S(1)} %collective-permute-done.10.other_ref), custom_call_target="tpu_custom_call" | custom-call | bytes 1966084 | tf_op jit(solution)/shard_map/pallas_call | solution.py:196
  (23 shorter events, 0.0 us)
Async XLA Ops:
  0.6 33.6 %copy-start.15 = (bf16[27,64,64]{2,1,0:T(8,128)(2,1)S(1)}, bf16[27,64,64]{2,1,0:T(8,128)(2,1)}, u32[]{:S(2)}) copy-start(bf16[27,64,64]{2,1,0:T(8,128)(2,1)} %param.12) | copy-start | bytes 663556
  3.3 5.8 %collective-permute-start = (bf16[768,128]{1,0:T(8,128)(2,1)S(1)}, bf16[768,128]{1,0:T(8,128)(2,1)S(1)}, u32[]{:S(2)}, u32[]{:S(2)}) collective-permute-start(bf16[768,128]{1,0:T(8,128)(2,1)S(1)} %pad_maximum_fusion.a0), channel_id=1, source_target_pairs={{0,4},{4,8},{8,12},{12,0},{1,5},{5,9},{9,13},{13,1},{2,6},{6,10},{... | collective-permute-start | bytes 589832 | tf_op jit(solution)/shard_map/ppermute | solution.py:371
  3.4 21.1 %collective-permute-start.1 = (bf16[768,128]{1,0:T(8,128)(2,1)S(1)}, bf16[768,128]{1,0:T(8,128)(2,1)S(1)}, u32[]{:S(2)}, u32[]{:S(2)}) collective-permute-start(bf16[768,128]{1,0:T(8,128)(2,1)S(1)} %pad_maximum_fusion.a0), channel_id=1, source_target_pairs={{0,8},{4,12},{8,0},{12,4},{1,9},{5,13},{9,1},{13,5},{2,10},{6,14},... | collective-permute-start | bytes 589832 | tf_op jit(solution)/shard_map/ppermute | solution.py:371
  4.7 19.8 %collective-permute-start.2 = (bf16[768,128]{1,0:T(8,128)(2,1)S(1)}, bf16[768,128]{1,0:T(8,128)(2,1)S(1)}, u32[]{:S(2)}, u32[]{:S(2)}) collective-permute-start(bf16[768,128]{1,0:T(8,128)(2,1)S(1)} %pad_maximum_fusion.a0), channel_id=1, source_target_pairs={{0,12},{4,0},{8,4},{12,8},{1,13},{5,1},{9,5},{13,9},{2,14},{6,2},{... | collective-permute-start | bytes 589832 | tf_op jit(solution)/shard_map/ppermute | solution.py:371
  5.8 35.2 %collective-permute-start.5 = (bf16[256,128]{1,0:T(8,128)(2,1)S(1)}, bf16[256,128]{1,0:T(8,128)(2,1)S(1)}, u32[]{:S(2)}, u32[]{:S(2)}) collective-permute-start(bf16[256,128]{1,0:T(8,128)(2,1)S(1)} %reshape.54.i0), channel_id=1, source_target_pairs={{0,4},{4,8},{8,12},{12,0},{1,5},{5,9},{9,13},{13,1},{2,6},{6,10},{... | collective-permute-start | bytes 196616 | tf_op jit(solution)/shard_map/ppermute | solution.py:371
  8.9 32.7 %collective-permute-start.6 = (bf16[256,128]{1,0:T(8,128)(2,1)S(1)}, bf16[256,128]{1,0:T(8,128)(2,1)S(1)}, u32[]{:S(2)}, u32[]{:S(2)}) collective-permute-start(bf16[256,128]{1,0:T(8,128)(2,1)S(1)} %reshape.54.i0), channel_id=1, source_target_pairs={{0,8},{4,12},{8,0},{12,4},{1,9},{5,13},{9,1},{13,5},{2,10},{6,14},... | collective-permute-start | bytes 196616 | tf_op jit(solution)/shard_map/ppermute | solution.py:371
  9.1 33.1 %collective-permute-start.7 = (bf16[256,128]{1,0:T(8,128)(2,1)S(1)}, bf16[256,128]{1,0:T(8,128)(2,1)S(1)}, u32[]{:S(2)}, u32[]{:S(2)}) collective-permute-start(bf16[256,128]{1,0:T(8,128)(2,1)S(1)} %reshape.54.i0), channel_id=1, source_target_pairs={{0,12},{4,0},{8,4},{12,8},{1,13},{5,1},{9,5},{13,9},{2,14},{6,2},{... | collective-permute-start | bytes 196616 | tf_op jit(solution)/shard_map/ppermute | solution.py:371
  24.5 1.0 %copy-start.1 = (bf16[512,512]{1,0:T(8,128)(2,1)S(1)}, bf16[512,512]{1,0:T(8,128)(2,1)}, u32[]{:S(2)}) copy-start(bf16[512,512]{1,0:T(8,128)(2,1)} %w_ref.1) | copy-start | bytes 1572868
  25.5 0.7 copy-start.2
  26.2 9.4 %copy-start.16 = (bf16[27,64,64]{2,1,0:T(8,128)(2,1)S(1)}, bf16[27,64,64]{2,1,0:T(8,128)(2,1)}, u32[]{:S(2)}) copy-start(bf16[27,64,64]{2,1,0:T(8,128)(2,1)} %param.11) | copy-start | bytes 663556
  27.7 11.0 %copy-start.3 = (f32[512,512]{1,0:T(8,128)}, f32[512,512]{1,0:T(8,128)S(1)}, u32[]{:S(2)}) copy-start(f32[512,512]{1,0:T(8,128)S(1)} %get-tuple-element.18.trans_ref) | copy-start | bytes 3145732
  27.7 15.1 %collective-permute-start.3 = (bf16[8,2,48,128]{3,2,1,0:T(8,128)(2,1)}, bf16[8,2,48,128]{3,2,1,0:T(8,128)(2,1)S(1)}, u32[]{:S(2)}, u32[]{:S(2)}) collective-permute-start(bf16[8,2,48,128]{3,2,1,0:T(8,128)(2,1)} %get-tuple-element.16), channel_id=1, source_target_pairs={{0,1},{1,2},{2,3},{4,5},{5,6},{6,7},{8,9},{9,10},{10,11},{12,13},{... | collective-permute-start | bytes 589832 | tf_op jit(solution)/shard_map/ppermute | solution.py:410
  29.0 14.5 %collective-permute-start.4 = (bf16[8,2,48,128]{3,2,1,0:T(8,128)(2,1)}, bf16[8,2,48,128]{3,2,1,0:T(8,128)(2,1)S(1)}, u32[]{:S(2)}, u32[]{:S(2)}) collective-permute-start(bf16[8,2,48,128]{3,2,1,0:T(8,128)(2,1)} %get-tuple-element.17), channel_id=1, source_target_pairs={{1,0},{2,1},{3,2},{5,4},{6,5},{7,6},{9,8},{10,9},{11,10},{13,12},{... | collective-permute-start | bytes 589832 | tf_op jit(solution)/shard_map/ppermute | solution.py:411
  40.9 0.6 copy-start.9
  41.6 0.6 copy-start.11
  42.2 0.6 copy-start.13
  42.8 0.7 copy-start.5
  43.5 0.7 copy-start.7
  44.2 1.2 %copy-start = (bf16[27,128,128]{2,1,0:T(8,128)(2,1)S(1)}, bf16[27,128,128]{2,1,0:T(8,128)(2,1)}, u32[]{:S(2)}) copy-start(bf16[27,128,128]{2,1,0:T(8,128)(2,1)} %copy.13) | copy-start | bytes 2654212
  45.4 1.2 %copy-start.4 = (f32[512,512]{1,0:T(8,128)S(1)}, f32[512,512]{1,0:T(8,128)}, u32[]{:S(2)}) copy-start(f32[512,512]{1,0:T(8,128)} %copy-done.3) | copy-start | bytes 3145732
  46.6 0.9 %copy-start.6 = (bf16[8,2,48,128]{3,2,1,0:T(8,128)(2,1)S(1)}, bf16[8,2,48,128]{3,2,1,0:T(8,128)(2,1)}, u32[]{:S(2)}) copy-start(bf16[8,2,48,128]{3,2,1,0:T(8,128)(2,1)} %copy-done.5) | copy-start | bytes 589828
  47.5 0.9 %copy-start.8 = (bf16[8,2,48,128]{3,2,1,0:T(8,128)(2,1)S(1)}, bf16[8,2,48,128]{3,2,1,0:T(8,128)(2,1)}, u32[]{:S(2)}) copy-start(bf16[8,2,48,128]{3,2,1,0:T(8,128)(2,1)} %copy-done.7) | copy-start | bytes 589828
  48.4 0.8 %copy-start.10 = (bf16[256,128]{1,0:T(8,128)(2,1)S(1)}, bf16[256,128]{1,0:T(8,128)(2,1)}, u32[]{:S(2)}) copy-start(bf16[256,128]{1,0:T(8,128)(2,1)} %copy-done.9) | copy-start | bytes 196612
  49.3 0.8 %copy-start.12 = (bf16[256,128]{1,0:T(8,128)(2,1)S(1)}, bf16[256,128]{1,0:T(8,128)(2,1)}, u32[]{:S(2)}) copy-start(bf16[256,128]{1,0:T(8,128)(2,1)} %copy-done.11) | copy-start | bytes 196612
  50.1 0.8 %copy-start.14 = (bf16[256,128]{1,0:T(8,128)(2,1)S(1)}, bf16[256,128]{1,0:T(8,128)(2,1)}, u32[]{:S(2)}) copy-start(bf16[256,128]{1,0:T(8,128)(2,1)} %copy-done.13) | copy-start | bytes 196612
  58.3 4.3 %collective-permute-start.8 = (f32[1920,128]{1,0:T(8,128)}, f32[1920,128]{1,0:T(8,128)}, u32[]{:S(2)}, u32[]{:S(2)}) collective-permute-start(f32[1920,128]{1,0:T(8,128)} %dynamic-slice_bitcast_fusion), channel_id=1, source_target_pairs={{0,1},{1,0},{2,3},{3,2},{4,5},{5,4},{6,7},{7,6},{8,9},{9,8},{10,11... | collective-permute-start | bytes 2949128 | tf_op jit(solution)/shard_map/ppermute | solution.py:376
  63.8 12.5 %collective-permute-start.9 = (bf16[1920,128]{1,0:T(8,128)(2,1)S(1)}, bf16[1920,128]{1,0:T(8,128)(2,1)S(1)}, u32[]{:S(2)}, u32[]{:S(2)}) collective-permute-start(bf16[1920,128]{1,0:T(8,128)(2,1)S(1)} %fusion.4), channel_id=1, source_target_pairs={{0,2},{1,3},{2,0},{3,1},{4,6},{5,7},{6,4},{7,5},{8,10},{9,11},{10,... | collective-permute-start | bytes 1474568 | tf_op jit(solution)/shard_map/ppermute | solution.py:376
  76.4 3.5 %collective-permute-start.10 = (f32[1920,128]{1,0:T(8,128)S(1)}, f32[1920,128]{1,0:T(8,128)S(1)}, u32[]{:S(2)}, u32[]{:S(2)}) collective-permute-start(f32[1920,128]{1,0:T(8,128)S(1)} %convert_add_fusion.mine_ref), channel_id=1, source_target_pairs={{0,1},{1,0},{2,3},{3,2},{4,5},{5,4},{6,7},{7,6},{8,9},{9,8},{10,11... | collective-permute-start | bytes 2949128 | tf_op jit(solution)/shard_map/ppermute | solution.py:376

commit v2 on v1

--- a/solution.py
+++ b/solution.py
@@ -187,41 +187,55 @@
     return (grad_in, grad_w_one, grad_w_two, grad_w_trans)
 
 
-def call(kernel, out_shape, scratch, flops, *args):
-    spec = [
-        pl.BlockSpec(memory_space=SMEM if a.dtype == jnp.int32 and a.ndim == 1 else VMEM)
-        for a in args
-    ]
-    outs = jax.tree.map(lambda _: pl.BlockSpec(memory_space=VMEM), out_shape)
+def call(kernel, out_shape, scratch, flops, limit, *args):
+    spec = []
+    for a in args:
+        if isinstance(a, tuple):
+            spec.append(pl.BlockSpec(memory_space=pltpu.MemorySpace.HBM))
+        elif a.dtype == jnp.int32:
+            spec.append(pl.BlockSpec(memory_space=SMEM))
+        else:
+            spec.append(pl.BlockSpec(memory_space=VMEM))
+    arrays = [a[0] if isinstance(a, tuple) else a for a in args]
     return pl.pallas_call(
         kernel,
         out_shape=out_shape,
         in_specs=spec,
-        out_specs=outs,
+        out_specs=jax.tree.map(lambda _: pl.BlockSpec(memory_space=VMEM), out_shape),
         scratch_shapes=scratch,
         cost_estimate=pl.CostEstimate(
-            flops=flops, transcendentals=0, bytes_accessed=sum(a.size * a.dtype.itemsize for a in args)
+            flops=flops,
+            transcendentals=0,
+            bytes_accessed=sum(a.size * a.dtype.itemsize for a in arrays),
         ),
-        compiler_params=pltpu.CompilerParams(vmem_limit_bytes=48 * 1024 * 1024),
-    )(*args)
-
-
-def transition_kernel(
-    factor, at_ref, a0, a1, a2, a3, w_ref, keep_ref, back_ref, one_ref, low_ref, high_ref, trans_ref, og_ref, two_ref
-):
-    me = at_ref[0]
-    parts = (a0, a1, a2, a3)
-    n = len(parts)
-    rows = a0.shape[0] // 3
-    for s, part in enumerate(parts):
-        src = lax.rem(me + n - s, n)
-        og_ref[src] = part[0:rows]
-        spot = pl.ds(src * 4, 4)
-        two_ref[spot] = part[rows : 2 * rows].reshape(4, rows // 4, 128)
-        one_ref[spot] = part[2 * rows : 3 * rows].reshape(4, rows // 4, 128)
-    og = jnp.concatenate([og_ref[j] for j in range(n)], axis=1)
-    width = w_ref.shape[0]
-    blocks = keep_ref.shape[0]
+        compiler_params=pltpu.CompilerParams(vmem_limit_bytes=limit * 1024 * 1024),
+    )(*arrays)
+
+
+def fetch(pairs, sems):
+    copies = [pltpu.make_async_copy(src, dst, sems.at[k]) for k, (src, dst) in enumerate(pairs)]
+    for copy in copies:
+        copy.start()
+    return copies
+
+
+def pack_kernel(og, two, one, act, first_ref, second_ref, og_v, two_v, one_v, act_v, turn_ref, sems):
+    copies = fetch(((og, og_v), (two, two_v), (one, one_v), (act, act_v)), sems)
+    copies[0].wait()
+    first_ref[0:256] = og_v[...].astype(F32).reshape(256, 128).astype(BF16)
+    for k, (ref, out, at) in enumerate(((two_v, first_ref, 256), (one_v, first_ref, 512), (act_v, second_ref, 0))):
+        copies[k + 1].wait()
+        for x in range(4):
+            for t in range(8):
+                turn_ref[k, pl.ds(64 * x + t, 8, stride=8), :] = ref[x, :, 128 * t : 128 * t + 128].astype(F32)
+        out[at : at + 256] = turn_ref[k].astype(BF16)
+
+
+def weight_kernel(wt, keep, w2, w1, kept_ref, mask_ref, d2_ref, d1_ref, wt_v, keep_v, w2_v, w1_v, sems):
+    copies = fetch(((keep, keep_v), (wt, wt_v), (w2, w2_v), (w1, w1_v)), sems)
+    copies[0].wait()
+    width = wt_v.shape[0]
+    blocks = keep_v.shape[0]
     side = width // blocks
     left = (
         lax.broadcasted_iota(jnp.int32, (width, blocks), 0) // side
@@ -231,11 +245,35 @@
         lax.broadcasted_iota(jnp.int32, (blocks, width), 1) // side
         == lax.broadcasted_iota(jnp.int32, (blocks, width), 0)
     ).astype(BF16)
-    keep = keep_ref[...].astype(F32).astype(BF16)
-    wide = jnp.dot(keep, right, preferred_element_type=F32).astype(BF16)
+    wide = jnp.dot(keep_v[...].astype(F32).astype(BF16), right, preferred_element_type=F32).astype(BF16)
     mask = jnp.dot(left, wide, preferred_element_type=F32)
-    kept = (w_ref[...].astype(F32) * mask).astype(BF16)
-    back = lax.dot_general(og, kept, (((1,), (1,)), ((), ())), preferred_element_type=F32)
+    mask_ref[...] = mask.astype(BF16)
+    copies[1].wait()
+    kept_ref[...] = (wt_v[...].astype(F32) * mask).astype(BF16)
+    none = jnp.zeros((64, 64), BF16)
+    for k, (ref, out) in enumerate(((w2_v, d2_ref), (w1_v, d1_ref))):
+        copies[k + 2].wait()
+        for tap in range(27):
+            w = ref[tap]
+            at = 128 * (tap % 3)
+            out[tap // 3, 0:64, at : at + 128] = jnp.concatenate([w, none], axis=1)
+            out[tap // 3, 64:128, at : at + 128] = jnp.concatenate([none, w], axis=1)
+
+
+def transition_kernel(
+    factor, at_ref, a0, a1, a2, a3, kept_ref, mask_ref, back_ref, one_ref, low_ref, high_ref, mine_ref, send_ref, og_ref, two_ref
+):
+    me = at_ref[0]
+    parts = (a0, a1, a2, a3)
+    n = len(parts)
+    for s, part in enumerate(parts):
+        src = lax.rem(me + n - s, n)
+        og_ref[src] = part[0:256]
+        spot = pl.ds(src * 4, 4)
+        two_ref[spot] = part[256:512].reshape(4, 64, 128)
+        one_ref[spot] = part[512:768].reshape(4, 64, 128)
+    og = jnp.concatenate([og_ref[j] for j in range(n)], axis=1)
+    back = lax.dot_general(og, kept_ref[...], (((1,), (1,)), ((), ())), preferred_element_type=F32)
     two = two_ref[...].astype(F32).reshape(8, 2, 4, 2, 8, 128)
     cells = []
     for p in range(2):
@@ -247,13 +285,31 @@
             halves.append(jnp.where(pre > 0, grad, 0.0))
             cells.append(jnp.maximum(pre, 0.0).reshape(256, 128).astype(BF16))
         back_ref[:, p] = jnp.stack(halves, axis=2).reshape(8, 64, 128).astype(BF16)
-    flat = jnp.concatenate(cells, axis=1)
-    trans = lax.dot_general(flat, og, (((0,), (0,)), ((), ())), preferred_element_type=F32)
-    trans_ref[...] = trans * mask * factor
     low_ref[:, :, 0:32] = back_ref[:, :, 0:32]
     high_ref[:, :, 0:32] = back_ref[:, :, 32:64]
     low_ref[:, :, 32:48] = one_ref[:, 0:16].reshape(8, 2, 16, 128)
     high_ref[:, :, 32:48] = one_ref[:, 48:64].reshape(8, 2, 16, 128)
+    flat = jnp.concatenate(cells, axis=1)
+    trans = lax.dot_general(flat, og, (((0,), (0,)), ((), ())), preferred_element_type=F32)
+    trans = trans * mask_ref[...].astype(F32) * factor
+
+    def emit(half, ref):
+        for m in range(4):
+            ref[256 * m : 256 * m + 256] = trans[256 * half : 256 * half + 256, 128 * m : 128 * m + 128].astype(ref.dtype)
+
+    share(at_ref[1], emit, mine_ref, send_ref)
+
+
+def share(core, emit, mine_ref, send_ref):
+    @pl.when(core == 0)
+    def _():
+        emit(0, mine_ref)
+        emit(1, send_ref)
+
+    @pl.when(core != 0)
+    def _():
+        emit(1, mine_ref)
+        emit(0, send_ref)
 
 
 def triple(v):
@@ -266,7 +322,7 @@
     return wide.astype(BF16).reshape(x, rows, 384)
 
 
-def fold(sums, factor, out_ref, at):
+def fold(sums, factor):
     lane = lax.broadcasted_iota(jnp.int32, (64, 128), 1)
     taps = []
     for g in sums:
@@ -275,14 +331,16 @@
             f = jnp.where(lane < 64, part[0:64], part[64:128])
             taps.append((f + pltpu.roll(f, 64, 1)) * factor)
     taps.append(taps[-1])
-    for m in range(14):
-        row = at + (m % 7) * 64
-        out_ref[m // 7, row : row + 64] = jnp.where(lane < 64, taps[2 * m], taps[2 * m + 1])
+    return [jnp.where(lane < 64, taps[2 * m], taps[2 * m + 1]) for m in range(14)]
+
+
+def apply_taps(rows, taps):
+    return lax.dot_general(rows, taps, (((1,), (1,)), ((), ())), preferred_element_type=F32)
 
 
 def conv_kernel(
-    factor, at_ref, back_ref, one_ref, left_ref, right_ref, w2_ref, w1_ref, i0, i1, i2, i3, trans_ref,
-    grad_ref, sums_ref, wide_ref, outer_ref, in_ref, acc_ref,
+    factor, at_ref, back_ref, one_ref, left_ref, right_ref, w2_ref, w1_ref, i0, i1, i2, i3,
+    grad_ref, mine_ref, send_ref, wide_ref, outer_ref, in_ref, acc_ref, turn_ref,
 ):
     me = at_ref[0]
     parts = (i0, i1, i2, i3)
@@ -300,21 +358,20 @@
     for i in range(3):
         for j in range(3):
             rows = wide_ref[4 - 2 * i : 20 - 2 * i, 32 - 16 * j : 128 - 16 * j].reshape(1536, 384)
-            part = jnp.dot(rows, w2_ref[i * 3 + j], preferred_element_type=F32)
+            part = apply_taps(rows, w2_ref[i * 3 + j])
             if i == 0 and j == 0:
                 acc_ref[...] = part
             else:
                 acc_ref[...] += part
     pre = jnp.concatenate([left_ref[:, 32:48], one_ref[...], right_ref[:, 32:48]], axis=1).astype(F32)
-    first = jnp.where(pre > 0, acc_ref[...].reshape(16, 96, 128), 0.0)
-    outer_ref[2:18] = triple(first)
+    outer_ref[2:18] = triple(jnp.where(pre > 0, acc_ref[...].reshape(16, 96, 128), 0.0))
     act = jnp.maximum(one_ref[...].astype(F32), 0.0).reshape(1024, 128).T.astype(BF16)
     sums = []
     for i in range(3):
         for j in range(3):
             rows = wide_ref[4 - 2 * i : 20 - 2 * i, 48 - 16 * j : 112 - 16 * j].reshape(1024, 384)
             sums.append(jnp.dot(act, rows, preferred_element_type=F32))
-    fold(sums, factor, sums_ref, 448)
+    second = fold(sums, factor)
     act = in_ref[...].astype(F32).reshape(1024, 128).T.astype(BF16)
     sums = []
     grad = jnp.zeros((256, 128), F32)
@@ -323,47 +380,42 @@
             rows = outer_ref[4 - 2 * i : 20 - 2 * i, 32 - 16 * j : 96 - 16 * j].reshape(1024, 384)
             sums.append(jnp.dot(act, rows, preferred_element_type=F32))
             mine = outer_ref[pl.ds(me * 4 + 4 - 2 * i, 4), 32 - 16 * j : 96 - 16 * j].reshape(256, 384)
-            grad += jnp.dot(mine, w1_ref[i * 3 + j], preferred_element_type=F32)
-    fold(sums, factor, sums_ref, 0)
-    grad_ref[...] = grad.reshape(4, 64, 128).astype(BF16)
-    for h in range(2):
+            grad += apply_taps(mine, w1_ref[i * 3 + j])
+    first = fold(sums, factor)
+    turn_ref[...] = grad
+    for x in range(4):
+        for t in range(8):
+            grad_ref[x, :, 128 * t : 128 * t + 128] = turn_ref[pl.ds(64 * x + t, 8, stride=8), :].astype(BF16)
+
+    def emit(half, ref):
+        for m in range(7):
+            ref[64 * m : 64 * m + 64] = first[7 * half + m].astype(ref.dtype)
+            ref[448 + 64 * m : 512 + 64 * m] = second[7 * half + m].astype(ref.dtype)
+
+    share(at_ref[1], emit, mine_ref, send_ref)
+
+
+def spread_kernel(at_ref, mine_ref, other_ref, tmine_ref, tother_ref, one_ref, two_ref, trans_ref):
+    def emit(half, ref, tref):
+        for out, at in ((one_ref, 0), (two_ref, 448)):
+            for m in range(7):
+                block = ref[at + 64 * m : at + 64 * m + 64].astype(F32)
+                tap = 2 * (7 * half + m)
+                out[tap] = block[:, 0:64]
+                if tap < 26:
+                    out[tap + 1] = block[:, 64:128]
         for m in range(4):
-            sums_ref[h, 896 + 256 * m : 1152 + 256 * m] = trans_ref[
-                256 * h : 256 * h + 256, 128 * m : 128 * m + 128
-            ]
-
-
-def spread_kernel(at_ref, mine_ref, other_ref, one_ref, two_ref, trans_ref):
-    def emit(low_ref, high_ref):
-        for h, ref in enumerate((low_ref, high_ref)):
-            for out, at in ((one_ref, 0), (two_ref, 448)):
-                for m in range(7):
-                    block = ref[at + 64 * m : at + 64 * m + 64]
-                    tap = 2 * (7 * h + m)
-                    out[tap] = block[:, 0:64]
-                    if tap < 26:
-                        out[tap + 1] = block[:, 64:128]
-            for m in range(4):
-                trans_ref[256 * h : 256 * h + 256, 128 * m : 128 * m + 128] = ref[
-                    896 + 256 * m : 1152 + 256 * m
-                ]
-
-    @pl.when(at_ref[0] == 0)
+            trans_ref[256 * half : 256 * half + 256, 128 * m : 128 * m + 128] = tref[256 * m : 256 * m + 256].astype(F32)
+
+    @pl.when(at_ref[1] == 0)
     def _():
-        emit(mine_ref, other_ref)
-
-    @pl.when(at_ref[0] != 0)
+        emit(0, mine_ref, tmine_ref)
+        emit(1, other_ref, tother_ref)
+
+    @pl.when(at_ref[1] != 0)
     def _():
-        emit(other_ref, mine_ref)
-
-
-def twin(weights):
-    turned = jnp.transpose(weights, (0, 2, 1))
-    none = jnp.zeros_like(turned)
-    both = jnp.concatenate(
-        [jnp.concatenate([turned, none], axis=2), jnp.concatenate([none, turned], axis=2)], axis=1
-    )
-    return both.reshape(9, 384, 128)
+        emit(1, mine_ref, tmine_ref)
+        emit(0, other_ref, tother_ref)
 
 
 def rotate(value, axis, step):
@@ -376,74 +428,118 @@
     return lax.ppermute(value, axis, [(i, i ^ bit) for i in range(n)])
 
 
+def on_chip(mine, send):
+    return (mine + swap(send, "gy", 1).astype(F32)).astype(BF16)
+
+
+def across(mine):
+    return mine.astype(F32) + swap(mine, "gy", 2).astype(F32)
+
+
 def slab_body(input_activation, pre_one, pre_two, w_one, w_two, w_trans, keep_mask, out_grad):
     factor = 1.0 / math.sqrt(
         input_activation.shape[0] * 4 * input_activation.shape[1] * 4 * (input_activation.shape[2] // 64)
     )
-    gx = lax.axis_index("gx").astype(jnp.int32)
-    gy = lax.axis_index("gy").astype(jnp.int32)
-    core = lax.rem(gy, 2)
-    first = jnp.concatenate(
-        [out_grad.reshape(256, 128), pre_two.reshape(256, 128), pre_one.reshape(256, 128)], axis=0
+    at = jnp.stack([lax.axis_index("gx"), lax.rem(lax.axis_index("gy"), 2)]).astype(jnp.int32)
+    shape = jax.ShapeDtypeStruct
+    vmem = pltpu.VMEM
+    natural = vmem((4, 8, 1024), BF16)
+    first, second = call(
+        pack_kernel,
+        (shape((768, 128), BF16), shape((256, 128), BF16)),
+        [
+            vmem((8, 4, 8, 128), BF16), natural, natural, natural, vmem((3, 256, 128), F32),
+            pltpu.SemaphoreType.DMA((4,)),
+        ],
+        0,
+        56,
+        (out_grad,),
+        (pre_two,),
+        (pre_one,),
+        (input_activation,),
     )
     firsts = [first] + [rotate(first, "gx", s) for s in (1, 2, 3)]
-    second = input_activation.reshape(256, 128)
     seconds = [second] + [rotate(second, "gx", s) for s in (1, 2, 3)]
-    shape = jax.ShapeDtypeStruct
-    back, one, low, high, trans = call(
+    kept, mask, d2, d1 = call(
+        weight_kernel,
+        (
+            shape((512, 512), BF16), shape((512, 512), BF16),
+            shape((9, 128, 384), BF16), shape((9, 128, 384), BF16),
+        ),
+        [
+            vmem((512, 512), BF16), vmem((8, 8), jnp.int32),
+            vmem((27, 64, 64), BF16), vmem((27, 64, 64), BF16),
+            pltpu.SemaphoreType.DMA((4,)),
+        ],
+        10**7,
+        8,
+        (w_trans,),
+        (keep_mask,),
+        (w_two,),
+        (w_one,),
+    )
+    back, one, low, high, tmine, tsend = call(
         functools.partial(transition_kernel, factor),
         (
             shape((8, 2, 64, 128), BF16),
             shape((16, 64, 128), BF16),
             shape((8, 2, 48, 128), BF16),
             shape((8, 2, 48, 128), BF16),
-            shape((512, 512), F32),
+            shape((1024, 128), F32),
+            shape((1024, 128), BF16),
         ),
-        [pltpu.VMEM((4, 256, 128), BF16), pltpu.VMEM((16, 64, 128), BF16)],
+        [vmem((4, 256, 128), BF16), vmem((16, 64, 128), BF16)],
         4 * 256 * 512 * 512,
-        gx.reshape(1),
+        12,
+        at,
         *firsts,
-        w_trans,
-        keep_mask,
+        kept,
+        mask,
     )
     n = lax.axis_size("gy")
     from_left = lax.ppermute(high, "gy", [(i, i + 1) for i in range(n - 1)])
     from_right = lax.ppermute(low, "gy", [(i + 1, i) for i in range(n - 1)])
-    grad_in, sums = call(
+    tmine = on_chip(tmine, tsend)
+    tmine, from_left, from_right = lax.optimization_barrier((tmine, from_left, from_right))
+    tmine = across(tmine)
+    grad_in, mine, send = call(
         functools.partial(conv_kernel, factor),
-        (shape((4, 64, 128), BF16), shape((2, 1920, 128), F32)),
+        (shape((4, 8, 1024), BF16), shape((896, 128), F32), shape((896, 128), BF16)),
         [
-            pltpu.VMEM((20, 128, 384), BF16),
-            pltpu.VMEM((20, 96, 384), BF16),
-            pltpu.VMEM((16, 64, 128), BF16),
-            pltpu.VMEM((1536, 128), F32),
+            vmem((20, 128, 384), BF16),
+            vmem((20, 96, 384), BF16),
+            vmem((16, 64, 128), BF16),
+            vmem((1536, 128), F32),
+            vmem((256, 128), F32),
         ],
         2 * 128 * 3456 * (1536 + 1024 + 1024 + 256),
-        gx.reshape(1),
+        20,
+        at,
         back.reshape(16, 64, 128),
         one,
         from_left.reshape(16, 48, 128),
         from_right.reshape(16, 48, 128),
-        twin(w_two),
-        twin(w_one),
+        d2,
+        d1,
         *seconds,
-        trans,
-    )
-    mine = lax.dynamic_index_in_dim(sums, core, 0, keepdims=False)
-    other = lax.dynamic_index_in_dim(sums, 1 - core, 0, keepdims=False)
-    mine = (mine + swap(other, "gy", 1)).astype(BF16)
-    mine = mine.astype(F32) + swap(mine, "gy", 2).astype(F32)
+    )
+    send, tmine = lax.optimization_barrier((send, tmine))
+    mine = across(on_chip(mine, send))
+    tother = swap(tmine, "gy", 1)
     other = swap(mine, "gy", 1)
     grad_w_one, grad_w_two, grad_w_trans = call(
         spread_kernel,
         (shape((27, 64, 64), F32), shape((27, 64, 64), F32), shape((512, 512), F32)),
         [],
         0,
-        core.reshape(1),
+        12,
+        at,
         mine,
         other,
-    )
-    return (grad_in.reshape(input_activation.shape), grad_w_one, grad_w_two, grad_w_trans)
+        tmine,
+        tother,
+    )
+    return (grad_in, grad_w_one, grad_w_two, grad_w_trans)
 
 
 def solution(mesh):

time: 82.5 us -> 61.5 us (0.75)
  the two profiles are of different devices: /device:TPU:27 before, /device:TPU:0 now
where the time goes in v2:
time: 61.5 us; the launch traced here: 61.2 us
  starting transfers between devices  23.3 us (38%)
  waiting for transfers between devices  18.8 us (31%)
  Pallas kernels  14.2 us (23%)
  local copies, waits for them, and re-layouts  3.76 us (6%)
  between operations  0.76 us (1%)
    pallas_call x5, Pallas kernels, call(): pl.pallas_call(kernel, out_shape=out_shape, in_specs=spec, out_specs=jax....  14.2 us
    ppermute x6, starting transfers between devices, rotate(): return lax.ppermute(value, axis, [(i, (i + step) % n) for i in range(n)])  14.2 us
    ppermute x6, waiting for transfers between devices, swap(): return lax.ppermute(value, axis, [(i, i ^ bit) for i in range(n)])  9.06 us
    ppermute x6, waiting for transfers between devices, rotate(): return lax.ppermute(value, axis, [(i, (i + step) % n) for i in range(n)])  6.49 us
    ppermute x6, starting transfers between devices, swap(): return lax.ppermute(value, axis, [(i, i ^ bit) for i in range(n)])  6.17 us
    unnamed x12, local copies, waits for them, and re-layouts  3.76 us
    ppermute x1, waiting for transfers between devices, slab_body(): from_right = lax.ppermute(low, 'gy', [(i + 1, i) for i in range(n - 1)])  3.23 us
    ppermute x1, starting transfers between devices, slab_body(): from_left = lax.ppermute(high, 'gy', [(i, i + 1) for i in range(n - 1)])  1.69 us
  transfers between devices with their start and end apart: 14, of which 5 were waited for; matrix products, arithmetic and copies ran while one was open for 0% of the time, Pallas kernels for 15%

profile of v2, /device:TPU:0, one launch (start us, length us, event | category | flops | bytes accessed | tf_op | source)
XLA Modules:
  0.0 61.2 jit_solution(5268101273394666928)
XLA Ops:
  0.6 1.7 %shard_map.111 = (bf16[768,128]{1,0:T(8,128)(2,1)}, bf16[256,128]{1,0:T(8,128)(2,1)}) custom-call(bf16[8,4,8,128]{3,2,1,0:T(8,128)(2,1)} %og.1, bf16[4,8,1024]{2,1,0:T(8,128)(2,1)} %two.1, bf16[4,8,1024]{2,1,0:T(8,128)(2,1)} %one.1, bf16[4,8,1024]{2,1,0:T(8,128)(2,1)} %act.1), custom_call_target="tpu_custom_call" | custom-call | bytes 262144 | tf_op jit(solution)/shard_map/pallas_call | solution.py:200
  2.3 3.1 %collective-permute-start = (bf16[768,128]{1,0:T(8,128)(2,1)}, bf16[768,128]{1,0:T(8,128)(2,1)S(1)}, u32[]{:S(2)}, u32[]{:S(2)}) collective-permute-start(bf16[768,128]{1,0:T(8,128)(2,1)} %get-tuple-element.27.a0), channel_id=1, source_target_pairs={{0,4},{4,8},{8,12},{12,0},{1,5},{5,9},{9,13},{13,1},{2,6},{6,10},{... | collective-permute-start | bytes 589832 | tf_op jit(solution)/shard_map/ppermute | solution.py:423
  5.4 2.6 %collective-permute-start.1 = (bf16[768,128]{1,0:T(8,128)(2,1)}, bf16[768,128]{1,0:T(8,128)(2,1)S(1)}, u32[]{:S(2)}, u32[]{:S(2)}) collective-permute-start(bf16[768,128]{1,0:T(8,128)(2,1)} %get-tuple-element.27.a0), channel_id=1, source_target_pairs={{0,8},{4,12},{8,0},{12,4},{1,9},{5,13},{9,1},{13,5},{2,10},{6,14},... | collective-permute-start | bytes 589832 | tf_op jit(solution)/shard_map/ppermute | solution.py:423
  8.0 1.3 %collective-permute-start.2 = (bf16[768,128]{1,0:T(8,128)(2,1)}, bf16[768,128]{1,0:T(8,128)(2,1)S(1)}, u32[]{:S(2)}, u32[]{:S(2)}) collective-permute-start(bf16[768,128]{1,0:T(8,128)(2,1)} %get-tuple-element.27.a0), channel_id=1, source_target_pairs={{0,12},{4,0},{8,4},{12,8},{1,13},{5,1},{9,5},{13,9},{2,14},{6,2},{... | collective-permute-start | bytes 589832 | tf_op jit(solution)/shard_map/ppermute | solution.py:423
  9.3 0.0 copy-start.4
  9.3 0.7 %copy-done.4 = s32[8,8]{1,0:T(8,128)S(1)} copy-done((s32[8,8]{1,0:T(8,128)S(1)}, s32[8,8]{1,0:T(8,128)}, u32[]{:S(2)}) %copy-start.4) | copy-done | bytes 280
  10.0 0.0 copy-start
  10.0 1.0 %copy-done = bf16[512,512]{1,0:T(8,128)(2,1)S(1)} copy-done((bf16[512,512]{1,0:T(8,128)(2,1)S(1)}, bf16[512,512]{1,0:T(8,128)(2,1)}, u32[]{:S(2)}) %copy-start) | copy-done | bytes 524312
  11.0 0.0 copy-start.1
  11.0 1.0 %copy-done.1 = bf16[27,64,64]{2,1,0:T(8,128)(2,1)S(1)} copy-done((bf16[27,64,64]{2,1,0:T(8,128)(2,1)S(1)}, bf16[27,64,64]{2,1,0:T(8,128)(2,1)}, u32[]{:S(2)}) %copy-start.1) | copy-done | bytes 221208
  12.1 0.0 copy-start.2
  12.1 1.0 %copy-done.2 = bf16[27,64,64]{2,1,0:T(8,128)(2,1)S(1)} copy-done((bf16[27,64,64]{2,1,0:T(8,128)(2,1)S(1)}, bf16[27,64,64]{2,1,0:T(8,128)(2,1)}, u32[]{:S(2)}) %copy-start.2) | copy-done | bytes 221208
  13.1 0.0 copy-start.3
  13.1 1.4 %shard_map.112 = (bf16[512,512]{1,0:T(8,128)(2,1)S(1)}, bf16[512,512]{1,0:T(8,128)(2,1)S(1)}, bf16[9,128,384]{2,1,0:T(8,128)(2,1)S(1)}, bf16[9,128,384]{2,1,0:T(8,128)(2,1)S(1)}) custom-call(bf16[512,512]{1,0:T(8,128)(2,1)S(1)} %copy-done, s32[8,8]{1,0:T(8,128)S(1)} %copy-done.4, bf16[27,64,64]{2,1,0:T(8,128)(2,1)S(1)} %copy-done.1, ...), custom_call_target="tpu_custom_call" | custom-call | flops 10000000 | bytes 966912 | tf_op jit(solution)/shard_map/pallas_call | solution.py:200
  14.5 0.1 pad_add_fusion.at_ref
  14.6 0.0 collective-permute-done.a1
  14.6 6.5 %collective-permute-done.1.a2 = bf16[768,128]{1,0:T(8,128)(2,1)S(1)} collective-permute-done((bf16[768,128]{1,0:T(8,128)(2,1)}, bf16[768,128]{1,0:T(8,128)(2,1)S(1)}, u32[]{:S(2)}, u32[]{:S(2)}) %collective-permute-start.1) | collective-permute-done | bytes 196640 | tf_op jit(solution)/shard_map/ppermute | solution.py:423
  21.1 0.0 collective-permute-done.2.a3
  21.1 0.0 copy-done.3
  21.1 0.0 copy-start.5
  21.1 1.2 %shard_map.113 = (bf16[8,2,64,128]{3,2,1,0:T(8,128)(2,1)S(1)}, bf16[16,64,128]{2,1,0:T(8,128)(2,1)S(1)}, bf16[8,2,48,128]{3,2,1,0:T(8,128)(2,1)S(1)}, bf16[8,2,4...) custom-call(s32[2]{0:T(128)S(1)} %pad_add_fusion.at_ref, ...), custom_call_target="tpu_custom_call" | custom-call | flops 268435456 | bytes 1835016 | tf_op jit(solution)/shard_map/pallas_call | solution.py:200
  22.3 0.1 collective-permute-start.3
  22.3 0.0 copy-done.5
  22.4 4.7 %collective-permute-start.6 = (bf16[256,128]{1,0:T(8,128)(2,1)S(1)}, bf16[256,128]{1,0:T(8,128)(2,1)S(1)}, u32[]{:S(2)}, u32[]{:S(2)}) collective-permute-start(bf16[256,128]{1,0:T(8,128)(2,1)S(1)} %copy-done.5), channel_id=1, source_target_pairs={{0,4},{4,8},{8,12},{12,0},{1,5},{5,9},{9,13},{13,1},{2,6},{6,10},{... | collective-permute-start | bytes 196616 | tf_op jit(solution)/shard_map/ppermute | solution.py:423
  27.1 1.6 %collective-permute-start.7 = (bf16[256,128]{1,0:T(8,128)(2,1)S(1)}, bf16[256,128]{1,0:T(8,128)(2,1)S(1)}, u32[]{:S(2)}, u32[]{:S(2)}) collective-permute-start(bf16[256,128]{1,0:T(8,128)(2,1)S(1)} %copy-done.5), channel_id=1, source_target_pairs={{0,8},{4,12},{8,0},{12,4},{1,9},{5,13},{9,1},{13,5},{2,10},{6,14},... | collective-permute-start | bytes 196616 | tf_op jit(solution)/shard_map/ppermute | solution.py:423
  28.7 0.8 %collective-permute-start.8 = (bf16[256,128]{1,0:T(8,128)(2,1)S(1)}, bf16[256,128]{1,0:T(8,128)(2,1)S(1)}, u32[]{:S(2)}, u32[]{:S(2)}) collective-permute-start(bf16[256,128]{1,0:T(8,128)(2,1)S(1)} %copy-done.5), channel_id=1, source_target_pairs={{0,12},{4,0},{8,4},{12,8},{1,13},{5,1},{9,5},{13,9},{2,14},{6,2},{... | collective-permute-start | bytes 196616 | tf_op jit(solution)/shard_map/ppermute | solution.py:423
  29.5 1.7 %collective-permute-start.4 = (bf16[8,2,48,128]{3,2,1,0:T(8,128)(2,1)S(1)}, bf16[8,2,48,128]{3,2,1,0:T(8,128)(2,1)S(1)}, u32[]{:S(2)}, u32[]{:S(2)}) collective-permute-start(bf16[8,2,48,128]{3,2,1,0:T(8,128)(2,1)S(1)} %get-tuple-element.34), channel_id=1, source_target_pairs={{0,1},{1,2},{2,3},{4,5},{5,6},{6,7},{8,9},{9,10},{10,11},{12,13},{... | collective-permute-start | bytes 589832 | tf_op jit(solution)/shard_map/ppermute | solution.py:500
  31.2 0.0 collective-permute-done.3
  31.2 1.3 %collective-permute-start.5 = (bf16[8,2,48,128]{3,2,1,0:T(8,128)(2,1)S(1)}, bf16[8,2,48,128]{3,2,1,0:T(8,128)(2,1)S(1)}, u32[]{:S(2)}, u32[]{:S(2)}) collective-permute-start(bf16[8,2,48,128]{3,2,1,0:T(8,128)(2,1)S(1)} %get-tuple-element.35), channel_id=1, source_target_pairs={{1,0},{2,1},{3,2},{5,4},{6,5},{7,6},{9,8},{10,9},{11,10},{13,12},{... | collective-permute-start | bytes 589832 | tf_op jit(solution)/shard_map/ppermute | solution.py:501
  32.5 0.1 add_convert_fusion
  32.6 0.0 collective-permute-done.4
  32.6 3.2 %collective-permute-done.5 = bf16[8,2,48,128]{3,2,1,0:T(8,128)(2,1)S(1)} collective-permute-done((bf16[8,2,48,128]{3,2,1,0:T(8,128)(2,1)S(1)}, bf16[8,2,48,128]{3,2,1,0:T(8,128)(2,1)S(1)}, u32[]{:S(2)}, u32[]{:S(2)}) %collective-permute-start.5) | collective-permute-done | bytes 196640 | tf_op jit(solution)/shard_map/ppermute | solution.py:501
  35.9 3.9 %collective-permute-start.9 = (bf16[1024,128]{1,0:T(8,128)(2,1)S(1)}, bf16[1024,128]{1,0:T(8,128)(2,1)S(1)}, u32[]{:S(2)}, u32[]{:S(2)}) collective-permute-start(bf16[1024,128]{1,0:T(8,128)(2,1)S(1)} %add_convert_fusion), channel_id=1, source_target_pairs={{0,2},{1,3},{2,0},{3,1},{4,6},{5,7},{6,4},{7,5},{8,10},{9,11},{10,... | collective-permute-start | bytes 786440 | tf_op jit(solution)/shard_map/ppermute | solution.py:428
  39.7 0.0 collective-permute-done.6.i1
  39.7 0.0 collective-permute-done.7.i2
  39.7 0.0 collective-permute-done.8.i3
  39.7 7.6 %shard_map.114 = (bf16[4,8,1024]{2,1,0:T(8,128)(2,1)}, f32[896,128]{1,0:T(8,128)S(1)}, bf16[896,128]{1,0:T(8,128)(2,1)S(1)}) custom-call(s32[2]{0:T(128)S(1)} %pad_add_fusion.at_ref, bf16[16,64,128]{2,1,0:T(8,128)(2,1)S(1)} %bitcast.5, bf16[16,64,128]{2,1,0:T(8,128)(2,1)S(1)} %get-tuple-element.31.one_ref, bf16[16,48,128]{2,1,0:T(8,128)(2,1)S(1)} %bitcast.6, ...), custom_call_target="tpu_custom_call" | custom-call | flops 3397386240 | bytes 2949128 | tf_op jit(solution)/shard_map/pallas_call | solution.py:200
  47.3 0.0 collective-permute-done.9
  47.3 0.1 convert_add_fusion.tmine_ref
  47.4 0.4 collective-permute-start.10
  47.7 1.2 %collective-permute-done.10 = bf16[896,128]{1,0:T(8,128)(2,1)S(1)} collective-permute-done((bf16[896,128]{1,0:T(8,128)(2,1)S(1)}, bf16[896,128]{1,0:T(8,128)(2,1)S(1)}, u32[]{:S(2)}, u32[]{:S(2)}) %collective-permute-start.10) | collective-permute-done | bytes 229408 | tf_op jit(solution)/shard_map/ppermute | solution.py:428
  49.0 1.7 %collective-permute-start.11 = (bf16[896,128]{1,0:T(8,128)(2,1)S(1)}, bf16[896,128]{1,0:T(8,128)(2,1)S(1)}, u32[]{:S(2)}, u32[]{:S(2)}) collective-permute-start(bf16[896,128]{1,0:T(8,128)(2,1)S(1)} %add_convert_fusion.1), channel_id=1, source_target_pairs={{0,2},{1,3},{2,0},{3,1},{4,6},{5,7},{6,4},{7,5},{8,10},{9,11},{10,... | collective-permute-start | bytes 688136 | tf_op jit(solution)/shard_map/ppermute | solution.py:428
  50.7 0.1 collective-permute-start.13
  50.8 6.1 %collective-permute-done.11 = bf16[896,128]{1,0:T(8,128)(2,1)S(1)} collective-permute-done((bf16[896,128]{1,0:T(8,128)(2,1)S(1)}, bf16[896,128]{1,0:T(8,128)(2,1)S(1)}, u32[]{:S(2)}, u32[]{:S(2)}) %collective-permute-start.11) | collective-permute-done | bytes 229408 | tf_op jit(solution)/shard_map/ppermute | solution.py:428
  56.9 0.1 collective-permute-start.12
  57.0 0.0 collective-permute-done.13.tother_ref
  57.0 1.8 %collective-permute-done.12.other_ref = f32[896,128]{1,0:T(8,128)S(1)} collective-permute-done((f32[896,128]{1,0:T(8,128)S(1)}, f32[896,128]{1,0:T(8,128)S(1)}, u32[]{:S(2)}, u32[]{:S(2)}) %collective-permute-start.12) | collective-permute-done | bytes 458784 | tf_op jit(solution)/shard_map/ppermute | solution.py:428
  58.8 2.4 %shard_map.115 = (f32[27,64,64]{2,1,0:T(8,128)}, f32[27,64,64]{2,1,0:T(8,128)}, f32[512,512]{1,0:T(8,128)}) custom-call(s32[2]{0:T(128)S(1)} %pad_add_fusion.at_ref, f32[896,128]{1,0:T(8,128)S(1)} %convert_add_fusion.1.mine_ref, f32[896,128]{1,0:T(8,128)S(1)} %collective-permute-done.12.other_ref, f32[1024,128]{1,0:T(8,128)S(1)} %convert_add_fusion.tmine_ref, ...), custom_call_target="tpu_custom_call" | custom-call | bytes 1966088 | tf_op jit(solution)/shard_map/pallas_call | solution.py:200
  (2 shorter events, 0.1 us)
Async XLA Ops:
  2.3 12.3 %collective-permute-start = (bf16[768,128]{1,0:T(8,128)(2,1)}, bf16[768,128]{1,0:T(8,128)(2,1)S(1)}, u32[]{:S(2)}, u32[]{:S(2)}) collective-permute-start(bf16[768,128]{1,0:T(8,128)(2,1)} %get-tuple-element.27.a0), channel_id=1, source_target_pairs={{0,4},{4,8},{8,12},{12,0},{1,5},{5,9},{9,13},{13,1},{2,6},{6,10},{... | collective-permute-start | bytes 589832 | tf_op jit(solution)/shard_map/ppermute | solution.py:423
  5.4 15.7 %collective-permute-start.1 = (bf16[768,128]{1,0:T(8,128)(2,1)}, bf16[768,128]{1,0:T(8,128)(2,1)S(1)}, u32[]{:S(2)}, u32[]{:S(2)}) collective-permute-start(bf16[768,128]{1,0:T(8,128)(2,1)} %get-tuple-element.27.a0), channel_id=1, source_target_pairs={{0,8},{4,12},{8,0},{12,4},{1,9},{5,13},{9,1},{13,5},{2,10},{6,14},... | collective-permute-start | bytes 589832 | tf_op jit(solution)/shard_map/ppermute | solution.py:423
  8.0 13.1 %collective-permute-start.2 = (bf16[768,128]{1,0:T(8,128)(2,1)}, bf16[768,128]{1,0:T(8,128)(2,1)S(1)}, u32[]{:S(2)}, u32[]{:S(2)}) collective-permute-start(bf16[768,128]{1,0:T(8,128)(2,1)} %get-tuple-element.27.a0), channel_id=1, source_target_pairs={{0,12},{4,0},{8,4},{12,8},{1,13},{5,1},{9,5},{13,9},{2,14},{6,2},{... | collective-permute-start | bytes 589832 | tf_op jit(solution)/shard_map/ppermute | solution.py:423
  9.3 0.7 %copy-start.4 = (s32[8,8]{1,0:T(8,128)S(1)}, s32[8,8]{1,0:T(8,128)}, u32[]{:S(2)}) copy-start(s32[8,8]{1,0:T(8,128)} %keep.1) | copy-start | bytes 772
  10.0 1.0 %copy-start = (bf16[512,512]{1,0:T(8,128)(2,1)S(1)}, bf16[512,512]{1,0:T(8,128)(2,1)}, u32[]{:S(2)}) copy-start(bf16[512,512]{1,0:T(8,128)(2,1)} %wt.1) | copy-start | bytes 1572868
  11.0 1.0 %copy-start.1 = (bf16[27,64,64]{2,1,0:T(8,128)(2,1)S(1)}, bf16[27,64,64]{2,1,0:T(8,128)(2,1)}, u32[]{:S(2)}) copy-start(bf16[27,64,64]{2,1,0:T(8,128)(2,1)} %w2.1) | copy-start | bytes 663556
  12.1 1.0 %copy-start.2 = (bf16[27,64,64]{2,1,0:T(8,128)(2,1)S(1)}, bf16[27,64,64]{2,1,0:T(8,128)(2,1)}, u32[]{:S(2)}) copy-start(bf16[27,64,64]{2,1,0:T(8,128)(2,1)} %w1.1) | copy-start | bytes 663556
  13.1 8.0 %copy-start.3 = (bf16[768,128]{1,0:T(8,128)(2,1)S(1)}, bf16[768,128]{1,0:T(8,128)(2,1)}, u32[]{:S(2)}) copy-start(bf16[768,128]{1,0:T(8,128)(2,1)} %get-tuple-element.27.a0) | copy-start | bytes 589828
  21.1 1.3 %copy-start.5 = (bf16[256,128]{1,0:T(8,128)(2,1)S(1)}, bf16[256,128]{1,0:T(8,128)(2,1)}, u32[]{:S(2)}) copy-start(bf16[256,128]{1,0:T(8,128)(2,1)} %get-tuple-element.40.i0) | copy-start | bytes 196612
  22.3 9.0 %collective-permute-start.3 = (bf16[1024,128]{1,0:T(8,128)(2,1)S(1)}, bf16[1024,128]{1,0:T(8,128)(2,1)S(1)}, u32[]{:S(2)}, u32[]{:S(2)}) collective-permute-start(bf16[1024,128]{1,0:T(8,128)(2,1)S(1)} %get-tuple-element.33), channel_id=1, source_target_pairs={{0,1},{1,0},{2,3},{3,2},{4,5},{5,4},{6,7},{7,6},{8,9},{9,8},{10,11... | collective-permute-start | bytes 786440 | tf_op jit(solution)/shard_map/ppermute | solution.py:428
  22.4 17.4 %collective-permute-start.6 = (bf16[256,128]{1,0:T(8,128)(2,1)S(1)}, bf16[256,128]{1,0:T(8,128)(2,1)S(1)}, u32[]{:S(2)}, u32[]{:S(2)}) collective-permute-start(bf16[256,128]{1,0:T(8,128)(2,1)S(1)} %copy-done.5), channel_id=1, source_target_pairs={{0,4},{4,8},{8,12},{12,0},{1,5},{5,9},{9,13},{13,1},{2,6},{6,10},{... | collective-permute-start | bytes 196616 | tf_op jit(solution)/shard_map/ppermute | solution.py:423
  27.1 12.7 %collective-permute-start.7 = (bf16[256,128]{1,0:T(8,128)(2,1)S(1)}, bf16[256,128]{1,0:T(8,128)(2,1)S(1)}, u32[]{:S(2)}, u32[]{:S(2)}) collective-permute-start(bf16[256,128]{1,0:T(8,128)(2,1)S(1)} %copy-done.5), channel_id=1, source_target_pairs={{0,8},{4,12},{8,0},{12,4},{1,9},{5,13},{9,1},{13,5},{2,10},{6,14},... | collective-permute-start | bytes 196616 | tf_op jit(solution)/shard_map/ppermute | solution.py:423
  28.7 11.1 %collective-permute-start.8 = (bf16[256,128]{1,0:T(8,128)(2,1)S(1)}, bf16[256,128]{1,0:T(8,128)(2,1)S(1)}, u32[]{:S(2)}, u32[]{:S(2)}) collective-permute-start(bf16[256,128]{1,0:T(8,128)(2,1)S(1)} %copy-done.5), channel_id=1, source_target_pairs={{0,12},{4,0},{8,4},{12,8},{1,13},{5,1},{9,5},{13,9},{2,14},{6,2},{... | collective-permute-start | bytes 196616 | tf_op jit(solution)/shard_map/ppermute | solution.py:423
  29.5 3.1 %collective-permute-start.4 = (bf16[8,2,48,128]{3,2,1,0:T(8,128)(2,1)S(1)}, bf16[8,2,48,128]{3,2,1,0:T(8,128)(2,1)S(1)}, u32[]{:S(2)}, u32[]{:S(2)}) collective-permute-start(bf16[8,2,48,128]{3,2,1,0:T(8,128)(2,1)S(1)} %get-tuple-element.34), channel_id=1, source_target_pairs={{0,1},{1,2},{2,3},{4,5},{5,6},{6,7},{8,9},{9,10},{10,11},{12,13},{... | collective-permute-start | bytes 589832 | tf_op jit(solution)/shard_map/ppermute | solution.py:500
  31.2 4.6 %collective-permute-start.5 = (bf16[8,2,48,128]{3,2,1,0:T(8,128)(2,1)S(1)}, bf16[8,2,48,128]{3,2,1,0:T(8,128)(2,1)S(1)}, u32[]{:S(2)}, u32[]{:S(2)}) collective-permute-start(bf16[8,2,48,128]{3,2,1,0:T(8,128)(2,1)S(1)} %get-tuple-element.35), channel_id=1, source_target_pairs={{1,0},{2,1},{3,2},{5,4},{6,5},{7,6},{9,8},{10,9},{11,10},{13,12},{... | collective-permute-start | bytes 589832 | tf_op jit(solution)/shard_map/ppermute | solution.py:501
  35.9 11.5 %collective-permute-start.9 = (bf16[1024,128]{1,0:T(8,128)(2,1)S(1)}, bf16[1024,128]{1,0:T(8,128)(2,1)S(1)}, u32[]{:S(2)}, u32[]{:S(2)}) collective-permute-start(bf16[1024,128]{1,0:T(8,128)(2,1)S(1)} %add_convert_fusion), channel_id=1, source_target_pairs={{0,2},{1,3},{2,0},{3,1},{4,6},{5,7},{6,4},{7,5},{8,10},{9,11},{10,... | collective-permute-start | bytes 786440 | tf_op jit(solution)/shard_map/ppermute | solution.py:428
  47.4 1.6 %collective-permute-start.10 = (bf16[896,128]{1,0:T(8,128)(2,1)S(1)}, bf16[896,128]{1,0:T(8,128)(2,1)S(1)}, u32[]{:S(2)}, u32[]{:S(2)}) collective-permute-start(bf16[896,128]{1,0:T(8,128)(2,1)S(1)} %get-tuple-element.45), channel_id=1, source_target_pairs={{0,1},{1,0},{2,3},{3,2},{4,5},{5,4},{6,7},{7,6},{8,9},{9,8},{10,11... | collective-permute-start | bytes 688136 | tf_op jit(solution)/shard_map/ppermute | solution.py:428
  49.0 7.9 %collective-permute-start.11 = (bf16[896,128]{1,0:T(8,128)(2,1)S(1)}, bf16[896,128]{1,0:T(8,128)(2,1)S(1)}, u32[]{:S(2)}, u32[]{:S(2)}) collective-permute-start(bf16[896,128]{1,0:T(8,128)(2,1)S(1)} %add_convert_fusion.1), channel_id=1, source_target_pairs={{0,2},{1,3},{2,0},{3,1},{4,6},{5,7},{6,4},{7,5},{8,10},{9,11},{10,... | collective-permute-start | bytes 688136 | tf_op jit(solution)/shard_map/ppermute | solution.py:428
  50.7 6.3 %collective-permute-start.13 = (f32[1024,128]{1,0:T(8,128)S(1)}, f32[1024,128]{1,0:T(8,128)S(1)}, u32[]{:S(2)}, u32[]{:S(2)}) collective-permute-start(f32[1024,128]{1,0:T(8,128)S(1)} %convert_add_fusion.tmine_ref), channel_id=1, source_target_pairs={{0,1},{1,0},{2,3},{3,2},{4,5},{5,4},{6,7},{7,6},{8,9},{9,8},{10,11... | collective-permute-start | bytes 1572872 | tf_op jit(solution)/shard_map/ppermute | solution.py:428
  56.9 1.9 %collective-permute-start.12 = (f32[896,128]{1,0:T(8,128)S(1)}, f32[896,128]{1,0:T(8,128)S(1)}, u32[]{:S(2)}, u32[]{:S(2)}) collective-permute-start(f32[896,128]{1,0:T(8,128)S(1)} %convert_add_fusion.1.mine_ref), channel_id=1, source_target_pairs={{0,1},{1,0},{2,3},{3,2},{4,5},{5,4},{6,7},{7,6},{8,9},{9,8},{10,11... | collective-permute-start | bytes 1376264 | tf_op jit(solution)/shard_map/ppermute | solution.py:428

commit v3 on v2

--- a/solution.py
+++ b/solution.py
@@ -395,8 +395,8 @@
     share(at_ref[1], emit, mine_ref, send_ref)
 
 
-def spread_kernel(at_ref, mine_ref, other_ref, tmine_ref, tother_ref, one_ref, two_ref, trans_ref):
-    def emit(half, ref, tref):
+def spread_kernel(at_ref, mine_ref, other_ref, one_ref, two_ref):
+    def emit(half, ref):
         for out, at in ((one_ref, 0), (two_ref, 448)):
             for m in range(7):
                 block = ref[at + 64 * m : at + 64 * m + 64].astype(F32)
@@ -404,18 +404,16 @@
                 out[tap] = block[:, 0:64]
                 if tap < 26:
                     out[tap + 1] = block[:, 64:128]
+
+    share(at_ref[1], emit, mine_ref, other_ref)
+
+
+def trans_kernel(at_ref, mine_ref, other_ref, trans_ref):
+    def emit(half, ref):
         for m in range(4):
-            trans_ref[256 * half : 256 * half + 256, 128 * m : 128 * m + 128] = tref[256 * m : 256 * m + 256].astype(F32)
-
-    @pl.when(at_ref[1] == 0)
-    def _():
-        emit(0, mine_ref, tmine_ref)
-        emit(1, other_ref, tother_ref)
-
-    @pl.when(at_ref[1] != 0)
-    def _():
-        emit(1, mine_ref, tmine_ref)
-        emit(0, other_ref, tother_ref)
+            trans_ref[256 * half : 256 * half + 256, 128 * m : 128 * m + 128] = ref[256 * m : 256 * m + 256].astype(F32)
+
+    share(at_ref[1], emit, mine_ref, other_ref)
 
 
 def rotate(value, axis, step):
@@ -496,6 +494,7 @@
         kept,
         mask,
     )
+    tsend, *seconds = lax.optimization_barrier((tsend, *seconds))
     n = lax.axis_size("gy")
     from_left = lax.ppermute(high, "gy", [(i, i + 1) for i in range(n - 1)])
     from_right = lax.ppermute(low, "gy", [(i + 1, i) for i in range(n - 1)])
@@ -527,17 +526,16 @@
     mine = across(on_chip(mine, send))
     tother = swap(tmine, "gy", 1)
     other = swap(mine, "gy", 1)
-    grad_w_one, grad_w_two, grad_w_trans = call(
+    grad_w_trans = call(trans_kernel, shape((512, 512), F32), [], 10**7, 6, at, tmine, tother)
+    grad_w_one, grad_w_two = call(
         spread_kernel,
-        (shape((27, 64, 64), F32), shape((27, 64, 64), F32), shape((512, 512), F32)),
+        (shape((27, 64, 64), F32), shape((27, 64, 64), F32)),
         [],
         0,
-        12,
+        6,
         at,
         mine,
         other,
-        tmine,
-        tother,
     )
     return (grad_in, grad_w_one, grad_w_two, grad_w_trans)
 

time: 61.5 us -> 61.1 us (level)
  starting transfers between devices: 23.3 us -> 19.9 us
  waiting for transfers between devices: 18.8 us -> 21.3 us
  Pallas kernels: 14.2 us -> 15.5 us
  local copies, waits for them, and re-layouts: 3.76 us -> 3.08 us
    ppermute x6, waiting for transfers between devices: 6.49 us -> 11.4 us  [rotate(): return lax.ppermute(value, axis, [(i, (i + step) % n) for i in range(n)])]
    ppermute x6, starting transfers between devices: 14.2 us -> 10.1 us  [rotate(): return lax.ppermute(value, axis, [(i, (i + step) % n) for i in range(n)])]
    ppermute x6, waiting for transfers between devices: 9.06 us -> 7.41 us  [swap(): return lax.ppermute(value, axis, [(i, i ^ bit) for i in range(n)])]
    pallas_call x5 -> x6, Pallas kernels: 14.2 us -> 15.5 us  [call(): pl.pallas_call(kernel, out_shape=out_shape, in_specs=spec, out_specs=jax....]
    ppermute x1, waiting for transfers between devices: 3.23 us -> 2.49 us  [slab_body(): from_right = lax.ppermute(low, 'gy', [(i + 1, i) for i in range(n - 1)])]
    ppermute x1, starting transfers between devices: 1.69 us -> 2.41 us  [slab_body(): from_left = lax.ppermute(high, 'gy', [(i, i + 1) for i in range(n - 1)])]
    unnamed x12, local copies, waits for them, and re-layouts: 3.76 us -> 3.08 us
  transfers between devices with their start and end apart: 14 -> 14, of which waited for: 5 -> 8; matrix products, arithmetic and copies ran while one was open for 0% -> 0% of each run, Pallas kernels for 15% -> 19%
where the time goes in v3:
time: 61.1 us; the launch traced here: 60.8 us
  waiting for transfers between devices  21.3 us (35%)
  starting transfers between devices  19.9 us (33%)
  Pallas kernels  15.5 us (25%)
  local copies, waits for them, and re-layouts  3.08 us (5%)
  between operations  0.74 us (1%)
    pallas_call x6, Pallas kernels, call(): pl.pallas_call(kernel, out_shape=out_shape, in_specs=spec, out_specs=jax....  15.5 us
    ppermute x6, waiting for transfers between devices, rotate(): return lax.ppermute(value, axis, [(i, (i + step) % n) for i in range(n)])  11.4 us
    ppermute x6, starting transfers between devices, rotate(): return lax.ppermute(value, axis, [(i, (i + step) % n) for i in range(n)])  10.1 us
    ppermute x6, waiting for transfers between devices, swap(): return lax.ppermute(value, axis, [(i, i ^ bit) for i in range(n)])  7.41 us
    ppermute x6, starting transfers between devices, swap(): return lax.ppermute(value, axis, [(i, i ^ bit) for i in range(n)])  6.11 us
    unnamed x12, local copies, waits for them, and re-layouts  3.08 us
    ppermute x1, waiting for transfers between devices, slab_body(): from_right = lax.ppermute(low, 'gy', [(i + 1, i) for i in range(n - 1)])  2.49 us
    ppermute x1, starting transfers between devices, slab_body(): from_left = lax.ppermute(high, 'gy', [(i, i + 1) for i in range(n - 1)])  2.41 us
  transfers between devices with their start and end apart: 14, of which 8 were waited for; matrix products, arithmetic and copies ran while one was open for 0% of the time, Pallas kernels for 19%

profile of v3, /device:TPU:0, one launch (start us, length us, event | category | flops | bytes accessed | tf_op | source)
XLA Modules:
  0.0 60.8 jit_solution(14706653340337482071)
XLA Ops:
  0.6 1.7 %shard_map.111 = (bf16[768,128]{1,0:T(8,128)(2,1)}, bf16[256,128]{1,0:T(8,128)(2,1)}) custom-call(bf16[8,4,8,128]{3,2,1,0:T(8,128)(2,1)} %og.1, bf16[4,8,1024]{2,1,0:T(8,128)(2,1)} %two.1, bf16[4,8,1024]{2,1,0:T(8,128)(2,1)} %one.1, bf16[4,8,1024]{2,1,0:T(8,128)(2,1)} %act.1), custom_call_target="tpu_custom_call" | custom-call | bytes 262144 | tf_op jit(solution)/shard_map/pallas_call | solution.py:200
  2.3 3.1 %collective-permute-start = (bf16[768,128]{1,0:T(8,128)(2,1)}, bf16[768,128]{1,0:T(8,128)(2,1)S(1)}, u32[]{:S(2)}, u32[]{:S(2)}) collective-permute-start(bf16[768,128]{1,0:T(8,128)(2,1)} %get-tuple-element.31.a0), channel_id=1, source_target_pairs={{0,4},{4,8},{8,12},{12,0},{1,5},{5,9},{9,13},{13,1},{2,6},{6,10},{... | collective-permute-start | bytes 589832 | tf_op jit(solution)/shard_map/ppermute | solution.py:421
  5.4 2.6 %collective-permute-start.1 = (bf16[768,128]{1,0:T(8,128)(2,1)}, bf16[768,128]{1,0:T(8,128)(2,1)S(1)}, u32[]{:S(2)}, u32[]{:S(2)}) collective-permute-start(bf16[768,128]{1,0:T(8,128)(2,1)} %get-tuple-element.31.a0), channel_id=1, source_target_pairs={{0,8},{4,12},{8,0},{12,4},{1,9},{5,13},{9,1},{13,5},{2,10},{6,14},... | collective-permute-start | bytes 589832 | tf_op jit(solution)/shard_map/ppermute | solution.py:421
  8.0 1.3 %collective-permute-start.2 = (bf16[768,128]{1,0:T(8,128)(2,1)}, bf16[768,128]{1,0:T(8,128)(2,1)S(1)}, u32[]{:S(2)}, u32[]{:S(2)}) collective-permute-start(bf16[768,128]{1,0:T(8,128)(2,1)} %get-tuple-element.31.a0), channel_id=1, source_target_pairs={{0,12},{4,0},{8,4},{12,8},{1,13},{5,1},{9,5},{13,9},{2,14},{6,2},{... | collective-permute-start | bytes 589832 | tf_op jit(solution)/shard_map/ppermute | solution.py:421
  9.3 0.7 %collective-permute-start.3 = (bf16[256,128]{1,0:T(8,128)(2,1)}, bf16[256,128]{1,0:T(8,128)(2,1)S(1)}, u32[]{:S(2)}, u32[]{:S(2)}) collective-permute-start(bf16[256,128]{1,0:T(8,128)(2,1)} %get-tuple-element.46.i0), channel_id=1, source_target_pairs={{0,4},{4,8},{8,12},{12,0},{1,5},{5,9},{9,13},{13,1},{2,6},{6,10},{... | collective-permute-start | bytes 196616 | tf_op jit(solution)/shard_map/ppermute | solution.py:421
  10.0 0.3 collective-permute-start.4
  10.3 0.0 copy-start.4
  10.3 3.1 %collective-permute-done.a1 = bf16[768,128]{1,0:T(8,128)(2,1)S(1)} collective-permute-done((bf16[768,128]{1,0:T(8,128)(2,1)}, bf16[768,128]{1,0:T(8,128)(2,1)S(1)}, u32[]{:S(2)}, u32[]{:S(2)}) %collective-permute-start) | collective-permute-done | bytes 196640 | tf_op jit(solution)/shard_map/ppermute | solution.py:421
  13.5 2.1 %collective-permute-start.5 = (bf16[256,128]{1,0:T(8,128)(2,1)}, bf16[256,128]{1,0:T(8,128)(2,1)S(1)}, u32[]{:S(2)}, u32[]{:S(2)}) collective-permute-start(bf16[256,128]{1,0:T(8,128)(2,1)} %get-tuple-element.46.i0), channel_id=1, source_target_pairs={{0,12},{4,0},{8,4},{12,8},{1,13},{5,1},{9,5},{13,9},{2,14},{6,2},{... | collective-permute-start | bytes 196616 | tf_op jit(solution)/shard_map/ppermute | solution.py:421
  15.5 0.1 pad_add_fusion.at_ref
  15.6 0.0 copy-done.4
  15.6 0.0 copy-start
  15.6 1.0 %copy-done = bf16[512,512]{1,0:T(8,128)(2,1)S(1)} copy-done((bf16[512,512]{1,0:T(8,128)(2,1)S(1)}, bf16[512,512]{1,0:T(8,128)(2,1)}, u32[]{:S(2)}) %copy-start) | copy-done | bytes 524312
  16.6 0.0 copy-start.1
  16.7 1.0 %copy-done.1 = bf16[27,64,64]{2,1,0:T(8,128)(2,1)S(1)} copy-done((bf16[27,64,64]{2,1,0:T(8,128)(2,1)S(1)}, bf16[27,64,64]{2,1,0:T(8,128)(2,1)}, u32[]{:S(2)}) %copy-start.1) | copy-done | bytes 221208
  17.7 0.0 copy-start.2
  17.7 1.0 %copy-done.2 = bf16[27,64,64]{2,1,0:T(8,128)(2,1)S(1)} copy-done((bf16[27,64,64]{2,1,0:T(8,128)(2,1)S(1)}, bf16[27,64,64]{2,1,0:T(8,128)(2,1)}, u32[]{:S(2)}) %copy-start.2) | copy-done | bytes 221208
  18.7 1.4 %shard_map.112 = (bf16[512,512]{1,0:T(8,128)(2,1)S(1)}, bf16[512,512]{1,0:T(8,128)(2,1)S(1)}, bf16[9,128,384]{2,1,0:T(8,128)(2,1)S(1)}, bf16[9,128,384]{2,1,0:T(8,128)(2,1)S(1)}) custom-call(bf16[512,512]{1,0:T(8,128)(2,1)S(1)} %copy-done, s32[8,8]{1,0:T(8,128)S(1)} %copy-done.4, bf16[27,64,64]{2,1,0:T(8,128)(2,1)S(1)} %copy-done.1, ...), custom_call_target="tpu_custom_call" | custom-call | flops 10000000 | bytes 966912 | tf_op jit(solution)/shard_map/pallas_call | solution.py:200
  20.1 1.8 %collective-permute-done.1.a2 = bf16[768,128]{1,0:T(8,128)(2,1)S(1)} collective-permute-done((bf16[768,128]{1,0:T(8,128)(2,1)}, bf16[768,128]{1,0:T(8,128)(2,1)S(1)}, u32[]{:S(2)}, u32[]{:S(2)}) %collective-permute-start.1) | collective-permute-done | bytes 196640 | tf_op jit(solution)/shard_map/ppermute | solution.py:421
  21.9 0.0 collective-permute-done.2.a3
  21.9 0.0 copy-done.3
  22.0 1.2 %shard_map.113 = (bf16[8,2,64,128]{3,2,1,0:T(8,128)(2,1)S(1)}, bf16[16,64,128]{2,1,0:T(8,128)(2,1)S(1)}, bf16[8,2,48,128]{3,2,1,0:T(8,128)(2,1)S(1)}, bf16[8,2,4...) custom-call(s32[2]{0:T(128)S(1)} %pad_add_fusion.at_ref, ...), custom_call_target="tpu_custom_call" | custom-call | flops 268435456 | bytes 1835016 | tf_op jit(solution)/shard_map/pallas_call | solution.py:200
  23.1 0.2 collective-permute-done.3.i1
  23.3 6.2 %collective-permute-done.4.i2 = bf16[256,128]{1,0:T(8,128)(2,1)S(1)} collective-permute-done((bf16[256,128]{1,0:T(8,128)(2,1)}, bf16[256,128]{1,0:T(8,128)(2,1)S(1)}, u32[]{:S(2)}, u32[]{:S(2)}) %collective-permute-start.4) | collective-permute-done | bytes 65568 | tf_op jit(solution)/shard_map/ppermute | solution.py:421
  29.5 0.0 collective-permute-done.5.i3
  29.5 0.0 collective-permute-start.6
  29.5 2.4 %collective-permute-start.7 = (bf16[8,2,48,128]{3,2,1,0:T(8,128)(2,1)S(1)}, bf16[8,2,48,128]{3,2,1,0:T(8,128)(2,1)S(1)}, u32[]{:S(2)}, u32[]{:S(2)}) collective-permute-start(bf16[8,2,48,128]{3,2,1,0:T(8,128)(2,1)S(1)} %get-tuple-element.40), channel_id=1, source_target_pairs={{0,1},{1,2},{2,3},{4,5},{5,6},{6,7},{8,9},{9,10},{10,11},{12,13},{... | collective-permute-start | bytes 589832 | tf_op jit(solution)/shard_map/ppermute | solution.py:499
  32.0 1.3 %collective-permute-start.8 = (bf16[8,2,48,128]{3,2,1,0:T(8,128)(2,1)S(1)}, bf16[8,2,48,128]{3,2,1,0:T(8,128)(2,1)S(1)}, u32[]{:S(2)}, u32[]{:S(2)}) collective-permute-start(bf16[8,2,48,128]{3,2,1,0:T(8,128)(2,1)S(1)} %get-tuple-element.41), channel_id=1, source_target_pairs={{1,0},{2,1},{3,2},{5,4},{6,5},{7,6},{9,8},{10,9},{11,10},{13,12},{... | collective-permute-start | bytes 589832 | tf_op jit(solution)/shard_map/ppermute | solution.py:500
  33.3 0.0 collective-permute-done.6
  33.3 0.0 copy-start.5
  33.3 0.1 add_convert_fusion
  33.4 0.0 collective-permute-done.7
  33.4 2.5 %collective-permute-done.8 = bf16[8,2,48,128]{3,2,1,0:T(8,128)(2,1)S(1)} collective-permute-done((bf16[8,2,48,128]{3,2,1,0:T(8,128)(2,1)S(1)}, bf16[8,2,48,128]{3,2,1,0:T(8,128)(2,1)S(1)}, u32[]{:S(2)}, u32[]{:S(2)}) %collective-permute-start.8) | collective-permute-done | bytes 196640 | tf_op jit(solution)/shard_map/ppermute | solution.py:500
  35.9 3.9 %collective-permute-start.9 = (bf16[1024,128]{1,0:T(8,128)(2,1)S(1)}, bf16[1024,128]{1,0:T(8,128)(2,1)S(1)}, u32[]{:S(2)}, u32[]{:S(2)}) collective-permute-start(bf16[1024,128]{1,0:T(8,128)(2,1)S(1)} %add_convert_fusion), channel_id=1, source_target_pairs={{0,2},{1,3},{2,0},{3,1},{4,6},{5,7},{6,4},{7,5},{8,10},{9,11},{10,... | collective-permute-start | bytes 786440 | tf_op jit(solution)/shard_map/ppermute | solution.py:426
  39.7 0.0 copy-done.5
  39.7 7.6 %shard_map.114 = (bf16[4,8,1024]{2,1,0:T(8,128)(2,1)}, f32[896,128]{1,0:T(8,128)S(1)}, bf16[896,128]{1,0:T(8,128)(2,1)S(1)}) custom-call(s32[2]{0:T(128)S(1)} %pad_add_fusion.at_ref, bf16[16,64,128]{2,1,0:T(8,128)(2,1)S(1)} %bitcast.5, bf16[16,64,128]{2,1,0:T(8,128)(2,1)S(1)} %get-tuple-element.35.one_ref, bf16[16,48,128]{2,1,0:T(8,128)(2,1)S(1)} %bitcast.6, ...), custom_call_target="tpu_custom_call" | custom-call | flops 3397386240 | bytes 2949128 | tf_op jit(solution)/shard_map/pallas_call | solution.py:200
  47.3 0.0 collective-permute-done.9
  47.3 0.1 convert_add_fusion.mine_ref
  47.4 0.3 collective-permute-start.10
  47.7 1.2 %collective-permute-done.10 = bf16[896,128]{1,0:T(8,128)(2,1)S(1)} collective-permute-done((bf16[896,128]{1,0:T(8,128)(2,1)S(1)}, bf16[896,128]{1,0:T(8,128)(2,1)S(1)}, u32[]{:S(2)}, u32[]{:S(2)}) %collective-permute-start.10) | collective-permute-done | bytes 229408 | tf_op jit(solution)/shard_map/ppermute | solution.py:426
  49.0 1.7 %collective-permute-start.11 = (bf16[896,128]{1,0:T(8,128)(2,1)S(1)}, bf16[896,128]{1,0:T(8,128)(2,1)S(1)}, u32[]{:S(2)}, u32[]{:S(2)}) collective-permute-start(bf16[896,128]{1,0:T(8,128)(2,1)S(1)} %add_convert_fusion.1), channel_id=1, source_target_pairs={{0,2},{1,3},{2,0},{3,1},{4,6},{5,7},{6,4},{7,5},{8,10},{9,11},{10,... | collective-permute-start | bytes 688136 | tf_op jit(solution)/shard_map/ppermute | solution.py:426
  50.7 0.1 collective-permute-start.13
  50.8 6.0 %collective-permute-done.11 = bf16[896,128]{1,0:T(8,128)(2,1)S(1)} collective-permute-done((bf16[896,128]{1,0:T(8,128)(2,1)S(1)}, bf16[896,128]{1,0:T(8,128)(2,1)S(1)}, u32[]{:S(2)}, u32[]{:S(2)}) %collective-permute-start.11) | collective-permute-done | bytes 229408 | tf_op jit(solution)/shard_map/ppermute | solution.py:426
  56.9 0.1 collective-permute-start.12
  57.0 0.0 collective-permute-done.13.other_ref
  57.0 1.6 %shard_map.116 = f32[512,512]{1,0:T(8,128)} custom-call(s32[2]{0:T(128)S(1)} %pad_add_fusion.at_ref, f32[1024,128]{1,0:T(8,128)S(1)} %convert_add_fusion.mine_ref, f32[1024,128]{1,0:T(8,128)S(1)} %collective-permute-done.13.other_ref), custom_call_target="tpu_custom_call" | custom-call | flops 10000000 | bytes 1048584 | tf_op jit(solution)/shard_map/pallas_call | solution.py:200
  58.6 0.1 collective-permute-done.12.other_ref
  58.8 2.0 %shard_map.115 = (f32[27,64,64]{2,1,0:T(8,128)}, f32[27,64,64]{2,1,0:T(8,128)}) custom-call(s32[2]{0:T(128)S(1)} %pad_add_fusion.at_ref, f32[896,128]{1,0:T(8,128)S(1)} %convert_add_fusion.1.mine_ref, f32[896,128]{1,0:T(8,128)S(1)} %collective-permute-done.12.other_ref), custom_call_target="tpu_custom_call" | custom-call | bytes 917512 | tf_op jit(solution)/shard_map/pallas_call | solution.py:200
  (3 shorter events, 0.1 us)
Async XLA Ops:
  2.3 11.2 %collective-permute-start = (bf16[768,128]{1,0:T(8,128)(2,1)}, bf16[768,128]{1,0:T(8,128)(2,1)S(1)}, u32[]{:S(2)}, u32[]{:S(2)}) collective-permute-start(bf16[768,128]{1,0:T(8,128)(2,1)} %get-tuple-element.31.a0), channel_id=1, source_target_pairs={{0,4},{4,8},{8,12},{12,0},{1,5},{5,9},{9,13},{13,1},{2,6},{6,10},{... | collective-permute-start | bytes 589832 | tf_op jit(solution)/shard_map/ppermute | solution.py:421
  5.4 16.6 %collective-permute-start.1 = (bf16[768,128]{1,0:T(8,128)(2,1)}, bf16[768,128]{1,0:T(8,128)(2,1)S(1)}, u32[]{:S(2)}, u32[]{:S(2)}) collective-permute-start(bf16[768,128]{1,0:T(8,128)(2,1)} %get-tuple-element.31.a0), channel_id=1, source_target_pairs={{0,8},{4,12},{8,0},{12,4},{1,9},{5,13},{9,1},{13,5},{2,10},{6,14},... | collective-permute-start | bytes 589832 | tf_op jit(solution)/shard_map/ppermute | solution.py:421
  8.0 14.0 %collective-permute-start.2 = (bf16[768,128]{1,0:T(8,128)(2,1)}, bf16[768,128]{1,0:T(8,128)(2,1)S(1)}, u32[]{:S(2)}, u32[]{:S(2)}) collective-permute-start(bf16[768,128]{1,0:T(8,128)(2,1)} %get-tuple-element.31.a0), channel_id=1, source_target_pairs={{0,12},{4,0},{8,4},{12,8},{1,13},{5,1},{9,5},{13,9},{2,14},{6,2},{... | collective-permute-start | bytes 589832 | tf_op jit(solution)/shard_map/ppermute | solution.py:421
  9.3 14.0 %collective-permute-start.3 = (bf16[256,128]{1,0:T(8,128)(2,1)}, bf16[256,128]{1,0:T(8,128)(2,1)S(1)}, u32[]{:S(2)}, u32[]{:S(2)}) collective-permute-start(bf16[256,128]{1,0:T(8,128)(2,1)} %get-tuple-element.46.i0), channel_id=1, source_target_pairs={{0,4},{4,8},{8,12},{12,0},{1,5},{5,9},{9,13},{13,1},{2,6},{6,10},{... | collective-permute-start | bytes 196616 | tf_op jit(solution)/shard_map/ppermute | solution.py:421
  10.0 19.5 %collective-permute-start.4 = (bf16[256,128]{1,0:T(8,128)(2,1)}, bf16[256,128]{1,0:T(8,128)(2,1)S(1)}, u32[]{:S(2)}, u32[]{:S(2)}) collective-permute-start(bf16[256,128]{1,0:T(8,128)(2,1)} %get-tuple-element.46.i0), channel_id=1, source_target_pairs={{0,8},{4,12},{8,0},{12,4},{1,9},{5,13},{9,1},{13,5},{2,10},{6,14},... | collective-permute-start | bytes 196616 | tf_op jit(solution)/shard_map/ppermute | solution.py:421
  10.3 5.3 %copy-start.4 = (s32[8,8]{1,0:T(8,128)S(1)}, s32[8,8]{1,0:T(8,128)}, u32[]{:S(2)}) copy-start(s32[8,8]{1,0:T(8,128)} %keep.1) | copy-start | bytes 772
  13.5 16.1 %collective-permute-start.5 = (bf16[256,128]{1,0:T(8,128)(2,1)}, bf16[256,128]{1,0:T(8,128)(2,1)S(1)}, u32[]{:S(2)}, u32[]{:S(2)}) collective-permute-start(bf16[256,128]{1,0:T(8,128)(2,1)} %get-tuple-element.46.i0), channel_id=1, source_target_pairs={{0,12},{4,0},{8,4},{12,8},{1,13},{5,1},{9,5},{13,9},{2,14},{6,2},{... | collective-permute-start | bytes 196616 | tf_op jit(solution)/shard_map/ppermute | solution.py:421
  15.6 1.0 %copy-start = (bf16[512,512]{1,0:T(8,128)(2,1)S(1)}, bf16[512,512]{1,0:T(8,128)(2,1)}, u32[]{:S(2)}) copy-start(bf16[512,512]{1,0:T(8,128)(2,1)} %wt.1) | copy-start | bytes 1572868
  16.6 1.0 %copy-start.1 = (bf16[27,64,64]{2,1,0:T(8,128)(2,1)S(1)}, bf16[27,64,64]{2,1,0:T(8,128)(2,1)}, u32[]{:S(2)}) copy-start(bf16[27,64,64]{2,1,0:T(8,128)(2,1)} %w2.1) | copy-start | bytes 663556
  17.7 1.0 %copy-start.2 = (bf16[27,64,64]{2,1,0:T(8,128)(2,1)S(1)}, bf16[27,64,64]{2,1,0:T(8,128)(2,1)}, u32[]{:S(2)}) copy-start(bf16[27,64,64]{2,1,0:T(8,128)(2,1)} %w1.1) | copy-start | bytes 663556
  18.7 3.3 %copy-start.3 = (bf16[768,128]{1,0:T(8,128)(2,1)S(1)}, bf16[768,128]{1,0:T(8,128)(2,1)}, u32[]{:S(2)}) copy-start(bf16[768,128]{1,0:T(8,128)(2,1)} %get-tuple-element.31.a0) | copy-start | bytes 589828
  29.5 3.7 %collective-permute-start.6 = (bf16[1024,128]{1,0:T(8,128)(2,1)S(1)}, bf16[1024,128]{1,0:T(8,128)(2,1)S(1)}, u32[]{:S(2)}, u32[]{:S(2)}) collective-permute-start(bf16[1024,128]{1,0:T(8,128)(2,1)S(1)} %get-tuple-element.39), channel_id=1, source_target_pairs={{0,1},{1,0},{2,3},{3,2},{4,5},{5,4},{6,7},{7,6},{8,9},{9,8},{10,11... | collective-permute-start | bytes 786440 | tf_op jit(solution)/shard_map/ppermute | solution.py:426
  29.5 3.8 %collective-permute-start.7 = (bf16[8,2,48,128]{3,2,1,0:T(8,128)(2,1)S(1)}, bf16[8,2,48,128]{3,2,1,0:T(8,128)(2,1)S(1)}, u32[]{:S(2)}, u32[]{:S(2)}) collective-permute-start(bf16[8,2,48,128]{3,2,1,0:T(8,128)(2,1)S(1)} %get-tuple-element.40), channel_id=1, source_target_pairs={{0,1},{1,2},{2,3},{4,5},{5,6},{6,7},{8,9},{9,10},{10,11},{12,13},{... | collective-permute-start | bytes 589832 | tf_op jit(solution)/shard_map/ppermute | solution.py:499
  32.0 3.9 %collective-permute-start.8 = (bf16[8,2,48,128]{3,2,1,0:T(8,128)(2,1)S(1)}, bf16[8,2,48,128]{3,2,1,0:T(8,128)(2,1)S(1)}, u32[]{:S(2)}, u32[]{:S(2)}) collective-permute-start(bf16[8,2,48,128]{3,2,1,0:T(8,128)(2,1)S(1)} %get-tuple-element.41), channel_id=1, source_target_pairs={{1,0},{2,1},{3,2},{5,4},{6,5},{7,6},{9,8},{10,9},{11,10},{13,12},{... | collective-permute-start | bytes 589832 | tf_op jit(solution)/shard_map/ppermute | solution.py:500
  33.3 6.5 %copy-start.5 = (bf16[256,128]{1,0:T(8,128)(2,1)S(1)}, bf16[256,128]{1,0:T(8,128)(2,1)}, u32[]{:S(2)}) copy-start(bf16[256,128]{1,0:T(8,128)(2,1)} %get-tuple-element.46.i0) | copy-start | bytes 196612
  35.9 11.4 %collective-permute-start.9 = (bf16[1024,128]{1,0:T(8,128)(2,1)S(1)}, bf16[1024,128]{1,0:T(8,128)(2,1)S(1)}, u32[]{:S(2)}, u32[]{:S(2)}) collective-permute-start(bf16[1024,128]{1,0:T(8,128)(2,1)S(1)} %add_convert_fusion), channel_id=1, source_target_pairs={{0,2},{1,3},{2,0},{3,1},{4,6},{5,7},{6,4},{7,5},{8,10},{9,11},{10,... | collective-permute-start | bytes 786440 | tf_op jit(solution)/shard_map/ppermute | solution.py:426
  47.4 1.6 %collective-permute-start.10 = (bf16[896,128]{1,0:T(8,128)(2,1)S(1)}, bf16[896,128]{1,0:T(8,128)(2,1)S(1)}, u32[]{:S(2)}, u32[]{:S(2)}) collective-permute-start(bf16[896,128]{1,0:T(8,128)(2,1)S(1)} %get-tuple-element.54), channel_id=1, source_target_pairs={{0,1},{1,0},{2,3},{3,2},{4,5},{5,4},{6,7},{7,6},{8,9},{9,8},{10,11... | collective-permute-start | bytes 688136 | tf_op jit(solution)/shard_map/ppermute | solution.py:426
  49.0 7.9 %collective-permute-start.11 = (bf16[896,128]{1,0:T(8,128)(2,1)S(1)}, bf16[896,128]{1,0:T(8,128)(2,1)S(1)}, u32[]{:S(2)}, u32[]{:S(2)}) collective-permute-start(bf16[896,128]{1,0:T(8,128)(2,1)S(1)} %add_convert_fusion.1), channel_id=1, source_target_pairs={{0,2},{1,3},{2,0},{3,1},{4,6},{5,7},{6,4},{7,5},{8,10},{9,11},{10,... | collective-permute-start | bytes 688136 | tf_op jit(solution)/shard_map/ppermute | solution.py:426
  50.7 6.3 %collective-permute-start.13 = (f32[1024,128]{1,0:T(8,128)S(1)}, f32[1024,128]{1,0:T(8,128)S(1)}, u32[]{:S(2)}, u32[]{:S(2)}) collective-permute-start(f32[1024,128]{1,0:T(8,128)S(1)} %convert_add_fusion.mine_ref), channel_id=1, source_target_pairs={{0,1},{1,0},{2,3},{3,2},{4,5},{5,4},{6,7},{7,6},{8,9},{9,8},{10,11... | collective-permute-start | bytes 1572872 | tf_op jit(solution)/shard_map/ppermute | solution.py:426
  56.9 1.9 %collective-permute-start.12 = (f32[896,128]{1,0:T(8,128)S(1)}, f32[896,128]{1,0:T(8,128)S(1)}, u32[]{:S(2)}, u32[]{:S(2)}) collective-permute-start(f32[896,128]{1,0:T(8,128)S(1)} %convert_add_fusion.1.mine_ref), channel_id=1, source_target_pairs={{0,1},{1,0},{2,3},{3,2},{4,5},{5,4},{6,7},{7,6},{8,9},{9,8},{10,11... | collective-permute-start | bytes 1376264 | tf_op jit(solution)/shard_map/ppermute | solution.py:426

commit v4 on v3

--- a/solution.py
+++ b/solution.py
@@ -223,7 +223,7 @@
     copies = fetch(((og, og_v), (two, two_v), (one, one_v), (act, act_v)), sems)
     copies[0].wait()
     first_ref[0:256] = og_v[...].astype(F32).reshape(256, 128).astype(BF16)
-    for k, (ref, out, at) in enumerate(((two_v, first_ref, 256), (one_v, first_ref, 512), (act_v, second_ref, 0))):
+    for k, (ref, out, at) in enumerate(((two_v, first_ref, 256), (one_v, second_ref, 0), (act_v, second_ref, 256))):
         copies[k + 1].wait()
         for x in range(4):
             for t in range(8):
@@ -261,7 +261,7 @@
 
 
 def transition_kernel(
-    factor, at_ref, a0, a1, a2, a3, kept_ref, mask_ref, back_ref, one_ref, low_ref, high_ref, mine_ref, send_ref, og_ref, two_ref
+    factor, at_ref, a0, a1, a2, a3, kept_ref, mask_ref, back_ref, low_ref, high_ref, mine_ref, send_ref, og_ref, two_ref
 ):
     me = at_ref[0]
     parts = (a0, a1, a2, a3)
@@ -269,9 +269,7 @@
     for s, part in enumerate(parts):
         src = lax.rem(me + n - s, n)
         og_ref[src] = part[0:256]
-        spot = pl.ds(src * 4, 4)
-        two_ref[spot] = part[256:512].reshape(4, 64, 128)
-        one_ref[spot] = part[512:768].reshape(4, 64, 128)
+        two_ref[pl.ds(src * 4, 4)] = part[256:512].reshape(4, 64, 128)
     og = jnp.concatenate([og_ref[j] for j in range(n)], axis=1)
     back = lax.dot_general(og, kept_ref[...], (((1,), (1,)), ((), ())), preferred_element_type=F32)
     two = two_ref[...].astype(F32).reshape(8, 2, 4, 2, 8, 128)
@@ -285,10 +283,8 @@
             halves.append(jnp.where(pre > 0, grad, 0.0))
             cells.append(jnp.maximum(pre, 0.0).reshape(256, 128).astype(BF16))
         back_ref[:, p] = jnp.stack(halves, axis=2).reshape(8, 64, 128).astype(BF16)
-    low_ref[:, :, 0:32] = back_ref[:, :, 0:32]
-    high_ref[:, :, 0:32] = back_ref[:, :, 32:64]
-    low_ref[:, :, 32:48] = one_ref[:, 0:16].reshape(8, 2, 16, 128)
-    high_ref[:, :, 32:48] = one_ref[:, 48:64].reshape(8, 2, 16, 128)
+    low_ref[...] = back_ref[:, :, 0:16].reshape(16, 16, 128)
+    high_ref[...] = back_ref[:, :, 48:64].reshape(16, 16, 128)
     flat = jnp.concatenate(cells, axis=1)
     trans = lax.dot_general(flat, og, (((0,), (0,)), ((), ())), preferred_element_type=F32)
     trans = trans * mask_ref[...].astype(F32) * factor
@@ -338,50 +334,74 @@
     return lax.dot_general(rows, taps, (((1,), (1,)), ((), ())), preferred_element_type=F32)
 
 
-def conv_kernel(
-    factor, at_ref, back_ref, one_ref, left_ref, right_ref, w2_ref, w1_ref, i0, i1, i2, i3,
-    grad_ref, mine_ref, send_ref, wide_ref, outer_ref, in_ref, acc_ref, turn_ref,
-):
-    me = at_ref[0]
-    parts = (i0, i1, i2, i3)
-    n = len(parts)
-    for s, part in enumerate(parts):
-        in_ref[pl.ds(lax.rem(me + n - s, n) * 4, 4)] = part[...].reshape(4, 64, 128)
-    edge = jnp.zeros((2, 128, 384), BF16)
+def widen(wide_ref, left_ref, own_ref, right_ref):
+    edge = jnp.zeros((2, 96, 384), BF16)
     wide_ref[0:2] = edge
     wide_ref[18:20] = edge
-    outer_ref[0:2] = edge[:, :96]
-    outer_ref[18:20] = edge[:, :96]
-    wide_ref[2:18, 0:32] = triple(left_ref[:, 0:32].astype(F32))
-    wide_ref[2:18, 32:96] = triple(back_ref[...].astype(F32))
-    wide_ref[2:18, 96:128] = triple(right_ref[:, 0:32].astype(F32))
+    wide_ref[2:18, 0:16] = triple(left_ref[...].astype(F32))
+    wide_ref[2:18, 16:80] = triple(own_ref[...].astype(F32))
+    wide_ref[2:18, 80:96] = triple(right_ref[...].astype(F32))
+
+
+def weight_sums(act, wide_ref):
+    turned = act.T.astype(BF16)
+    sums = []
     for i in range(3):
         for j in range(3):
-            rows = wide_ref[4 - 2 * i : 20 - 2 * i, 32 - 16 * j : 128 - 16 * j].reshape(1536, 384)
-            part = apply_taps(rows, w2_ref[i * 3 + j])
+            rows = wide_ref[4 - 2 * i : 20 - 2 * i, 32 - 16 * j : 96 - 16 * j].reshape(1024, 384)
+            sums.append(jnp.dot(turned, rows, preferred_element_type=F32))
+    return sums
+
+
+def first_kernel(back_ref, left_ref, right_ref, w_ref, wide_ref, acc_ref):
+    widen(wide_ref, left_ref, back_ref, right_ref)
+    for i in range(3):
+        for j in range(3):
+            rows = wide_ref[4 - 2 * i : 20 - 2 * i, 32 - 16 * j : 96 - 16 * j].reshape(1024, 384)
+            part = apply_taps(rows, w_ref[i * 3 + j])
             if i == 0 and j == 0:
                 acc_ref[...] = part
             else:
                 acc_ref[...] += part
-    pre = jnp.concatenate([left_ref[:, 32:48], one_ref[...], right_ref[:, 32:48]], axis=1).astype(F32)
-    outer_ref[2:18] = triple(jnp.where(pre > 0, acc_ref[...].reshape(16, 96, 128), 0.0))
-    act = jnp.maximum(one_ref[...].astype(F32), 0.0).reshape(1024, 128).T.astype(BF16)
-    sums = []
-    for i in range(3):
-        for j in range(3):
-            rows = wide_ref[4 - 2 * i : 20 - 2 * i, 48 - 16 * j : 112 - 16 * j].reshape(1024, 384)
-            sums.append(jnp.dot(act, rows, preferred_element_type=F32))
-    second = fold(sums, factor)
-    act = in_ref[...].astype(F32).reshape(1024, 128).T.astype(BF16)
-    sums = []
+
+
+def mask_kernel(at_ref, acc_ref, p0, p1, p2, p3, first_ref, low_ref, high_ref, one_ref, act_ref):
+    parts = (p0, p1, p2, p3)
+    n = len(parts)
+    for s, part in enumerate(parts):
+        spot = pl.ds(lax.rem(at_ref[0] + n - s, n) * 4, 4)
+        pre = part[0:256].reshape(4, 64, 128)
+        one_ref[spot] = pre
+        act_ref[spot] = part[256:512].reshape(4, 64, 128)
+        grad = jnp.where(pre.astype(F32) > 0, acc_ref[spot], 0.0).astype(BF16)
+        first_ref[spot] = grad
+        low_ref[spot] = grad[:, 0:16]
+        high_ref[spot] = grad[:, 48:64]
+
+
+def second_kernel(factor, at_ref, one_ref, wide_ref, mine_ref, send_ref):
+    act = jnp.maximum(one_ref[...].astype(F32), 0.0).reshape(1024, 128)
+    taps = fold(weight_sums(act, wide_ref), factor)
+
+    def emit(half, ref):
+        for m in range(7):
+            ref[64 * m : 64 * m + 64] = taps[7 * half + m].astype(ref.dtype)
+
+    share(at_ref[1], emit, mine_ref, send_ref)
+
+
+def last_kernel(
+    factor, at_ref, first_ref, left_ref, right_ref, w_ref, mine2_ref, send2_ref, act_ref,
+    grad_ref, mine_ref, send_ref, wide_ref, turn_ref,
+):
+    me = at_ref[0]
+    widen(wide_ref, left_ref, first_ref, right_ref)
+    taps = fold(weight_sums(act_ref[...].astype(F32).reshape(1024, 128), wide_ref), factor)
     grad = jnp.zeros((256, 128), F32)
     for i in range(3):
         for j in range(3):
-            rows = outer_ref[4 - 2 * i : 20 - 2 * i, 32 - 16 * j : 96 - 16 * j].reshape(1024, 384)
-            sums.append(jnp.dot(act, rows, preferred_element_type=F32))
-            mine = outer_ref[pl.ds(me * 4 + 4 - 2 * i, 4), 32 - 16 * j : 96 - 16 * j].reshape(256, 384)
-            grad += apply_taps(mine, w1_ref[i * 3 + j])
-    first = fold(sums, factor)
+            rows = wide_ref[pl.ds(me * 4 + 4 - 2 * i, 4), 32 - 16 * j : 96 - 16 * j].reshape(256, 384)
+            grad += apply_taps(rows, w_ref[i * 3 + j])
     turn_ref[...] = grad
     for x in range(4):
         for t in range(8):
@@ -389,10 +409,11 @@
 
     def emit(half, ref):
         for m in range(7):
-            ref[64 * m : 64 * m + 64] = first[7 * half + m].astype(ref.dtype)
-            ref[448 + 64 * m : 512 + 64 * m] = second[7 * half + m].astype(ref.dtype)
+            ref[64 * m : 64 * m + 64] = taps[7 * half + m].astype(ref.dtype)
 
     share(at_ref[1], emit, mine_ref, send_ref)
+    mine_ref[448:896] = mine2_ref[...]
+    send_ref[448:896] = send2_ref[...]
 
 
 def spread_kernel(at_ref, mine_ref, other_ref, one_ref, two_ref):
@@ -426,6 +447,13 @@
     return lax.ppermute(value, axis, [(i, i ^ bit) for i in range(n)])
 
 
+def rims(low, high):
+    n = lax.axis_size("gy")
+    left = lax.ppermute(high, "gy", [(i, i + 1) for i in range(n - 1)])
+    right = lax.ppermute(low, "gy", [(i + 1, i) for i in range(n - 1)])
+    return left, right
+
+
 def on_chip(mine, send):
     return (mine + swap(send, "gy", 1).astype(F32)).astype(BF16)
 
@@ -442,9 +470,9 @@
     shape = jax.ShapeDtypeStruct
     vmem = pltpu.VMEM
     natural = vmem((4, 8, 1024), BF16)
-    first, second = call(
+    packed = call(
         pack_kernel,
-        (shape((768, 128), BF16), shape((256, 128), BF16)),
+        (shape((512, 128), BF16), shape((512, 128), BF16)),
         [
             vmem((8, 4, 8, 128), BF16), natural, natural, natural, vmem((3, 256, 128), F32),
             pltpu.SemaphoreType.DMA((4,)),
@@ -456,8 +484,7 @@
         (pre_one,),
         (input_activation,),
     )
-    firsts = [first] + [rotate(first, "gx", s) for s in (1, 2, 3)]
-    seconds = [second] + [rotate(second, "gx", s) for s in (1, 2, 3)]
+    firsts, seconds = [[v] + [rotate(v, "gx", s) for s in (1, 2, 3)] for v in packed]
     kept, mask, d2, d1 = call(
         weight_kernel,
         (
@@ -476,16 +503,11 @@
         (w_two,),
         (w_one,),
     )
-    back, one, low, high, tmine, tsend = call(
+    rim = shape((16, 16, 128), BF16)
+    slab = shape((16, 64, 128), BF16)
+    back, low, high, tmine, tsend = call(
         functools.partial(transition_kernel, factor),
-        (
-            shape((8, 2, 64, 128), BF16),
-            shape((16, 64, 128), BF16),
-            shape((8, 2, 48, 128), BF16),
-            shape((8, 2, 48, 128), BF16),
-            shape((1024, 128), F32),
-            shape((1024, 128), BF16),
-        ),
+        (shape((8, 2, 64, 128), BF16), rim, rim, shape((1024, 128), F32), shape((1024, 128), BF16)),
         [vmem((4, 256, 128), BF16), vmem((16, 64, 128), BF16)],
         4 * 256 * 512 * 512,
         12,
@@ -494,33 +516,48 @@
         kept,
         mask,
     )
-    tsend, *seconds = lax.optimization_barrier((tsend, *seconds))
-    n = lax.axis_size("gy")
-    from_left = lax.ppermute(high, "gy", [(i, i + 1) for i in range(n - 1)])
-    from_right = lax.ppermute(low, "gy", [(i + 1, i) for i in range(n - 1)])
-    tmine = on_chip(tmine, tsend)
-    tmine, from_left, from_right = lax.optimization_barrier((tmine, from_left, from_right))
-    tmine = across(tmine)
+    left, right = rims(low, high)
+    left, right, tsend, *seconds = lax.optimization_barrier((left, right, tsend, *seconds))
+    tmine = across(on_chip(tmine, tsend))
+    wide, acc = call(
+        first_kernel,
+        (shape((20, 96, 384), BF16), shape((1024, 128), F32)),
+        [],
+        2 * 128 * 3456 * 1024,
+        12,
+        back.reshape(16, 64, 128),
+        left,
+        right,
+        d2,
+    )
+    first, low, high, one, act = call(
+        mask_kernel, (slab, rim, rim, slab, slab), [], 10**7, 6, at, acc.reshape(16, 64, 128), *seconds
+    )
+    left, right = rims(low, high)
+    mine2, send2 = call(
+        functools.partial(second_kernel, factor),
+        (shape((448, 128), F32), shape((448, 128), BF16)),
+        [],
+        2 * 128 * 3456 * 1024,
+        16,
+        at,
+        one,
+        wide,
+    )
     grad_in, mine, send = call(
-        functools.partial(conv_kernel, factor),
+        functools.partial(last_kernel, factor),
         (shape((4, 8, 1024), BF16), shape((896, 128), F32), shape((896, 128), BF16)),
-        [
-            vmem((20, 128, 384), BF16),
-            vmem((20, 96, 384), BF16),
-            vmem((16, 64, 128), BF16),
-            vmem((1536, 128), F32),
-            vmem((256, 128), F32),
-        ],
-        2 * 128 * 3456 * (1536 + 1024 + 1024 + 256),
-        20,
+        [vmem((20, 96, 384), BF16), vmem((256, 128), F32)],
+        2 * 128 * 3456 * (1024 + 256),
+        16,
         at,
-        back.reshape(16, 64, 128),
-        one,
-        from_left.reshape(16, 48, 128),
-        from_right.reshape(16, 48, 128),
-        d2,
+        first,
+        left,
+        right,
         d1,
-        *seconds,
+        mine2,
+        send2,
+        act,
     )
     send, tmine = lax.optimization_barrier((send, tmine))
     mine = across(on_chip(mine, send))

time: 61.1 us -> 65.6 us (1.074)
  the two profiles are of different devices: /device:TPU:0 before, /device:TPU:17 now
where the time goes in v4:
time: 65.6 us; the launch traced here: 65.1 us
  starting transfers between devices  22.3 us (34%)
  waiting for transfers between devices  21.6 us (33%)
  Pallas kernels  16.3 us (25%)
  local copies, waits for them, and re-layouts  3.76 us (6%)
  between operations  0.83 us (1%)
    pallas_call x9, Pallas kernels, call(): pl.pallas_call(kernel, out_shape=out_shape, in_specs=spec, out_specs=jax....  16.3 us
    ppermute x6, waiting for transfers between devices, swap(): return lax.ppermute(value, axis, [(i, i ^ bit) for i in range(n)])  9.46 us
    ppermute x2, starting transfers between devices, rims(): left = lax.ppermute(high, 'gy', [(i, i + 1) for i in range(n - 1)])  8.83 us
    ppermute x6, starting transfers between devices, rotate(): return lax.ppermute(value, axis, [(i, (i + step) % n) for i in range(n)])  7.81 us
    ppermute x6, waiting for transfers between devices, rotate(): return lax.ppermute(value, axis, [(i, (i + step) % n) for i in range(n)])  7.06 us
    ppermute x2, waiting for transfers between devices, rims(): right = lax.ppermute(low, 'gy', [(i + 1, i) for i in range(n - 1)])  5.11 us
    ppermute x2, starting transfers between devices, rims(): right = lax.ppermute(low, 'gy', [(i + 1, i) for i in range(n - 1)])  3.84 us
    unnamed x12, local copies, waits for them, and re-layouts  3.76 us
  transfers between devices with their start and end apart: 16, of which 6 were waited for; matrix products, arithmetic and copies ran while one was open for 0% of the time, Pallas kernels for 19%

profile of v4, /device:TPU:17, one launch (start us, length us, event | category | flops | bytes accessed | tf_op | source)
XLA Modules:
  0.0 65.1 jit_solution(8060633211948219867)
XLA Ops:
  0.6 1.7 %shard_map.111 = (bf16[512,128]{1,0:T(8,128)(2,1)}, bf16[512,128]{1,0:T(8,128)(2,1)}) custom-call(bf16[8,4,8,128]{3,2,1,0:T(8,128)(2,1)} %og.1, bf16[4,8,1024]{2,1,0:T(8,128)(2,1)} %two.1, bf16[4,8,1024]{2,1,0:T(8,128)(2,1)} %one.1, bf16[4,8,1024]{2,1,0:T(8,128)(2,1)} %act.1), custom_call_target="tpu_custom_call" | custom-call | bytes 262144 | tf_op jit(solution)/shard_map/pallas_call | solution.py:200
  2.3 0.2 collective-permute-start.2
  2.5 3.2 %collective-permute-start.1 = (bf16[512,128]{1,0:T(8,128)(2,1)}, bf16[512,128]{1,0:T(8,128)(2,1)S(1)}, u32[]{:S(2)}, u32[]{:S(2)}) collective-permute-start(bf16[512,128]{1,0:T(8,128)(2,1)} %get-tuple-element.38.a0), channel_id=1, source_target_pairs={{0,8},{4,12},{8,0},{12,4},{1,9},{5,13},{9,1},{13,5},{2,10},{6,14},... | collective-permute-start | bytes 393224 | tf_op jit(solution)/shard_map/ppermute | solution.py:442
  5.7 0.0 collective-permute-start
  5.7 1.5 %collective-permute-start.7 = (bf16[512,128]{1,0:T(8,128)(2,1)}, bf16[512,128]{1,0:T(8,128)(2,1)S(1)}, u32[]{:S(2)}, u32[]{:S(2)}) collective-permute-start(bf16[512,128]{1,0:T(8,128)(2,1)} %get-tuple-element.50.p0), channel_id=1, source_target_pairs={{0,12},{4,0},{8,4},{12,8},{1,13},{5,1},{9,5},{13,9},{2,14},{6,2},{... | collective-permute-start | bytes 393224 | tf_op jit(solution)/shard_map/ppermute | solution.py:442
  7.2 1.8 %collective-permute-start.6 = (bf16[512,128]{1,0:T(8,128)(2,1)}, bf16[512,128]{1,0:T(8,128)(2,1)S(1)}, u32[]{:S(2)}, u32[]{:S(2)}) collective-permute-start(bf16[512,128]{1,0:T(8,128)(2,1)} %get-tuple-element.50.p0), channel_id=1, source_target_pairs={{0,8},{4,12},{8,0},{12,4},{1,9},{5,13},{9,1},{13,5},{2,10},{6,14},... | collective-permute-start | bytes 393224 | tf_op jit(solution)/shard_map/ppermute | solution.py:442
  9.0 0.0 collective-permute-done.2.a3
  9.0 1.1 %collective-permute-start.5 = (bf16[512,128]{1,0:T(8,128)(2,1)}, bf16[512,128]{1,0:T(8,128)(2,1)S(1)}, u32[]{:S(2)}, u32[]{:S(2)}) collective-permute-start(bf16[512,128]{1,0:T(8,128)(2,1)} %get-tuple-element.50.p0), channel_id=1, source_target_pairs={{0,4},{4,8},{8,12},{12,0},{1,5},{5,9},{9,13},{13,1},{2,6},{6,10},{... | collective-permute-start | bytes 393224 | tf_op jit(solution)/shard_map/ppermute | solution.py:442
  10.1 0.1 pad_add_fusion.at_ref
  10.2 1.0 %copy-done = bf16[512,512]{1,0:T(8,128)(2,1)S(1)} copy-done((bf16[512,512]{1,0:T(8,128)(2,1)S(1)}, bf16[512,512]{1,0:T(8,128)(2,1)}, u32[]{:S(2)}) %copy-start) | copy-done | bytes 524312
  11.2 1.0 %copy-done.1 = bf16[27,64,64]{2,1,0:T(8,128)(2,1)S(1)} copy-done((bf16[27,64,64]{2,1,0:T(8,128)(2,1)S(1)}, bf16[27,64,64]{2,1,0:T(8,128)(2,1)}, u32[]{:S(2)}) %copy-start.1) | copy-done | bytes 221208
  12.3 1.0 %copy-done.2 = bf16[27,64,64]{2,1,0:T(8,128)(2,1)S(1)} copy-done((bf16[27,64,64]{2,1,0:T(8,128)(2,1)S(1)}, bf16[27,64,64]{2,1,0:T(8,128)(2,1)}, u32[]{:S(2)}) %copy-start.2) | copy-done | bytes 221208
  13.3 0.7 %copy-done.5 = s32[8,8]{1,0:T(8,128)S(1)} copy-done((s32[8,8]{1,0:T(8,128)S(1)}, s32[8,8]{1,0:T(8,128)}, u32[]{:S(2)}) %copy-start.5) | copy-done | bytes 280
  14.0 1.4 %shard_map.112 = (bf16[512,512]{1,0:T(8,128)(2,1)S(1)}, bf16[512,512]{1,0:T(8,128)(2,1)S(1)}, bf16[9,128,384]{2,1,0:T(8,128)(2,1)S(1)}, bf16[9,128,384]{2,1,0:T(8,128)(2,1)S(1)}) custom-call(bf16[512,512]{1,0:T(8,128)(2,1)S(1)} %copy-done, s32[8,8]{1,0:T(8,128)S(1)} %copy-done.5, bf16[27,64,64]{2,1,0:T(8,128)(2,1)S(1)} %copy-done.1, ...), custom_call_target="tpu_custom_call" | custom-call | flops 10000000 | bytes 966912 | tf_op jit(solution)/shard_map/pallas_call | solution.py:200
  15.4 0.0 collective-permute-done.1.a2
  15.4 7.0 %collective-permute-done.a1 = bf16[512,128]{1,0:T(8,128)(2,1)S(1)} collective-permute-done((bf16[512,128]{1,0:T(8,128)(2,1)}, bf16[512,128]{1,0:T(8,128)(2,1)S(1)}, u32[]{:S(2)}, u32[]{:S(2)}) %collective-permute-start) | collective-permute-done | bytes 131104 | tf_op jit(solution)/shard_map/ppermute | solution.py:442
  22.4 1.1 %shard_map.113 = (bf16[8,2,64,128]{3,2,1,0:T(8,128)(2,1)S(1)}, bf16[16,16,128]{2,1,0:T(8,128)(2,1)S(1)}, bf16[16,16,128]{2,1,0:T(8,128)(2,1)S(1)}, f32[1024,128]{1,0:T(8,128)S(1)}, bf16[1024,128]{1,0:T(8,128)(2,1)S(1)}) custom-call(s32[2]{0:T(128)S(1)} %pad_add_fusion.at_ref, bf16[512,128]{1,0:T(8,128)(2,1)S(1)} %copy-done.3, ...), custom_call_target="tpu_custom_call" | custom-call | flops 268435456 | bytes 1572872 | tf_op jit(solution)/shard_map/pallas_call | solution.py:200
  23.6 5.2 %collective-permute-start.3 = (bf16[16,16,128]{2,1,0:T(8,128)(2,1)S(1)}, bf16[16,16,128]{2,1,0:T(8,128)(2,1)S(1)}, u32[]{:S(2)}, u32[]{:S(2)}) collective-permute-start(bf16[16,16,128]{2,1,0:T(8,128)(2,1)S(1)} %get-tuple-element.42), channel_id=1, source_target_pairs={{0,1},{1,2},{2,3},{4,5},{5,6},{6,7},{8,9},{9,10},{10,11},{12,13},{... | collective-permute-start | bytes 196616 | tf_op jit(solution)/shard_map/ppermute | solution.py:452
  28.8 1.9 %collective-permute-start.4 = (bf16[16,16,128]{2,1,0:T(8,128)(2,1)S(1)}, bf16[16,16,128]{2,1,0:T(8,128)(2,1)S(1)}, u32[]{:S(2)}, u32[]{:S(2)}) collective-permute-start(bf16[16,16,128]{2,1,0:T(8,128)(2,1)S(1)} %get-tuple-element.43), channel_id=1, source_target_pairs={{1,0},{2,1},{3,2},{5,4},{6,5},{7,6},{9,8},{10,9},{11,10},{13,12},{... | collective-permute-start | bytes 196616 | tf_op jit(solution)/shard_map/ppermute | solution.py:453
  30.7 0.0 collective-permute-done.7.p3
  30.7 0.0 collective-permute-done.6.p2
  30.7 0.0 collective-permute-done.5.p1
  30.7 0.0 collective-permute-done.3.left_ref
  30.7 3.6 %collective-permute-done.4.right_ref = bf16[16,16,128]{2,1,0:T(8,128)(2,1)S(1)} collective-permute-done((bf16[16,16,128]{2,1,0:T(8,128)(2,1)S(1)}, bf16[16,16,128]{2,1,0:T(8,128)(2,1)S(1)}, u32[]{:S(2)}, u32[]{:S(2)}) %collective-permute-start.4) | collective-permute-done | bytes 65568 | tf_op jit(solution)/shard_map/ppermute | solution.py:453
  34.3 0.0 collective-permute-start.10
  34.3 1.5 %collective-permute-done.10 = bf16[1024,128]{1,0:T(8,128)(2,1)S(1)} collective-permute-done((bf16[1024,128]{1,0:T(8,128)(2,1)S(1)}, bf16[1024,128]{1,0:T(8,128)(2,1)S(1)}, u32[]{:S(2)}, u32[]{:S(2)}) %collective-permute-start.10) | collective-permute-done | bytes 262176 | tf_op jit(solution)/shard_map/ppermute | solution.py:447
  35.9 0.1 add_convert_fusion
  35.9 0.1 collective-permute-start.11
  36.0 0.0 copy-start.4
  36.0 2.2 %shard_map.114 = (bf16[20,96,384]{2,1,0:T(8,128)(2,1)S(1)}, f32[1024,128]{1,0:T(8,128)S(1)}) custom-call(bf16[16,64,128]{2,1,0:T(8,128)(2,1)S(1)} %bitcast.5, bf16[16,16,128]{2,1,0:T(8,128)(2,1)S(1)} %collective-permute-done.3.left_ref, bf16[16,16,128]{2,1,0:T(8,128)(2,1)S(1)} %collective-permute-done.4.right_ref, ...), custom_call_target="tpu_custom_call" | custom-call | flops 905969664 | bytes 1277952 | tf_op jit(solution)/shard_map/pallas_call | solution.py:200
  38.3 0.7 shard_map.115
  38.9 3.7 %collective-permute-start.8 = (bf16[16,16,128]{2,1,0:T(8,128)(2,1)S(1)}, bf16[16,16,128]{2,1,0:T(8,128)(2,1)S(1)}, u32[]{:S(2)}, u32[]{:S(2)}) collective-permute-start(bf16[16,16,128]{2,1,0:T(8,128)(2,1)S(1)} %get-tuple-element.55), channel_id=1, source_target_pairs={{0,1},{1,2},{2,3},{4,5},{5,6},{6,7},{8,9},{9,10},{10,11},{12,13},{... | collective-permute-start | bytes 196616 | tf_op jit(solution)/shard_map/ppermute | solution.py:452
  42.6 1.9 %collective-permute-start.9 = (bf16[16,16,128]{2,1,0:T(8,128)(2,1)S(1)}, bf16[16,16,128]{2,1,0:T(8,128)(2,1)S(1)}, u32[]{:S(2)}, u32[]{:S(2)}) collective-permute-start(bf16[16,16,128]{2,1,0:T(8,128)(2,1)S(1)} %get-tuple-element.56), channel_id=1, source_target_pairs={{1,0},{2,1},{3,2},{5,4},{6,5},{7,6},{9,8},{10,9},{11,10},{13,12},{... | collective-permute-start | bytes 196616 | tf_op jit(solution)/shard_map/ppermute | solution.py:453
  44.5 2.1 %shard_map.116 = (f32[448,128]{1,0:T(8,128)S(1)}, bf16[448,128]{1,0:T(8,128)(2,1)S(1)}) custom-call(s32[2]{0:T(128)S(1)} %pad_add_fusion.at_ref, bf16[16,64,128]{2,1,0:T(8,128)(2,1)S(1)} %get-tuple-element.58.one_ref, bf16[20,96,384]{2,1,0:T(8,128)(2,1)S(1)} %get-tuple-element.59.wide_ref), custom_call_target="tpu_custom_call" | custom-call | flops 905969664 | bytes 1736712 | tf_op jit(solution)/shard_map/pallas_call | solution.py:200
  46.7 0.0 collective-permute-done.8.left_ref
  46.7 1.5 %collective-permute-done.9.right_ref = bf16[16,16,128]{2,1,0:T(8,128)(2,1)S(1)} collective-permute-done((bf16[16,16,128]{2,1,0:T(8,128)(2,1)S(1)}, bf16[16,16,128]{2,1,0:T(8,128)(2,1)S(1)}, u32[]{:S(2)}, u32[]{:S(2)}) %collective-permute-start.9) | collective-permute-done | bytes 65568 | tf_op jit(solution)/shard_map/ppermute | solution.py:453
  48.2 3.4 %shard_map.117 = (bf16[4,8,1024]{2,1,0:T(8,128)(2,1)}, f32[896,128]{1,0:T(8,128)S(1)}, bf16[896,128]{1,0:T(8,128)(2,1)S(1)}) custom-call(s32[2]{0:T(128)S(1)} %pad_add_fusion.at_ref, bf16[16,64,128]{2,1,0:T(8,128)(2,1)S(1)} %get-tuple-element.54.first_ref, bf16[16,16,128]{2,1,0:T(8,128)(2,1)S(1)} %collective-permute-done.8.left_ref, ...), custom_call_target="tpu_custom_call" | custom-call | flops 1132462080 | bytes 1884168 | tf_op jit(solution)/shard_map/pallas_call | solution.py:200
  51.6 0.0 collective-permute-done.11
  51.6 0.1 convert_add_fusion.mine_ref
  51.6 0.1 collective-permute-start.12
  51.7 1.5 %collective-permute-done.12 = bf16[896,128]{1,0:T(8,128)(2,1)S(1)} collective-permute-done((bf16[896,128]{1,0:T(8,128)(2,1)S(1)}, bf16[896,128]{1,0:T(8,128)(2,1)S(1)}, u32[]{:S(2)}, u32[]{:S(2)}) %collective-permute-start.12) | collective-permute-done | bytes 229408 | tf_op jit(solution)/shard_map/ppermute | solution.py:447
  53.3 0.1 collective-permute-start.13
  53.3 0.6 collective-permute-start.15
  53.9 6.4 %collective-permute-done.13 = bf16[896,128]{1,0:T(8,128)(2,1)S(1)} collective-permute-done((bf16[896,128]{1,0:T(8,128)(2,1)S(1)}, bf16[896,128]{1,0:T(8,128)(2,1)S(1)}, u32[]{:S(2)}, u32[]{:S(2)}) %collective-permute-start.13) | collective-permute-done | bytes 229408 | tf_op jit(solution)/shard_map/ppermute | solution.py:447
  60.4 1.0 %collective-permute-start.14 = (f32[896,128]{1,0:T(8,128)S(1)}, f32[896,128]{1,0:T(8,128)S(1)}, u32[]{:S(2)}, u32[]{:S(2)}) collective-permute-start(f32[896,128]{1,0:T(8,128)S(1)} %convert_add_fusion.1.mine_ref), channel_id=1, source_target_pairs={{0,1},{1,0},{2,3},{3,2},{4,5},{5,4},{6,7},{7,6},{8,9},{9,8},{10,11... | collective-permute-start | bytes 1376264 | tf_op jit(solution)/shard_map/ppermute | solution.py:447
  61.5 0.0 collective-permute-done.15.other_ref
  61.5 1.6 %shard_map.119 = f32[512,512]{1,0:T(8,128)} custom-call(s32[2]{0:T(128)S(1)} %pad_add_fusion.at_ref, f32[1024,128]{1,0:T(8,128)S(1)} %convert_add_fusion.mine_ref, f32[1024,128]{1,0:T(8,128)S(1)} %collective-permute-done.15.other_ref), custom_call_target="tpu_custom_call" | custom-call | flops 10000000 | bytes 1048584 | tf_op jit(solution)/shard_map/pallas_call | solution.py:200
  63.1 2.0 %shard_map.118 = (f32[27,64,64]{2,1,0:T(8,128)}, f32[27,64,64]{2,1,0:T(8,128)}) custom-call(s32[2]{0:T(128)S(1)} %pad_add_fusion.at_ref, f32[896,128]{1,0:T(8,128)S(1)} %convert_add_fusion.1.mine_ref, f32[896,128]{1,0:T(8,128)S(1)} %collective-permute-done.14.other_ref), custom_call_target="tpu_custom_call" | custom-call | bytes 917512 | tf_op jit(solution)/shard_map/pallas_call | solution.py:200
  (10 shorter events, 0.1 us)
Async XLA Ops:
  2.3 6.7 %collective-permute-start.2 = (bf16[512,128]{1,0:T(8,128)(2,1)}, bf16[512,128]{1,0:T(8,128)(2,1)S(1)}, u32[]{:S(2)}, u32[]{:S(2)}) collective-permute-start(bf16[512,128]{1,0:T(8,128)(2,1)} %get-tuple-element.38.a0), channel_id=1, source_target_pairs={{0,12},{4,0},{8,4},{12,8},{1,13},{5,1},{9,5},{13,9},{2,14},{6,2},{... | collective-permute-start | bytes 393224 | tf_op jit(solution)/shard_map/ppermute | solution.py:442
  2.5 12.8 %collective-permute-start.1 = (bf16[512,128]{1,0:T(8,128)(2,1)}, bf16[512,128]{1,0:T(8,128)(2,1)S(1)}, u32[]{:S(2)}, u32[]{:S(2)}) collective-permute-start(bf16[512,128]{1,0:T(8,128)(2,1)} %get-tuple-element.38.a0), channel_id=1, source_target_pairs={{0,8},{4,12},{8,0},{12,4},{1,9},{5,13},{9,1},{13,5},{2,10},{6,14},... | collective-permute-start | bytes 393224 | tf_op jit(solution)/shard_map/ppermute | solution.py:442
  5.7 16.7 %collective-permute-start = (bf16[512,128]{1,0:T(8,128)(2,1)}, bf16[512,128]{1,0:T(8,128)(2,1)S(1)}, u32[]{:S(2)}, u32[]{:S(2)}) collective-permute-start(bf16[512,128]{1,0:T(8,128)(2,1)} %get-tuple-element.38.a0), channel_id=1, source_target_pairs={{0,4},{4,8},{8,12},{12,0},{1,5},{5,9},{9,13},{13,1},{2,6},{6,10},{... | collective-permute-start | bytes 393224 | tf_op jit(solution)/shard_map/ppermute | solution.py:442
  5.7 24.9 %collective-permute-start.7 = (bf16[512,128]{1,0:T(8,128)(2,1)}, bf16[512,128]{1,0:T(8,128)(2,1)S(1)}, u32[]{:S(2)}, u32[]{:S(2)}) collective-permute-start(bf16[512,128]{1,0:T(8,128)(2,1)} %get-tuple-element.50.p0), channel_id=1, source_target_pairs={{0,12},{4,0},{8,4},{12,8},{1,13},{5,1},{9,5},{13,9},{2,14},{6,2},{... | collective-permute-start | bytes 393224 | tf_op jit(solution)/shard_map/ppermute | solution.py:442
  7.2 23.5 %collective-permute-start.6 = (bf16[512,128]{1,0:T(8,128)(2,1)}, bf16[512,128]{1,0:T(8,128)(2,1)S(1)}, u32[]{:S(2)}, u32[]{:S(2)}) collective-permute-start(bf16[512,128]{1,0:T(8,128)(2,1)} %get-tuple-element.50.p0), channel_id=1, source_target_pairs={{0,8},{4,12},{8,0},{12,4},{1,9},{5,13},{9,1},{13,5},{2,10},{6,14},... | collective-permute-start | bytes 393224 | tf_op jit(solution)/shard_map/ppermute | solution.py:442
  9.0 21.7 %collective-permute-start.5 = (bf16[512,128]{1,0:T(8,128)(2,1)}, bf16[512,128]{1,0:T(8,128)(2,1)S(1)}, u32[]{:S(2)}, u32[]{:S(2)}) collective-permute-start(bf16[512,128]{1,0:T(8,128)(2,1)} %get-tuple-element.50.p0), channel_id=1, source_target_pairs={{0,4},{4,8},{8,12},{12,0},{1,5},{5,9},{9,13},{13,1},{2,6},{6,10},{... | collective-permute-start | bytes 393224 | tf_op jit(solution)/shard_map/ppermute | solution.py:442
  10.2 1.0 %copy-start = (bf16[512,512]{1,0:T(8,128)(2,1)S(1)}, bf16[512,512]{1,0:T(8,128)(2,1)}, u32[]{:S(2)}) copy-start(bf16[512,512]{1,0:T(8,128)(2,1)} %wt.1) | copy-start | bytes 1572868
  11.2 1.0 %copy-start.1 = (bf16[27,64,64]{2,1,0:T(8,128)(2,1)S(1)}, bf16[27,64,64]{2,1,0:T(8,128)(2,1)}, u32[]{:S(2)}) copy-start(bf16[27,64,64]{2,1,0:T(8,128)(2,1)} %w2.1) | copy-start | bytes 663556
  12.2 1.0 %copy-start.2 = (bf16[27,64,64]{2,1,0:T(8,128)(2,1)S(1)}, bf16[27,64,64]{2,1,0:T(8,128)(2,1)}, u32[]{:S(2)}) copy-start(bf16[27,64,64]{2,1,0:T(8,128)(2,1)} %w1.1) | copy-start | bytes 663556
  13.3 0.7 %copy-start.5 = (s32[8,8]{1,0:T(8,128)S(1)}, s32[8,8]{1,0:T(8,128)}, u32[]{:S(2)}) copy-start(s32[8,8]{1,0:T(8,128)} %keep.1) | copy-start | bytes 772
  13.9 8.5 %copy-start.3 = (bf16[512,128]{1,0:T(8,128)(2,1)S(1)}, bf16[512,128]{1,0:T(8,128)(2,1)}, u32[]{:S(2)}) copy-start(bf16[512,128]{1,0:T(8,128)(2,1)} %get-tuple-element.38.a0) | copy-start | bytes 393220
  23.6 7.1 %collective-permute-start.3 = (bf16[16,16,128]{2,1,0:T(8,128)(2,1)S(1)}, bf16[16,16,128]{2,1,0:T(8,128)(2,1)S(1)}, u32[]{:S(2)}, u32[]{:S(2)}) collective-permute-start(bf16[16,16,128]{2,1,0:T(8,128)(2,1)S(1)} %get-tuple-element.42), channel_id=1, source_target_pairs={{0,1},{1,2},{2,3},{4,5},{5,6},{6,7},{8,9},{9,10},{10,11},{12,13},{... | collective-permute-start | bytes 196616 | tf_op jit(solution)/shard_map/ppermute | solution.py:452
  28.8 5.6 %collective-permute-start.4 = (bf16[16,16,128]{2,1,0:T(8,128)(2,1)S(1)}, bf16[16,16,128]{2,1,0:T(8,128)(2,1)S(1)}, u32[]{:S(2)}, u32[]{:S(2)}) collective-permute-start(bf16[16,16,128]{2,1,0:T(8,128)(2,1)S(1)} %get-tuple-element.43), channel_id=1, source_target_pairs={{1,0},{2,1},{3,2},{5,4},{6,5},{7,6},{9,8},{10,9},{11,10},{13,12},{... | collective-permute-start | bytes 196616 | tf_op jit(solution)/shard_map/ppermute | solution.py:453
  34.3 1.5 %collective-permute-start.10 = (bf16[1024,128]{1,0:T(8,128)(2,1)S(1)}, bf16[1024,128]{1,0:T(8,128)(2,1)S(1)}, u32[]{:S(2)}, u32[]{:S(2)}) collective-permute-start(bf16[1024,128]{1,0:T(8,128)(2,1)S(1)} %get-tuple-element.67), channel_id=1, source_target_pairs={{0,1},{1,0},{2,3},{3,2},{4,5},{5,4},{6,7},{7,6},{8,9},{9,8},{10,11... | collective-permute-start | bytes 786440 | tf_op jit(solution)/shard_map/ppermute | solution.py:447
  35.9 15.7 %collective-permute-start.11 = (bf16[1024,128]{1,0:T(8,128)(2,1)S(1)}, bf16[1024,128]{1,0:T(8,128)(2,1)S(1)}, u32[]{:S(2)}, u32[]{:S(2)}) collective-permute-start(bf16[1024,128]{1,0:T(8,128)(2,1)S(1)} %add_convert_fusion), channel_id=1, source_target_pairs={{0,2},{1,3},{2,0},{3,1},{4,6},{5,7},{6,4},{7,5},{8,10},{9,11},{10,... | collective-permute-start | bytes 786440 | tf_op jit(solution)/shard_map/ppermute | solution.py:447
  36.0 2.2 %copy-start.4 = (bf16[512,128]{1,0:T(8,128)(2,1)S(1)}, bf16[512,128]{1,0:T(8,128)(2,1)}, u32[]{:S(2)}) copy-start(bf16[512,128]{1,0:T(8,128)(2,1)} %get-tuple-element.50.p0) | copy-start | bytes 393220
  38.9 7.8 %collective-permute-start.8 = (bf16[16,16,128]{2,1,0:T(8,128)(2,1)S(1)}, bf16[16,16,128]{2,1,0:T(8,128)(2,1)S(1)}, u32[]{:S(2)}, u32[]{:S(2)}) collective-permute-start(bf16[16,16,128]{2,1,0:T(8,128)(2,1)S(1)} %get-tuple-element.55), channel_id=1, source_target_pairs={{0,1},{1,2},{2,3},{4,5},{5,6},{6,7},{8,9},{9,10},{10,11},{12,13},{... | collective-permute-start | bytes 196616 | tf_op jit(solution)/shard_map/ppermute | solution.py:452
  42.6 5.6 %collective-permute-start.9 = (bf16[16,16,128]{2,1,0:T(8,128)(2,1)S(1)}, bf16[16,16,128]{2,1,0:T(8,128)(2,1)S(1)}, u32[]{:S(2)}, u32[]{:S(2)}) collective-permute-start(bf16[16,16,128]{2,1,0:T(8,128)(2,1)S(1)} %get-tuple-element.56), channel_id=1, source_target_pairs={{1,0},{2,1},{3,2},{5,4},{6,5},{7,6},{9,8},{10,9},{11,10},{13,12},{... | collective-permute-start | bytes 196616 | tf_op jit(solution)/shard_map/ppermute | solution.py:453
  51.6 1.6 %collective-permute-start.12 = (bf16[896,128]{1,0:T(8,128)(2,1)S(1)}, bf16[896,128]{1,0:T(8,128)(2,1)S(1)}, u32[]{:S(2)}, u32[]{:S(2)}) collective-permute-start(bf16[896,128]{1,0:T(8,128)(2,1)S(1)} %get-tuple-element.68), channel_id=1, source_target_pairs={{0,1},{1,0},{2,3},{3,2},{4,5},{5,4},{6,7},{7,6},{8,9},{9,8},{10,11... | collective-permute-start | bytes 688136 | tf_op jit(solution)/shard_map/ppermute | solution.py:447
  53.3 7.1 %collective-permute-start.13 = (bf16[896,128]{1,0:T(8,128)(2,1)S(1)}, bf16[896,128]{1,0:T(8,128)(2,1)S(1)}, u32[]{:S(2)}, u32[]{:S(2)}) collective-permute-start(bf16[896,128]{1,0:T(8,128)(2,1)S(1)} %add_convert_fusion.1), channel_id=1, source_target_pairs={{0,2},{1,3},{2,0},{3,1},{4,6},{5,7},{6,4},{7,5},{8,10},{9,11},{10,... | collective-permute-start | bytes 688136 | tf_op jit(solution)/shard_map/ppermute | solution.py:447
  53.3 8.1 %collective-permute-start.15 = (f32[1024,128]{1,0:T(8,128)S(1)}, f32[1024,128]{1,0:T(8,128)S(1)}, u32[]{:S(2)}, u32[]{:S(2)}) collective-permute-start(f32[1024,128]{1,0:T(8,128)S(1)} %convert_add_fusion.mine_ref), channel_id=1, source_target_pairs={{0,1},{1,0},{2,3},{3,2},{4,5},{5,4},{6,7},{7,6},{8,9},{9,8},{10,11... | collective-permute-start | bytes 1572872 | tf_op jit(solution)/shard_map/ppermute | solution.py:447
  60.4 2.7 %collective-permute-start.14 = (f32[896,128]{1,0:T(8,128)S(1)}, f32[896,128]{1,0:T(8,128)S(1)}, u32[]{:S(2)}, u32[]{:S(2)}) collective-permute-start(f32[896,128]{1,0:T(8,128)S(1)} %convert_add_fusion.1.mine_ref), channel_id=1, source_target_pairs={{0,1},{1,0},{2,3},{3,2},{4,5},{5,4},{6,7},{7,6},{8,9},{9,8},{10,11... | collective-permute-start | bytes 1376264 | tf_op jit(solution)/shard_map/ppermute | solution.py:447

commit v5 on v4

--- a/solution.py
+++ b/solution.py
@@ -219,16 +219,31 @@
     return copies
 
 
-def pack_kernel(og, two, one, act, first_ref, second_ref, og_v, two_v, one_v, act_v, turn_ref, sems):
-    copies = fetch(((og, og_v), (two, two_v), (one, one_v), (act, act_v)), sems)
+def turn(ref, rows, scratch, at, step):
+    for x in range(4):
+        for t in range(8):
+            scratch[pl.ds(step * x + at + t, rows, stride=8), :] = ref[x, :, 128 * t : 128 * t + 128].astype(F32)
+
+
+def pack_kernel(og, two, out_ref, og_v, two_v, turn_ref, sems):
+    copies = fetch(((og, og_v), (two, two_v)), sems)
     copies[0].wait()
-    first_ref[0:256] = og_v[...].astype(F32).reshape(256, 128).astype(BF16)
-    for k, (ref, out, at) in enumerate(((two_v, first_ref, 256), (one_v, second_ref, 0), (act_v, second_ref, 256))):
-        copies[k + 1].wait()
-        for x in range(4):
-            for t in range(8):
-                turn_ref[k, pl.ds(64 * x + t, 8, stride=8), :] = ref[x, :, 128 * t : 128 * t + 128].astype(F32)
-        out[at : at + 256] = turn_ref[k].astype(BF16)
+    out_ref[0:256] = og_v[...].astype(F32).reshape(256, 128).astype(BF16)
+    copies[1].wait()
+    turn(two_v, 8, turn_ref, 0, 64)
+    out_ref[256:512] = turn_ref[...].astype(BF16)
+
+
+def pack_more_kernel(one, act, left_ref, right_ref, out_ref, one_v, act_v, turn_ref, wide_ref, sems):
+    copies = fetch(((one, one_v), (act, act_v)), sems)
+    turn(left_ref, 2, wide_ref, 0, 96)
+    turn(right_ref, 2, wide_ref, 80, 96)
+    copies[0].wait()
+    turn(one_v, 8, wide_ref, 16, 96)
+    out_ref[0:384] = wide_ref[...].astype(BF16)
+    copies[1].wait()
+    turn(act_v, 8, turn_ref, 0, 64)
+    out_ref[384:640] = turn_ref[...].astype(BF16)
 
 
 def weight_kernel(wt, keep, w2, w1, kept_ref, mask_ref, d2_ref, d1_ref, wt_v, keep_v, w2_v, w1_v, sems):
@@ -283,8 +298,8 @@
             halves.append(jnp.where(pre > 0, grad, 0.0))
             cells.append(jnp.maximum(pre, 0.0).reshape(256, 128).astype(BF16))
         back_ref[:, p] = jnp.stack(halves, axis=2).reshape(8, 64, 128).astype(BF16)
-    low_ref[...] = back_ref[:, :, 0:16].reshape(16, 16, 128)
-    high_ref[...] = back_ref[:, :, 48:64].reshape(16, 16, 128)
+    low_ref[...] = back_ref[:, :, 0:32].reshape(16, 32, 128)
+    high_ref[...] = back_ref[:, :, 32:64].reshape(16, 32, 128)
     flat = jnp.concatenate(cells, axis=1)
     trans = lax.dot_general(flat, og, (((0,), (0,)), ((), ())), preferred_element_type=F32)
     trans = trans * mask_ref[...].astype(F32) * factor
@@ -334,30 +349,32 @@
     return lax.dot_general(rows, taps, (((1,), (1,)), ((), ())), preferred_element_type=F32)
 
 
-def widen(wide_ref, left_ref, own_ref, right_ref):
-    edge = jnp.zeros((2, 96, 384), BF16)
+def widen(wide_ref, pieces):
+    rows = wide_ref.shape[1]
+    edge = jnp.zeros((2, rows, 384), BF16)
     wide_ref[0:2] = edge
     wide_ref[18:20] = edge
-    wide_ref[2:18, 0:16] = triple(left_ref[...].astype(F32))
-    wide_ref[2:18, 16:80] = triple(own_ref[...].astype(F32))
-    wide_ref[2:18, 80:96] = triple(right_ref[...].astype(F32))
-
-
-def weight_sums(act, wide_ref):
+    at = 0
+    for piece in pieces:
+        wide_ref[2:18, at : at + piece.shape[1]] = triple(piece.astype(F32))
+        at += piece.shape[1]
+
+
+def weight_sums(act, wide_ref, at):
     turned = act.T.astype(BF16)
     sums = []
     for i in range(3):
         for j in range(3):
-            rows = wide_ref[4 - 2 * i : 20 - 2 * i, 32 - 16 * j : 96 - 16 * j].reshape(1024, 384)
+            rows = wide_ref[4 - 2 * i : 20 - 2 * i, at - 16 * j : at + 64 - 16 * j].reshape(1024, 384)
             sums.append(jnp.dot(turned, rows, preferred_element_type=F32))
     return sums
 
 
 def first_kernel(back_ref, left_ref, right_ref, w_ref, wide_ref, acc_ref):
-    widen(wide_ref, left_ref, back_ref, right_ref)
+    widen(wide_ref, (left_ref[...], back_ref[...], right_ref[...]))
     for i in range(3):
         for j in range(3):
-            rows = wide_ref[4 - 2 * i : 20 - 2 * i, 32 - 16 * j : 96 - 16 * j].reshape(1024, 384)
+            rows = wide_ref[4 - 2 * i : 20 - 2 * i, 32 - 16 * j : 128 - 16 * j].reshape(1536, 384)
             part = apply_taps(rows, w_ref[i * 3 + j])
             if i == 0 and j == 0:
                 acc_ref[...] = part
@@ -365,42 +382,24 @@
                 acc_ref[...] += part
 
 
-def mask_kernel(at_ref, acc_ref, p0, p1, p2, p3, first_ref, low_ref, high_ref, one_ref, act_ref):
+def last_kernel(
+    factor, at_ref, acc_ref, wide_ref, w_ref, p0, p1, p2, p3, grad_ref, mine_ref, send_ref, outer_ref, one_ref, act_ref, turn_ref
+):
+    me = at_ref[0]
     parts = (p0, p1, p2, p3)
     n = len(parts)
     for s, part in enumerate(parts):
-        spot = pl.ds(lax.rem(at_ref[0] + n - s, n) * 4, 4)
-        pre = part[0:256].reshape(4, 64, 128)
-        one_ref[spot] = pre
-        act_ref[spot] = part[256:512].reshape(4, 64, 128)
-        grad = jnp.where(pre.astype(F32) > 0, acc_ref[spot], 0.0).astype(BF16)
-        first_ref[spot] = grad
-        low_ref[spot] = grad[:, 0:16]
-        high_ref[spot] = grad[:, 48:64]
-
-
-def second_kernel(factor, at_ref, one_ref, wide_ref, mine_ref, send_ref):
-    act = jnp.maximum(one_ref[...].astype(F32), 0.0).reshape(1024, 128)
-    taps = fold(weight_sums(act, wide_ref), factor)
-
-    def emit(half, ref):
-        for m in range(7):
-            ref[64 * m : 64 * m + 64] = taps[7 * half + m].astype(ref.dtype)
-
-    share(at_ref[1], emit, mine_ref, send_ref)
-
-
-def last_kernel(
-    factor, at_ref, first_ref, left_ref, right_ref, w_ref, mine2_ref, send2_ref, act_ref,
-    grad_ref, mine_ref, send_ref, wide_ref, turn_ref,
-):
-    me = at_ref[0]
-    widen(wide_ref, left_ref, first_ref, right_ref)
-    taps = fold(weight_sums(act_ref[...].astype(F32).reshape(1024, 128), wide_ref), factor)
+        spot = pl.ds(lax.rem(me + n - s, n) * 4, 4)
+        one_ref[spot] = part[0:384].reshape(4, 96, 128)
+        act_ref[spot] = part[384:640].reshape(4, 64, 128)
+    widen(outer_ref, (jnp.where(one_ref[...].astype(F32) > 0, acc_ref[...], 0.0),))
+    act = jnp.maximum(one_ref[:, 16:80].astype(F32), 0.0).reshape(1024, 128)
+    second = fold(weight_sums(act, wide_ref, 48), factor)
+    first = fold(weight_sums(act_ref[...].astype(F32).reshape(1024, 128), outer_ref, 32), factor)
     grad = jnp.zeros((256, 128), F32)
     for i in range(3):
         for j in range(3):
-            rows = wide_ref[pl.ds(me * 4 + 4 - 2 * i, 4), 32 - 16 * j : 96 - 16 * j].reshape(256, 384)
+            rows = outer_ref[pl.ds(me * 4 + 4 - 2 * i, 4), 32 - 16 * j : 96 - 16 * j].reshape(256, 384)
             grad += apply_taps(rows, w_ref[i * 3 + j])
     turn_ref[...] = grad
     for x in range(4):
@@ -409,11 +408,10 @@
 
     def emit(half, ref):
         for m in range(7):
-            ref[64 * m : 64 * m + 64] = taps[7 * half + m].astype(ref.dtype)
+            ref[64 * m : 64 * m + 64] = first[7 * half + m].astype(ref.dtype)
+            ref[448 + 64 * m : 512 + 64 * m] = second[7 * half + m].astype(ref.dtype)
 
     share(at_ref[1], emit, mine_ref, send_ref)
-    mine_ref[448:896] = mine2_ref[...]
-    send_ref[448:896] = send2_ref[...]
 
 
 def spread_kernel(at_ref, mine_ref, other_ref, one_ref, two_ref):
@@ -472,19 +470,27 @@
     natural = vmem((4, 8, 1024), BF16)
     packed = call(
         pack_kernel,
-        (shape((512, 128), BF16), shape((512, 128), BF16)),
-        [
-            vmem((8, 4, 8, 128), BF16), natural, natural, natural, vmem((3, 256, 128), F32),
-            pltpu.SemaphoreType.DMA((4,)),
-        ],
+        shape((512, 128), BF16),
+        [vmem((8, 4, 8, 128), BF16), natural, vmem((256, 128), F32), pltpu.SemaphoreType.DMA((2,))],
         0,
         56,
         (out_grad,),
         (pre_two,),
+    )
+    firsts = [packed] + [rotate(packed, "gx", s) for s in (1, 2, 3)]
+    left, right = rims(pre_one[:, 0:2], pre_one[:, 6:8])
+    packed = call(
+        pack_more_kernel,
+        shape((640, 128), BF16),
+        [natural, natural, vmem((256, 128), F32), vmem((384, 128), F32), pltpu.SemaphoreType.DMA((2,))],
+        0,
+        8,
         (pre_one,),
         (input_activation,),
-    )
-    firsts, seconds = [[v] + [rotate(v, "gx", s) for s in (1, 2, 3)] for v in packed]
+        left,
+        right,
+    )
+    seconds = [packed] + [rotate(packed, "gx", s) for s in (1, 2, 3)]
     kept, mask, d2, d1 = call(
         weight_kernel,
         (
@@ -503,8 +509,8 @@
         (w_two,),
         (w_one,),
     )
-    rim = shape((16, 16, 128), BF16)
-    slab = shape((16, 64, 128), BF16)
+    rim = shape((16, 32, 128), BF16)
+    kept, seconds[0] = lax.optimization_barrier((kept, seconds[0]))
     back, low, high, tmine, tsend = call(
         functools.partial(transition_kernel, factor),
         (shape((8, 2, 64, 128), BF16), rim, rim, shape((1024, 128), F32), shape((1024, 128), BF16)),
@@ -517,47 +523,30 @@
         mask,
     )
     left, right = rims(low, high)
-    left, right, tsend, *seconds = lax.optimization_barrier((left, right, tsend, *seconds))
-    tmine = across(on_chip(tmine, tsend))
     wide, acc = call(
         first_kernel,
-        (shape((20, 96, 384), BF16), shape((1024, 128), F32)),
+        (shape((20, 128, 384), BF16), shape((1536, 128), F32)),
         [],
-        2 * 128 * 3456 * 1024,
-        12,
+        0,
+        16,
         back.reshape(16, 64, 128),
         left,
         right,
         d2,
     )
-    first, low, high, one, act = call(
-        mask_kernel, (slab, rim, rim, slab, slab), [], 10**7, 6, at, acc.reshape(16, 64, 128), *seconds
-    )
-    left, right = rims(low, high)
-    mine2, send2 = call(
-        functools.partial(second_kernel, factor),
-        (shape((448, 128), F32), shape((448, 128), BF16)),
-        [],
-        2 * 128 * 3456 * 1024,
-        16,
-        at,
-        one,
-        wide,
-    )
+    acc, tsend, *seconds = lax.optimization_barrier((acc, tsend, *seconds))
+    tmine = across(on_chip(tmine, tsend))
     grad_in, mine, send = call(
         functools.partial(last_kernel, factor),
         (shape((4, 8, 1024), BF16), shape((896, 128), F32), shape((896, 128), BF16)),
-        [vmem((20, 96, 384), BF16), vmem((256, 128), F32)],
-        2 * 128 * 3456 * (1024 + 256),
-        16,
+        [vmem((20, 96, 384), BF16), vmem((16, 96, 128), BF16), vmem((16, 64, 128), BF16), vmem((256, 128), F32)],
+        2 * 128 * 3456 * (2048 + 256),
+        20,
         at,
-        first,
-        left,
-        right,
+        acc.reshape(16, 96, 128),
+        wide,
         d1,
-        mine2,
-        send2,
-        act,
+        *seconds,
     )
     send, tmine = lax.optimization_barrier((send, tmine))
     mine = across(on_chip(mine, send))

time: 65.6 us -> 67.3 us (1.026)
  the two profiles are of different devices: /device:TPU:17 before, /device:TPU:0 now
where the time goes in v5:
time: 67.3 us; the launch traced here: 66.7 us
  starting transfers between devices  22.9 us (34%)
  waiting for transfers between devices  19.3 us (29%)
  Pallas kernels  16.2 us (24%)
  local copies, waits for them, and re-layouts  7.27 us (11%)
  between operations  0.83 us (1%)
    pallas_call x8, Pallas kernels, call(): pl.pallas_call(kernel, out_shape=out_shape, in_specs=spec, out_specs=jax....  16.2 us
    ppermute x6, waiting for transfers between devices, swap(): return lax.ppermute(value, axis, [(i, i ^ bit) for i in range(n)])  13.7 us
    ppermute x6, starting transfers between devices, rotate(): return lax.ppermute(value, axis, [(i, (i + step) % n) for i in range(n)])  10.9 us
    unnamed x14, local copies, waits for them, and re-layouts  6.33 us
    ppermute x2, waiting for transfers between devices, rims(): right = lax.ppermute(low, 'gy', [(i + 1, i) for i in range(n - 1)])  5.51 us
    ppermute x2, starting transfers between devices, rims(): left = lax.ppermute(high, 'gy', [(i, i + 1) for i in range(n - 1)])  5.11 us
    ppermute x6, starting transfers between devices, swap(): return lax.ppermute(value, axis, [(i, i ^ bit) for i in range(n)])  4.3 us
    ppermute x2, starting transfers between devices, rims(): right = lax.ppermute(low, 'gy', [(i + 1, i) for i in range(n - 1)])  2.58 us
  transfers between devices with their start and end apart: 16, of which 7 were waited for; matrix products, arithmetic and copies ran while one was open for 2% of the time, Pallas kernels for 19%

profile of v5, /device:TPU:0, one launch (start us, length us, event | category | flops | bytes accessed | tf_op | source)
XLA Modules:
  0.0 66.7 jit_solution(11717127856876205070)
XLA Ops:
  0.6 1.6 %shard_map.111.a0 = bf16[512,128]{1,0:T(8,128)(2,1)} custom-call(bf16[8,4,8,128]{3,2,1,0:T(8,128)(2,1)} %og.1, bf16[4,8,1024]{2,1,0:T(8,128)(2,1)} %two.1), custom_call_target="tpu_custom_call" | custom-call | bytes 131072 | tf_op jit(solution)/shard_map/pallas_call | solution.py:200
  2.2 3.1 %collective-permute-start = (bf16[512,128]{1,0:T(8,128)(2,1)}, bf16[512,128]{1,0:T(8,128)(2,1)S(1)}, u32[]{:S(2)}, u32[]{:S(2)}) collective-permute-start(bf16[512,128]{1,0:T(8,128)(2,1)} %shard_map.111.a0), channel_id=1, source_target_pairs={{0,4},{4,8},{8,12},{12,0},{1,5},{5,9},{9,13},{13,1},{2,6},{6,10},{... | collective-permute-start | bytes 393224 | tf_op jit(solution)/shard_map/ppermute | solution.py:440
  5.3 2.6 %collective-permute-start.1 = (bf16[512,128]{1,0:T(8,128)(2,1)}, bf16[512,128]{1,0:T(8,128)(2,1)S(1)}, u32[]{:S(2)}, u32[]{:S(2)}) collective-permute-start(bf16[512,128]{1,0:T(8,128)(2,1)} %shard_map.111.a0), channel_id=1, source_target_pairs={{0,8},{4,12},{8,0},{12,4},{1,9},{5,13},{9,1},{13,5},{2,10},{6,14},... | collective-permute-start | bytes 393224 | tf_op jit(solution)/shard_map/ppermute | solution.py:440
  7.9 1.3 %collective-permute-start.2 = (bf16[512,128]{1,0:T(8,128)(2,1)}, bf16[512,128]{1,0:T(8,128)(2,1)S(1)}, u32[]{:S(2)}, u32[]{:S(2)}) collective-permute-start(bf16[512,128]{1,0:T(8,128)(2,1)} %shard_map.111.a0), channel_id=1, source_target_pairs={{0,12},{4,0},{8,4},{12,8},{1,13},{5,1},{9,5},{13,9},{2,14},{6,2},{... | collective-permute-start | bytes 393224 | tf_op jit(solution)/shard_map/ppermute | solution.py:440
  9.2 0.9 %fusion = (bf16[4,2,1024]{2,1,0:T(2,128)(2,1)S(1)}, bf16[4,2,1024]{2,1,0:T(2,128)(2,1)S(1)}) fusion(bf16[4,8,1024]{2,1,0:T(8,128)(2,1)} %one.1), kind=kLoop, calls=%fused_computation.5 | loop fusion | bytes 65536 | tf_op jit(solution)/shard_map/slice | solution.py:481
  10.2 1.3 %collective-permute-start.3 = (bf16[4,2,1024]{2,1,0:T(2,128)(2,1)S(1)}, bf16[4,2,1024]{2,1,0:T(2,128)(2,1)S(1)}, u32[]{:S(2)}, u32[]{:S(2)}) collective-permute-start(bf16[4,2,1024]{2,1,0:T(2,128)(2,1)S(1)} %get-tuple-element.57), channel_id=1, source_target_pairs={{0,1},{1,2},{2,3},{4,5},{5,6},{6,7},{8,9},{9,10},{10,11},{12,13},{... | collective-permute-start | bytes 49160 | tf_op jit(solution)/shard_map/ppermute | solution.py:450
  11.5 1.3 %collective-permute-start.4 = (bf16[4,2,1024]{2,1,0:T(2,128)(2,1)S(1)}, bf16[4,2,1024]{2,1,0:T(2,128)(2,1)S(1)}, u32[]{:S(2)}, u32[]{:S(2)}) collective-permute-start(bf16[4,2,1024]{2,1,0:T(2,128)(2,1)S(1)} %get-tuple-element.56), channel_id=1, source_target_pairs={{1,0},{2,1},{3,2},{5,4},{6,5},{7,6},{9,8},{10,9},{11,10},{13,12},{... | collective-permute-start | bytes 49160 | tf_op jit(solution)/shard_map/ppermute | solution.py:451
  12.8 0.0 collective-permute-done.3.left_ref
  12.8 3.5 %collective-permute-done.4.right_ref = bf16[4,2,1024]{2,1,0:T(2,128)(2,1)S(1)} collective-permute-done((bf16[4,2,1024]{2,1,0:T(2,128)(2,1)S(1)}, bf16[4,2,1024]{2,1,0:T(2,128)(2,1)S(1)}, u32[]{:S(2)}, u32[]{:S(2)}) %collective-permute-start.4) | collective-permute-done | bytes 16416 | tf_op jit(solution)/shard_map/ppermute | solution.py:451
  16.3 0.8 %copy-done.4 = bf16[4,8,1024]{2,1,0:T(8,128)(2,1)S(1)} copy-done((bf16[4,8,1024]{2,1,0:T(8,128)(2,1)S(1)}, bf16[4,8,1024]{2,1,0:T(8,128)(2,1)}, u32[]{:S(2)}) %copy-start.4) | copy-done | bytes 65560
  17.1 0.8 %copy-done.5 = bf16[4,8,1024]{2,1,0:T(8,128)(2,1)S(1)} copy-done((bf16[4,8,1024]{2,1,0:T(8,128)(2,1)S(1)}, bf16[4,8,1024]{2,1,0:T(8,128)(2,1)}, u32[]{:S(2)}) %copy-start.5) | copy-done | bytes 65560
  18.0 0.2 shard_map.113.p0
  18.2 0.7 %collective-permute-start.7 = (bf16[640,128]{1,0:T(8,128)(2,1)S(1)}, bf16[640,128]{1,0:T(8,128)(2,1)S(1)}, u32[]{:S(2)}, u32[]{:S(2)}) collective-permute-start(bf16[640,128]{1,0:T(8,128)(2,1)S(1)} %shard_map.113.p0), channel_id=1, source_target_pairs={{0,4},{4,8},{8,12},{12,0},{1,5},{5,9},{9,13},{13,1},{2,6},{6,10},{... | collective-permute-start | bytes 491528 | tf_op jit(solution)/shard_map/ppermute | solution.py:440
  18.9 0.3 collective-permute-start.8
  19.3 0.0 collective-permute-done.a1
  19.3 2.8 %collective-permute-start.9 = (bf16[640,128]{1,0:T(8,128)(2,1)S(1)}, bf16[640,128]{1,0:T(8,128)(2,1)S(1)}, u32[]{:S(2)}, u32[]{:S(2)}) collective-permute-start(bf16[640,128]{1,0:T(8,128)(2,1)S(1)} %shard_map.113.p0), channel_id=1, source_target_pairs={{0,12},{4,0},{8,4},{12,8},{1,13},{5,1},{9,5},{13,9},{2,14},{6,2},{... | collective-permute-start | bytes 491528 | tf_op jit(solution)/shard_map/ppermute | solution.py:440
  22.1 0.1 pad_add_fusion.at_ref
  22.2 1.0 %copy-done.1 = bf16[512,512]{1,0:T(8,128)(2,1)S(1)} copy-done((bf16[512,512]{1,0:T(8,128)(2,1)S(1)}, bf16[512,512]{1,0:T(8,128)(2,1)}, u32[]{:S(2)}) %copy-start.1) | copy-done | bytes 524312
  23.2 1.0 %copy-done.2 = bf16[27,64,64]{2,1,0:T(8,128)(2,1)S(1)} copy-done((bf16[27,64,64]{2,1,0:T(8,128)(2,1)S(1)}, bf16[27,64,64]{2,1,0:T(8,128)(2,1)}, u32[]{:S(2)}) %copy-start.2) | copy-done | bytes 221208
  24.2 1.0 %copy-done.3 = bf16[27,64,64]{2,1,0:T(8,128)(2,1)S(1)} copy-done((bf16[27,64,64]{2,1,0:T(8,128)(2,1)S(1)}, bf16[27,64,64]{2,1,0:T(8,128)(2,1)}, u32[]{:S(2)}) %copy-start.3) | copy-done | bytes 221208
  25.2 0.7 %copy-done.6 = s32[8,8]{1,0:T(8,128)S(1)} copy-done((s32[8,8]{1,0:T(8,128)S(1)}, s32[8,8]{1,0:T(8,128)}, u32[]{:S(2)}) %copy-start.6) | copy-done | bytes 280
  25.9 1.4 %shard_map.112 = (bf16[512,512]{1,0:T(8,128)(2,1)S(1)}, bf16[512,512]{1,0:T(8,128)(2,1)S(1)}, bf16[9,128,384]{2,1,0:T(8,128)(2,1)S(1)}, bf16[9,128,384]{2,1,0:T(8,128)(2,1)S(1)}) custom-call(bf16[512,512]{1,0:T(8,128)(2,1)S(1)} %copy-done.1, s32[8,8]{1,0:T(8,128)S(1)} %copy-done.6, bf16[27,64,64]{2,1,0:T(8,128)(2,1)S(1)} %copy-done.2, ...), custom_call_target="tpu_custom_call" | custom-call | flops 10000000 | bytes 966912 | tf_op jit(solution)/shard_map/pallas_call | solution.py:200
  27.3 0.0 collective-permute-done.1.a2
  27.4 0.0 copy-start
  27.4 0.9 %copy-done = bf16[512,128]{1,0:T(8,128)(2,1)S(1)} copy-done((bf16[512,128]{1,0:T(8,128)(2,1)S(1)}, bf16[512,128]{1,0:T(8,128)(2,1)}, u32[]{:S(2)}) %copy-start) | copy-done | bytes 131096
  28.3 1.1 %shard_map.114 = (bf16[8,2,64,128]{3,2,1,0:T(8,128)(2,1)S(1)}, bf16[16,32,128]{2,1,0:T(8,128)(2,1)S(1)}, bf16[16,32,128]{2,1,0:T(8,128)(2,1)S(1)}, f32[1024,128]{1,0:T(8,128)S(1)}, bf16[1024,128]{1,0:T(8,128)(2,1)S(1)}) custom-call(s32[2]{0:T(128)S(1)} %pad_add_fusion.at_ref, bf16[512,128]{1,0:T(8,128)(2,1)S(1)} %copy-done, ...), custom_call_target="tpu_custom_call" | custom-call | flops 268435456 | bytes 1572872 | tf_op jit(solution)/shard_map/pallas_call | solution.py:200
  29.4 3.8 %collective-permute-start.5 = (bf16[16,32,128]{2,1,0:T(8,128)(2,1)S(1)}, bf16[16,32,128]{2,1,0:T(8,128)(2,1)S(1)}, u32[]{:S(2)}, u32[]{:S(2)}) collective-permute-start(bf16[16,32,128]{2,1,0:T(8,128)(2,1)S(1)} %get-tuple-element.34), channel_id=1, source_target_pairs={{0,1},{1,2},{2,3},{4,5},{5,6},{6,7},{8,9},{9,10},{10,11},{12,13},{... | collective-permute-start | bytes 393224 | tf_op jit(solution)/shard_map/ppermute | solution.py:450
  33.3 1.3 %collective-permute-start.6 = (bf16[16,32,128]{2,1,0:T(8,128)(2,1)S(1)}, bf16[16,32,128]{2,1,0:T(8,128)(2,1)S(1)}, u32[]{:S(2)}, u32[]{:S(2)}) collective-permute-start(bf16[16,32,128]{2,1,0:T(8,128)(2,1)S(1)} %get-tuple-element.35), channel_id=1, source_target_pairs={{1,0},{2,1},{3,2},{5,4},{6,5},{7,6},{9,8},{10,9},{11,10},{13,12},{... | collective-permute-start | bytes 393224 | tf_op jit(solution)/shard_map/ppermute | solution.py:451
  34.6 0.0 collective-permute-done.5.left_ref
  34.6 2.0 %collective-permute-done.6.right_ref = bf16[16,32,128]{2,1,0:T(8,128)(2,1)S(1)} collective-permute-done((bf16[16,32,128]{2,1,0:T(8,128)(2,1)S(1)}, bf16[16,32,128]{2,1,0:T(8,128)(2,1)S(1)}, u32[]{:S(2)}, u32[]{:S(2)}) %collective-permute-start.6) | collective-permute-done | bytes 131104 | tf_op jit(solution)/shard_map/ppermute | solution.py:451
  36.6 3.2 %shard_map.115 = (bf16[20,128,384]{2,1,0:T(8,128)(2,1)S(1)}, f32[1536,128]{1,0:T(8,128)S(1)}) custom-call(bf16[16,64,128]{2,1,0:T(8,128)(2,1)S(1)} %bitcast.4, bf16[16,32,128]{2,1,0:T(8,128)(2,1)S(1)} %collective-permute-done.5.left_ref, bf16[16,32,128]{2,1,0:T(8,128)(2,1)S(1)} %collective-permute-done.6.right_ref, ...), custom_call_target="tpu_custom_call" | custom-call | bytes 1409024 | tf_op jit(solution)/shard_map/pallas_call | solution.py:200
  39.9 3.6 %collective-permute-start.10 = (bf16[1024,128]{1,0:T(8,128)(2,1)S(1)}, bf16[1024,128]{1,0:T(8,128)(2,1)S(1)}, u32[]{:S(2)}, u32[]{:S(2)}) collective-permute-start(bf16[1024,128]{1,0:T(8,128)(2,1)S(1)} %get-tuple-element.51), channel_id=1, source_target_pairs={{0,1},{1,0},{2,3},{3,2},{4,5},{5,4},{6,7},{7,6},{8,9},{9,8},{10,11... | collective-permute-start | bytes 786440 | tf_op jit(solution)/shard_map/ppermute | solution.py:445
  43.5 1.2 %collective-permute-done.10 = bf16[1024,128]{1,0:T(8,128)(2,1)S(1)} collective-permute-done((bf16[1024,128]{1,0:T(8,128)(2,1)S(1)}, bf16[1024,128]{1,0:T(8,128)(2,1)S(1)}, u32[]{:S(2)}, u32[]{:S(2)}) %collective-permute-start.10) | collective-permute-done | bytes 262176 | tf_op jit(solution)/shard_map/ppermute | solution.py:445
  44.6 0.1 add_convert_fusion
  44.7 0.2 collective-permute-start.11
  44.9 4.9 %shard_map.116 = (bf16[4,8,1024]{2,1,0:T(8,128)(2,1)}, f32[896,128]{1,0:T(8,128)S(1)}, bf16[896,128]{1,0:T(8,128)(2,1)S(1)}) custom-call(s32[2]{0:T(128)S(1)} %pad_add_fusion.at_ref, f32[16,96,128]{2,1,0:T(8,128)S(1)} %bitcast.5, bf16[20,128,384]{2,1,0:T(8,128)(2,1)S(1)} %get-tuple-element.41.wide_ref, bf16[9,128,384]{2,1,0:T(8,128)(2,1)S(1)} %get-tuple-element.42.w_ref, ...), custom_call_target="tpu_custom_call" | custom-call | flops 2038431744 | bytes 4292616 | tf_op jit(solution)/shard_map/pallas_call | solution.py:200
  49.8 3.6 %collective-permute-done.11 = bf16[1024,128]{1,0:T(8,128)(2,1)S(1)} collective-permute-done((bf16[1024,128]{1,0:T(8,128)(2,1)S(1)}, bf16[1024,128]{1,0:T(8,128)(2,1)S(1)}, u32[]{:S(2)}, u32[]{:S(2)}) %collective-permute-start.11) | collective-permute-done | bytes 262176 | tf_op jit(solution)/shard_map/ppermute | solution.py:445
  53.3 0.1 convert_add_fusion.mine_ref
  53.4 0.1 collective-permute-start.12
  53.5 1.5 %collective-permute-done.12 = bf16[896,128]{1,0:T(8,128)(2,1)S(1)} collective-permute-done((bf16[896,128]{1,0:T(8,128)(2,1)S(1)}, bf16[896,128]{1,0:T(8,128)(2,1)S(1)}, u32[]{:S(2)}, u32[]{:S(2)}) %collective-permute-start.12) | collective-permute-done | bytes 229408 | tf_op jit(solution)/shard_map/ppermute | solution.py:445
  55.0 0.1 add_convert_fusion.1
  55.0 0.4 collective-permute-start.13
  55.4 7.4 %collective-permute-done.13 = bf16[896,128]{1,0:T(8,128)(2,1)S(1)} collective-permute-done((bf16[896,128]{1,0:T(8,128)(2,1)S(1)}, bf16[896,128]{1,0:T(8,128)(2,1)S(1)}, u32[]{:S(2)}, u32[]{:S(2)}) %collective-permute-start.13) | collective-permute-done | bytes 229408 | tf_op jit(solution)/shard_map/ppermute | solution.py:445
  62.7 0.1 convert_add_fusion.1.mine_ref
  62.8 0.1 collective-permute-start.14
  62.9 1.6 %shard_map.118 = f32[512,512]{1,0:T(8,128)} custom-call(s32[2]{0:T(128)S(1)} %pad_add_fusion.at_ref, f32[1024,128]{1,0:T(8,128)S(1)} %convert_add_fusion.mine_ref, f32[1024,128]{1,0:T(8,128)S(1)} %collective-permute-done.15.other_ref), custom_call_target="tpu_custom_call" | custom-call | flops 10000000 | bytes 1048584 | tf_op jit(solution)/shard_map/pallas_call | solution.py:200
  64.5 0.1 collective-permute-done.14.other_ref
  64.7 2.0 %shard_map.117 = (f32[27,64,64]{2,1,0:T(8,128)}, f32[27,64,64]{2,1,0:T(8,128)}) custom-call(s32[2]{0:T(128)S(1)} %pad_add_fusion.at_ref, f32[896,128]{1,0:T(8,128)S(1)} %convert_add_fusion.1.mine_ref, f32[896,128]{1,0:T(8,128)S(1)} %collective-permute-done.14.other_ref), custom_call_target="tpu_custom_call" | custom-call | bytes 917512 | tf_op jit(solution)/shard_map/pallas_call | solution.py:200
  (12 shorter events, 0.0 us)
Async XLA Ops:
  2.2 17.1 %collective-permute-start = (bf16[512,128]{1,0:T(8,128)(2,1)}, bf16[512,128]{1,0:T(8,128)(2,1)S(1)}, u32[]{:S(2)}, u32[]{:S(2)}) collective-permute-start(bf16[512,128]{1,0:T(8,128)(2,1)} %shard_map.111.a0), channel_id=1, source_target_pairs={{0,4},{4,8},{8,12},{12,0},{1,5},{5,9},{9,13},{13,1},{2,6},{6,10},{... | collective-permute-start | bytes 393224 | tf_op jit(solution)/shard_map/ppermute | solution.py:440
  5.3 22.1 %collective-permute-start.1 = (bf16[512,128]{1,0:T(8,128)(2,1)}, bf16[512,128]{1,0:T(8,128)(2,1)S(1)}, u32[]{:S(2)}, u32[]{:S(2)}) collective-permute-start(bf16[512,128]{1,0:T(8,128)(2,1)} %shard_map.111.a0), channel_id=1, source_target_pairs={{0,8},{4,12},{8,0},{12,4},{1,9},{5,13},{9,1},{13,5},{2,10},{6,14},... | collective-permute-start | bytes 393224 | tf_op jit(solution)/shard_map/ppermute | solution.py:440
  7.9 19.5 %collective-permute-start.2 = (bf16[512,128]{1,0:T(8,128)(2,1)}, bf16[512,128]{1,0:T(8,128)(2,1)S(1)}, u32[]{:S(2)}, u32[]{:S(2)}) collective-permute-start(bf16[512,128]{1,0:T(8,128)(2,1)} %shard_map.111.a0), channel_id=1, source_target_pairs={{0,12},{4,0},{8,4},{12,8},{1,13},{5,1},{9,5},{13,9},{2,14},{6,2},{... | collective-permute-start | bytes 393224 | tf_op jit(solution)/shard_map/ppermute | solution.py:440
  10.2 2.6 %collective-permute-start.3 = (bf16[4,2,1024]{2,1,0:T(2,128)(2,1)S(1)}, bf16[4,2,1024]{2,1,0:T(2,128)(2,1)S(1)}, u32[]{:S(2)}, u32[]{:S(2)}) collective-permute-start(bf16[4,2,1024]{2,1,0:T(2,128)(2,1)S(1)} %get-tuple-element.57), channel_id=1, source_target_pairs={{0,1},{1,2},{2,3},{4,5},{5,6},{6,7},{8,9},{9,10},{10,11},{12,13},{... | collective-permute-start | bytes 49160 | tf_op jit(solution)/shard_map/ppermute | solution.py:450
  11.5 4.8 %collective-permute-start.4 = (bf16[4,2,1024]{2,1,0:T(2,128)(2,1)S(1)}, bf16[4,2,1024]{2,1,0:T(2,128)(2,1)S(1)}, u32[]{:S(2)}, u32[]{:S(2)}) collective-permute-start(bf16[4,2,1024]{2,1,0:T(2,128)(2,1)S(1)} %get-tuple-element.56), channel_id=1, source_target_pairs={{1,0},{2,1},{3,2},{5,4},{6,5},{7,6},{9,8},{10,9},{11,10},{13,12},{... | collective-permute-start | bytes 49160 | tf_op jit(solution)/shard_map/ppermute | solution.py:451
  16.3 0.8 %copy-start.4 = (bf16[4,8,1024]{2,1,0:T(8,128)(2,1)S(1)}, bf16[4,8,1024]{2,1,0:T(8,128)(2,1)}, u32[]{:S(2)}) copy-start(bf16[4,8,1024]{2,1,0:T(8,128)(2,1)} %one.1) | copy-start | bytes 196612
  17.1 0.8 %copy-start.5 = (bf16[4,8,1024]{2,1,0:T(8,128)(2,1)S(1)}, bf16[4,8,1024]{2,1,0:T(8,128)(2,1)}, u32[]{:S(2)}) copy-start(bf16[4,8,1024]{2,1,0:T(8,128)(2,1)} %act.1) | copy-start | bytes 196612
  18.2 21.6 %collective-permute-start.7 = (bf16[640,128]{1,0:T(8,128)(2,1)S(1)}, bf16[640,128]{1,0:T(8,128)(2,1)S(1)}, u32[]{:S(2)}, u32[]{:S(2)}) collective-permute-start(bf16[640,128]{1,0:T(8,128)(2,1)S(1)} %shard_map.113.p0), channel_id=1, source_target_pairs={{0,4},{4,8},{8,12},{12,0},{1,5},{5,9},{9,13},{13,1},{2,6},{6,10},{... | collective-permute-start | bytes 491528 | tf_op jit(solution)/shard_map/ppermute | solution.py:440
  18.9 20.9 %collective-permute-start.8 = (bf16[640,128]{1,0:T(8,128)(2,1)S(1)}, bf16[640,128]{1,0:T(8,128)(2,1)S(1)}, u32[]{:S(2)}, u32[]{:S(2)}) collective-permute-start(bf16[640,128]{1,0:T(8,128)(2,1)S(1)} %shard_map.113.p0), channel_id=1, source_target_pairs={{0,8},{4,12},{8,0},{12,4},{1,9},{5,13},{9,1},{13,5},{2,10},{6,14},... | collective-permute-start | bytes 491528 | tf_op jit(solution)/shard_map/ppermute | solution.py:440
  19.3 20.6 %collective-permute-start.9 = (bf16[640,128]{1,0:T(8,128)(2,1)S(1)}, bf16[640,128]{1,0:T(8,128)(2,1)S(1)}, u32[]{:S(2)}, u32[]{:S(2)}) collective-permute-start(bf16[640,128]{1,0:T(8,128)(2,1)S(1)} %shard_map.113.p0), channel_id=1, source_target_pairs={{0,12},{4,0},{8,4},{12,8},{1,13},{5,1},{9,5},{13,9},{2,14},{6,2},{... | collective-permute-start | bytes 491528 | tf_op jit(solution)/shard_map/ppermute | solution.py:440
  22.2 1.0 %copy-start.1 = (bf16[512,512]{1,0:T(8,128)(2,1)S(1)}, bf16[512,512]{1,0:T(8,128)(2,1)}, u32[]{:S(2)}) copy-start(bf16[512,512]{1,0:T(8,128)(2,1)} %wt.1) | copy-start | bytes 1572868
  23.2 1.0 %copy-start.2 = (bf16[27,64,64]{2,1,0:T(8,128)(2,1)S(1)}, bf16[27,64,64]{2,1,0:T(8,128)(2,1)}, u32[]{:S(2)}) copy-start(bf16[27,64,64]{2,1,0:T(8,128)(2,1)} %w2.1) | copy-start | bytes 663556
  24.2 1.0 %copy-start.3 = (bf16[27,64,64]{2,1,0:T(8,128)(2,1)S(1)}, bf16[27,64,64]{2,1,0:T(8,128)(2,1)}, u32[]{:S(2)}) copy-start(bf16[27,64,64]{2,1,0:T(8,128)(2,1)} %w1.1) | copy-start | bytes 663556
  25.2 0.7 %copy-start.6 = (s32[8,8]{1,0:T(8,128)S(1)}, s32[8,8]{1,0:T(8,128)}, u32[]{:S(2)}) copy-start(s32[8,8]{1,0:T(8,128)} %keep.1) | copy-start | bytes 772
  27.4 0.9 %copy-start = (bf16[512,128]{1,0:T(8,128)(2,1)S(1)}, bf16[512,128]{1,0:T(8,128)(2,1)}, u32[]{:S(2)}) copy-start(bf16[512,128]{1,0:T(8,128)(2,1)} %shard_map.111.a0) | copy-start | bytes 393220
  29.4 5.1 %collective-permute-start.5 = (bf16[16,32,128]{2,1,0:T(8,128)(2,1)S(1)}, bf16[16,32,128]{2,1,0:T(8,128)(2,1)S(1)}, u32[]{:S(2)}, u32[]{:S(2)}) collective-permute-start(bf16[16,32,128]{2,1,0:T(8,128)(2,1)S(1)} %get-tuple-element.34), channel_id=1, source_target_pairs={{0,1},{1,2},{2,3},{4,5},{5,6},{6,7},{8,9},{9,10},{10,11},{12,13},{... | collective-permute-start | bytes 393224 | tf_op jit(solution)/shard_map/ppermute | solution.py:450
  33.3 3.3 %collective-permute-start.6 = (bf16[16,32,128]{2,1,0:T(8,128)(2,1)S(1)}, bf16[16,32,128]{2,1,0:T(8,128)(2,1)S(1)}, u32[]{:S(2)}, u32[]{:S(2)}) collective-permute-start(bf16[16,32,128]{2,1,0:T(8,128)(2,1)S(1)} %get-tuple-element.35), channel_id=1, source_target_pairs={{1,0},{2,1},{3,2},{5,4},{6,5},{7,6},{9,8},{10,9},{11,10},{13,12},{... | collective-permute-start | bytes 393224 | tf_op jit(solution)/shard_map/ppermute | solution.py:451
  39.9 4.8 %collective-permute-start.10 = (bf16[1024,128]{1,0:T(8,128)(2,1)S(1)}, bf16[1024,128]{1,0:T(8,128)(2,1)S(1)}, u32[]{:S(2)}, u32[]{:S(2)}) collective-permute-start(bf16[1024,128]{1,0:T(8,128)(2,1)S(1)} %get-tuple-element.51), channel_id=1, source_target_pairs={{0,1},{1,0},{2,3},{3,2},{4,5},{5,4},{6,7},{7,6},{8,9},{9,8},{10,11... | collective-permute-start | bytes 786440 | tf_op jit(solution)/shard_map/ppermute | solution.py:445
  44.7 8.7 %collective-permute-start.11 = (bf16[1024,128]{1,0:T(8,128)(2,1)S(1)}, bf16[1024,128]{1,0:T(8,128)(2,1)S(1)}, u32[]{:S(2)}, u32[]{:S(2)}) collective-permute-start(bf16[1024,128]{1,0:T(8,128)(2,1)S(1)} %add_convert_fusion), channel_id=1, source_target_pairs={{0,2},{1,3},{2,0},{3,1},{4,6},{5,7},{6,4},{7,5},{8,10},{9,11},{10,... | collective-permute-start | bytes 786440 | tf_op jit(solution)/shard_map/ppermute | solution.py:445
  53.4 1.6 %collective-permute-start.12 = (bf16[896,128]{1,0:T(8,128)(2,1)S(1)}, bf16[896,128]{1,0:T(8,128)(2,1)S(1)}, u32[]{:S(2)}, u32[]{:S(2)}) collective-permute-start(bf16[896,128]{1,0:T(8,128)(2,1)S(1)} %get-tuple-element.52), channel_id=1, source_target_pairs={{0,1},{1,0},{2,3},{3,2},{4,5},{5,4},{6,7},{7,6},{8,9},{9,8},{10,11... | collective-permute-start | bytes 688136 | tf_op jit(solution)/shard_map/ppermute | solution.py:445
  55.0 7.7 %collective-permute-start.13 = (bf16[896,128]{1,0:T(8,128)(2,1)S(1)}, bf16[896,128]{1,0:T(8,128)(2,1)S(1)}, u32[]{:S(2)}, u32[]{:S(2)}) collective-permute-start(bf16[896,128]{1,0:T(8,128)(2,1)S(1)} %add_convert_fusion.1), channel_id=1, source_target_pairs={{0,2},{1,3},{2,0},{3,1},{4,6},{5,7},{6,4},{7,5},{8,10},{9,11},{10,... | collective-permute-start | bytes 688136 | tf_op jit(solution)/shard_map/ppermute | solution.py:445
  55.4 7.5 %collective-permute-start.15 = (f32[1024,128]{1,0:T(8,128)S(1)}, f32[1024,128]{1,0:T(8,128)S(1)}, u32[]{:S(2)}, u32[]{:S(2)}) collective-permute-start(f32[1024,128]{1,0:T(8,128)S(1)} %convert_add_fusion.mine_ref), channel_id=1, source_target_pairs={{0,1},{1,0},{2,3},{3,2},{4,5},{5,4},{6,7},{7,6},{8,9},{9,8},{10,11... | collective-permute-start | bytes 1572872 | tf_op jit(solution)/shard_map/ppermute | solution.py:445
  62.8 1.9 %collective-permute-start.14 = (f32[896,128]{1,0:T(8,128)S(1)}, f32[896,128]{1,0:T(8,128)S(1)}, u32[]{:S(2)}, u32[]{:S(2)}) collective-permute-start(f32[896,128]{1,0:T(8,128)S(1)} %convert_add_fusion.1.mine_ref), channel_id=1, source_target_pairs={{0,1},{1,0},{2,3},{3,2},{4,5},{5,4},{6,7},{7,6},{8,9},{9,8},{10,11... | collective-permute-start | bytes 1376264 | tf_op jit(solution)/shard_map/ppermute | solution.py:445

commit v6 on v3

--- a/solution.py
+++ b/solution.py
@@ -261,7 +261,7 @@
 
 
 def transition_kernel(
-    factor, at_ref, a0, a1, a2, a3, kept_ref, mask_ref, back_ref, one_ref, low_ref, high_ref, mine_ref, send_ref, og_ref, two_ref
+    factor, at_ref, a0, a1, a2, a3, kept_ref, mask_ref, back_ref, one_ref, chip_ref, cross_ref, mine_ref, send_ref, og_ref, two_ref
 ):
     me = at_ref[0]
     parts = (a0, a1, a2, a3)
@@ -285,10 +285,14 @@
             halves.append(jnp.where(pre > 0, grad, 0.0))
             cells.append(jnp.maximum(pre, 0.0).reshape(256, 128).astype(BF16))
         back_ref[:, p] = jnp.stack(halves, axis=2).reshape(8, 64, 128).astype(BF16)
-    low_ref[:, :, 0:32] = back_ref[:, :, 0:32]
-    high_ref[:, :, 0:32] = back_ref[:, :, 32:64]
-    low_ref[:, :, 32:48] = one_ref[:, 0:16].reshape(8, 2, 16, 128)
-    high_ref[:, :, 32:48] = one_ref[:, 48:64].reshape(8, 2, 16, 128)
+
+    def rim(high, ref):
+        at = 32 if high else 0
+        ref[:, :, 0:32] = back_ref[:, :, at : at + 32]
+        at = 48 if high else 0
+        ref[:, :, 32:48] = one_ref[:, at : at + 16].reshape(8, 2, 16, 128)
+
+    share(at_ref[1], rim, cross_ref, chip_ref)
     flat = jnp.concatenate(cells, axis=1)
     trans = lax.dot_general(flat, og, (((0,), (0,)), ((), ())), preferred_element_type=F32)
     trans = trans * mask_ref[...].astype(F32) * factor
@@ -327,6 +331,9 @@
     taps = []
     for g in sums:
         for l in range(3):
+            if g is None:
+                taps.append(jnp.zeros((64, 128), F32))
+                continue
             part = g[:, l * 128 : (l + 1) * 128]
             f = jnp.where(lane < 64, part[0:64], part[64:128])
             taps.append((f + pltpu.roll(f, 64, 1)) * factor)
@@ -338,40 +345,71 @@
     return lax.dot_general(rows, taps, (((1,), (1,)), ((), ())), preferred_element_type=F32)
 
 
+def own_kernel(factor, back_ref, one_ref, w_ref, acc_ref, sums_ref, wide_ref):
+    wide_ref[0:2] = jnp.zeros((2, 96, 384), BF16)
+    wide_ref[18:20] = jnp.zeros((2, 96, 384), BF16)
+    wide_ref[2:18, 0:16] = jnp.zeros((16, 16, 384), BF16)
+    wide_ref[2:18, 80:96] = jnp.zeros((16, 16, 384), BF16)
+    wide_ref[2:18, 16:80] = triple(back_ref[...].astype(F32))
+    act = jnp.maximum(one_ref[...].astype(F32), 0.0).reshape(1024, 128).T.astype(BF16)
+    sums = [None] * 9
+    for j in range(3):
+        part = jnp.zeros((1024, 128), F32)
+        for i in range(3):
+            part += apply_taps(wide_ref[4 - 2 * i : 20 - 2 * i, 16:80].reshape(1024, 384), w_ref[i * 3 + j])
+            rows = wide_ref[4 - 2 * i : 20 - 2 * i, 32 - 16 * j : 96 - 16 * j].reshape(1024, 384)
+            sums[i * 3 + j] = jnp.dot(act, rows, preferred_element_type=F32)
+        part = part.reshape(16, 64, 128)
+        if j == 0:
+            acc_ref[:, 0:64] = part
+            acc_ref[:, 64:96] = jnp.zeros((16, 32, 128), F32)
+        else:
+            acc_ref[:, 16 * j : 16 * j + 64] += part
+    for m, block in enumerate(fold(sums, factor)):
+        sums_ref[64 * m : 64 * m + 64] = block
+
+
 def conv_kernel(
-    factor, at_ref, back_ref, one_ref, left_ref, right_ref, w2_ref, w1_ref, i0, i1, i2, i3,
-    grad_ref, mine_ref, send_ref, wide_ref, outer_ref, in_ref, acc_ref, turn_ref,
+    factor, at_ref, acc_ref, sums_ref, one_ref, chip_ref, cross_ref, w2_ref, w1_ref, i0, i1, i2, i3,
+    grad_ref, mine_ref, send_ref, rim_ref, wide_ref, outer_ref, in_ref, turn_ref, first_ref,
 ):
     me = at_ref[0]
     parts = (i0, i1, i2, i3)
     n = len(parts)
     for s, part in enumerate(parts):
         in_ref[pl.ds(lax.rem(me + n - s, n) * 4, 4)] = part[...].reshape(4, 64, 128)
-    edge = jnp.zeros((2, 128, 384), BF16)
-    wide_ref[0:2] = edge
-    wide_ref[18:20] = edge
-    outer_ref[0:2] = edge[:, :96]
-    outer_ref[18:20] = edge[:, :96]
-    wide_ref[2:18, 0:32] = triple(left_ref[:, 0:32].astype(F32))
-    wide_ref[2:18, 32:96] = triple(back_ref[...].astype(F32))
-    wide_ref[2:18, 96:128] = triple(right_ref[:, 0:32].astype(F32))
-    for i in range(3):
-        for j in range(3):
-            rows = wide_ref[4 - 2 * i : 20 - 2 * i, 32 - 16 * j : 128 - 16 * j].reshape(1536, 384)
-            part = apply_taps(rows, w2_ref[i * 3 + j])
-            if i == 0 and j == 0:
-                acc_ref[...] = part
-            else:
-                acc_ref[...] += part
-    pre = jnp.concatenate([left_ref[:, 32:48], one_ref[...], right_ref[:, 32:48]], axis=1).astype(F32)
-    outer_ref[2:18] = triple(jnp.where(pre > 0, acc_ref[...].reshape(16, 96, 128), 0.0))
-    act = jnp.maximum(one_ref[...].astype(F32), 0.0).reshape(1024, 128).T.astype(BF16)
-    sums = []
-    for i in range(3):
-        for j in range(3):
-            rows = wide_ref[4 - 2 * i : 20 - 2 * i, 48 - 16 * j : 112 - 16 * j].reshape(1024, 384)
-            sums.append(jnp.dot(act, rows, preferred_element_type=F32))
+
+    def put(side, ref):
+        rim_ref[side] = ref[...]
+
+    share(at_ref[1], put, cross_ref, chip_ref)
+    wide_ref[:, 0:2] = jnp.zeros((2, 2, 32, 384), BF16)
+    wide_ref[:, 18:20] = jnp.zeros((2, 2, 32, 384), BF16)
+    outer_ref[0:2] = jnp.zeros((2, 96, 384), BF16)
+    outer_ref[18:20] = jnp.zeros((2, 96, 384), BF16)
+    for side in range(2):
+        wide_ref[side, 2:18] = triple(rim_ref[side, :, 0:32].astype(F32))
+    first_ref[...] = acc_ref[...]
+    act = jnp.maximum(one_ref[...].astype(F32), 0.0)
+    sums = [None] * 9
+    for side in range(2):
+        j = 2 - 2 * side
+        near = 16 - 16 * side
+        own = 48 * side
+        turned = act[:, own : own + 16].reshape(256, 128).T.astype(BF16)
+        far = jnp.zeros((512, 128), F32)
+        close = jnp.zeros((256, 128), F32)
+        for i in range(3):
+            xs = slice(4 - 2 * i, 20 - 2 * i)
+            rows = wide_ref[side, xs, near : near + 16].reshape(256, 384)
+            far += apply_taps(wide_ref[side, xs].reshape(512, 384), w2_ref[i * 3 + j])
+            close += apply_taps(rows, w2_ref[i * 3 + 1])
+            sums[i * 3 + j] = jnp.dot(turned, rows, preferred_element_type=F32)
+        first_ref[:, 64 * side : 64 * side + 32] += far.reshape(16, 32, 128)
+        first_ref[:, 80 * side : 80 * side + 16] += close.reshape(16, 16, 128)
     second = fold(sums, factor)
+    pre = jnp.concatenate([rim_ref[0, :, 32:48], one_ref[...], rim_ref[1, :, 32:48]], axis=1).astype(F32)
+    outer_ref[2:18] = triple(jnp.where(pre > 0, first_ref[...], 0.0))
     act = in_ref[...].astype(F32).reshape(1024, 128).T.astype(BF16)
     sums = []
     grad = jnp.zeros((256, 128), F32)
@@ -390,7 +428,9 @@
     def emit(half, ref):
         for m in range(7):
             ref[64 * m : 64 * m + 64] = first[7 * half + m].astype(ref.dtype)
-            ref[448 + 64 * m : 512 + 64 * m] = second[7 * half + m].astype(ref.dtype)
+            at = 448 * half + 64 * m
+            block = second[7 * half + m] + sums_ref[at : at + 64]
+            ref[448 + 64 * m : 512 + 64 * m] = block.astype(ref.dtype)
 
     share(at_ref[1], emit, mine_ref, send_ref)
 
@@ -476,7 +516,7 @@
         (w_two,),
         (w_one,),
     )
-    back, one, low, high, tmine, tsend = call(
+    back, one, chip, cross, tmine, tsend = call(
         functools.partial(transition_kernel, factor),
         (
             shape((8, 2, 64, 128), BF16),
@@ -496,37 +536,53 @@
     )
     tsend, *seconds = lax.optimization_barrier((tsend, *seconds))
     n = lax.axis_size("gy")
-    from_left = lax.ppermute(high, "gy", [(i, i + 1) for i in range(n - 1)])
-    from_right = lax.ppermute(low, "gy", [(i + 1, i) for i in range(n - 1)])
+    pairs = [(i, i + 1) for i in range(1, n - 1, 2)]
+    cross = lax.ppermute(cross, "gy", pairs + [(j, i) for i, j in pairs])
+    chip = swap(chip, "gy", 1)
+    acc, sums = call(
+        functools.partial(own_kernel, factor),
+        (shape((16, 96, 128), F32), shape((896, 128), F32)),
+        [vmem((20, 96, 384), BF16)],
+        2 * 128 * 3456 * 2048,
+        16,
+        back.reshape(16, 64, 128),
+        one,
+        d2,
+    )
     tmine = on_chip(tmine, tsend)
-    tmine, from_left, from_right = lax.optimization_barrier((tmine, from_left, from_right))
+    tmine, chip, cross, acc = lax.optimization_barrier((tmine, chip, cross, acc))
     tmine = across(tmine)
     grad_in, mine, send = call(
         functools.partial(conv_kernel, factor),
         (shape((4, 8, 1024), BF16), shape((896, 128), F32), shape((896, 128), BF16)),
         [
-            vmem((20, 128, 384), BF16),
+            vmem((2, 16, 48, 128), BF16),
+            vmem((2, 20, 32, 384), BF16),
             vmem((20, 96, 384), BF16),
             vmem((16, 64, 128), BF16),
-            vmem((1536, 128), F32),
             vmem((256, 128), F32),
+            vmem((16, 96, 128), F32),
         ],
-        2 * 128 * 3456 * (1536 + 1024 + 1024 + 256),
+        2 * 128 * 3456 * (512 + 1024 + 256),
         20,
         at,
-        back.reshape(16, 64, 128),
+        acc,
+        sums,
         one,
-        from_left.reshape(16, 48, 128),
-        from_right.reshape(16, 48, 128),
+        chip.reshape(16, 48, 128),
+        cross.reshape(16, 48, 128),
         d2,
         d1,
         *seconds,
     )
     send, tmine = lax.optimization_barrier((send, tmine))
-    mine = across(on_chip(mine, send))
+    mine = on_chip(mine, send)
+    away = swap(mine, "gy", 2)
     tother = swap(tmine, "gy", 1)
+    grad_w_trans = call(trans_kernel, shape((512, 512), F32), [], 10**7, 6, at, tmine, tother)
+    away, grad_w_trans = lax.optimization_barrier((away, grad_w_trans))
+    mine = mine.astype(F32) + away.astype(F32)
     other = swap(mine, "gy", 1)
-    grad_w_trans = call(trans_kernel, shape((512, 512), F32), [], 10**7, 6, at, tmine, tother)
     grad_w_one, grad_w_two = call(
         spread_kernel,
         (shape((27, 64, 64), F32), shape((27, 64, 64), F32)),

time: 61.1 us -> 59.2 us (0.969)
  starting transfers between devices: 19.9 us -> 16.3 us
  Pallas kernels: 15.5 us -> 16.5 us
    ppermute x6 -> x7, waiting for transfers between devices: 7.41 us -> 10.6 us  [swap(): return lax.ppermute(value, axis, [(i, i ^ bit) for i in range(n)])]
    ppermute x2 -> x1, starting transfers between devices: 3.7 us -> 0.66 us  [slab_body(): cross = lax.ppermute(cross, 'gy', pairs + [(j, i) for i, j in pairs])]
    ppermute x2 -> x1, waiting for transfers between devices: 2.49 us -> 0.01 us  [slab_body(): cross = lax.ppermute(cross, 'gy', pairs + [(j, i) for i, j in pairs])]
    pallas_call x6 -> x7, Pallas kernels: 15.5 us -> 16.5 us  [call(): pl.pallas_call(kernel, out_shape=out_shape, in_specs=spec, out_specs=jax....]
    ppermute x6 -> x7, starting transfers between devices: 6.11 us -> 5.6 us  [swap(): return lax.ppermute(value, axis, [(i, i ^ bit) for i in range(n)])]
  transfers between devices with their start and end apart: 14 -> 14, of which waited for: 8 -> 8; matrix products, arithmetic and copies ran while one was open for 0% -> 0% of each run, Pallas kernels for 19% -> 22%
where the time goes in v6:
time: 59.2 us; the launch traced here: 58.8 us
  waiting for transfers between devices  21.8 us (37%)
  Pallas kernels  16.5 us (28%)
  starting transfers between devices  16.3 us (28%)
  local copies, waits for them, and re-layouts  3.08 us (5%)
  between operations  0.75 us (1%)
    pallas_call x7, Pallas kernels, call(): pl.pallas_call(kernel, out_shape=out_shape, in_specs=spec, out_specs=jax....  16.5 us
    ppermute x6, waiting for transfers between devices, rotate(): return lax.ppermute(value, axis, [(i, (i + step) % n) for i in range(n)])  11.2 us
    ppermute x7, waiting for transfers between devices, swap(): return lax.ppermute(value, axis, [(i, i ^ bit) for i in range(n)])  10.6 us
    ppermute x6, starting transfers between devices, rotate(): return lax.ppermute(value, axis, [(i, (i + step) % n) for i in range(n)])  10.1 us
    ppermute x7, starting transfers between devices, swap(): return lax.ppermute(value, axis, [(i, i ^ bit) for i in range(n)])  5.6 us
    unnamed x12, local copies, waits for them, and re-layouts  3.08 us
  transfers between devices with their start and end apart: 14, of which 8 were waited for; matrix products, arithmetic and copies ran while one was open for 0% of the time, Pallas kernels for 22%

profile of v6, /device:TPU:0, one launch (start us, length us, event | category | flops | bytes accessed | tf_op | source)
XLA Modules:
  0.0 58.8 jit_solution(2947423681254578569)
XLA Ops:
  0.6 1.7 %shard_map.111 = (bf16[768,128]{1,0:T(8,128)(2,1)}, bf16[256,128]{1,0:T(8,128)(2,1)}) custom-call(bf16[8,4,8,128]{3,2,1,0:T(8,128)(2,1)} %og.1, bf16[4,8,1024]{2,1,0:T(8,128)(2,1)} %two.1, bf16[4,8,1024]{2,1,0:T(8,128)(2,1)} %one.1, bf16[4,8,1024]{2,1,0:T(8,128)(2,1)} %act.1), custom_call_target="tpu_custom_call" | custom-call | bytes 262144 | tf_op jit(solution)/shard_map/pallas_call | solution.py:200
  2.3 3.1 %collective-permute-start = (bf16[768,128]{1,0:T(8,128)(2,1)}, bf16[768,128]{1,0:T(8,128)(2,1)S(1)}, u32[]{:S(2)}, u32[]{:S(2)}) collective-permute-start(bf16[768,128]{1,0:T(8,128)(2,1)} %get-tuple-element.36.a0), channel_id=1, source_target_pairs={{0,4},{4,8},{8,12},{12,0},{1,5},{5,9},{9,13},{13,1},{2,6},{6,10},{... | collective-permute-start | bytes 589832 | tf_op jit(solution)/shard_map/ppermute | solution.py:461
  5.4 2.6 %collective-permute-start.1 = (bf16[768,128]{1,0:T(8,128)(2,1)}, bf16[768,128]{1,0:T(8,128)(2,1)S(1)}, u32[]{:S(2)}, u32[]{:S(2)}) collective-permute-start(bf16[768,128]{1,0:T(8,128)(2,1)} %get-tuple-element.36.a0), channel_id=1, source_target_pairs={{0,8},{4,12},{8,0},{12,4},{1,9},{5,13},{9,1},{13,5},{2,10},{6,14},... | collective-permute-start | bytes 589832 | tf_op jit(solution)/shard_map/ppermute | solution.py:461
  8.0 1.3 %collective-permute-start.2 = (bf16[768,128]{1,0:T(8,128)(2,1)}, bf16[768,128]{1,0:T(8,128)(2,1)S(1)}, u32[]{:S(2)}, u32[]{:S(2)}) collective-permute-start(bf16[768,128]{1,0:T(8,128)(2,1)} %get-tuple-element.36.a0), channel_id=1, source_target_pairs={{0,12},{4,0},{8,4},{12,8},{1,13},{5,1},{9,5},{13,9},{2,14},{6,2},{... | collective-permute-start | bytes 589832 | tf_op jit(solution)/shard_map/ppermute | solution.py:461
  9.3 0.7 %collective-permute-start.3 = (bf16[256,128]{1,0:T(8,128)(2,1)}, bf16[256,128]{1,0:T(8,128)(2,1)S(1)}, u32[]{:S(2)}, u32[]{:S(2)}) collective-permute-start(bf16[256,128]{1,0:T(8,128)(2,1)} %get-tuple-element.54.i0), channel_id=1, source_target_pairs={{0,4},{4,8},{8,12},{12,0},{1,5},{5,9},{9,13},{13,1},{2,6},{6,10},{... | collective-permute-start | bytes 196616 | tf_op jit(solution)/shard_map/ppermute | solution.py:461
  10.0 0.3 collective-permute-start.4
  10.3 0.0 copy-start.4
  10.3 3.1 %collective-permute-done.a1 = bf16[768,128]{1,0:T(8,128)(2,1)S(1)} collective-permute-done((bf16[768,128]{1,0:T(8,128)(2,1)}, bf16[768,128]{1,0:T(8,128)(2,1)S(1)}, u32[]{:S(2)}, u32[]{:S(2)}) %collective-permute-start) | collective-permute-done | bytes 196640 | tf_op jit(solution)/shard_map/ppermute | solution.py:461
  13.5 2.1 %collective-permute-start.5 = (bf16[256,128]{1,0:T(8,128)(2,1)}, bf16[256,128]{1,0:T(8,128)(2,1)S(1)}, u32[]{:S(2)}, u32[]{:S(2)}) collective-permute-start(bf16[256,128]{1,0:T(8,128)(2,1)} %get-tuple-element.54.i0), channel_id=1, source_target_pairs={{0,12},{4,0},{8,4},{12,8},{1,13},{5,1},{9,5},{13,9},{2,14},{6,2},{... | collective-permute-start | bytes 196616 | tf_op jit(solution)/shard_map/ppermute | solution.py:461
  15.5 0.1 pad_add_fusion.at_ref
  15.6 0.0 copy-done.4
  15.6 0.0 copy-start
  15.6 1.0 %copy-done = bf16[512,512]{1,0:T(8,128)(2,1)S(1)} copy-done((bf16[512,512]{1,0:T(8,128)(2,1)S(1)}, bf16[512,512]{1,0:T(8,128)(2,1)}, u32[]{:S(2)}) %copy-start) | copy-done | bytes 524312
  16.7 1.0 %copy-done.1 = bf16[27,64,64]{2,1,0:T(8,128)(2,1)S(1)} copy-done((bf16[27,64,64]{2,1,0:T(8,128)(2,1)S(1)}, bf16[27,64,64]{2,1,0:T(8,128)(2,1)}, u32[]{:S(2)}) %copy-start.1) | copy-done | bytes 221208
  17.7 0.0 copy-start.2
  17.7 1.0 %copy-done.2 = bf16[27,64,64]{2,1,0:T(8,128)(2,1)S(1)} copy-done((bf16[27,64,64]{2,1,0:T(8,128)(2,1)S(1)}, bf16[27,64,64]{2,1,0:T(8,128)(2,1)}, u32[]{:S(2)}) %copy-start.2) | copy-done | bytes 221208
  18.7 1.4 %shard_map.112 = (bf16[512,512]{1,0:T(8,128)(2,1)S(1)}, bf16[512,512]{1,0:T(8,128)(2,1)S(1)}, bf16[9,128,384]{2,1,0:T(8,128)(2,1)S(1)}, bf16[9,128,384]{2,1,0:T(8,128)(2,1)S(1)}) custom-call(bf16[512,512]{1,0:T(8,128)(2,1)S(1)} %copy-done, s32[8,8]{1,0:T(8,128)S(1)} %copy-done.4, bf16[27,64,64]{2,1,0:T(8,128)(2,1)S(1)} %copy-done.1, ...), custom_call_target="tpu_custom_call" | custom-call | flops 10000000 | bytes 966912 | tf_op jit(solution)/shard_map/pallas_call | solution.py:200
  20.1 1.8 %collective-permute-done.1.a2 = bf16[768,128]{1,0:T(8,128)(2,1)S(1)} collective-permute-done((bf16[768,128]{1,0:T(8,128)(2,1)}, bf16[768,128]{1,0:T(8,128)(2,1)S(1)}, u32[]{:S(2)}, u32[]{:S(2)}) %collective-permute-start.1) | collective-permute-done | bytes 196640 | tf_op jit(solution)/shard_map/ppermute | solution.py:461
  21.9 0.0 collective-permute-done.2.a3
  21.9 0.0 copy-done.3
  22.0 1.3 %shard_map.113 = (bf16[8,2,64,128]{3,2,1,0:T(8,128)(2,1)S(1)}, bf16[16,64,128]{2,1,0:T(8,128)(2,1)S(1)}, bf16[8,2,48,128]{3,2,1,0:T(8,128)(2,1)S(1)}, bf16[8,2,4...) custom-call(s32[2]{0:T(128)S(1)} %pad_add_fusion.at_ref, ...), custom_call_target="tpu_custom_call" | custom-call | flops 268435456 | bytes 1835016 | tf_op jit(solution)/shard_map/pallas_call | solution.py:200
  23.3 0.0 collective-permute-done.3.i1
  23.3 6.2 %collective-permute-done.4.i2 = bf16[256,128]{1,0:T(8,128)(2,1)S(1)} collective-permute-done((bf16[256,128]{1,0:T(8,128)(2,1)}, bf16[256,128]{1,0:T(8,128)(2,1)S(1)}, u32[]{:S(2)}, u32[]{:S(2)}) %collective-permute-start.4) | collective-permute-done | bytes 65568 | tf_op jit(solution)/shard_map/ppermute | solution.py:461
  29.5 0.0 collective-permute-done.5.i3
  29.5 0.0 collective-permute-start.6
  29.5 0.5 collective-permute-start.7
  30.0 0.7 %collective-permute-start.8 = (bf16[8,2,48,128]{3,2,1,0:T(8,128)(2,1)S(1)}, bf16[8,2,48,128]{3,2,1,0:T(8,128)(2,1)S(1)}, u32[]{:S(2)}, u32[]{:S(2)}) collective-permute-start(bf16[8,2,48,128]{3,2,1,0:T(8,128)(2,1)S(1)} %get-tuple-element.44), channel_id=1, source_target_pairs={{1,2},{2,1},{5,6},{6,5},{9,10},{10,9},{13,14},{14,13},{17,18},{18,... | collective-permute-start | bytes 589832 | tf_op jit(solution)/shard_map/ppermute | solution.py:540
  30.7 3.6 %shard_map.114 = (f32[16,96,128]{2,1,0:T(8,128)S(1)}, f32[896,128]{1,0:T(8,128)S(1)}) custom-call(bf16[16,64,128]{2,1,0:T(8,128)(2,1)S(1)} %bitcast.5, bf16[16,64,128]{2,1,0:T(8,128)(2,1)S(1)} %get-tuple-element.46.one_ref, bf16[9,128,384]{2,1,0:T(8,128)(2,1)S(1)} %get-tuple-element.47.w_ref.w2_ref), custom_call_target="tpu_custom_call" | custom-call | flops 1811939328 | bytes 1409024 | tf_op jit(solution)/shard_map/pallas_call | solution.py:200
  34.3 0.0 collective-permute-done.6
  34.3 0.0 copy-start.5
  34.3 0.1 add_convert_fusion
  34.4 0.0 collective-permute-done.7
  34.4 0.0 collective-permute-done.8
  34.4 4.1 %collective-permute-start.9 = (bf16[1024,128]{1,0:T(8,128)(2,1)S(1)}, bf16[1024,128]{1,0:T(8,128)(2,1)S(1)}, u32[]{:S(2)}, u32[]{:S(2)}) collective-permute-start(bf16[1024,128]{1,0:T(8,128)(2,1)S(1)} %add_convert_fusion), channel_id=1, source_target_pairs={{0,2},{1,3},{2,0},{3,1},{4,6},{5,7},{6,4},{7,5},{8,10},{9,11},{10,... | collective-permute-start | bytes 786440 | tf_op jit(solution)/shard_map/ppermute | solution.py:466
  38.5 0.0 copy-done.5
  38.5 4.9 %shard_map.115 = (bf16[4,8,1024]{2,1,0:T(8,128)(2,1)}, f32[896,128]{1,0:T(8,128)S(1)}, bf16[896,128]{1,0:T(8,128)(2,1)S(1)}) custom-call(s32[2]{0:T(128)S(1)} %pad_add_fusion.at_ref, f32[16,96,128]{2,1,0:T(8,128)S(1)} %get-tuple-element.49.acc_ref, f32[896,128]{1,0:T(8,128)S(1)} %get-tuple-element.50.sums_ref, ...), custom_call_target="tpu_custom_call" | custom-call | flops 1585446912 | bytes 3932168 | tf_op jit(solution)/shard_map/pallas_call | solution.py:200
  43.4 2.1 %collective-permute-done.9 = bf16[1024,128]{1,0:T(8,128)(2,1)S(1)} collective-permute-done((bf16[1024,128]{1,0:T(8,128)(2,1)S(1)}, bf16[1024,128]{1,0:T(8,128)(2,1)S(1)}, u32[]{:S(2)}, u32[]{:S(2)}) %collective-permute-start.9) | collective-permute-done | bytes 262176 | tf_op jit(solution)/shard_map/ppermute | solution.py:466
  45.5 0.1 convert_add_fusion.mine_ref
  45.5 0.1 collective-permute-start.10
  45.6 0.5 collective-permute-start.12
  46.1 1.0 %collective-permute-done.10 = bf16[896,128]{1,0:T(8,128)(2,1)S(1)} collective-permute-done((bf16[896,128]{1,0:T(8,128)(2,1)S(1)}, bf16[896,128]{1,0:T(8,128)(2,1)S(1)}, u32[]{:S(2)}, u32[]{:S(2)}) %collective-permute-start.10) | collective-permute-done | bytes 229408 | tf_op jit(solution)/shard_map/ppermute | solution.py:466
  47.1 0.4 collective-permute-start.11
  47.5 0.3 collective-permute-done.12.other_ref
  47.8 1.6 %shard_map.116 = f32[512,512]{1,0:T(8,128)} custom-call(s32[2]{0:T(128)S(1)} %pad_add_fusion.at_ref, f32[1024,128]{1,0:T(8,128)S(1)} %convert_add_fusion.mine_ref, f32[1024,128]{1,0:T(8,128)S(1)} %collective-permute-done.12.other_ref), custom_call_target="tpu_custom_call" | custom-call | flops 10000000 | bytes 1048584 | tf_op jit(solution)/shard_map/pallas_call | solution.py:200
  49.5 5.4 %collective-permute-done.11 = bf16[896,128]{1,0:T(8,128)(2,1)S(1)} collective-permute-done((bf16[896,128]{1,0:T(8,128)(2,1)S(1)}, bf16[896,128]{1,0:T(8,128)(2,1)S(1)}, u32[]{:S(2)}, u32[]{:S(2)}) %collective-permute-start.11) | collective-permute-done | bytes 229408 | tf_op jit(solution)/shard_map/ppermute | solution.py:466
  54.9 0.1 collective-permute-start.13
  55.0 1.8 %collective-permute-done.13.other_ref = f32[896,128]{1,0:T(8,128)S(1)} collective-permute-done((f32[896,128]{1,0:T(8,128)S(1)}, f32[896,128]{1,0:T(8,128)S(1)}, u32[]{:S(2)}, u32[]{:S(2)}) %collective-permute-start.13) | collective-permute-done | bytes 458784 | tf_op jit(solution)/shard_map/ppermute | solution.py:466
  56.8 2.0 %shard_map.117 = (f32[27,64,64]{2,1,0:T(8,128)}, f32[27,64,64]{2,1,0:T(8,128)}) custom-call(s32[2]{0:T(128)S(1)} %pad_add_fusion.at_ref, f32[896,128]{1,0:T(8,128)S(1)} %convert_add_fusion.1.mine_ref, f32[896,128]{1,0:T(8,128)S(1)} %collective-permute-done.13.other_ref), custom_call_target="tpu_custom_call" | custom-call | bytes 917512 | tf_op jit(solution)/shard_map/pallas_call | solution.py:200
  (4 shorter events, 0.1 us)
Async XLA Ops:
  2.3 11.2 %collective-permute-start = (bf16[768,128]{1,0:T(8,128)(2,1)}, bf16[768,128]{1,0:T(8,128)(2,1)S(1)}, u32[]{:S(2)}, u32[]{:S(2)}) collective-permute-start(bf16[768,128]{1,0:T(8,128)(2,1)} %get-tuple-element.36.a0), channel_id=1, source_target_pairs={{0,4},{4,8},{8,12},{12,0},{1,5},{5,9},{9,13},{13,1},{2,6},{6,10},{... | collective-permute-start | bytes 589832 | tf_op jit(solution)/shard_map/ppermute | solution.py:461
  5.4 16.6 %collective-permute-start.1 = (bf16[768,128]{1,0:T(8,128)(2,1)}, bf16[768,128]{1,0:T(8,128)(2,1)S(1)}, u32[]{:S(2)}, u32[]{:S(2)}) collective-permute-start(bf16[768,128]{1,0:T(8,128)(2,1)} %get-tuple-element.36.a0), channel_id=1, source_target_pairs={{0,8},{4,12},{8,0},{12,4},{1,9},{5,13},{9,1},{13,5},{2,10},{6,14},... | collective-permute-start | bytes 589832 | tf_op jit(solution)/shard_map/ppermute | solution.py:461
  8.0 14.0 %collective-permute-start.2 = (bf16[768,128]{1,0:T(8,128)(2,1)}, bf16[768,128]{1,0:T(8,128)(2,1)S(1)}, u32[]{:S(2)}, u32[]{:S(2)}) collective-permute-start(bf16[768,128]{1,0:T(8,128)(2,1)} %get-tuple-element.36.a0), channel_id=1, source_target_pairs={{0,12},{4,0},{8,4},{12,8},{1,13},{5,1},{9,5},{13,9},{2,14},{6,2},{... | collective-permute-start | bytes 589832 | tf_op jit(solution)/shard_map/ppermute | solution.py:461
  9.3 14.0 %collective-permute-start.3 = (bf16[256,128]{1,0:T(8,128)(2,1)}, bf16[256,128]{1,0:T(8,128)(2,1)S(1)}, u32[]{:S(2)}, u32[]{:S(2)}) collective-permute-start(bf16[256,128]{1,0:T(8,128)(2,1)} %get-tuple-element.54.i0), channel_id=1, source_target_pairs={{0,4},{4,8},{8,12},{12,0},{1,5},{5,9},{9,13},{13,1},{2,6},{6,10},{... | collective-permute-start | bytes 196616 | tf_op jit(solution)/shard_map/ppermute | solution.py:461
  10.0 19.5 %collective-permute-start.4 = (bf16[256,128]{1,0:T(8,128)(2,1)}, bf16[256,128]{1,0:T(8,128)(2,1)S(1)}, u32[]{:S(2)}, u32[]{:S(2)}) collective-permute-start(bf16[256,128]{1,0:T(8,128)(2,1)} %get-tuple-element.54.i0), channel_id=1, source_target_pairs={{0,8},{4,12},{8,0},{12,4},{1,9},{5,13},{9,1},{13,5},{2,10},{6,14},... | collective-permute-start | bytes 196616 | tf_op jit(solution)/shard_map/ppermute | solution.py:461
  10.3 5.3 %copy-start.4 = (s32[8,8]{1,0:T(8,128)S(1)}, s32[8,8]{1,0:T(8,128)}, u32[]{:S(2)}) copy-start(s32[8,8]{1,0:T(8,128)} %keep.1) | copy-start | bytes 772
  13.5 16.1 %collective-permute-start.5 = (bf16[256,128]{1,0:T(8,128)(2,1)}, bf16[256,128]{1,0:T(8,128)(2,1)S(1)}, u32[]{:S(2)}, u32[]{:S(2)}) collective-permute-start(bf16[256,128]{1,0:T(8,128)(2,1)} %get-tuple-element.54.i0), channel_id=1, source_target_pairs={{0,12},{4,0},{8,4},{12,8},{1,13},{5,1},{9,5},{13,9},{2,14},{6,2},{... | collective-permute-start | bytes 196616 | tf_op jit(solution)/shard_map/ppermute | solution.py:461
  15.6 1.0 %copy-start = (bf16[512,512]{1,0:T(8,128)(2,1)S(1)}, bf16[512,512]{1,0:T(8,128)(2,1)}, u32[]{:S(2)}) copy-start(bf16[512,512]{1,0:T(8,128)(2,1)} %wt.1) | copy-start | bytes 1572868
  16.6 1.0 %copy-start.1 = (bf16[27,64,64]{2,1,0:T(8,128)(2,1)S(1)}, bf16[27,64,64]{2,1,0:T(8,128)(2,1)}, u32[]{:S(2)}) copy-start(bf16[27,64,64]{2,1,0:T(8,128)(2,1)} %w2.1) | copy-start | bytes 663556
  17.7 1.0 %copy-start.2 = (bf16[27,64,64]{2,1,0:T(8,128)(2,1)S(1)}, bf16[27,64,64]{2,1,0:T(8,128)(2,1)}, u32[]{:S(2)}) copy-start(bf16[27,64,64]{2,1,0:T(8,128)(2,1)} %w1.1) | copy-start | bytes 663556
  18.7 3.3 %copy-start.3 = (bf16[768,128]{1,0:T(8,128)(2,1)S(1)}, bf16[768,128]{1,0:T(8,128)(2,1)}, u32[]{:S(2)}) copy-start(bf16[768,128]{1,0:T(8,128)(2,1)} %get-tuple-element.36.a0) | copy-start | bytes 589828
  29.5 4.8 %collective-permute-start.6 = (bf16[1024,128]{1,0:T(8,128)(2,1)S(1)}, bf16[1024,128]{1,0:T(8,128)(2,1)S(1)}, u32[]{:S(2)}, u32[]{:S(2)}) collective-permute-start(bf16[1024,128]{1,0:T(8,128)(2,1)S(1)} %get-tuple-element.42), channel_id=1, source_target_pairs={{0,1},{1,0},{2,3},{3,2},{4,5},{5,4},{6,7},{7,6},{8,9},{9,8},{10,11... | collective-permute-start | bytes 786440 | tf_op jit(solution)/shard_map/ppermute | solution.py:466
  29.5 4.8 %collective-permute-start.7 = (bf16[8,2,48,128]{3,2,1,0:T(8,128)(2,1)S(1)}, bf16[8,2,48,128]{3,2,1,0:T(8,128)(2,1)S(1)}, u32[]{:S(2)}, u32[]{:S(2)}) collective-permute-start(bf16[8,2,48,128]{3,2,1,0:T(8,128)(2,1)S(1)} %get-tuple-element.43), channel_id=1, source_target_pairs={{0,1},{1,0},{2,3},{3,2},{4,5},{5,4},{6,7},{7,6},{8,9},{9,8},{10,11... | collective-permute-start | bytes 589832 | tf_op jit(solution)/shard_map/ppermute | solution.py:466
  30.0 4.3 %collective-permute-start.8 = (bf16[8,2,48,128]{3,2,1,0:T(8,128)(2,1)S(1)}, bf16[8,2,48,128]{3,2,1,0:T(8,128)(2,1)S(1)}, u32[]{:S(2)}, u32[]{:S(2)}) collective-permute-start(bf16[8,2,48,128]{3,2,1,0:T(8,128)(2,1)S(1)} %get-tuple-element.44), channel_id=1, source_target_pairs={{1,2},{2,1},{5,6},{6,5},{9,10},{10,9},{13,14},{14,13},{17,18},{18,... | collective-permute-start | bytes 589832 | tf_op jit(solution)/shard_map/ppermute | solution.py:540
  34.3 4.2 %copy-start.5 = (bf16[256,128]{1,0:T(8,128)(2,1)S(1)}, bf16[256,128]{1,0:T(8,128)(2,1)}, u32[]{:S(2)}) copy-start(bf16[256,128]{1,0:T(8,128)(2,1)} %get-tuple-element.54.i0) | copy-start | bytes 196612
  34.4 11.1 %collective-permute-start.9 = (bf16[1024,128]{1,0:T(8,128)(2,1)S(1)}, bf16[1024,128]{1,0:T(8,128)(2,1)S(1)}, u32[]{:S(2)}, u32[]{:S(2)}) collective-permute-start(bf16[1024,128]{1,0:T(8,128)(2,1)S(1)} %add_convert_fusion), channel_id=1, source_target_pairs={{0,2},{1,3},{2,0},{3,1},{4,6},{5,7},{6,4},{7,5},{8,10},{9,11},{10,... | collective-permute-start | bytes 786440 | tf_op jit(solution)/shard_map/ppermute | solution.py:466
  45.5 1.6 %collective-permute-start.10 = (bf16[896,128]{1,0:T(8,128)(2,1)S(1)}, bf16[896,128]{1,0:T(8,128)(2,1)S(1)}, u32[]{:S(2)}, u32[]{:S(2)}) collective-permute-start(bf16[896,128]{1,0:T(8,128)(2,1)S(1)} %get-tuple-element.62), channel_id=1, source_target_pairs={{0,1},{1,0},{2,3},{3,2},{4,5},{5,4},{6,7},{7,6},{8,9},{9,8},{10,11... | collective-permute-start | bytes 688136 | tf_op jit(solution)/shard_map/ppermute | solution.py:466
  45.6 2.2 %collective-permute-start.12 = (f32[1024,128]{1,0:T(8,128)S(1)}, f32[1024,128]{1,0:T(8,128)S(1)}, u32[]{:S(2)}, u32[]{:S(2)}) collective-permute-start(f32[1024,128]{1,0:T(8,128)S(1)} %convert_add_fusion.mine_ref), channel_id=1, source_target_pairs={{0,1},{1,0},{2,3},{3,2},{4,5},{5,4},{6,7},{7,6},{8,9},{9,8},{10,11... | collective-permute-start | bytes 1572872 | tf_op jit(solution)/shard_map/ppermute | solution.py:466
  47.1 7.7 %collective-permute-start.11 = (bf16[896,128]{1,0:T(8,128)(2,1)S(1)}, bf16[896,128]{1,0:T(8,128)(2,1)S(1)}, u32[]{:S(2)}, u32[]{:S(2)}) collective-permute-start(bf16[896,128]{1,0:T(8,128)(2,1)S(1)} %add_convert_fusion.1), channel_id=1, source_target_pairs={{0,2},{1,3},{2,0},{3,1},{4,6},{5,7},{6,4},{7,5},{8,10},{9,11},{10,... | collective-permute-start | bytes 688136 | tf_op jit(solution)/shard_map/ppermute | solution.py:466
  54.9 1.9 %collective-permute-start.13 = (f32[896,128]{1,0:T(8,128)S(1)}, f32[896,128]{1,0:T(8,128)S(1)}, u32[]{:S(2)}, u32[]{:S(2)}) collective-permute-start(f32[896,128]{1,0:T(8,128)S(1)} %convert_add_fusion.1.mine_ref), channel_id=1, source_target_pairs={{0,1},{1,0},{2,3},{3,2},{4,5},{5,4},{6,7},{7,6},{8,9},{9,8},{10,11... | collective-permute-start | bytes 1376264 | tf_op jit(solution)/shard_map/ppermute | solution.py:466

commit v7 on v6

--- a/solution.py
+++ b/solution.py
@@ -187,7 +187,7 @@
     return (grad_in, grad_w_one, grad_w_two, grad_w_trans)
 
 
-def call(kernel, out_shape, scratch, flops, limit, *args):
+def call(kernel, out_shape, scratch, flops, limit, *args, out_space=VMEM):
     spec = []
     for a in args:
         if isinstance(a, tuple):
@@ -201,12 +201,12 @@
         kernel,
         out_shape=out_shape,
         in_specs=spec,
-        out_specs=jax.tree.map(lambda _: pl.BlockSpec(memory_space=VMEM), out_shape),
+        out_specs=jax.tree.map(lambda _: pl.BlockSpec(memory_space=out_space), out_shape),
         scratch_shapes=scratch,
         cost_estimate=pl.CostEstimate(
             flops=flops,
             transcendentals=0,
-            bytes_accessed=sum(a.size * a.dtype.itemsize for a in arrays),
+            bytes_accessed=sum(a.size * a.dtype.itemsize for a in arrays) if flops else 0,
         ),
         compiler_params=pltpu.CompilerParams(vmem_limit_bytes=limit * 1024 * 1024),
     )(*arrays)
@@ -370,8 +370,8 @@
 
 
 def conv_kernel(
-    factor, at_ref, acc_ref, sums_ref, one_ref, chip_ref, cross_ref, w2_ref, w1_ref, i0, i1, i2, i3,
-    grad_ref, mine_ref, send_ref, rim_ref, wide_ref, outer_ref, in_ref, turn_ref, first_ref,
+    factor, at_ref, acc_ref, sums_ref, one_ref, chip_ref, cross_ref, w_ref, i0, i1, i2, i3,
+    mine_ref, send_ref, outer_ref, rim_ref, wide_ref, in_ref, first_ref,
 ):
     me = at_ref[0]
     parts = (i0, i1, i2, i3)
@@ -402,8 +402,8 @@
         for i in range(3):
             xs = slice(4 - 2 * i, 20 - 2 * i)
             rows = wide_ref[side, xs, near : near + 16].reshape(256, 384)
-            far += apply_taps(wide_ref[side, xs].reshape(512, 384), w2_ref[i * 3 + j])
-            close += apply_taps(rows, w2_ref[i * 3 + 1])
+            far += apply_taps(wide_ref[side, xs].reshape(512, 384), w_ref[i * 3 + j])
+            close += apply_taps(rows, w_ref[i * 3 + 1])
             sums[i * 3 + j] = jnp.dot(turned, rows, preferred_element_type=F32)
         first_ref[:, 64 * side : 64 * side + 32] += far.reshape(16, 32, 128)
         first_ref[:, 80 * side : 80 * side + 16] += close.reshape(16, 16, 128)
@@ -412,18 +412,11 @@
     outer_ref[2:18] = triple(jnp.where(pre > 0, first_ref[...], 0.0))
     act = in_ref[...].astype(F32).reshape(1024, 128).T.astype(BF16)
     sums = []
-    grad = jnp.zeros((256, 128), F32)
     for i in range(3):
         for j in range(3):
             rows = outer_ref[4 - 2 * i : 20 - 2 * i, 32 - 16 * j : 96 - 16 * j].reshape(1024, 384)
             sums.append(jnp.dot(act, rows, preferred_element_type=F32))
-            mine = outer_ref[pl.ds(me * 4 + 4 - 2 * i, 4), 32 - 16 * j : 96 - 16 * j].reshape(256, 384)
-            grad += apply_taps(mine, w1_ref[i * 3 + j])
     first = fold(sums, factor)
-    turn_ref[...] = grad
-    for x in range(4):
-        for t in range(8):
-            grad_ref[x, :, 128 * t : 128 * t + 128] = turn_ref[pl.ds(64 * x + t, 8, stride=8), :].astype(BF16)
 
     def emit(half, ref):
         for m in range(7):
@@ -435,17 +428,35 @@
     share(at_ref[1], emit, mine_ref, send_ref)
 
 
-def spread_kernel(at_ref, mine_ref, other_ref, one_ref, two_ref):
-    def emit(half, ref):
-        for out, at in ((one_ref, 0), (two_ref, 448)):
+def grad_kernel(at_ref, outer_ref, w_ref, grad_ref, turn_ref):
+    grad = jnp.zeros((256, 128), F32)
+    for i in range(3):
+        for j in range(3):
+            mine = outer_ref[pl.ds(at_ref[0] * 4 + 4 - 2 * i, 4), 32 - 16 * j : 96 - 16 * j].reshape(256, 384)
+            grad += apply_taps(mine, w_ref[i * 3 + j])
+    turn_ref[...] = grad
+    for x in range(4):
+        for t in range(8):
+            grad_ref[x, :, 128 * t : 128 * t + 128] = turn_ref[pl.ds(64 * x + t, 8, stride=8), :].astype(BF16)
+
+
+def spread_kernel(at_ref, mine_ref, other_ref, one_hbm, two_hbm, one_ref, two_ref, sems):
+    copies = []
+    for k, (out, hbm, at) in enumerate(((one_ref, one_hbm, 0), (two_ref, two_hbm, 448))):
+
+        def emit(half, ref):
             for m in range(7):
-                block = ref[at + 64 * m : at + 64 * m + 64].astype(F32)
+                block = ref[at + 64 * m : at + 64 * m + 64]
                 tap = 2 * (7 * half + m)
                 out[tap] = block[:, 0:64]
                 if tap < 26:
                     out[tap + 1] = block[:, 64:128]
 
-    share(at_ref[1], emit, mine_ref, other_ref)
+        share(at_ref[1], emit, mine_ref, other_ref)
+        copies.append(pltpu.make_async_copy(out, hbm, sems.at[k]))
+        copies[-1].start()
+    for copy in copies:
+        copy.wait()
 
 
 def trans_kernel(at_ref, mine_ref, other_ref, trans_ref):
@@ -534,11 +545,13 @@
         kept,
         mask,
     )
-    tsend, *seconds = lax.optimization_barrier((tsend, *seconds))
     n = lax.axis_size("gy")
     pairs = [(i, i + 1) for i in range(1, n - 1, 2)]
     cross = lax.ppermute(cross, "gy", pairs + [(j, i) for i, j in pairs])
     chip = swap(chip, "gy", 1)
+    tsend, *seconds = lax.optimization_barrier((tsend, *seconds))
+    tmine = on_chip(tmine, tsend)
+    one, tmine = lax.optimization_barrier((one, tmine))
     acc, sums = call(
         functools.partial(own_kernel, factor),
         (shape((16, 96, 128), F32), shape((896, 128), F32)),
@@ -549,21 +562,17 @@
         one,
         d2,
     )
-    tmine = on_chip(tmine, tsend)
-    tmine, chip, cross, acc = lax.optimization_barrier((tmine, chip, cross, acc))
     tmine = across(tmine)
-    grad_in, mine, send = call(
+    mine, send, outer = call(
         functools.partial(conv_kernel, factor),
-        (shape((4, 8, 1024), BF16), shape((896, 128), F32), shape((896, 128), BF16)),
+        (shape((896, 128), F32), shape((896, 128), BF16), shape((20, 96, 384), BF16)),
         [
             vmem((2, 16, 48, 128), BF16),
             vmem((2, 20, 32, 384), BF16),
-            vmem((20, 96, 384), BF16),
             vmem((16, 64, 128), BF16),
-            vmem((256, 128), F32),
             vmem((16, 96, 128), F32),
         ],
-        2 * 128 * 3456 * (512 + 1024 + 256),
+        2 * 128 * 3456 * 900,
         20,
         at,
         acc,
@@ -572,7 +581,6 @@
         chip.reshape(16, 48, 128),
         cross.reshape(16, 48, 128),
         d2,
-        d1,
         *seconds,
     )
     send, tmine = lax.optimization_barrier((send, tmine))
@@ -580,18 +588,23 @@
     away = swap(mine, "gy", 2)
     tother = swap(tmine, "gy", 1)
     grad_w_trans = call(trans_kernel, shape((512, 512), F32), [], 10**7, 6, at, tmine, tother)
-    away, grad_w_trans = lax.optimization_barrier((away, grad_w_trans))
+    grad_in = call(
+        grad_kernel, shape((4, 8, 1024), BF16), [vmem((256, 128), F32)], 2 * 128 * 3456 * 256, 12, at, outer, d1
+    )
+    away, grad_w_trans, grad_in = lax.optimization_barrier((away, grad_w_trans, grad_in))
     mine = mine.astype(F32) + away.astype(F32)
     other = swap(mine, "gy", 1)
+    taps = shape((27, 64, 64), F32)
     grad_w_one, grad_w_two = call(
         spread_kernel,
-        (shape((27, 64, 64), F32), shape((27, 64, 64), F32)),
-        [],
+        (taps, taps),
+        [vmem(taps.shape, F32), vmem(taps.shape, F32), pltpu.SemaphoreType.DMA((2,))],
         0,
-        6,
+        8,
         at,
         mine,
         other,
+        out_space=pltpu.MemorySpace.HBM,
     )
     return (grad_in, grad_w_one, grad_w_two, grad_w_trans)
 

time: 59.2 us -> 56.4 us (0.953)
  waiting for transfers between devices: 21.8 us -> 18.5 us
  starting transfers between devices: 16.3 us -> 15.4 us
  Pallas kernels: 16.5 us -> 17.4 us
  local copies, waits for them, and re-layouts: 3.08 us -> 3.76 us
    ppermute x7, waiting for transfers between devices: 10.6 us -> 7.97 us  [swap(): return lax.ppermute(value, axis, [(i, i ^ bit) for i in range(n)])]
    ppermute x7, starting transfers between devices: 5.6 us -> 4.66 us  [swap(): return lax.ppermute(value, axis, [(i, i ^ bit) for i in range(n)])]
    pallas_call x7 -> x8, Pallas kernels: 16.5 us -> 17.4 us  [call(): pl.pallas_call(kernel, out_shape=out_shape, in_specs=spec, out_specs=jax....]
    unnamed x12, local copies, waits for them, and re-layouts: 3.08 us -> 3.76 us
    ppermute x6, waiting for transfers between devices: 11.2 us -> 10.5 us  [rotate(): return lax.ppermute(value, axis, [(i, (i + step) % n) for i in range(n)])]
  transfers between devices with their start and end apart: 14 -> 14, of which waited for: 8 -> 8; matrix products, arithmetic and copies ran while one was open for 0% -> 0% of each run, Pallas kernels for 22% -> 25%
where the time goes in v7:
time: 56.4 us; the launch traced here: 56.1 us
  waiting for transfers between devices  18.5 us (33%)
  Pallas kernels  17.4 us (31%)
  starting transfers between devices  15.4 us (27%)
  local copies, waits for them, and re-layouts  3.76 us (7%)
  between operations  0.75 us (1%)
    pallas_call x8, Pallas kernels, call(): pl.pallas_call(kernel, out_shape=out_shape, in_specs=spec, out_specs=jax....  17.4 us
    ppermute x6, waiting for transfers between devices, rotate(): return lax.ppermute(value, axis, [(i, (i + step) % n) for i in range(n)])  10.5 us
    ppermute x6, starting transfers between devices, rotate(): return lax.ppermute(value, axis, [(i, (i + step) % n) for i in range(n)])  10.1 us
    ppermute x7, waiting for transfers between devices, swap(): return lax.ppermute(value, axis, [(i, i ^ bit) for i in range(n)])  7.97 us
    ppermute x7, starting transfers between devices, swap(): return lax.ppermute(value, axis, [(i, i ^ bit) for i in range(n)])  4.66 us
    unnamed x12, local copies, waits for them, and re-layouts  3.76 us
  transfers between devices with their start and end apart: 14, of which 8 were waited for; matrix products, arithmetic and copies ran while one was open for 0% of the time, Pallas kernels for 25%

profile of v7, /device:TPU:0, one launch (start us, length us, event | category | flops | bytes accessed | tf_op | source)
XLA Modules:
  0.0 56.1 jit_solution(17421726441607776454)
XLA Ops:
  0.6 1.7 %shard_map.111 = (bf16[768,128]{1,0:T(8,128)(2,1)}, bf16[256,128]{1,0:T(8,128)(2,1)}) custom-call(bf16[8,4,8,128]{3,2,1,0:T(8,128)(2,1)} %og.1, bf16[4,8,1024]{2,1,0:T(8,128)(2,1)} %two.1, bf16[4,8,1024]{2,1,0:T(8,128)(2,1)} %one.1, bf16[4,8,1024]{2,1,0:T(8,128)(2,1)} %act.1), custom_call_target="tpu_custom_call" | custom-call | tf_op jit(solution)/shard_map/pallas_call | solution.py:200
  2.3 3.1 %collective-permute-start = (bf16[768,128]{1,0:T(8,128)(2,1)}, bf16[768,128]{1,0:T(8,128)(2,1)S(1)}, u32[]{:S(2)}, u32[]{:S(2)}) collective-permute-start(bf16[768,128]{1,0:T(8,128)(2,1)} %get-tuple-element.35.a0), channel_id=1, source_target_pairs={{0,4},{4,8},{8,12},{12,0},{1,5},{5,9},{9,13},{13,1},{2,6},{6,10},{... | collective-permute-start | bytes 589832 | tf_op jit(solution)/shard_map/ppermute | solution.py:472
  5.4 2.6 %collective-permute-start.1 = (bf16[768,128]{1,0:T(8,128)(2,1)}, bf16[768,128]{1,0:T(8,128)(2,1)S(1)}, u32[]{:S(2)}, u32[]{:S(2)}) collective-permute-start(bf16[768,128]{1,0:T(8,128)(2,1)} %get-tuple-element.35.a0), channel_id=1, source_target_pairs={{0,8},{4,12},{8,0},{12,4},{1,9},{5,13},{9,1},{13,5},{2,10},{6,14},... | collective-permute-start | bytes 589832 | tf_op jit(solution)/shard_map/ppermute | solution.py:472
  8.0 1.3 %collective-permute-start.2 = (bf16[768,128]{1,0:T(8,128)(2,1)}, bf16[768,128]{1,0:T(8,128)(2,1)S(1)}, u32[]{:S(2)}, u32[]{:S(2)}) collective-permute-start(bf16[768,128]{1,0:T(8,128)(2,1)} %get-tuple-element.35.a0), channel_id=1, source_target_pairs={{0,12},{4,0},{8,4},{12,8},{1,13},{5,1},{9,5},{13,9},{2,14},{6,2},{... | collective-permute-start | bytes 589832 | tf_op jit(solution)/shard_map/ppermute | solution.py:472
  9.3 0.7 %collective-permute-start.3 = (bf16[256,128]{1,0:T(8,128)(2,1)}, bf16[256,128]{1,0:T(8,128)(2,1)S(1)}, u32[]{:S(2)}, u32[]{:S(2)}) collective-permute-start(bf16[256,128]{1,0:T(8,128)(2,1)} %get-tuple-element.50.i0), channel_id=1, source_target_pairs={{0,4},{4,8},{8,12},{12,0},{1,5},{5,9},{9,13},{13,1},{2,6},{6,10},{... | collective-permute-start | bytes 196616 | tf_op jit(solution)/shard_map/ppermute | solution.py:472
  10.0 0.3 collective-permute-start.4
  10.3 3.1 %collective-permute-done.a1 = bf16[768,128]{1,0:T(8,128)(2,1)S(1)} collective-permute-done((bf16[768,128]{1,0:T(8,128)(2,1)}, bf16[768,128]{1,0:T(8,128)(2,1)S(1)}, u32[]{:S(2)}, u32[]{:S(2)}) %collective-permute-start) | collective-permute-done | bytes 196640 | tf_op jit(solution)/shard_map/ppermute | solution.py:472
  13.5 2.1 %collective-permute-start.5 = (bf16[256,128]{1,0:T(8,128)(2,1)}, bf16[256,128]{1,0:T(8,128)(2,1)S(1)}, u32[]{:S(2)}, u32[]{:S(2)}) collective-permute-start(bf16[256,128]{1,0:T(8,128)(2,1)} %get-tuple-element.50.i0), channel_id=1, source_target_pairs={{0,12},{4,0},{8,4},{12,8},{1,13},{5,1},{9,5},{13,9},{2,14},{6,2},{... | collective-permute-start | bytes 196616 | tf_op jit(solution)/shard_map/ppermute | solution.py:472
  15.5 0.1 pad_add_fusion.at_ref
  15.6 0.0 copy-start
  15.6 1.0 %copy-done = bf16[512,512]{1,0:T(8,128)(2,1)S(1)} copy-done((bf16[512,512]{1,0:T(8,128)(2,1)S(1)}, bf16[512,512]{1,0:T(8,128)(2,1)}, u32[]{:S(2)}) %copy-start) | copy-done | bytes 524312
  16.6 1.0 %copy-done.1 = bf16[27,64,64]{2,1,0:T(8,128)(2,1)S(1)} copy-done((bf16[27,64,64]{2,1,0:T(8,128)(2,1)S(1)}, bf16[27,64,64]{2,1,0:T(8,128)(2,1)}, u32[]{:S(2)}) %copy-start.1) | copy-done | bytes 221208
  17.7 1.0 %copy-done.2 = bf16[27,64,64]{2,1,0:T(8,128)(2,1)S(1)} copy-done((bf16[27,64,64]{2,1,0:T(8,128)(2,1)S(1)}, bf16[27,64,64]{2,1,0:T(8,128)(2,1)}, u32[]{:S(2)}) %copy-start.2) | copy-done | bytes 221208
  18.7 0.7 %copy-done.5 = s32[8,8]{1,0:T(8,128)S(1)} copy-done((s32[8,8]{1,0:T(8,128)S(1)}, s32[8,8]{1,0:T(8,128)}, u32[]{:S(2)}) %copy-start.5) | copy-done | bytes 280
  19.4 1.4 %shard_map.112 = (bf16[512,512]{1,0:T(8,128)(2,1)S(1)}, bf16[512,512]{1,0:T(8,128)(2,1)S(1)}, bf16[9,128,384]{2,1,0:T(8,128)(2,1)S(1)}, bf16[9,128,384]{2,1,0:T(8,128)(2,1)S(1)}) custom-call(bf16[512,512]{1,0:T(8,128)(2,1)S(1)} %copy-done, s32[8,8]{1,0:T(8,128)S(1)} %copy-done.5, bf16[27,64,64]{2,1,0:T(8,128)(2,1)S(1)} %copy-done.1, ...), custom_call_target="tpu_custom_call" | custom-call | flops 10000000 | bytes 966912 | tf_op jit(solution)/shard_map/pallas_call | solution.py:200
  20.8 1.2 %collective-permute-done.1.a2 = bf16[768,128]{1,0:T(8,128)(2,1)S(1)} collective-permute-done((bf16[768,128]{1,0:T(8,128)(2,1)}, bf16[768,128]{1,0:T(8,128)(2,1)S(1)}, u32[]{:S(2)}, u32[]{:S(2)}) %collective-permute-start.1) | collective-permute-done | bytes 196640 | tf_op jit(solution)/shard_map/ppermute | solution.py:472
  21.9 0.0 collective-permute-done.2.a3
  21.9 0.0 copy-done.3
  22.0 1.3 %shard_map.113 = (bf16[8,2,64,128]{3,2,1,0:T(8,128)(2,1)S(1)}, bf16[16,64,128]{2,1,0:T(8,128)(2,1)S(1)}, bf16[8,2,48,128]{3,2,1,0:T(8,128)(2,1)S(1)}, bf16[8,2,4...) custom-call(s32[2]{0:T(128)S(1)} %pad_add_fusion.at_ref, ...), custom_call_target="tpu_custom_call" | custom-call | flops 268435456 | bytes 1835016 | tf_op jit(solution)/shard_map/pallas_call | solution.py:200
  23.3 0.0 collective-permute-done.3.i1
  23.3 6.2 %collective-permute-done.4.i2 = bf16[256,128]{1,0:T(8,128)(2,1)S(1)} collective-permute-done((bf16[256,128]{1,0:T(8,128)(2,1)}, bf16[256,128]{1,0:T(8,128)(2,1)S(1)}, u32[]{:S(2)}, u32[]{:S(2)}) %collective-permute-start.4) | collective-permute-done | bytes 65568 | tf_op jit(solution)/shard_map/ppermute | solution.py:472
  29.5 0.0 collective-permute-done.5.i3
  29.5 0.0 collective-permute-start.6
  29.5 0.5 collective-permute-start.7
  30.0 0.7 %collective-permute-start.8 = (bf16[8,2,48,128]{3,2,1,0:T(8,128)(2,1)S(1)}, bf16[8,2,48,128]{3,2,1,0:T(8,128)(2,1)S(1)}, u32[]{:S(2)}, u32[]{:S(2)}) collective-permute-start(bf16[8,2,48,128]{3,2,1,0:T(8,128)(2,1)S(1)} %get-tuple-element.49), channel_id=1, source_target_pairs={{1,2},{2,1},{5,6},{6,5},{9,10},{10,9},{13,14},{14,13},{17,18},{18,... | collective-permute-start | bytes 589832 | tf_op jit(solution)/shard_map/ppermute | solution.py:550
  30.7 0.4 collective-permute-done.6
  31.1 0.1 add_convert_fusion
  31.1 2.6 %collective-permute-start.9 = (bf16[1024,128]{1,0:T(8,128)(2,1)S(1)}, bf16[1024,128]{1,0:T(8,128)(2,1)S(1)}, u32[]{:S(2)}, u32[]{:S(2)}) collective-permute-start(bf16[1024,128]{1,0:T(8,128)(2,1)S(1)} %add_convert_fusion), channel_id=1, source_target_pairs={{0,2},{1,3},{2,0},{3,1},{4,6},{5,7},{6,4},{7,5},{8,10},{9,11},{10,... | collective-permute-start | bytes 786440 | tf_op jit(solution)/shard_map/ppermute | solution.py:477
  33.7 3.6 %shard_map.114 = (f32[16,96,128]{2,1,0:T(8,128)S(1)}, f32[896,128]{1,0:T(8,128)S(1)}) custom-call(bf16[16,64,128]{2,1,0:T(8,128)(2,1)S(1)} %bitcast.7, bf16[16,64,128]{2,1,0:T(8,128)(2,1)S(1)} %get-tuple-element.44.one_ref, bf16[9,128,384]{2,1,0:T(8,128)(2,1)S(1)} %get-tuple-element.45.w_ref), custom_call_target="tpu_custom_call" | custom-call | flops 1811939328 | bytes 1409024 | tf_op jit(solution)/shard_map/pallas_call | solution.py:200
  37.3 0.0 collective-permute-done.7
  37.3 0.0 collective-permute-done.8
  37.3 0.0 copy-done.4
  37.3 4.0 %shard_map.115 = (f32[896,128]{1,0:T(8,128)S(1)}, bf16[896,128]{1,0:T(8,128)(2,1)S(1)}, bf16[20,96,384]{2,1,0:T(8,128)(2,1)S(1)}) custom-call(s32[2]{0:T(128)S(1)} %pad_add_fusion.at_ref, f32[16,96,128]{2,1,0:T(8,128)S(1)} %get-tuple-element.46.acc_ref, f32[896,128]{1,0:T(8,128)S(1)} %get-tuple-element.47.sums_ref, ...), custom_call_target="tpu_custom_call" | custom-call | flops 796262400 | bytes 3047432 | tf_op jit(solution)/shard_map/pallas_call | solution.py:200
  41.3 1.5 %collective-permute-done.9 = bf16[1024,128]{1,0:T(8,128)(2,1)S(1)} collective-permute-done((bf16[1024,128]{1,0:T(8,128)(2,1)S(1)}, bf16[1024,128]{1,0:T(8,128)(2,1)S(1)}, u32[]{:S(2)}, u32[]{:S(2)}) %collective-permute-start.9) | collective-permute-done | bytes 262176 | tf_op jit(solution)/shard_map/ppermute | solution.py:477
  42.8 0.1 convert_add_fusion.mine_ref
  42.9 0.1 collective-permute-start.10
  43.0 0.5 collective-permute-start.12
  43.5 1.0 %collective-permute-done.10 = bf16[896,128]{1,0:T(8,128)(2,1)S(1)} collective-permute-done((bf16[896,128]{1,0:T(8,128)(2,1)S(1)}, bf16[896,128]{1,0:T(8,128)(2,1)S(1)}, u32[]{:S(2)}, u32[]{:S(2)}) %collective-permute-start.10) | collective-permute-done | bytes 229408 | tf_op jit(solution)/shard_map/ppermute | solution.py:477
  44.4 0.1 add_convert_fusion.1
  44.5 0.9 %collective-permute-start.11 = (bf16[896,128]{1,0:T(8,128)(2,1)S(1)}, bf16[896,128]{1,0:T(8,128)(2,1)S(1)}, u32[]{:S(2)}, u32[]{:S(2)}) collective-permute-start(bf16[896,128]{1,0:T(8,128)(2,1)S(1)} %add_convert_fusion.1), channel_id=1, source_target_pairs={{0,2},{1,3},{2,0},{3,1},{4,6},{5,7},{6,4},{7,5},{8,10},{9,11},{10,... | collective-permute-start | bytes 688136 | tf_op jit(solution)/shard_map/ppermute | solution.py:477
  45.4 1.8 %shard_map.117 = bf16[4,8,1024]{2,1,0:T(8,128)(2,1)} custom-call(s32[2]{0:T(128)S(1)} %pad_add_fusion.at_ref, bf16[20,96,384]{2,1,0:T(8,128)(2,1)S(1)} %get-tuple-element.59.outer_ref, bf16[9,128,384]{2,1,0:T(8,128)(2,1)S(1)} %get-tuple-element.60.w_ref), custom_call_target="tpu_custom_call" | custom-call | flops 226492416 | bytes 2359304 | tf_op jit(solution)/shard_map/pallas_call | solution.py:200
  47.3 0.0 collective-permute-done.12.other_ref
  47.3 1.6 %shard_map.116 = f32[512,512]{1,0:T(8,128)} custom-call(s32[2]{0:T(128)S(1)} %pad_add_fusion.at_ref, f32[1024,128]{1,0:T(8,128)S(1)} %convert_add_fusion.mine_ref, f32[1024,128]{1,0:T(8,128)S(1)} %collective-permute-done.12.other_ref), custom_call_target="tpu_custom_call" | custom-call | flops 10000000 | bytes 1048584 | tf_op jit(solution)/shard_map/pallas_call | solution.py:200
  48.9 3.3 %collective-permute-done.11 = bf16[896,128]{1,0:T(8,128)(2,1)S(1)} collective-permute-done((bf16[896,128]{1,0:T(8,128)(2,1)S(1)}, bf16[896,128]{1,0:T(8,128)(2,1)S(1)}, u32[]{:S(2)}, u32[]{:S(2)}) %collective-permute-start.11) | collective-permute-done | bytes 229408 | tf_op jit(solution)/shard_map/ppermute | solution.py:477
  52.2 0.1 convert_add_fusion.1.mine_ref
  52.3 0.1 collective-permute-start.13
  52.4 1.8 %collective-permute-done.13.other_ref = f32[896,128]{1,0:T(8,128)S(1)} collective-permute-done((f32[896,128]{1,0:T(8,128)S(1)}, f32[896,128]{1,0:T(8,128)S(1)}, u32[]{:S(2)}, u32[]{:S(2)}) %collective-permute-start.13) | collective-permute-done | bytes 458784 | tf_op jit(solution)/shard_map/ppermute | solution.py:477
  54.2 1.9 %shard_map.118 = (f32[27,64,64]{2,1,0:T(8,128)}, f32[27,64,64]{2,1,0:T(8,128)}) custom-call(s32[2]{0:T(128)S(1)} %pad_add_fusion.at_ref, f32[896,128]{1,0:T(8,128)S(1)} %convert_add_fusion.1.mine_ref, f32[896,128]{1,0:T(8,128)S(1)} %collective-permute-done.13.other_ref), custom_call_target="tpu_custom_call" | custom-call | tf_op jit(solution)/shard_map/pallas_call | solution.py:200
  (5 shorter events, 0.0 us)
Async XLA Ops:
  2.3 11.2 %collective-permute-start = (bf16[768,128]{1,0:T(8,128)(2,1)}, bf16[768,128]{1,0:T(8,128)(2,1)S(1)}, u32[]{:S(2)}, u32[]{:S(2)}) collective-permute-start(bf16[768,128]{1,0:T(8,128)(2,1)} %get-tuple-element.35.a0), channel_id=1, source_target_pairs={{0,4},{4,8},{8,12},{12,0},{1,5},{5,9},{9,13},{13,1},{2,6},{6,10},{... | collective-permute-start | bytes 589832 | tf_op jit(solution)/shard_map/ppermute | solution.py:472
  5.4 16.6 %collective-permute-start.1 = (bf16[768,128]{1,0:T(8,128)(2,1)}, bf16[768,128]{1,0:T(8,128)(2,1)S(1)}, u32[]{:S(2)}, u32[]{:S(2)}) collective-permute-start(bf16[768,128]{1,0:T(8,128)(2,1)} %get-tuple-element.35.a0), channel_id=1, source_target_pairs={{0,8},{4,12},{8,0},{12,4},{1,9},{5,13},{9,1},{13,5},{2,10},{6,14},... | collective-permute-start | bytes 589832 | tf_op jit(solution)/shard_map/ppermute | solution.py:472
  8.0 14.0 %collective-permute-start.2 = (bf16[768,128]{1,0:T(8,128)(2,1)}, bf16[768,128]{1,0:T(8,128)(2,1)S(1)}, u32[]{:S(2)}, u32[]{:S(2)}) collective-permute-start(bf16[768,128]{1,0:T(8,128)(2,1)} %get-tuple-element.35.a0), channel_id=1, source_target_pairs={{0,12},{4,0},{8,4},{12,8},{1,13},{5,1},{9,5},{13,9},{2,14},{6,2},{... | collective-permute-start | bytes 589832 | tf_op jit(solution)/shard_map/ppermute | solution.py:472
  9.3 14.0 %collective-permute-start.3 = (bf16[256,128]{1,0:T(8,128)(2,1)}, bf16[256,128]{1,0:T(8,128)(2,1)S(1)}, u32[]{:S(2)}, u32[]{:S(2)}) collective-permute-start(bf16[256,128]{1,0:T(8,128)(2,1)} %get-tuple-element.50.i0), channel_id=1, source_target_pairs={{0,4},{4,8},{8,12},{12,0},{1,5},{5,9},{9,13},{13,1},{2,6},{6,10},{... | collective-permute-start | bytes 196616 | tf_op jit(solution)/shard_map/ppermute | solution.py:472
  10.0 19.5 %collective-permute-start.4 = (bf16[256,128]{1,0:T(8,128)(2,1)}, bf16[256,128]{1,0:T(8,128)(2,1)S(1)}, u32[]{:S(2)}, u32[]{:S(2)}) collective-permute-start(bf16[256,128]{1,0:T(8,128)(2,1)} %get-tuple-element.50.i0), channel_id=1, source_target_pairs={{0,8},{4,12},{8,0},{12,4},{1,9},{5,13},{9,1},{13,5},{2,10},{6,14},... | collective-permute-start | bytes 196616 | tf_op jit(solution)/shard_map/ppermute | solution.py:472
  13.5 16.1 %collective-permute-start.5 = (bf16[256,128]{1,0:T(8,128)(2,1)}, bf16[256,128]{1,0:T(8,128)(2,1)S(1)}, u32[]{:S(2)}, u32[]{:S(2)}) collective-permute-start(bf16[256,128]{1,0:T(8,128)(2,1)} %get-tuple-element.50.i0), channel_id=1, source_target_pairs={{0,12},{4,0},{8,4},{12,8},{1,13},{5,1},{9,5},{13,9},{2,14},{6,2},{... | collective-permute-start | bytes 196616 | tf_op jit(solution)/shard_map/ppermute | solution.py:472
  15.6 1.0 %copy-start = (bf16[512,512]{1,0:T(8,128)(2,1)S(1)}, bf16[512,512]{1,0:T(8,128)(2,1)}, u32[]{:S(2)}) copy-start(bf16[512,512]{1,0:T(8,128)(2,1)} %wt.1) | copy-start | bytes 1572868
  16.6 1.0 %copy-start.1 = (bf16[27,64,64]{2,1,0:T(8,128)(2,1)S(1)}, bf16[27,64,64]{2,1,0:T(8,128)(2,1)}, u32[]{:S(2)}) copy-start(bf16[27,64,64]{2,1,0:T(8,128)(2,1)} %w2.1) | copy-start | bytes 663556
  17.7 1.0 %copy-start.2 = (bf16[27,64,64]{2,1,0:T(8,128)(2,1)S(1)}, bf16[27,64,64]{2,1,0:T(8,128)(2,1)}, u32[]{:S(2)}) copy-start(bf16[27,64,64]{2,1,0:T(8,128)(2,1)} %w1.1) | copy-start | bytes 663556
  18.7 0.7 %copy-start.5 = (s32[8,8]{1,0:T(8,128)S(1)}, s32[8,8]{1,0:T(8,128)}, u32[]{:S(2)}) copy-start(s32[8,8]{1,0:T(8,128)} %keep.1) | copy-start | bytes 772
  19.4 2.6 %copy-start.3 = (bf16[768,128]{1,0:T(8,128)(2,1)S(1)}, bf16[768,128]{1,0:T(8,128)(2,1)}, u32[]{:S(2)}) copy-start(bf16[768,128]{1,0:T(8,128)(2,1)} %get-tuple-element.35.a0) | copy-start | bytes 589828
  29.5 1.5 %collective-permute-start.6 = (bf16[1024,128]{1,0:T(8,128)(2,1)S(1)}, bf16[1024,128]{1,0:T(8,128)(2,1)S(1)}, u32[]{:S(2)}, u32[]{:S(2)}) collective-permute-start(bf16[1024,128]{1,0:T(8,128)(2,1)S(1)} %get-tuple-element.43), channel_id=1, source_target_pairs={{0,1},{1,0},{2,3},{3,2},{4,5},{5,4},{6,7},{7,6},{8,9},{9,8},{10,11... | collective-permute-start | bytes 786440 | tf_op jit(solution)/shard_map/ppermute | solution.py:477
  29.5 7.8 %collective-permute-start.7 = (bf16[8,2,48,128]{3,2,1,0:T(8,128)(2,1)S(1)}, bf16[8,2,48,128]{3,2,1,0:T(8,128)(2,1)S(1)}, u32[]{:S(2)}, u32[]{:S(2)}) collective-permute-start(bf16[8,2,48,128]{3,2,1,0:T(8,128)(2,1)S(1)} %get-tuple-element.48), channel_id=1, source_target_pairs={{0,1},{1,0},{2,3},{3,2},{4,5},{5,4},{6,7},{7,6},{8,9},{9,8},{10,11... | collective-permute-start | bytes 589832 | tf_op jit(solution)/shard_map/ppermute | solution.py:477
  30.0 7.3 %collective-permute-start.8 = (bf16[8,2,48,128]{3,2,1,0:T(8,128)(2,1)S(1)}, bf16[8,2,48,128]{3,2,1,0:T(8,128)(2,1)S(1)}, u32[]{:S(2)}, u32[]{:S(2)}) collective-permute-start(bf16[8,2,48,128]{3,2,1,0:T(8,128)(2,1)S(1)} %get-tuple-element.49), channel_id=1, source_target_pairs={{1,2},{2,1},{5,6},{6,5},{9,10},{10,9},{13,14},{14,13},{17,18},{18,... | collective-permute-start | bytes 589832 | tf_op jit(solution)/shard_map/ppermute | solution.py:550
  31.1 11.7 %collective-permute-start.9 = (bf16[1024,128]{1,0:T(8,128)(2,1)S(1)}, bf16[1024,128]{1,0:T(8,128)(2,1)S(1)}, u32[]{:S(2)}, u32[]{:S(2)}) collective-permute-start(bf16[1024,128]{1,0:T(8,128)(2,1)S(1)} %add_convert_fusion), channel_id=1, source_target_pairs={{0,2},{1,3},{2,0},{3,1},{4,6},{5,7},{6,4},{7,5},{8,10},{9,11},{10,... | collective-permute-start | bytes 786440 | tf_op jit(solution)/shard_map/ppermute | solution.py:477
  33.7 3.6 %copy-start.4 = (bf16[256,128]{1,0:T(8,128)(2,1)S(1)}, bf16[256,128]{1,0:T(8,128)(2,1)}, u32[]{:S(2)}) copy-start(bf16[256,128]{1,0:T(8,128)(2,1)} %get-tuple-element.50.i0) | copy-start | bytes 196612
  42.9 1.6 %collective-permute-start.10 = (bf16[896,128]{1,0:T(8,128)(2,1)S(1)}, bf16[896,128]{1,0:T(8,128)(2,1)S(1)}, u32[]{:S(2)}, u32[]{:S(2)}) collective-permute-start(bf16[896,128]{1,0:T(8,128)(2,1)S(1)} %get-tuple-element.57), channel_id=1, source_target_pairs={{0,1},{1,0},{2,3},{3,2},{4,5},{5,4},{6,7},{7,6},{8,9},{9,8},{10,11... | collective-permute-start | bytes 688136 | tf_op jit(solution)/shard_map/ppermute | solution.py:477
  43.0 4.3 %collective-permute-start.12 = (f32[1024,128]{1,0:T(8,128)S(1)}, f32[1024,128]{1,0:T(8,128)S(1)}, u32[]{:S(2)}, u32[]{:S(2)}) collective-permute-start(f32[1024,128]{1,0:T(8,128)S(1)} %convert_add_fusion.mine_ref), channel_id=1, source_target_pairs={{0,1},{1,0},{2,3},{3,2},{4,5},{5,4},{6,7},{7,6},{8,9},{9,8},{10,11... | collective-permute-start | bytes 1572872 | tf_op jit(solution)/shard_map/ppermute | solution.py:477
  44.5 7.7 %collective-permute-start.11 = (bf16[896,128]{1,0:T(8,128)(2,1)S(1)}, bf16[896,128]{1,0:T(8,128)(2,1)S(1)}, u32[]{:S(2)}, u32[]{:S(2)}) collective-permute-start(bf16[896,128]{1,0:T(8,128)(2,1)S(1)} %add_convert_fusion.1), channel_id=1, source_target_pairs={{0,2},{1,3},{2,0},{3,1},{4,6},{5,7},{6,4},{7,5},{8,10},{9,11},{10,... | collective-permute-start | bytes 688136 | tf_op jit(solution)/shard_map/ppermute | solution.py:477
  52.3 1.9 %collective-permute-start.13 = (f32[896,128]{1,0:T(8,128)S(1)}, f32[896,128]{1,0:T(8,128)S(1)}, u32[]{:S(2)}, u32[]{:S(2)}) collective-permute-start(f32[896,128]{1,0:T(8,128)S(1)} %convert_add_fusion.1.mine_ref), channel_id=1, source_target_pairs={{0,1},{1,0},{2,3},{3,2},{4,5},{5,4},{6,7},{7,6},{8,9},{9,8},{10,11... | collective-permute-start | bytes 1376264 | tf_op jit(solution)/shard_map/ppermute | solution.py:477

commit v8 on v7

--- a/solution.py
+++ b/solution.py
@@ -345,33 +345,42 @@
     return lax.dot_general(rows, taps, (((1,), (1,)), ((), ())), preferred_element_type=F32)
 
 
-def own_kernel(factor, back_ref, one_ref, w_ref, acc_ref, sums_ref, wide_ref):
-    wide_ref[0:2] = jnp.zeros((2, 96, 384), BF16)
-    wide_ref[18:20] = jnp.zeros((2, 96, 384), BF16)
+def weight_sums(act, wide_ref, act_ref):
+    act_ref[0:128] = jnp.zeros((128, 128), F32)
+    act_ref[128:1152] = act.reshape(1024, 128)
+    act_ref[1152:1280] = jnp.zeros((128, 128), F32)
+    turned = act_ref[...].T.astype(BF16)
+    stacked = jnp.concatenate([turned[:, 128 * i : 128 * i + 1024] for i in range(3)], axis=0)
+    sums = [None] * 9
+    for j in range(3):
+        rows = wide_ref[2:18, 32 - 16 * j : 96 - 16 * j].reshape(1024, 384)
+        part = jnp.dot(stacked, rows, preferred_element_type=F32)
+        for i in range(3):
+            sums[i * 3 + j] = part[128 * i : 128 * i + 128]
+    return sums
+
+
+def own_kernel(factor, back_ref, one_ref, w_ref, acc_ref, sums_ref, wide_ref, act_ref):
     wide_ref[2:18, 0:16] = jnp.zeros((16, 16, 384), BF16)
     wide_ref[2:18, 80:96] = jnp.zeros((16, 16, 384), BF16)
     wide_ref[2:18, 16:80] = triple(back_ref[...].astype(F32))
-    act = jnp.maximum(one_ref[...].astype(F32), 0.0).reshape(1024, 128).T.astype(BF16)
-    sums = [None] * 9
+    acc_ref[...] = jnp.zeros((16, 96, 128), F32)
+    rows = wide_ref[2:18, 16:80].reshape(1024, 384)
     for j in range(3):
-        part = jnp.zeros((1024, 128), F32)
-        for i in range(3):
-            part += apply_taps(wide_ref[4 - 2 * i : 20 - 2 * i, 16:80].reshape(1024, 384), w_ref[i * 3 + j])
-            rows = wide_ref[4 - 2 * i : 20 - 2 * i, 32 - 16 * j : 96 - 16 * j].reshape(1024, 384)
-            sums[i * 3 + j] = jnp.dot(act, rows, preferred_element_type=F32)
-        part = part.reshape(16, 64, 128)
-        if j == 0:
-            acc_ref[:, 0:64] = part
-            acc_ref[:, 64:96] = jnp.zeros((16, 32, 128), F32)
-        else:
-            acc_ref[:, 16 * j : 16 * j + 64] += part
+        taps = jnp.concatenate([w_ref[i * 3 + j] for i in range(3)], axis=0)
+        part = apply_taps(rows, taps).reshape(16, 64, 384)
+        ys = slice(16 * j, 16 * j + 64)
+        acc_ref[0:14, ys] += part[2:16, :, 0:128]
+        acc_ref[:, ys] += part[:, :, 128:256]
+        acc_ref[2:16, ys] += part[0:14, :, 256:384]
+    sums = weight_sums(jnp.maximum(one_ref[...].astype(F32), 0.0), wide_ref, act_ref)
     for m, block in enumerate(fold(sums, factor)):
         sums_ref[64 * m : 64 * m + 64] = block
 
 
 def conv_kernel(
     factor, at_ref, acc_ref, sums_ref, one_ref, chip_ref, cross_ref, w_ref, i0, i1, i2, i3,
-    mine_ref, send_ref, outer_ref, rim_ref, wide_ref, in_ref, first_ref,
+    mine_ref, send_ref, outer_ref, rim_ref, wide_ref, in_ref, first_ref, act_ref,
 ):
     me = at_ref[0]
     parts = (i0, i1, i2, i3)
@@ -410,13 +419,7 @@
     second = fold(sums, factor)
     pre = jnp.concatenate([rim_ref[0, :, 32:48], one_ref[...], rim_ref[1, :, 32:48]], axis=1).astype(F32)
     outer_ref[2:18] = triple(jnp.where(pre > 0, first_ref[...], 0.0))
-    act = in_ref[...].astype(F32).reshape(1024, 128).T.astype(BF16)
-    sums = []
-    for i in range(3):
-        for j in range(3):
-            rows = outer_ref[4 - 2 * i : 20 - 2 * i, 32 - 16 * j : 96 - 16 * j].reshape(1024, 384)
-            sums.append(jnp.dot(act, rows, preferred_element_type=F32))
-    first = fold(sums, factor)
+    first = fold(weight_sums(in_ref[...].astype(F32), outer_ref, act_ref), factor)
 
     def emit(half, ref):
         for m in range(7):
@@ -440,23 +443,46 @@
             grad_ref[x, :, 128 * t : 128 * t + 128] = turn_ref[pl.ds(64 * x + t, 8, stride=8), :].astype(BF16)
 
 
-def spread_kernel(at_ref, mine_ref, other_ref, one_hbm, two_hbm, one_ref, two_ref, sems):
-    copies = []
-    for k, (out, hbm, at) in enumerate(((one_ref, one_hbm, 0), (two_ref, two_hbm, 448))):
-
-        def emit(half, ref):
-            for m in range(7):
-                block = ref[at + 64 * m : at + 64 * m + 64]
-                tap = 2 * (7 * half + m)
-                out[tap] = block[:, 0:64]
-                if tap < 26:
-                    out[tap + 1] = block[:, 64:128]
-
-        share(at_ref[1], emit, mine_ref, other_ref)
-        copies.append(pltpu.make_async_copy(out, hbm, sems.at[k]))
-        copies[-1].start()
-    for copy in copies:
-        copy.wait()
+def unpack(ref, at, out_ref):
+    for m in range(7):
+        block = ref[at + 64 * m : at + 64 * m + 64]
+        out_ref[2 * m] = block[:, 0:64]
+        out_ref[2 * m + 1] = block[:, 64:128]
+
+
+def half_kernel(mine_ref, one_ref, two_ref):
+    unpack(mine_ref, 0, one_ref)
+    unpack(mine_ref, 448, two_ref)
+
+
+def spread_kernel(at_ref, mine_one, mine_two, other_ref, one_hbm, two_hbm, one_ref, two_ref, sems):
+    def emit(core):
+        copies = []
+
+        def send(half, one, two):
+            count = 14 - half
+            for src, dst in ((one, one_hbm), (two, two_hbm)):
+                copies.append(
+                    pltpu.make_async_copy(
+                        src.at[0:count], dst.at[14 * half : 14 * half + count], sems.at[len(copies)]
+                    )
+                )
+                copies[-1].start()
+
+        send(core, mine_one, mine_two)
+        unpack(other_ref, 0, one_ref)
+        unpack(other_ref, 448, two_ref)
+        send(1 - core, one_ref, two_ref)
+        for copy in copies:
+            copy.wait()
+
+    @pl.when(at_ref[1] == 0)
+    def _():
+        emit(0)
+
+    @pl.when(at_ref[1] != 0)
+    def _():
+        emit(1)
 
 
 def trans_kernel(at_ref, mine_ref, other_ref, trans_ref):
@@ -555,7 +581,7 @@
     acc, sums = call(
         functools.partial(own_kernel, factor),
         (shape((16, 96, 128), F32), shape((896, 128), F32)),
-        [vmem((20, 96, 384), BF16)],
+        [vmem((20, 96, 384), BF16), vmem((1280, 128), F32)],
         2 * 128 * 3456 * 2048,
         16,
         back.reshape(16, 64, 128),
@@ -571,6 +597,7 @@
             vmem((2, 20, 32, 384), BF16),
             vmem((16, 64, 128), BF16),
             vmem((16, 96, 128), F32),
+            vmem((1280, 128), F32),
         ],
         2 * 128 * 3456 * 900,
         20,
@@ -595,14 +622,17 @@
     mine = mine.astype(F32) + away.astype(F32)
     other = swap(mine, "gy", 1)
     taps = shape((27, 64, 64), F32)
+    half = shape((14, 64, 64), F32)
+    mine_one, mine_two = call(half_kernel, (half, half), [], 10**8, 6, mine)
     grad_w_one, grad_w_two = call(
         spread_kernel,
         (taps, taps),
-        [vmem(taps.shape, F32), vmem(taps.shape, F32), pltpu.SemaphoreType.DMA((2,))],
+        [vmem(half.shape, F32), vmem(half.shape, F32), pltpu.SemaphoreType.DMA((4,))],
         0,
         8,
         at,
-        mine,
+        mine_one,
+        mine_two,
         other,
         out_space=pltpu.MemorySpace.HBM,
     )

time: 56.4 us -> 56.3 us (level)
  Pallas kernels: 17.4 us -> 16.8 us
    pallas_call x8 -> x9, Pallas kernels: 17.4 us -> 16.8 us  [call(): pl.pallas_call(kernel, out_shape=out_shape, in_specs=spec, out_specs=jax....]
  transfers between devices with their start and end apart: 14 -> 14, of which waited for: 8 -> 8; matrix products, arithmetic and copies ran while one was open for 0% -> 0% of each run, Pallas kernels for 25% -> 24%
where the time goes in v8:
time: 56.3 us; the launch traced here: 55.9 us
  waiting for transfers between devices  19 us (34%)
  Pallas kernels  16.8 us (30%)
  starting transfers between devices  15.3 us (27%)
  local copies, waits for them, and re-layouts  3.76 us (7%)
  between operations  0.77 us (1%)
    pallas_call x9, Pallas kernels, call(): pl.pallas_call(kernel, out_shape=out_shape, in_specs=spec, out_specs=jax....  16.8 us
    ppermute x6, waiting for transfers between devices, rotate(): return lax.ppermute(value, axis, [(i, (i + step) % n) for i in range(n)])  10.5 us
    ppermute x6, starting transfers between devices, rotate(): return lax.ppermute(value, axis, [(i, (i + step) % n) for i in range(n)])  10.1 us
    ppermute x7, waiting for transfers between devices, swap(): return lax.ppermute(value, axis, [(i, i ^ bit) for i in range(n)])  8.51 us
    ppermute x7, starting transfers between devices, swap(): return lax.ppermute(value, axis, [(i, i ^ bit) for i in range(n)])  4.56 us
    unnamed x12, local copies, waits for them, and re-layouts  3.76 us
  transfers between devices with their start and end apart: 14, of which 8 were waited for; matrix products, arithmetic and copies ran while one was open for 0% of the time, Pallas kernels for 24%

profile of v8, /device:TPU:0, one launch (start us, length us, event | category | flops | bytes accessed | tf_op | source)
XLA Modules:
  0.0 55.9 jit_solution(7465043520380677637)
XLA Ops:
  0.6 1.7 %shard_map.111 = (bf16[768,128]{1,0:T(8,128)(2,1)}, bf16[256,128]{1,0:T(8,128)(2,1)}) custom-call(bf16[8,4,8,128]{3,2,1,0:T(8,128)(2,1)} %og.1, bf16[4,8,1024]{2,1,0:T(8,128)(2,1)} %two.1, bf16[4,8,1024]{2,1,0:T(8,128)(2,1)} %one.1, bf16[4,8,1024]{2,1,0:T(8,128)(2,1)} %act.1), custom_call_target="tpu_custom_call" | custom-call | tf_op jit(solution)/shard_map/pallas_call | solution.py:200
  2.3 3.1 %collective-permute-start = (bf16[768,128]{1,0:T(8,128)(2,1)}, bf16[768,128]{1,0:T(8,128)(2,1)S(1)}, u32[]{:S(2)}, u32[]{:S(2)}) collective-permute-start(bf16[768,128]{1,0:T(8,128)(2,1)} %get-tuple-element.37.a0), channel_id=1, source_target_pairs={{0,4},{4,8},{8,12},{12,0},{1,5},{5,9},{9,13},{13,1},{2,6},{6,10},{... | collective-permute-start | bytes 589832 | tf_op jit(solution)/shard_map/ppermute | solution.py:498
  5.4 2.6 %collective-permute-start.1 = (bf16[768,128]{1,0:T(8,128)(2,1)}, bf16[768,128]{1,0:T(8,128)(2,1)S(1)}, u32[]{:S(2)}, u32[]{:S(2)}) collective-permute-start(bf16[768,128]{1,0:T(8,128)(2,1)} %get-tuple-element.37.a0), channel_id=1, source_target_pairs={{0,8},{4,12},{8,0},{12,4},{1,9},{5,13},{9,1},{13,5},{2,10},{6,14},... | collective-permute-start | bytes 589832 | tf_op jit(solution)/shard_map/ppermute | solution.py:498
  8.0 1.3 %collective-permute-start.2 = (bf16[768,128]{1,0:T(8,128)(2,1)}, bf16[768,128]{1,0:T(8,128)(2,1)S(1)}, u32[]{:S(2)}, u32[]{:S(2)}) collective-permute-start(bf16[768,128]{1,0:T(8,128)(2,1)} %get-tuple-element.37.a0), channel_id=1, source_target_pairs={{0,12},{4,0},{8,4},{12,8},{1,13},{5,1},{9,5},{13,9},{2,14},{6,2},{... | collective-permute-start | bytes 589832 | tf_op jit(solution)/shard_map/ppermute | solution.py:498
  9.3 0.7 %collective-permute-start.3 = (bf16[256,128]{1,0:T(8,128)(2,1)}, bf16[256,128]{1,0:T(8,128)(2,1)S(1)}, u32[]{:S(2)}, u32[]{:S(2)}) collective-permute-start(bf16[256,128]{1,0:T(8,128)(2,1)} %get-tuple-element.52.i0), channel_id=1, source_target_pairs={{0,4},{4,8},{8,12},{12,0},{1,5},{5,9},{9,13},{13,1},{2,6},{6,10},{... | collective-permute-start | bytes 196616 | tf_op jit(solution)/shard_map/ppermute | solution.py:498
  10.0 0.3 collective-permute-start.4
  10.3 3.1 %collective-permute-done.a1 = bf16[768,128]{1,0:T(8,128)(2,1)S(1)} collective-permute-done((bf16[768,128]{1,0:T(8,128)(2,1)}, bf16[768,128]{1,0:T(8,128)(2,1)S(1)}, u32[]{:S(2)}, u32[]{:S(2)}) %collective-permute-start) | collective-permute-done | bytes 196640 | tf_op jit(solution)/shard_map/ppermute | solution.py:498
  13.5 2.1 %collective-permute-start.5 = (bf16[256,128]{1,0:T(8,128)(2,1)}, bf16[256,128]{1,0:T(8,128)(2,1)S(1)}, u32[]{:S(2)}, u32[]{:S(2)}) collective-permute-start(bf16[256,128]{1,0:T(8,128)(2,1)} %get-tuple-element.52.i0), channel_id=1, source_target_pairs={{0,12},{4,0},{8,4},{12,8},{1,13},{5,1},{9,5},{13,9},{2,14},{6,2},{... | collective-permute-start | bytes 196616 | tf_op jit(solution)/shard_map/ppermute | solution.py:498
  15.5 0.1 pad_add_fusion.at_ref
  15.6 1.0 %copy-done = bf16[512,512]{1,0:T(8,128)(2,1)S(1)} copy-done((bf16[512,512]{1,0:T(8,128)(2,1)S(1)}, bf16[512,512]{1,0:T(8,128)(2,1)}, u32[]{:S(2)}) %copy-start) | copy-done | bytes 524312
  16.6 1.0 %copy-done.1 = bf16[27,64,64]{2,1,0:T(8,128)(2,1)S(1)} copy-done((bf16[27,64,64]{2,1,0:T(8,128)(2,1)S(1)}, bf16[27,64,64]{2,1,0:T(8,128)(2,1)}, u32[]{:S(2)}) %copy-start.1) | copy-done | bytes 221208
  17.7 1.0 %copy-done.2 = bf16[27,64,64]{2,1,0:T(8,128)(2,1)S(1)} copy-done((bf16[27,64,64]{2,1,0:T(8,128)(2,1)S(1)}, bf16[27,64,64]{2,1,0:T(8,128)(2,1)}, u32[]{:S(2)}) %copy-start.2) | copy-done | bytes 221208
  18.7 0.7 %copy-done.5 = s32[8,8]{1,0:T(8,128)S(1)} copy-done((s32[8,8]{1,0:T(8,128)S(1)}, s32[8,8]{1,0:T(8,128)}, u32[]{:S(2)}) %copy-start.5) | copy-done | bytes 280
  19.4 1.4 %shard_map.112 = (bf16[512,512]{1,0:T(8,128)(2,1)S(1)}, bf16[512,512]{1,0:T(8,128)(2,1)S(1)}, bf16[9,128,384]{2,1,0:T(8,128)(2,1)S(1)}, bf16[9,128,384]{2,1,0:T(8,128)(2,1)S(1)}) custom-call(bf16[512,512]{1,0:T(8,128)(2,1)S(1)} %copy-done, s32[8,8]{1,0:T(8,128)S(1)} %copy-done.5, bf16[27,64,64]{2,1,0:T(8,128)(2,1)S(1)} %copy-done.1, ...), custom_call_target="tpu_custom_call" | custom-call | flops 10000000 | bytes 966912 | tf_op jit(solution)/shard_map/pallas_call | solution.py:200
  20.8 1.2 %collective-permute-done.1.a2 = bf16[768,128]{1,0:T(8,128)(2,1)S(1)} collective-permute-done((bf16[768,128]{1,0:T(8,128)(2,1)}, bf16[768,128]{1,0:T(8,128)(2,1)S(1)}, u32[]{:S(2)}, u32[]{:S(2)}) %collective-permute-start.1) | collective-permute-done | bytes 196640 | tf_op jit(solution)/shard_map/ppermute | solution.py:498
  21.9 0.0 collective-permute-done.2.a3
  21.9 0.0 copy-done.3
  22.0 1.3 %shard_map.113 = (bf16[8,2,64,128]{3,2,1,0:T(8,128)(2,1)S(1)}, bf16[16,64,128]{2,1,0:T(8,128)(2,1)S(1)}, bf16[8,2,48,128]{3,2,1,0:T(8,128)(2,1)S(1)}, bf16[8,2,4...) custom-call(s32[2]{0:T(128)S(1)} %pad_add_fusion.at_ref, ...), custom_call_target="tpu_custom_call" | custom-call | flops 268435456 | bytes 1835016 | tf_op jit(solution)/shard_map/pallas_call | solution.py:200
  23.3 0.0 collective-permute-done.3.i1
  23.3 6.2 %collective-permute-done.4.i2 = bf16[256,128]{1,0:T(8,128)(2,1)S(1)} collective-permute-done((bf16[256,128]{1,0:T(8,128)(2,1)}, bf16[256,128]{1,0:T(8,128)(2,1)S(1)}, u32[]{:S(2)}, u32[]{:S(2)}) %collective-permute-start.4) | collective-permute-done | bytes 65568 | tf_op jit(solution)/shard_map/ppermute | solution.py:498
  29.5 0.0 collective-permute-done.5.i3
  29.5 0.0 collective-permute-start.6
  29.5 0.5 collective-permute-start.7
  30.0 0.7 %collective-permute-start.8 = (bf16[8,2,48,128]{3,2,1,0:T(8,128)(2,1)S(1)}, bf16[8,2,48,128]{3,2,1,0:T(8,128)(2,1)S(1)}, u32[]{:S(2)}, u32[]{:S(2)}) collective-permute-start(bf16[8,2,48,128]{3,2,1,0:T(8,128)(2,1)S(1)} %get-tuple-element.51), channel_id=1, source_target_pairs={{1,2},{2,1},{5,6},{6,5},{9,10},{10,9},{13,14},{14,13},{17,18},{18,... | collective-permute-start | bytes 589832 | tf_op jit(solution)/shard_map/ppermute | solution.py:576
  30.7 0.4 collective-permute-done.6
  31.1 0.1 add_convert_fusion
  31.1 2.6 %collective-permute-start.9 = (bf16[1024,128]{1,0:T(8,128)(2,1)S(1)}, bf16[1024,128]{1,0:T(8,128)(2,1)S(1)}, u32[]{:S(2)}, u32[]{:S(2)}) collective-permute-start(bf16[1024,128]{1,0:T(8,128)(2,1)S(1)} %add_convert_fusion), channel_id=1, source_target_pairs={{0,2},{1,3},{2,0},{3,1},{4,6},{5,7},{6,4},{7,5},{8,10},{9,11},{10,... | collective-permute-start | bytes 786440 | tf_op jit(solution)/shard_map/ppermute | solution.py:503
  33.7 3.0 %shard_map.114 = (f32[16,96,128]{2,1,0:T(8,128)S(1)}, f32[896,128]{1,0:T(8,128)S(1)}) custom-call(bf16[16,64,128]{2,1,0:T(8,128)(2,1)S(1)} %bitcast.7, bf16[16,64,128]{2,1,0:T(8,128)(2,1)S(1)} %get-tuple-element.46.one_ref, bf16[9,128,384]{2,1,0:T(8,128)(2,1)S(1)} %get-tuple-element.47.w_ref), custom_call_target="tpu_custom_call" | custom-call | flops 1811939328 | bytes 1409024 | tf_op jit(solution)/shard_map/pallas_call | solution.py:200
  36.8 0.0 collective-permute-done.7
  36.8 0.0 collective-permute-done.8
  36.8 0.0 copy-done.4
  36.8 3.9 %shard_map.115 = (f32[896,128]{1,0:T(8,128)S(1)}, bf16[896,128]{1,0:T(8,128)(2,1)S(1)}, bf16[20,96,384]{2,1,0:T(8,128)(2,1)S(1)}) custom-call(s32[2]{0:T(128)S(1)} %pad_add_fusion.at_ref, f32[16,96,128]{2,1,0:T(8,128)S(1)} %get-tuple-element.48.acc_ref, f32[896,128]{1,0:T(8,128)S(1)} %get-tuple-element.49.sums_ref, ...), custom_call_target="tpu_custom_call" | custom-call | flops 796262400 | bytes 3047432 | tf_op jit(solution)/shard_map/pallas_call | solution.py:200
  40.7 2.2 %collective-permute-done.9 = bf16[1024,128]{1,0:T(8,128)(2,1)S(1)} collective-permute-done((bf16[1024,128]{1,0:T(8,128)(2,1)S(1)}, bf16[1024,128]{1,0:T(8,128)(2,1)S(1)}, u32[]{:S(2)}, u32[]{:S(2)}) %collective-permute-start.9) | collective-permute-done | bytes 262176 | tf_op jit(solution)/shard_map/ppermute | solution.py:503
  42.8 0.1 convert_add_fusion.mine_ref
  42.9 0.1 collective-permute-start.10
  43.0 0.5 collective-permute-start.12
  43.5 1.0 %collective-permute-done.10 = bf16[896,128]{1,0:T(8,128)(2,1)S(1)} collective-permute-done((bf16[896,128]{1,0:T(8,128)(2,1)S(1)}, bf16[896,128]{1,0:T(8,128)(2,1)S(1)}, u32[]{:S(2)}, u32[]{:S(2)}) %collective-permute-start.10) | collective-permute-done | bytes 229408 | tf_op jit(solution)/shard_map/ppermute | solution.py:503
  44.4 0.1 add_convert_fusion.1
  44.5 0.8 %collective-permute-start.11 = (bf16[896,128]{1,0:T(8,128)(2,1)S(1)}, bf16[896,128]{1,0:T(8,128)(2,1)S(1)}, u32[]{:S(2)}, u32[]{:S(2)}) collective-permute-start(bf16[896,128]{1,0:T(8,128)(2,1)S(1)} %add_convert_fusion.1), channel_id=1, source_target_pairs={{0,2},{1,3},{2,0},{3,1},{4,6},{5,7},{6,4},{7,5},{8,10},{9,11},{10,... | collective-permute-start | bytes 688136 | tf_op jit(solution)/shard_map/ppermute | solution.py:503
  45.3 1.8 %shard_map.117 = bf16[4,8,1024]{2,1,0:T(8,128)(2,1)} custom-call(s32[2]{0:T(128)S(1)} %pad_add_fusion.at_ref, bf16[20,96,384]{2,1,0:T(8,128)(2,1)S(1)} %get-tuple-element.61.outer_ref, bf16[9,128,384]{2,1,0:T(8,128)(2,1)S(1)} %get-tuple-element.62.w_ref), custom_call_target="tpu_custom_call" | custom-call | flops 226492416 | bytes 2359304 | tf_op jit(solution)/shard_map/pallas_call | solution.py:200
  47.2 0.0 collective-permute-done.12.other_ref
  47.2 1.6 %shard_map.116 = f32[512,512]{1,0:T(8,128)} custom-call(s32[2]{0:T(128)S(1)} %pad_add_fusion.at_ref, f32[1024,128]{1,0:T(8,128)S(1)} %convert_add_fusion.mine_ref, f32[1024,128]{1,0:T(8,128)S(1)} %collective-permute-done.12.other_ref), custom_call_target="tpu_custom_call" | custom-call | flops 10000000 | bytes 1048584 | tf_op jit(solution)/shard_map/pallas_call | solution.py:200
  48.8 3.4 %collective-permute-done.11 = bf16[896,128]{1,0:T(8,128)(2,1)S(1)} collective-permute-done((bf16[896,128]{1,0:T(8,128)(2,1)S(1)}, bf16[896,128]{1,0:T(8,128)(2,1)S(1)}, u32[]{:S(2)}, u32[]{:S(2)}) %collective-permute-start.11) | collective-permute-done | bytes 229408 | tf_op jit(solution)/shard_map/ppermute | solution.py:503
  52.2 0.1 convert_add_fusion.1.mine_ref
  52.3 0.1 collective-permute-start.13
  52.4 0.2 shard_map.118
  52.5 1.6 %collective-permute-done.13.other_ref = f32[896,128]{1,0:T(8,128)S(1)} collective-permute-done((f32[896,128]{1,0:T(8,128)S(1)}, f32[896,128]{1,0:T(8,128)S(1)}, u32[]{:S(2)}, u32[]{:S(2)}) %collective-permute-start.13) | collective-permute-done | bytes 458784 | tf_op jit(solution)/shard_map/ppermute | solution.py:503
  54.2 1.8 %shard_map.119 = (f32[27,64,64]{2,1,0:T(8,128)}, f32[27,64,64]{2,1,0:T(8,128)}) custom-call(s32[2]{0:T(128)S(1)} %pad_add_fusion.at_ref, f32[14,64,64]{2,1,0:T(8,128)S(1)} %get-tuple-element.65.mine_one, f32[14,64,64]{2,1,0:T(8,128)S(1)} %get-tuple-element.66.mine_two, f32[896,128]{1,0:T(8,128)S(1)} %collective-permute-done.13.other_ref), custom_call_target="tpu_custom_call" | custom-call | tf_op jit(solution)/shard_map/pallas_call | solution.py:200
  (6 shorter events, 0.0 us)
Async XLA Ops:
  2.3 11.2 %collective-permute-start = (bf16[768,128]{1,0:T(8,128)(2,1)}, bf16[768,128]{1,0:T(8,128)(2,1)S(1)}, u32[]{:S(2)}, u32[]{:S(2)}) collective-permute-start(bf16[768,128]{1,0:T(8,128)(2,1)} %get-tuple-element.37.a0), channel_id=1, source_target_pairs={{0,4},{4,8},{8,12},{12,0},{1,5},{5,9},{9,13},{13,1},{2,6},{6,10},{... | collective-permute-start | bytes 589832 | tf_op jit(solution)/shard_map/ppermute | solution.py:498
  5.4 16.6 %collective-permute-start.1 = (bf16[768,128]{1,0:T(8,128)(2,1)}, bf16[768,128]{1,0:T(8,128)(2,1)S(1)}, u32[]{:S(2)}, u32[]{:S(2)}) collective-permute-start(bf16[768,128]{1,0:T(8,128)(2,1)} %get-tuple-element.37.a0), channel_id=1, source_target_pairs={{0,8},{4,12},{8,0},{12,4},{1,9},{5,13},{9,1},{13,5},{2,10},{6,14},... | collective-permute-start | bytes 589832 | tf_op jit(solution)/shard_map/ppermute | solution.py:498
  8.0 14.0 %collective-permute-start.2 = (bf16[768,128]{1,0:T(8,128)(2,1)}, bf16[768,128]{1,0:T(8,128)(2,1)S(1)}, u32[]{:S(2)}, u32[]{:S(2)}) collective-permute-start(bf16[768,128]{1,0:T(8,128)(2,1)} %get-tuple-element.37.a0), channel_id=1, source_target_pairs={{0,12},{4,0},{8,4},{12,8},{1,13},{5,1},{9,5},{13,9},{2,14},{6,2},{... | collective-permute-start | bytes 589832 | tf_op jit(solution)/shard_map/ppermute | solution.py:498
  9.3 14.0 %collective-permute-start.3 = (bf16[256,128]{1,0:T(8,128)(2,1)}, bf16[256,128]{1,0:T(8,128)(2,1)S(1)}, u32[]{:S(2)}, u32[]{:S(2)}) collective-permute-start(bf16[256,128]{1,0:T(8,128)(2,1)} %get-tuple-element.52.i0), channel_id=1, source_target_pairs={{0,4},{4,8},{8,12},{12,0},{1,5},{5,9},{9,13},{13,1},{2,6},{6,10},{... | collective-permute-start | bytes 196616 | tf_op jit(solution)/shard_map/ppermute | solution.py:498
  10.0 19.5 %collective-permute-start.4 = (bf16[256,128]{1,0:T(8,128)(2,1)}, bf16[256,128]{1,0:T(8,128)(2,1)S(1)}, u32[]{:S(2)}, u32[]{:S(2)}) collective-permute-start(bf16[256,128]{1,0:T(8,128)(2,1)} %get-tuple-element.52.i0), channel_id=1, source_target_pairs={{0,8},{4,12},{8,0},{12,4},{1,9},{5,13},{9,1},{13,5},{2,10},{6,14},... | collective-permute-start | bytes 196616 | tf_op jit(solution)/shard_map/ppermute | solution.py:498
  13.5 16.1 %collective-permute-start.5 = (bf16[256,128]{1,0:T(8,128)(2,1)}, bf16[256,128]{1,0:T(8,128)(2,1)S(1)}, u32[]{:S(2)}, u32[]{:S(2)}) collective-permute-start(bf16[256,128]{1,0:T(8,128)(2,1)} %get-tuple-element.52.i0), channel_id=1, source_target_pairs={{0,12},{4,0},{8,4},{12,8},{1,13},{5,1},{9,5},{13,9},{2,14},{6,2},{... | collective-permute-start | bytes 196616 | tf_op jit(solution)/shard_map/ppermute | solution.py:498
  15.6 1.0 %copy-start = (bf16[512,512]{1,0:T(8,128)(2,1)S(1)}, bf16[512,512]{1,0:T(8,128)(2,1)}, u32[]{:S(2)}) copy-start(bf16[512,512]{1,0:T(8,128)(2,1)} %wt.1) | copy-start | bytes 1572868
  16.6 1.0 %copy-start.1 = (bf16[27,64,64]{2,1,0:T(8,128)(2,1)S(1)}, bf16[27,64,64]{2,1,0:T(8,128)(2,1)}, u32[]{:S(2)}) copy-start(bf16[27,64,64]{2,1,0:T(8,128)(2,1)} %w2.1) | copy-start | bytes 663556
  17.7 1.0 %copy-start.2 = (bf16[27,64,64]{2,1,0:T(8,128)(2,1)S(1)}, bf16[27,64,64]{2,1,0:T(8,128)(2,1)}, u32[]{:S(2)}) copy-start(bf16[27,64,64]{2,1,0:T(8,128)(2,1)} %w1.1) | copy-start | bytes 663556
  18.7 0.7 %copy-start.5 = (s32[8,8]{1,0:T(8,128)S(1)}, s32[8,8]{1,0:T(8,128)}, u32[]{:S(2)}) copy-start(s32[8,8]{1,0:T(8,128)} %keep.1) | copy-start | bytes 772
  19.4 2.6 %copy-start.3 = (bf16[768,128]{1,0:T(8,128)(2,1)S(1)}, bf16[768,128]{1,0:T(8,128)(2,1)}, u32[]{:S(2)}) copy-start(bf16[768,128]{1,0:T(8,128)(2,1)} %get-tuple-element.37.a0) | copy-start | bytes 589828
  29.5 1.5 %collective-permute-start.6 = (bf16[1024,128]{1,0:T(8,128)(2,1)S(1)}, bf16[1024,128]{1,0:T(8,128)(2,1)S(1)}, u32[]{:S(2)}, u32[]{:S(2)}) collective-permute-start(bf16[1024,128]{1,0:T(8,128)(2,1)S(1)} %get-tuple-element.45), channel_id=1, source_target_pairs={{0,1},{1,0},{2,3},{3,2},{4,5},{5,4},{6,7},{7,6},{8,9},{9,8},{10,11... | collective-permute-start | bytes 786440 | tf_op jit(solution)/shard_map/ppermute | solution.py:503
  29.5 7.2 %collective-permute-start.7 = (bf16[8,2,48,128]{3,2,1,0:T(8,128)(2,1)S(1)}, bf16[8,2,48,128]{3,2,1,0:T(8,128)(2,1)S(1)}, u32[]{:S(2)}, u32[]{:S(2)}) collective-permute-start(bf16[8,2,48,128]{3,2,1,0:T(8,128)(2,1)S(1)} %get-tuple-element.50), channel_id=1, source_target_pairs={{0,1},{1,0},{2,3},{3,2},{4,5},{5,4},{6,7},{7,6},{8,9},{9,8},{10,11... | collective-permute-start | bytes 589832 | tf_op jit(solution)/shard_map/ppermute | solution.py:503
  30.0 6.7 %collective-permute-start.8 = (bf16[8,2,48,128]{3,2,1,0:T(8,128)(2,1)S(1)}, bf16[8,2,48,128]{3,2,1,0:T(8,128)(2,1)S(1)}, u32[]{:S(2)}, u32[]{:S(2)}) collective-permute-start(bf16[8,2,48,128]{3,2,1,0:T(8,128)(2,1)S(1)} %get-tuple-element.51), channel_id=1, source_target_pairs={{1,2},{2,1},{5,6},{6,5},{9,10},{10,9},{13,14},{14,13},{17,18},{18,... | collective-permute-start | bytes 589832 | tf_op jit(solution)/shard_map/ppermute | solution.py:576
  31.1 11.7 %collective-permute-start.9 = (bf16[1024,128]{1,0:T(8,128)(2,1)S(1)}, bf16[1024,128]{1,0:T(8,128)(2,1)S(1)}, u32[]{:S(2)}, u32[]{:S(2)}) collective-permute-start(bf16[1024,128]{1,0:T(8,128)(2,1)S(1)} %add_convert_fusion), channel_id=1, source_target_pairs={{0,2},{1,3},{2,0},{3,1},{4,6},{5,7},{6,4},{7,5},{8,10},{9,11},{10,... | collective-permute-start | bytes 786440 | tf_op jit(solution)/shard_map/ppermute | solution.py:503
  33.7 3.1 %copy-start.4 = (bf16[256,128]{1,0:T(8,128)(2,1)S(1)}, bf16[256,128]{1,0:T(8,128)(2,1)}, u32[]{:S(2)}) copy-start(bf16[256,128]{1,0:T(8,128)(2,1)} %get-tuple-element.52.i0) | copy-start | bytes 196612
  42.9 1.6 %collective-permute-start.10 = (bf16[896,128]{1,0:T(8,128)(2,1)S(1)}, bf16[896,128]{1,0:T(8,128)(2,1)S(1)}, u32[]{:S(2)}, u32[]{:S(2)}) collective-permute-start(bf16[896,128]{1,0:T(8,128)(2,1)S(1)} %get-tuple-element.59), channel_id=1, source_target_pairs={{0,1},{1,0},{2,3},{3,2},{4,5},{5,4},{6,7},{7,6},{8,9},{9,8},{10,11... | collective-permute-start | bytes 688136 | tf_op jit(solution)/shard_map/ppermute | solution.py:503
  43.0 4.2 %collective-permute-start.12 = (f32[1024,128]{1,0:T(8,128)S(1)}, f32[1024,128]{1,0:T(8,128)S(1)}, u32[]{:S(2)}, u32[]{:S(2)}) collective-permute-start(f32[1024,128]{1,0:T(8,128)S(1)} %convert_add_fusion.mine_ref), channel_id=1, source_target_pairs={{0,1},{1,0},{2,3},{3,2},{4,5},{5,4},{6,7},{7,6},{8,9},{9,8},{10,11... | collective-permute-start | bytes 1572872 | tf_op jit(solution)/shard_map/ppermute | solution.py:503
  44.5 7.7 %collective-permute-start.11 = (bf16[896,128]{1,0:T(8,128)(2,1)S(1)}, bf16[896,128]{1,0:T(8,128)(2,1)S(1)}, u32[]{:S(2)}, u32[]{:S(2)}) collective-permute-start(bf16[896,128]{1,0:T(8,128)(2,1)S(1)} %add_convert_fusion.1), channel_id=1, source_target_pairs={{0,2},{1,3},{2,0},{3,1},{4,6},{5,7},{6,4},{7,5},{8,10},{9,11},{10,... | collective-permute-start | bytes 688136 | tf_op jit(solution)/shard_map/ppermute | solution.py:503
  52.3 1.9 %collective-permute-start.13 = (f32[896,128]{1,0:T(8,128)S(1)}, f32[896,128]{1,0:T(8,128)S(1)}, u32[]{:S(2)}, u32[]{:S(2)}) collective-permute-start(f32[896,128]{1,0:T(8,128)S(1)} %convert_add_fusion.1.mine_ref), channel_id=1, source_target_pairs={{0,1},{1,0},{2,3},{3,2},{4,5},{5,4},{6,7},{7,6},{8,9},{9,8},{10,11... | collective-permute-start | bytes 1376264 | tf_op jit(solution)/shard_map/ppermute | solution.py:503

commit v9 on v8

--- a/solution.py
+++ b/solution.py
@@ -187,7 +187,7 @@
     return (grad_in, grad_w_one, grad_w_two, grad_w_trans)
 
 
-def call(kernel, out_shape, scratch, flops, limit, *args, out_space=VMEM):
+def call(kernel, out_shape, scratch, flops, limit, *args, out_space=VMEM, aliases={}):
     spec = []
     for a in args:
         if isinstance(a, tuple):
@@ -203,6 +203,7 @@
         in_specs=spec,
         out_specs=jax.tree.map(lambda _: pl.BlockSpec(memory_space=out_space), out_shape),
         scratch_shapes=scratch,
+        input_output_aliases=aliases,
         cost_estimate=pl.CostEstimate(
             flops=flops,
             transcendentals=0,
@@ -443,46 +444,40 @@
             grad_ref[x, :, 128 * t : 128 * t + 128] = turn_ref[pl.ds(64 * x + t, 8, stride=8), :].astype(BF16)
 
 
-def unpack(ref, at, out_ref):
-    for m in range(7):
-        block = ref[at + 64 * m : at + 64 * m + 64]
-        out_ref[2 * m] = block[:, 0:64]
-        out_ref[2 * m + 1] = block[:, 64:128]
-
-
-def half_kernel(mine_ref, one_ref, two_ref):
-    unpack(mine_ref, 0, one_ref)
-    unpack(mine_ref, 448, two_ref)
-
-
-def spread_kernel(at_ref, mine_one, mine_two, other_ref, one_hbm, two_hbm, one_ref, two_ref, sems):
-    def emit(core):
-        copies = []
-
-        def send(half, one, two):
-            count = 14 - half
-            for src, dst in ((one, one_hbm), (two, two_hbm)):
-                copies.append(
-                    pltpu.make_async_copy(
-                        src.at[0:count], dst.at[14 * half : 14 * half + count], sems.at[len(copies)]
-                    )
-                )
-                copies[-1].start()
-
-        send(core, mine_one, mine_two)
-        unpack(other_ref, 0, one_ref)
-        unpack(other_ref, 448, two_ref)
-        send(1 - core, one_ref, two_ref)
-        for copy in copies:
-            copy.wait()
-
+def spread(half, ref, hbm_refs, refs, sems):
+    copies = []
+    count = 14 - half
+    for k, (hbm, out) in enumerate(zip(hbm_refs, refs)):
+        for m in range(7):
+            block = ref[448 * k + 64 * m : 448 * k + 64 * m + 64].astype(F32)
+            out[2 * m] = block[:, 0:64]
+            out[2 * m + 1] = block[:, 64:128]
+        copies.append(
+            pltpu.make_async_copy(out.at[0:count], hbm.at[14 * half : 14 * half + count], sems.at[k])
+        )
+        copies[-1].start()
+    for copy in copies:
+        copy.wait()
+
+
+def half_kernel(at_ref, ref, one_hbm, two_hbm, one_ref, two_ref, sems):
     @pl.when(at_ref[1] == 0)
     def _():
-        emit(0)
+        spread(0, ref, (one_hbm, two_hbm), (one_ref, two_ref), sems)
 
     @pl.when(at_ref[1] != 0)
     def _():
-        emit(1)
+        spread(1, ref, (one_hbm, two_hbm), (one_ref, two_ref), sems)
+
+
+def rest_kernel(at_ref, ref, one_in, two_in, one_hbm, two_hbm, one_ref, two_ref, sems):
+    @pl.when(at_ref[1] == 0)
+    def _():
+        spread(1, ref, (one_hbm, two_hbm), (one_ref, two_ref), sems)
+
+    @pl.when(at_ref[1] != 0)
+    def _():
+        spread(0, ref, (one_hbm, two_hbm), (one_ref, two_ref), sems)
 
 
 def trans_kernel(at_ref, mine_ref, other_ref, trans_ref):
@@ -619,22 +614,24 @@
         grad_kernel, shape((4, 8, 1024), BF16), [vmem((256, 128), F32)], 2 * 128 * 3456 * 256, 12, at, outer, d1
     )
     away, grad_w_trans, grad_in = lax.optimization_barrier((away, grad_w_trans, grad_in))
-    mine = mine.astype(F32) + away.astype(F32)
+    mine = (mine.astype(F32) + away.astype(F32)).astype(BF16)
     other = swap(mine, "gy", 1)
     taps = shape((27, 64, 64), F32)
-    half = shape((14, 64, 64), F32)
-    mine_one, mine_two = call(half_kernel, (half, half), [], 10**8, 6, mine)
+    scratch = [vmem((14, 64, 64), F32), vmem((14, 64, 64), F32), pltpu.SemaphoreType.DMA((2,))]
+    hbm = pltpu.MemorySpace.HBM
+    grad_w_one, grad_w_two = call(half_kernel, (taps, taps), scratch, 10**8, 6, at, mine, out_space=hbm)
     grad_w_one, grad_w_two = call(
-        spread_kernel,
+        rest_kernel,
         (taps, taps),
-        [vmem(half.shape, F32), vmem(half.shape, F32), pltpu.SemaphoreType.DMA((4,))],
+        scratch,
         0,
-        8,
+        6,
         at,
-        mine_one,
-        mine_two,
         other,
-        out_space=pltpu.MemorySpace.HBM,
+        (grad_w_one,),
+        (grad_w_two,),
+        out_space=hbm,
+        aliases={2: 0, 3: 1},
     )
     return (grad_in, grad_w_one, grad_w_two, grad_w_trans)
 

time: 56.3 us -> 55.9 us (level)
  waiting for transfers between devices: 19 us -> 17.4 us
  Pallas kernels: 16.8 us -> 17.9 us
    ppermute x7, waiting for transfers between devices: 8.51 us -> 6.9 us  [swap(): return lax.ppermute(value, axis, [(i, i ^ bit) for i in range(n)])]
    pallas_call x9, Pallas kernels: 16.8 us -> 17.9 us  [call(): pl.pallas_call(kernel, out_shape=out_shape, in_specs=spec, out_specs=jax....]
  transfers between devices with their start and end apart: 14 -> 14, of which waited for: 8 -> 7; matrix products, arithmetic and copies ran while one was open for 0% -> 0% of each run, Pallas kernels for 24% -> 27%
where the time goes in v9:
time: 55.9 us; the launch traced here: 55.5 us
  Pallas kernels  17.9 us (32%)
  waiting for transfers between devices  17.4 us (31%)
  starting transfers between devices  15.3 us (27%)
  local copies, waits for them, and re-layouts  3.76 us (7%)
  between operations  0.77 us (1%)
    pallas_call x9, Pallas kernels, call(): pl.pallas_call(kernel, out_shape=out_shape, in_specs=spec, out_specs=jax....  17.9 us
    ppermute x6, waiting for transfers between devices, rotate(): return lax.ppermute(value, axis, [(i, (i + step) % n) for i in range(n)])  10.5 us
    ppermute x6, starting transfers between devices, rotate(): return lax.ppermute(value, axis, [(i, (i + step) % n) for i in range(n)])  10.1 us
    ppermute x7, waiting for transfers between devices, swap(): return lax.ppermute(value, axis, [(i, i ^ bit) for i in range(n)])  6.9 us
    ppermute x7, starting transfers between devices, swap(): return lax.ppermute(value, axis, [(i, i ^ bit) for i in range(n)])  4.56 us
    unnamed x12, local copies, waits for them, and re-layouts  3.76 us
  transfers between devices with their start and end apart: 14, of which 7 were waited for; matrix products, arithmetic and copies ran while one was open for 0% of the time, Pallas kernels for 27%

profile of v9, /device:TPU:0, one launch (start us, length us, event | category | flops | bytes accessed | tf_op | source)
XLA Modules:
  0.0 55.5 jit_solution(15114799804129813313)
XLA Ops:
  0.6 1.7 %shard_map.111 = (bf16[768,128]{1,0:T(8,128)(2,1)}, bf16[256,128]{1,0:T(8,128)(2,1)}) custom-call(bf16[8,4,8,128]{3,2,1,0:T(8,128)(2,1)} %og.1, bf16[4,8,1024]{2,1,0:T(8,128)(2,1)} %two.1, bf16[4,8,1024]{2,1,0:T(8,128)(2,1)} %one.1, bf16[4,8,1024]{2,1,0:T(8,128)(2,1)} %act.1), custom_call_target="tpu_custom_call" | custom-call | tf_op jit(solution)/shard_map/pallas_call | solution.py:200
  2.3 3.1 %collective-permute-start = (bf16[768,128]{1,0:T(8,128)(2,1)}, bf16[768,128]{1,0:T(8,128)(2,1)S(1)}, u32[]{:S(2)}, u32[]{:S(2)}) collective-permute-start(bf16[768,128]{1,0:T(8,128)(2,1)} %get-tuple-element.37.a0), channel_id=1, source_target_pairs={{0,4},{4,8},{8,12},{12,0},{1,5},{5,9},{9,13},{13,1},{2,6},{6,10},{... | collective-permute-start | bytes 589832 | tf_op jit(solution)/shard_map/ppermute | solution.py:493
  5.4 2.6 %collective-permute-start.1 = (bf16[768,128]{1,0:T(8,128)(2,1)}, bf16[768,128]{1,0:T(8,128)(2,1)S(1)}, u32[]{:S(2)}, u32[]{:S(2)}) collective-permute-start(bf16[768,128]{1,0:T(8,128)(2,1)} %get-tuple-element.37.a0), channel_id=1, source_target_pairs={{0,8},{4,12},{8,0},{12,4},{1,9},{5,13},{9,1},{13,5},{2,10},{6,14},... | collective-permute-start | bytes 589832 | tf_op jit(solution)/shard_map/ppermute | solution.py:493
  8.0 1.3 %collective-permute-start.2 = (bf16[768,128]{1,0:T(8,128)(2,1)}, bf16[768,128]{1,0:T(8,128)(2,1)S(1)}, u32[]{:S(2)}, u32[]{:S(2)}) collective-permute-start(bf16[768,128]{1,0:T(8,128)(2,1)} %get-tuple-element.37.a0), channel_id=1, source_target_pairs={{0,12},{4,0},{8,4},{12,8},{1,13},{5,1},{9,5},{13,9},{2,14},{6,2},{... | collective-permute-start | bytes 589832 | tf_op jit(solution)/shard_map/ppermute | solution.py:493
  9.3 0.7 %collective-permute-start.3 = (bf16[256,128]{1,0:T(8,128)(2,1)}, bf16[256,128]{1,0:T(8,128)(2,1)S(1)}, u32[]{:S(2)}, u32[]{:S(2)}) collective-permute-start(bf16[256,128]{1,0:T(8,128)(2,1)} %get-tuple-element.52.i0), channel_id=1, source_target_pairs={{0,4},{4,8},{8,12},{12,0},{1,5},{5,9},{9,13},{13,1},{2,6},{6,10},{... | collective-permute-start | bytes 196616 | tf_op jit(solution)/shard_map/ppermute | solution.py:493
  10.0 0.3 collective-permute-start.4
  10.3 3.1 %collective-permute-done.a1 = bf16[768,128]{1,0:T(8,128)(2,1)S(1)} collective-permute-done((bf16[768,128]{1,0:T(8,128)(2,1)}, bf16[768,128]{1,0:T(8,128)(2,1)S(1)}, u32[]{:S(2)}, u32[]{:S(2)}) %collective-permute-start) | collective-permute-done | bytes 196640 | tf_op jit(solution)/shard_map/ppermute | solution.py:493
  13.5 2.1 %collective-permute-start.5 = (bf16[256,128]{1,0:T(8,128)(2,1)}, bf16[256,128]{1,0:T(8,128)(2,1)S(1)}, u32[]{:S(2)}, u32[]{:S(2)}) collective-permute-start(bf16[256,128]{1,0:T(8,128)(2,1)} %get-tuple-element.52.i0), channel_id=1, source_target_pairs={{0,12},{4,0},{8,4},{12,8},{1,13},{5,1},{9,5},{13,9},{2,14},{6,2},{... | collective-permute-start | bytes 196616 | tf_op jit(solution)/shard_map/ppermute | solution.py:493
  15.5 0.1 pad_add_fusion.at_ref
  15.6 1.0 %copy-done = bf16[512,512]{1,0:T(8,128)(2,1)S(1)} copy-done((bf16[512,512]{1,0:T(8,128)(2,1)S(1)}, bf16[512,512]{1,0:T(8,128)(2,1)}, u32[]{:S(2)}) %copy-start) | copy-done | bytes 524312
  16.6 1.0 %copy-done.1 = bf16[27,64,64]{2,1,0:T(8,128)(2,1)S(1)} copy-done((bf16[27,64,64]{2,1,0:T(8,128)(2,1)S(1)}, bf16[27,64,64]{2,1,0:T(8,128)(2,1)}, u32[]{:S(2)}) %copy-start.1) | copy-done | bytes 221208
  17.7 1.0 %copy-done.2 = bf16[27,64,64]{2,1,0:T(8,128)(2,1)S(1)} copy-done((bf16[27,64,64]{2,1,0:T(8,128)(2,1)S(1)}, bf16[27,64,64]{2,1,0:T(8,128)(2,1)}, u32[]{:S(2)}) %copy-start.2) | copy-done | bytes 221208
  18.7 0.7 %copy-done.5 = s32[8,8]{1,0:T(8,128)S(1)} copy-done((s32[8,8]{1,0:T(8,128)S(1)}, s32[8,8]{1,0:T(8,128)}, u32[]{:S(2)}) %copy-start.5) | copy-done | bytes 280
  19.4 1.4 %shard_map.112 = (bf16[512,512]{1,0:T(8,128)(2,1)S(1)}, bf16[512,512]{1,0:T(8,128)(2,1)S(1)}, bf16[9,128,384]{2,1,0:T(8,128)(2,1)S(1)}, bf16[9,128,384]{2,1,0:T(8,128)(2,1)S(1)}) custom-call(bf16[512,512]{1,0:T(8,128)(2,1)S(1)} %copy-done, s32[8,8]{1,0:T(8,128)S(1)} %copy-done.5, bf16[27,64,64]{2,1,0:T(8,128)(2,1)S(1)} %copy-done.1, ...), custom_call_target="tpu_custom_call" | custom-call | flops 10000000 | bytes 966912 | tf_op jit(solution)/shard_map/pallas_call | solution.py:200
  20.8 1.2 %collective-permute-done.1.a2 = bf16[768,128]{1,0:T(8,128)(2,1)S(1)} collective-permute-done((bf16[768,128]{1,0:T(8,128)(2,1)}, bf16[768,128]{1,0:T(8,128)(2,1)S(1)}, u32[]{:S(2)}, u32[]{:S(2)}) %collective-permute-start.1) | collective-permute-done | bytes 196640 | tf_op jit(solution)/shard_map/ppermute | solution.py:493
  21.9 0.0 collective-permute-done.2.a3
  21.9 0.0 copy-done.3
  22.0 1.3 %shard_map.113 = (bf16[8,2,64,128]{3,2,1,0:T(8,128)(2,1)S(1)}, bf16[16,64,128]{2,1,0:T(8,128)(2,1)S(1)}, bf16[8,2,48,128]{3,2,1,0:T(8,128)(2,1)S(1)}, bf16[8,2,4...) custom-call(s32[2]{0:T(128)S(1)} %pad_add_fusion.at_ref, ...), custom_call_target="tpu_custom_call" | custom-call | flops 268435456 | bytes 1835016 | tf_op jit(solution)/shard_map/pallas_call | solution.py:200
  23.3 0.0 collective-permute-done.3.i1
  23.3 6.2 %collective-permute-done.4.i2 = bf16[256,128]{1,0:T(8,128)(2,1)S(1)} collective-permute-done((bf16[256,128]{1,0:T(8,128)(2,1)}, bf16[256,128]{1,0:T(8,128)(2,1)S(1)}, u32[]{:S(2)}, u32[]{:S(2)}) %collective-permute-start.4) | collective-permute-done | bytes 65568 | tf_op jit(solution)/shard_map/ppermute | solution.py:493
  29.5 0.0 collective-permute-done.5.i3
  29.5 0.0 collective-permute-start.6
  29.5 0.5 collective-permute-start.7
  30.0 0.7 %collective-permute-start.8 = (bf16[8,2,48,128]{3,2,1,0:T(8,128)(2,1)S(1)}, bf16[8,2,48,128]{3,2,1,0:T(8,128)(2,1)S(1)}, u32[]{:S(2)}, u32[]{:S(2)}) collective-permute-start(bf16[8,2,48,128]{3,2,1,0:T(8,128)(2,1)S(1)} %get-tuple-element.51), channel_id=1, source_target_pairs={{1,2},{2,1},{5,6},{6,5},{9,10},{10,9},{13,14},{14,13},{17,18},{18,... | collective-permute-start | bytes 589832 | tf_op jit(solution)/shard_map/ppermute | solution.py:571
  30.7 0.4 collective-permute-done.6
  31.1 0.1 add_convert_fusion
  31.1 2.6 %collective-permute-start.9 = (bf16[1024,128]{1,0:T(8,128)(2,1)S(1)}, bf16[1024,128]{1,0:T(8,128)(2,1)S(1)}, u32[]{:S(2)}, u32[]{:S(2)}) collective-permute-start(bf16[1024,128]{1,0:T(8,128)(2,1)S(1)} %add_convert_fusion), channel_id=1, source_target_pairs={{0,2},{1,3},{2,0},{3,1},{4,6},{5,7},{6,4},{7,5},{8,10},{9,11},{10,... | collective-permute-start | bytes 786440 | tf_op jit(solution)/shard_map/ppermute | solution.py:498
  33.7 3.0 %shard_map.114 = (f32[16,96,128]{2,1,0:T(8,128)S(1)}, f32[896,128]{1,0:T(8,128)S(1)}) custom-call(bf16[16,64,128]{2,1,0:T(8,128)(2,1)S(1)} %bitcast.7, bf16[16,64,128]{2,1,0:T(8,128)(2,1)S(1)} %get-tuple-element.46.one_ref, bf16[9,128,384]{2,1,0:T(8,128)(2,1)S(1)} %get-tuple-element.47.w_ref), custom_call_target="tpu_custom_call" | custom-call | flops 1811939328 | bytes 1409024 | tf_op jit(solution)/shard_map/pallas_call | solution.py:200
  36.8 0.0 collective-permute-done.7
  36.8 0.0 collective-permute-done.8
  36.8 0.0 copy-done.4
  36.8 3.9 %shard_map.115 = (f32[896,128]{1,0:T(8,128)S(1)}, bf16[896,128]{1,0:T(8,128)(2,1)S(1)}, bf16[20,96,384]{2,1,0:T(8,128)(2,1)S(1)}) custom-call(s32[2]{0:T(128)S(1)} %pad_add_fusion.at_ref, f32[16,96,128]{2,1,0:T(8,128)S(1)} %get-tuple-element.48.acc_ref, f32[896,128]{1,0:T(8,128)S(1)} %get-tuple-element.49.sums_ref, ...), custom_call_target="tpu_custom_call" | custom-call | flops 796262400 | bytes 3047432 | tf_op jit(solution)/shard_map/pallas_call | solution.py:200
  40.7 2.2 %collective-permute-done.9 = bf16[1024,128]{1,0:T(8,128)(2,1)S(1)} collective-permute-done((bf16[1024,128]{1,0:T(8,128)(2,1)S(1)}, bf16[1024,128]{1,0:T(8,128)(2,1)S(1)}, u32[]{:S(2)}, u32[]{:S(2)}) %collective-permute-start.9) | collective-permute-done | bytes 262176 | tf_op jit(solution)/shard_map/ppermute | solution.py:498
  42.8 0.1 convert_add_fusion.mine_ref
  42.9 0.1 collective-permute-start.10
  43.0 0.5 collective-permute-start.12
  43.5 1.0 %collective-permute-done.10 = bf16[896,128]{1,0:T(8,128)(2,1)S(1)} collective-permute-done((bf16[896,128]{1,0:T(8,128)(2,1)S(1)}, bf16[896,128]{1,0:T(8,128)(2,1)S(1)}, u32[]{:S(2)}, u32[]{:S(2)}) %collective-permute-start.10) | collective-permute-done | bytes 229408 | tf_op jit(solution)/shard_map/ppermute | solution.py:498
  44.4 0.1 add_convert_fusion.2
  44.5 0.8 %collective-permute-start.11 = (bf16[896,128]{1,0:T(8,128)(2,1)S(1)}, bf16[896,128]{1,0:T(8,128)(2,1)S(1)}, u32[]{:S(2)}, u32[]{:S(2)}) collective-permute-start(bf16[896,128]{1,0:T(8,128)(2,1)S(1)} %add_convert_fusion.2), channel_id=1, source_target_pairs={{0,2},{1,3},{2,0},{3,1},{4,6},{5,7},{6,4},{7,5},{8,10},{9,11},{10,... | collective-permute-start | bytes 688136 | tf_op jit(solution)/shard_map/ppermute | solution.py:498
  45.3 1.8 %shard_map.117 = bf16[4,8,1024]{2,1,0:T(8,128)(2,1)} custom-call(s32[2]{0:T(128)S(1)} %pad_add_fusion.at_ref, bf16[20,96,384]{2,1,0:T(8,128)(2,1)S(1)} %get-tuple-element.61.outer_ref, bf16[9,128,384]{2,1,0:T(8,128)(2,1)S(1)} %get-tuple-element.62.w_ref), custom_call_target="tpu_custom_call" | custom-call | flops 226492416 | bytes 2359304 | tf_op jit(solution)/shard_map/pallas_call | solution.py:200
  47.2 0.0 collective-permute-done.12.other_ref
  47.2 1.6 %shard_map.116 = f32[512,512]{1,0:T(8,128)} custom-call(s32[2]{0:T(128)S(1)} %pad_add_fusion.at_ref, f32[1024,128]{1,0:T(8,128)S(1)} %convert_add_fusion.mine_ref, f32[1024,128]{1,0:T(8,128)S(1)} %collective-permute-done.12.other_ref), custom_call_target="tpu_custom_call" | custom-call | flops 10000000 | bytes 1048584 | tf_op jit(solution)/shard_map/pallas_call | solution.py:200
  48.8 3.4 %collective-permute-done.11 = bf16[896,128]{1,0:T(8,128)(2,1)S(1)} collective-permute-done((bf16[896,128]{1,0:T(8,128)(2,1)S(1)}, bf16[896,128]{1,0:T(8,128)(2,1)S(1)}, u32[]{:S(2)}, u32[]{:S(2)}) %collective-permute-start.11) | collective-permute-done | bytes 229408 | tf_op jit(solution)/shard_map/ppermute | solution.py:498
  52.2 0.1 add_convert_fusion.1.ref
  52.3 0.1 collective-permute-start.13
  52.4 1.6 %shard_map.118 = (f32[27,64,64]{2,1,0:T(8,128)}, f32[27,64,64]{2,1,0:T(8,128)}) custom-call(s32[2]{0:T(128)S(1)} %pad_add_fusion.at_ref, bf16[896,128]{1,0:T(8,128)(2,1)S(1)} %add_convert_fusion.1.ref), custom_call_target="tpu_custom_call" | custom-call | flops 100000000 | bytes 229384 | tf_op jit(solution)/shard_map/pallas_call | solution.py:200
  53.9 0.0 collective-permute-done.13.ref
  54.0 1.6 %shard_map.119 = (f32[27,64,64]{2,1,0:T(8,128)}, f32[27,64,64]{2,1,0:T(8,128)}) custom-call(s32[2]{0:T(128)S(1)} %pad_add_fusion.at_ref, bf16[896,128]{1,0:T(8,128)(2,1)S(1)} %collective-permute-done.13.ref, f32[27,64,64]{2,1,0:T(8,128)} %get-tuple-element.65.one_in, ...), custom_call_target="tpu_custom_call", output_to_operand_aliasing={{0}: (2, {}), {1}: (3, {})} | custom-call | tf_op jit(solution)/shard_map/pallas_call | solution.py:200
  (6 shorter events, 0.0 us)
Async XLA Ops:
  2.3 11.2 %collective-permute-start = (bf16[768,128]{1,0:T(8,128)(2,1)}, bf16[768,128]{1,0:T(8,128)(2,1)S(1)}, u32[]{:S(2)}, u32[]{:S(2)}) collective-permute-start(bf16[768,128]{1,0:T(8,128)(2,1)} %get-tuple-element.37.a0), channel_id=1, source_target_pairs={{0,4},{4,8},{8,12},{12,0},{1,5},{5,9},{9,13},{13,1},{2,6},{6,10},{... | collective-permute-start | bytes 589832 | tf_op jit(solution)/shard_map/ppermute | solution.py:493
  5.4 16.6 %collective-permute-start.1 = (bf16[768,128]{1,0:T(8,128)(2,1)}, bf16[768,128]{1,0:T(8,128)(2,1)S(1)}, u32[]{:S(2)}, u32[]{:S(2)}) collective-permute-start(bf16[768,128]{1,0:T(8,128)(2,1)} %get-tuple-element.37.a0), channel_id=1, source_target_pairs={{0,8},{4,12},{8,0},{12,4},{1,9},{5,13},{9,1},{13,5},{2,10},{6,14},... | collective-permute-start | bytes 589832 | tf_op jit(solution)/shard_map/ppermute | solution.py:493
  8.0 14.0 %collective-permute-start.2 = (bf16[768,128]{1,0:T(8,128)(2,1)}, bf16[768,128]{1,0:T(8,128)(2,1)S(1)}, u32[]{:S(2)}, u32[]{:S(2)}) collective-permute-start(bf16[768,128]{1,0:T(8,128)(2,1)} %get-tuple-element.37.a0), channel_id=1, source_target_pairs={{0,12},{4,0},{8,4},{12,8},{1,13},{5,1},{9,5},{13,9},{2,14},{6,2},{... | collective-permute-start | bytes 589832 | tf_op jit(solution)/shard_map/ppermute | solution.py:493
  9.3 14.0 %collective-permute-start.3 = (bf16[256,128]{1,0:T(8,128)(2,1)}, bf16[256,128]{1,0:T(8,128)(2,1)S(1)}, u32[]{:S(2)}, u32[]{:S(2)}) collective-permute-start(bf16[256,128]{1,0:T(8,128)(2,1)} %get-tuple-element.52.i0), channel_id=1, source_target_pairs={{0,4},{4,8},{8,12},{12,0},{1,5},{5,9},{9,13},{13,1},{2,6},{6,10},{... | collective-permute-start | bytes 196616 | tf_op jit(solution)/shard_map/ppermute | solution.py:493
  10.0 19.5 %collective-permute-start.4 = (bf16[256,128]{1,0:T(8,128)(2,1)}, bf16[256,128]{1,0:T(8,128)(2,1)S(1)}, u32[]{:S(2)}, u32[]{:S(2)}) collective-permute-start(bf16[256,128]{1,0:T(8,128)(2,1)} %get-tuple-element.52.i0), channel_id=1, source_target_pairs={{0,8},{4,12},{8,0},{12,4},{1,9},{5,13},{9,1},{13,5},{2,10},{6,14},... | collective-permute-start | bytes 196616 | tf_op jit(solution)/shard_map/ppermute | solution.py:493
  13.5 16.1 %collective-permute-start.5 = (bf16[256,128]{1,0:T(8,128)(2,1)}, bf16[256,128]{1,0:T(8,128)(2,1)S(1)}, u32[]{:S(2)}, u32[]{:S(2)}) collective-permute-start(bf16[256,128]{1,0:T(8,128)(2,1)} %get-tuple-element.52.i0), channel_id=1, source_target_pairs={{0,12},{4,0},{8,4},{12,8},{1,13},{5,1},{9,5},{13,9},{2,14},{6,2},{... | collective-permute-start | bytes 196616 | tf_op jit(solution)/shard_map/ppermute | solution.py:493
  15.6 1.0 %copy-start = (bf16[512,512]{1,0:T(8,128)(2,1)S(1)}, bf16[512,512]{1,0:T(8,128)(2,1)}, u32[]{:S(2)}) copy-start(bf16[512,512]{1,0:T(8,128)(2,1)} %wt.1) | copy-start | bytes 1572868
  16.6 1.0 %copy-start.1 = (bf16[27,64,64]{2,1,0:T(8,128)(2,1)S(1)}, bf16[27,64,64]{2,1,0:T(8,128)(2,1)}, u32[]{:S(2)}) copy-start(bf16[27,64,64]{2,1,0:T(8,128)(2,1)} %w2.1) | copy-start | bytes 663556
  17.7 1.0 %copy-start.2 = (bf16[27,64,64]{2,1,0:T(8,128)(2,1)S(1)}, bf16[27,64,64]{2,1,0:T(8,128)(2,1)}, u32[]{:S(2)}) copy-start(bf16[27,64,64]{2,1,0:T(8,128)(2,1)} %w1.1) | copy-start | bytes 663556
  18.7 0.7 %copy-start.5 = (s32[8,8]{1,0:T(8,128)S(1)}, s32[8,8]{1,0:T(8,128)}, u32[]{:S(2)}) copy-start(s32[8,8]{1,0:T(8,128)} %keep.1) | copy-start | bytes 772
  19.4 2.6 %copy-start.3 = (bf16[768,128]{1,0:T(8,128)(2,1)S(1)}, bf16[768,128]{1,0:T(8,128)(2,1)}, u32[]{:S(2)}) copy-start(bf16[768,128]{1,0:T(8,128)(2,1)} %get-tuple-element.37.a0) | copy-start | bytes 589828
  29.5 1.5 %collective-permute-start.6 = (bf16[1024,128]{1,0:T(8,128)(2,1)S(1)}, bf16[1024,128]{1,0:T(8,128)(2,1)S(1)}, u32[]{:S(2)}, u32[]{:S(2)}) collective-permute-start(bf16[1024,128]{1,0:T(8,128)(2,1)S(1)} %get-tuple-element.45), channel_id=1, source_target_pairs={{0,1},{1,0},{2,3},{3,2},{4,5},{5,4},{6,7},{7,6},{8,9},{9,8},{10,11... | collective-permute-start | bytes 786440 | tf_op jit(solution)/shard_map/ppermute | solution.py:498
  29.5 7.2 %collective-permute-start.7 = (bf16[8,2,48,128]{3,2,1,0:T(8,128)(2,1)S(1)}, bf16[8,2,48,128]{3,2,1,0:T(8,128)(2,1)S(1)}, u32[]{:S(2)}, u32[]{:S(2)}) collective-permute-start(bf16[8,2,48,128]{3,2,1,0:T(8,128)(2,1)S(1)} %get-tuple-element.50), channel_id=1, source_target_pairs={{0,1},{1,0},{2,3},{3,2},{4,5},{5,4},{6,7},{7,6},{8,9},{9,8},{10,11... | collective-permute-start | bytes 589832 | tf_op jit(solution)/shard_map/ppermute | solution.py:498
  30.0 6.7 %collective-permute-start.8 = (bf16[8,2,48,128]{3,2,1,0:T(8,128)(2,1)S(1)}, bf16[8,2,48,128]{3,2,1,0:T(8,128)(2,1)S(1)}, u32[]{:S(2)}, u32[]{:S(2)}) collective-permute-start(bf16[8,2,48,128]{3,2,1,0:T(8,128)(2,1)S(1)} %get-tuple-element.51), channel_id=1, source_target_pairs={{1,2},{2,1},{5,6},{6,5},{9,10},{10,9},{13,14},{14,13},{17,18},{18,... | collective-permute-start | bytes 589832 | tf_op jit(solution)/shard_map/ppermute | solution.py:571
  31.1 11.7 %collective-permute-start.9 = (bf16[1024,128]{1,0:T(8,128)(2,1)S(1)}, bf16[1024,128]{1,0:T(8,128)(2,1)S(1)}, u32[]{:S(2)}, u32[]{:S(2)}) collective-permute-start(bf16[1024,128]{1,0:T(8,128)(2,1)S(1)} %add_convert_fusion), channel_id=1, source_target_pairs={{0,2},{1,3},{2,0},{3,1},{4,6},{5,7},{6,4},{7,5},{8,10},{9,11},{10,... | collective-permute-start | bytes 786440 | tf_op jit(solution)/shard_map/ppermute | solution.py:498
  33.7 3.1 %copy-start.4 = (bf16[256,128]{1,0:T(8,128)(2,1)S(1)}, bf16[256,128]{1,0:T(8,128)(2,1)}, u32[]{:S(2)}) copy-start(bf16[256,128]{1,0:T(8,128)(2,1)} %get-tuple-element.52.i0) | copy-start | bytes 196612
  42.9 1.6 %collective-permute-start.10 = (bf16[896,128]{1,0:T(8,128)(2,1)S(1)}, bf16[896,128]{1,0:T(8,128)(2,1)S(1)}, u32[]{:S(2)}, u32[]{:S(2)}) collective-permute-start(bf16[896,128]{1,0:T(8,128)(2,1)S(1)} %get-tuple-element.59), channel_id=1, source_target_pairs={{0,1},{1,0},{2,3},{3,2},{4,5},{5,4},{6,7},{7,6},{8,9},{9,8},{10,11... | collective-permute-start | bytes 688136 | tf_op jit(solution)/shard_map/ppermute | solution.py:498
  43.0 4.2 %collective-permute-start.12 = (f32[1024,128]{1,0:T(8,128)S(1)}, f32[1024,128]{1,0:T(8,128)S(1)}, u32[]{:S(2)}, u32[]{:S(2)}) collective-permute-start(f32[1024,128]{1,0:T(8,128)S(1)} %convert_add_fusion.mine_ref), channel_id=1, source_target_pairs={{0,1},{1,0},{2,3},{3,2},{4,5},{5,4},{6,7},{7,6},{8,9},{9,8},{10,11... | collective-permute-start | bytes 1572872 | tf_op jit(solution)/shard_map/ppermute | solution.py:498
  44.5 7.7 %collective-permute-start.11 = (bf16[896,128]{1,0:T(8,128)(2,1)S(1)}, bf16[896,128]{1,0:T(8,128)(2,1)S(1)}, u32[]{:S(2)}, u32[]{:S(2)}) collective-permute-start(bf16[896,128]{1,0:T(8,128)(2,1)S(1)} %add_convert_fusion.2), channel_id=1, source_target_pairs={{0,2},{1,3},{2,0},{3,1},{4,6},{5,7},{6,4},{7,5},{8,10},{9,11},{10,... | collective-permute-start | bytes 688136 | tf_op jit(solution)/shard_map/ppermute | solution.py:498
  52.3 1.7 %collective-permute-start.13 = (bf16[896,128]{1,0:T(8,128)(2,1)S(1)}, bf16[896,128]{1,0:T(8,128)(2,1)S(1)}, u32[]{:S(2)}, u32[]{:S(2)}) collective-permute-start(bf16[896,128]{1,0:T(8,128)(2,1)S(1)} %add_convert_fusion.1.ref), channel_id=1, source_target_pairs={{0,1},{1,0},{2,3},{3,2},{4,5},{5,4},{6,7},{7,6},{8,9},{9,8},{10,11... | collective-permute-start | bytes 688136 | tf_op jit(solution)/shard_map/ppermute | solution.py:498

commit v10 on v9

--- a/solution.py
+++ b/solution.py
@@ -262,7 +262,7 @@
 
 
 def transition_kernel(
-    factor, at_ref, a0, a1, a2, a3, kept_ref, mask_ref, back_ref, one_ref, chip_ref, cross_ref, mine_ref, send_ref, og_ref, two_ref
+    factor, at_ref, a0, a1, a2, a3, kept_ref, mask_ref, back_ref, one_ref, chip_ref, cross_ref, mine_ref, send0_ref, send1_ref, og_ref, two_ref
 ):
     me = at_ref[0]
     parts = (a0, a1, a2, a3)
@@ -298,11 +298,13 @@
     trans = lax.dot_general(flat, og, (((0,), (0,)), ((), ())), preferred_element_type=F32)
     trans = trans * mask_ref[...].astype(F32) * factor
 
-    def emit(half, ref):
+    def emit(half, refs):
         for m in range(4):
-            ref[256 * m : 256 * m + 256] = trans[256 * half : 256 * half + 256, 128 * m : 128 * m + 128].astype(ref.dtype)
-
-    share(at_ref[1], emit, mine_ref, send_ref)
+            ref = refs[256 * m // refs[0].shape[0]]
+            at = 256 * m % ref.shape[0]
+            ref[at : at + 256] = trans[256 * half : 256 * half + 256, 128 * m : 128 * m + 128].astype(ref.dtype)
+
+    share(at_ref[1], emit, (mine_ref,), (send0_ref, send1_ref))
 
 
 def share(core, emit, mine_ref, send_ref):
@@ -548,7 +550,7 @@
         (w_two,),
         (w_one,),
     )
-    back, one, chip, cross, tmine, tsend = call(
+    back, one, chip, cross, tmine, *tsend = call(
         functools.partial(transition_kernel, factor),
         (
             shape((8, 2, 64, 128), BF16),
@@ -556,7 +558,8 @@
             shape((8, 2, 48, 128), BF16),
             shape((8, 2, 48, 128), BF16),
             shape((1024, 128), F32),
-            shape((1024, 128), BF16),
+            shape((512, 128), BF16),
+            shape((512, 128), BF16),
         ),
         [vmem((4, 256, 128), BF16), vmem((16, 64, 128), BF16)],
         4 * 256 * 512 * 512,
@@ -570,9 +573,9 @@
     pairs = [(i, i + 1) for i in range(1, n - 1, 2)]
     cross = lax.ppermute(cross, "gy", pairs + [(j, i) for i, j in pairs])
     chip = swap(chip, "gy", 1)
-    tsend, *seconds = lax.optimization_barrier((tsend, *seconds))
-    tmine = on_chip(tmine, tsend)
-    one, tmine = lax.optimization_barrier((one, tmine))
+    *tsend, last = lax.optimization_barrier((*tsend, seconds[1:]))
+    seconds = [seconds[0], *last]
+    taken = jnp.concatenate([swap(piece, "gy", 1) for piece in tsend], axis=0)
     acc, sums = call(
         functools.partial(own_kernel, factor),
         (shape((16, 96, 128), F32), shape((896, 128), F32)),
@@ -583,6 +586,8 @@
         one,
         d2,
     )
+    tmine, chip, cross, acc = lax.optimization_barrier((tmine, chip, cross, acc))
+    tmine = (tmine + taken.astype(F32)).astype(BF16)
     tmine = across(tmine)
     mine, send, outer = call(
         functools.partial(conv_kernel, factor),

time: 55.9 us -> 58.4 us (1.045)
  starting transfers between devices: 15.3 us -> 17.7 us
    ppermute x7 -> x8, starting transfers between devices: 4.56 us -> 5.85 us  [swap(): return lax.ppermute(value, axis, [(i, i ^ bit) for i in range(n)])]
    ppermute x7 -> x8, waiting for transfers between devices: 6.9 us -> 8.16 us  [swap(): return lax.ppermute(value, axis, [(i, i ^ bit) for i in range(n)])]
    ppermute x6, waiting for transfers between devices: 10.5 us -> 9.28 us  [rotate(): return lax.ppermute(value, axis, [(i, (i + step) % n) for i in range(n)])]
    ppermute x6, starting transfers between devices: 10.1 us -> 11.2 us  [rotate(): return lax.ppermute(value, axis, [(i, (i + step) % n) for i in range(n)])]
  transfers between devices with their start and end apart: 14 -> 15, of which waited for: 7 -> 5; matrix products, arithmetic and copies ran while one was open for 0% -> 0% of each run, Pallas kernels for 27% -> 25%
where the time goes in v10:
time: 58.4 us; the launch traced here: 58 us
  Pallas kernels  17.9 us (31%)
  starting transfers between devices  17.7 us (30%)
  waiting for transfers between devices  17.4 us (30%)
  local copies, waits for them, and re-layouts  3.76 us (6%)
  between operations  0.81 us (1%)
    pallas_call x9, Pallas kernels, call(): pl.pallas_call(kernel, out_shape=out_shape, in_specs=spec, out_specs=jax....  17.9 us
    ppermute x6, starting transfers between devices, rotate(): return lax.ppermute(value, axis, [(i, (i + step) % n) for i in range(n)])  11.2 us
    ppermute x6, waiting for transfers between devices, rotate(): return lax.ppermute(value, axis, [(i, (i + step) % n) for i in range(n)])  9.28 us
    ppermute x8, waiting for transfers between devices, swap(): return lax.ppermute(value, axis, [(i, i ^ bit) for i in range(n)])  8.16 us
    ppermute x8, starting transfers between devices, swap(): return lax.ppermute(value, axis, [(i, i ^ bit) for i in range(n)])  5.85 us
    unnamed x12, local copies, waits for them, and re-layouts  3.76 us
  transfers between devices with their start and end apart: 15, of which 5 were waited for; matrix products, arithmetic and copies ran while one was open for 0% of the time, Pallas kernels for 25%

profile of v10, /device:TPU:0, one launch (start us, length us, event | category | flops | bytes accessed | tf_op | source)
XLA Modules:
  0.0 58.0 jit_solution(6568086541818365397)
XLA Ops:
  0.6 1.7 %shard_map.111 = (bf16[768,128]{1,0:T(8,128)(2,1)}, bf16[256,128]{1,0:T(8,128)(2,1)}) custom-call(bf16[8,4,8,128]{3,2,1,0:T(8,128)(2,1)} %og.1, bf16[4,8,1024]{2,1,0:T(8,128)(2,1)} %two.1, bf16[4,8,1024]{2,1,0:T(8,128)(2,1)} %one.1, bf16[4,8,1024]{2,1,0:T(8,128)(2,1)} %act.1), custom_call_target="tpu_custom_call" | custom-call | tf_op jit(solution)/shard_map/pallas_call | solution.py:200
  2.3 5.1 %collective-permute-start.2 = (bf16[768,128]{1,0:T(8,128)(2,1)}, bf16[768,128]{1,0:T(8,128)(2,1)S(1)}, u32[]{:S(2)}, u32[]{:S(2)}) collective-permute-start(bf16[768,128]{1,0:T(8,128)(2,1)} %get-tuple-element.40.a0), channel_id=1, source_target_pairs={{0,12},{4,0},{8,4},{12,8},{1,13},{5,1},{9,5},{13,9},{2,14},{6,2},{... | collective-permute-start | bytes 589832 | tf_op jit(solution)/shard_map/ppermute | solution.py:495
  7.4 0.0 collective-permute-start.1
  7.4 1.0 %collective-permute-start = (bf16[768,128]{1,0:T(8,128)(2,1)}, bf16[768,128]{1,0:T(8,128)(2,1)S(1)}, u32[]{:S(2)}, u32[]{:S(2)}) collective-permute-start(bf16[768,128]{1,0:T(8,128)(2,1)} %get-tuple-element.40.a0), channel_id=1, source_target_pairs={{0,4},{4,8},{8,12},{12,0},{1,5},{5,9},{9,13},{13,1},{2,6},{6,10},{... | collective-permute-start | bytes 589832 | tf_op jit(solution)/shard_map/ppermute | solution.py:495
  8.4 2.8 %collective-permute-start.7 = (bf16[256,128]{1,0:T(8,128)(2,1)}, bf16[256,128]{1,0:T(8,128)(2,1)S(1)}, u32[]{:S(2)}, u32[]{:S(2)}) collective-permute-start(bf16[256,128]{1,0:T(8,128)(2,1)} %get-tuple-element.54.i0), channel_id=1, source_target_pairs={{0,12},{4,0},{8,4},{12,8},{1,13},{5,1},{9,5},{13,9},{2,14},{6,2},{... | collective-permute-start | bytes 196616 | tf_op jit(solution)/shard_map/ppermute | solution.py:495
  11.2 1.1 %collective-permute-start.6 = (bf16[256,128]{1,0:T(8,128)(2,1)}, bf16[256,128]{1,0:T(8,128)(2,1)S(1)}, u32[]{:S(2)}, u32[]{:S(2)}) collective-permute-start(bf16[256,128]{1,0:T(8,128)(2,1)} %get-tuple-element.54.i0), channel_id=1, source_target_pairs={{0,8},{4,12},{8,0},{12,4},{1,9},{5,13},{9,1},{13,5},{2,10},{6,14},... | collective-permute-start | bytes 196616 | tf_op jit(solution)/shard_map/ppermute | solution.py:495
  12.4 0.7 %collective-permute-done.2.a3 = bf16[768,128]{1,0:T(8,128)(2,1)S(1)} collective-permute-done((bf16[768,128]{1,0:T(8,128)(2,1)}, bf16[768,128]{1,0:T(8,128)(2,1)S(1)}, u32[]{:S(2)}, u32[]{:S(2)}) %collective-permute-start.2) | collective-permute-done | bytes 196640 | tf_op jit(solution)/shard_map/ppermute | solution.py:495
  13.1 1.2 %collective-permute-start.5 = (bf16[256,128]{1,0:T(8,128)(2,1)}, bf16[256,128]{1,0:T(8,128)(2,1)S(1)}, u32[]{:S(2)}, u32[]{:S(2)}) collective-permute-start(bf16[256,128]{1,0:T(8,128)(2,1)} %get-tuple-element.54.i0), channel_id=1, source_target_pairs={{0,4},{4,8},{8,12},{12,0},{1,5},{5,9},{9,13},{13,1},{2,6},{6,10},{... | collective-permute-start | bytes 196616 | tf_op jit(solution)/shard_map/ppermute | solution.py:495
  14.2 0.1 pad_add_fusion.at_ref
  14.3 1.0 %copy-done = bf16[512,512]{1,0:T(8,128)(2,1)S(1)} copy-done((bf16[512,512]{1,0:T(8,128)(2,1)S(1)}, bf16[512,512]{1,0:T(8,128)(2,1)}, u32[]{:S(2)}) %copy-start) | copy-done | bytes 524312
  15.4 1.0 %copy-done.1 = bf16[27,64,64]{2,1,0:T(8,128)(2,1)S(1)} copy-done((bf16[27,64,64]{2,1,0:T(8,128)(2,1)S(1)}, bf16[27,64,64]{2,1,0:T(8,128)(2,1)}, u32[]{:S(2)}) %copy-start.1) | copy-done | bytes 221208
  16.4 1.0 %copy-done.2 = bf16[27,64,64]{2,1,0:T(8,128)(2,1)S(1)} copy-done((bf16[27,64,64]{2,1,0:T(8,128)(2,1)S(1)}, bf16[27,64,64]{2,1,0:T(8,128)(2,1)}, u32[]{:S(2)}) %copy-start.2) | copy-done | bytes 221208
  17.4 0.7 %copy-done.5 = s32[8,8]{1,0:T(8,128)S(1)} copy-done((s32[8,8]{1,0:T(8,128)S(1)}, s32[8,8]{1,0:T(8,128)}, u32[]{:S(2)}) %copy-start.5) | copy-done | bytes 280
  18.1 1.4 %shard_map.112 = (bf16[512,512]{1,0:T(8,128)(2,1)S(1)}, bf16[512,512]{1,0:T(8,128)(2,1)S(1)}, bf16[9,128,384]{2,1,0:T(8,128)(2,1)S(1)}, bf16[9,128,384]{2,1,0:T(8,128)(2,1)S(1)}) custom-call(bf16[512,512]{1,0:T(8,128)(2,1)S(1)} %copy-done, s32[8,8]{1,0:T(8,128)S(1)} %copy-done.5, bf16[27,64,64]{2,1,0:T(8,128)(2,1)S(1)} %copy-done.1, ...), custom_call_target="tpu_custom_call" | custom-call | flops 10000000 | bytes 966912 | tf_op jit(solution)/shard_map/pallas_call | solution.py:200
  19.5 8.6 %collective-permute-done.1.a2 = bf16[768,128]{1,0:T(8,128)(2,1)S(1)} collective-permute-done((bf16[768,128]{1,0:T(8,128)(2,1)}, bf16[768,128]{1,0:T(8,128)(2,1)S(1)}, u32[]{:S(2)}, u32[]{:S(2)}) %collective-permute-start.1) | collective-permute-done | bytes 196640 | tf_op jit(solution)/shard_map/ppermute | solution.py:495
  28.1 0.0 collective-permute-done.a1
  28.1 1.3 %shard_map.113 = (bf16[8,2,64,128]{3,2,1,0:T(8,128)(2,1)S(1)}, bf16[16,64,128]{2,1,0:T(8,128)(2,1)S(1)}, bf16[8,2,48,128]{3,2,1,0:T(8,128)(2,1)S(1)}, bf16[8,2,4...) custom-call(s32[2]{0:T(128)S(1)} %pad_add_fusion.at_ref, ...), custom_call_target="tpu_custom_call" | custom-call | flops 268435456 | bytes 1835016 | tf_op jit(solution)/shard_map/pallas_call | solution.py:200
  29.4 0.1 collective-permute-start.3
  29.5 0.7 %collective-permute-start.4 = (bf16[8,2,48,128]{3,2,1,0:T(8,128)(2,1)S(1)}, bf16[8,2,48,128]{3,2,1,0:T(8,128)(2,1)S(1)}, u32[]{:S(2)}, u32[]{:S(2)}) collective-permute-start(bf16[8,2,48,128]{3,2,1,0:T(8,128)(2,1)S(1)} %get-tuple-element.45), channel_id=1, source_target_pairs={{1,2},{2,1},{5,6},{6,5},{9,10},{10,9},{13,14},{14,13},{17,18},{18,... | collective-permute-start | bytes 589832 | tf_op jit(solution)/shard_map/ppermute | solution.py:574
  30.2 0.0 collective-permute-done.7.i3
  30.2 0.0 collective-permute-done.6.i2
  30.2 0.0 collective-permute-done.5.i1
  30.2 2.9 %collective-permute-start.8 = (bf16[512,128]{1,0:T(8,128)(2,1)S(1)}, bf16[512,128]{1,0:T(8,128)(2,1)S(1)}, u32[]{:S(2)}, u32[]{:S(2)}) collective-permute-start(bf16[512,128]{1,0:T(8,128)(2,1)S(1)} %get-tuple-element.63), channel_id=1, source_target_pairs={{0,1},{1,0},{2,3},{3,2},{4,5},{5,4},{6,7},{7,6},{8,9},{9,8},{10,11... | collective-permute-start | bytes 393224 | tf_op jit(solution)/shard_map/ppermute | solution.py:500
  33.1 0.1 collective-permute-start.9
  33.2 3.0 %shard_map.114 = (f32[16,96,128]{2,1,0:T(8,128)S(1)}, f32[896,128]{1,0:T(8,128)S(1)}) custom-call(bf16[16,64,128]{2,1,0:T(8,128)(2,1)S(1)} %bitcast.7, bf16[16,64,128]{2,1,0:T(8,128)(2,1)S(1)} %get-tuple-element.47.one_ref, bf16[9,128,384]{2,1,0:T(8,128)(2,1)S(1)} %get-tuple-element.48.w_ref), custom_call_target="tpu_custom_call" | custom-call | flops 1811939328 | bytes 1409024 | tf_op jit(solution)/shard_map/pallas_call | solution.py:200
  36.2 0.0 collective-permute-done.3
  36.2 0.0 collective-permute-done.4
  36.3 0.0 collective-permute-done.8
  36.3 0.0 collective-permute-done.9
  36.3 0.1 add_convert_fusion
  36.3 1.8 %collective-permute-start.10 = (bf16[1024,128]{1,0:T(8,128)(2,1)S(1)}, bf16[1024,128]{1,0:T(8,128)(2,1)S(1)}, u32[]{:S(2)}, u32[]{:S(2)}) collective-permute-start(bf16[1024,128]{1,0:T(8,128)(2,1)S(1)} %add_convert_fusion), channel_id=1, source_target_pairs={{0,2},{1,3},{2,0},{3,1},{4,6},{5,7},{6,4},{7,5},{8,10},{9,11},{10,... | collective-permute-start | bytes 786440 | tf_op jit(solution)/shard_map/ppermute | solution.py:500
  38.1 3.8 %shard_map.115 = (f32[896,128]{1,0:T(8,128)S(1)}, bf16[896,128]{1,0:T(8,128)(2,1)S(1)}, bf16[20,96,384]{2,1,0:T(8,128)(2,1)S(1)}) custom-call(s32[2]{0:T(128)S(1)} %pad_add_fusion.at_ref, f32[16,96,128]{2,1,0:T(8,128)S(1)} %get-tuple-element.50.acc_ref, f32[896,128]{1,0:T(8,128)S(1)} %get-tuple-element.51.sums_ref, ...), custom_call_target="tpu_custom_call" | custom-call | flops 796262400 | bytes 3047432 | tf_op jit(solution)/shard_map/pallas_call | solution.py:200
  42.0 3.3 %collective-permute-done.10 = bf16[1024,128]{1,0:T(8,128)(2,1)S(1)} collective-permute-done((bf16[1024,128]{1,0:T(8,128)(2,1)S(1)}, bf16[1024,128]{1,0:T(8,128)(2,1)S(1)}, u32[]{:S(2)}, u32[]{:S(2)}) %collective-permute-start.10) | collective-permute-done | bytes 262176 | tf_op jit(solution)/shard_map/ppermute | solution.py:500
  45.3 0.1 convert_add_fusion.mine_ref
  45.4 0.1 collective-permute-start.11
  45.4 0.5 collective-permute-start.13
  45.9 1.0 %collective-permute-done.11 = bf16[896,128]{1,0:T(8,128)(2,1)S(1)} collective-permute-done((bf16[896,128]{1,0:T(8,128)(2,1)S(1)}, bf16[896,128]{1,0:T(8,128)(2,1)S(1)}, u32[]{:S(2)}, u32[]{:S(2)}) %collective-permute-start.11) | collective-permute-done | bytes 229408 | tf_op jit(solution)/shard_map/ppermute | solution.py:500
  46.9 0.1 add_convert_fusion.2
  47.0 0.4 collective-permute-start.12
  47.4 1.8 %shard_map.117 = bf16[4,8,1024]{2,1,0:T(8,128)(2,1)} custom-call(s32[2]{0:T(128)S(1)} %pad_add_fusion.at_ref, bf16[20,96,384]{2,1,0:T(8,128)(2,1)S(1)} %get-tuple-element.67.outer_ref, bf16[9,128,384]{2,1,0:T(8,128)(2,1)S(1)} %get-tuple-element.68.w_ref), custom_call_target="tpu_custom_call" | custom-call | flops 226492416 | bytes 2359304 | tf_op jit(solution)/shard_map/pallas_call | solution.py:200
  49.2 0.0 collective-permute-done.13.other_ref
  49.2 1.6 %shard_map.116 = f32[512,512]{1,0:T(8,128)} custom-call(s32[2]{0:T(128)S(1)} %pad_add_fusion.at_ref, f32[1024,128]{1,0:T(8,128)S(1)} %convert_add_fusion.mine_ref, f32[1024,128]{1,0:T(8,128)S(1)} %collective-permute-done.13.other_ref), custom_call_target="tpu_custom_call" | custom-call | flops 10000000 | bytes 1048584 | tf_op jit(solution)/shard_map/pallas_call | solution.py:200
  50.9 3.8 %collective-permute-done.12 = bf16[896,128]{1,0:T(8,128)(2,1)S(1)} collective-permute-done((bf16[896,128]{1,0:T(8,128)(2,1)S(1)}, bf16[896,128]{1,0:T(8,128)(2,1)S(1)}, u32[]{:S(2)}, u32[]{:S(2)}) %collective-permute-start.12) | collective-permute-done | bytes 229408 | tf_op jit(solution)/shard_map/ppermute | solution.py:500
  54.7 0.1 add_convert_fusion.1.ref
  54.7 0.1 collective-permute-start.14
  54.8 1.6 %shard_map.118 = (f32[27,64,64]{2,1,0:T(8,128)}, f32[27,64,64]{2,1,0:T(8,128)}) custom-call(s32[2]{0:T(128)S(1)} %pad_add_fusion.at_ref, bf16[896,128]{1,0:T(8,128)(2,1)S(1)} %add_convert_fusion.1.ref), custom_call_target="tpu_custom_call" | custom-call | flops 100000000 | bytes 229384 | tf_op jit(solution)/shard_map/pallas_call | solution.py:200
  56.4 0.0 collective-permute-done.14.ref
  56.4 1.6 %shard_map.119 = (f32[27,64,64]{2,1,0:T(8,128)}, f32[27,64,64]{2,1,0:T(8,128)}) custom-call(s32[2]{0:T(128)S(1)} %pad_add_fusion.at_ref, bf16[896,128]{1,0:T(8,128)(2,1)S(1)} %collective-permute-done.14.ref, f32[27,64,64]{2,1,0:T(8,128)} %get-tuple-element.71.one_in, ...), custom_call_target="tpu_custom_call", output_to_operand_aliasing={{0}: (2, {}), {1}: (3, {})} | custom-call | tf_op jit(solution)/shard_map/pallas_call | solution.py:200
  (8 shorter events, 0.0 us)
Async XLA Ops:
  2.3 10.8 %collective-permute-start.2 = (bf16[768,128]{1,0:T(8,128)(2,1)}, bf16[768,128]{1,0:T(8,128)(2,1)S(1)}, u32[]{:S(2)}, u32[]{:S(2)}) collective-permute-start(bf16[768,128]{1,0:T(8,128)(2,1)} %get-tuple-element.40.a0), channel_id=1, source_target_pairs={{0,12},{4,0},{8,4},{12,8},{1,13},{5,1},{9,5},{13,9},{2,14},{6,2},{... | collective-permute-start | bytes 589832 | tf_op jit(solution)/shard_map/ppermute | solution.py:495
  7.4 20.6 %collective-permute-start.1 = (bf16[768,128]{1,0:T(8,128)(2,1)}, bf16[768,128]{1,0:T(8,128)(2,1)S(1)}, u32[]{:S(2)}, u32[]{:S(2)}) collective-permute-start(bf16[768,128]{1,0:T(8,128)(2,1)} %get-tuple-element.40.a0), channel_id=1, source_target_pairs={{0,8},{4,12},{8,0},{12,4},{1,9},{5,13},{9,1},{13,5},{2,10},{6,14},... | collective-permute-start | bytes 589832 | tf_op jit(solution)/shard_map/ppermute | solution.py:495
  7.4 20.6 %collective-permute-start = (bf16[768,128]{1,0:T(8,128)(2,1)}, bf16[768,128]{1,0:T(8,128)(2,1)S(1)}, u32[]{:S(2)}, u32[]{:S(2)}) collective-permute-start(bf16[768,128]{1,0:T(8,128)(2,1)} %get-tuple-element.40.a0), channel_id=1, source_target_pairs={{0,4},{4,8},{8,12},{12,0},{1,5},{5,9},{9,13},{13,1},{2,6},{6,10},{... | collective-permute-start | bytes 589832 | tf_op jit(solution)/shard_map/ppermute | solution.py:495
  8.4 21.7 %collective-permute-start.7 = (bf16[256,128]{1,0:T(8,128)(2,1)}, bf16[256,128]{1,0:T(8,128)(2,1)S(1)}, u32[]{:S(2)}, u32[]{:S(2)}) collective-permute-start(bf16[256,128]{1,0:T(8,128)(2,1)} %get-tuple-element.54.i0), channel_id=1, source_target_pairs={{0,12},{4,0},{8,4},{12,8},{1,13},{5,1},{9,5},{13,9},{2,14},{6,2},{... | collective-permute-start | bytes 196616 | tf_op jit(solution)/shard_map/ppermute | solution.py:495
  11.2 18.9 %collective-permute-start.6 = (bf16[256,128]{1,0:T(8,128)(2,1)}, bf16[256,128]{1,0:T(8,128)(2,1)S(1)}, u32[]{:S(2)}, u32[]{:S(2)}) collective-permute-start(bf16[256,128]{1,0:T(8,128)(2,1)} %get-tuple-element.54.i0), channel_id=1, source_target_pairs={{0,8},{4,12},{8,0},{12,4},{1,9},{5,13},{9,1},{13,5},{2,10},{6,14},... | collective-permute-start | bytes 196616 | tf_op jit(solution)/shard_map/ppermute | solution.py:495
  13.1 17.1 %collective-permute-start.5 = (bf16[256,128]{1,0:T(8,128)(2,1)}, bf16[256,128]{1,0:T(8,128)(2,1)S(1)}, u32[]{:S(2)}, u32[]{:S(2)}) collective-permute-start(bf16[256,128]{1,0:T(8,128)(2,1)} %get-tuple-element.54.i0), channel_id=1, source_target_pairs={{0,4},{4,8},{8,12},{12,0},{1,5},{5,9},{9,13},{13,1},{2,6},{6,10},{... | collective-permute-start | bytes 196616 | tf_op jit(solution)/shard_map/ppermute | solution.py:495
  14.3 1.0 %copy-start = (bf16[512,512]{1,0:T(8,128)(2,1)S(1)}, bf16[512,512]{1,0:T(8,128)(2,1)}, u32[]{:S(2)}) copy-start(bf16[512,512]{1,0:T(8,128)(2,1)} %wt.1) | copy-start | bytes 1572868
  15.4 1.0 %copy-start.1 = (bf16[27,64,64]{2,1,0:T(8,128)(2,1)S(1)}, bf16[27,64,64]{2,1,0:T(8,128)(2,1)}, u32[]{:S(2)}) copy-start(bf16[27,64,64]{2,1,0:T(8,128)(2,1)} %w2.1) | copy-start | bytes 663556
  16.4 1.0 %copy-start.2 = (bf16[27,64,64]{2,1,0:T(8,128)(2,1)S(1)}, bf16[27,64,64]{2,1,0:T(8,128)(2,1)}, u32[]{:S(2)}) copy-start(bf16[27,64,64]{2,1,0:T(8,128)(2,1)} %w1.1) | copy-start | bytes 663556
  17.4 0.7 %copy-start.5 = (s32[8,8]{1,0:T(8,128)S(1)}, s32[8,8]{1,0:T(8,128)}, u32[]{:S(2)}) copy-start(s32[8,8]{1,0:T(8,128)} %keep.1) | copy-start | bytes 772
  18.1 10.0 %copy-start.3 = (bf16[768,128]{1,0:T(8,128)(2,1)S(1)}, bf16[768,128]{1,0:T(8,128)(2,1)}, u32[]{:S(2)}) copy-start(bf16[768,128]{1,0:T(8,128)(2,1)} %get-tuple-element.40.a0) | copy-start | bytes 589828
  29.4 6.8 %collective-permute-start.3 = (bf16[8,2,48,128]{3,2,1,0:T(8,128)(2,1)S(1)}, bf16[8,2,48,128]{3,2,1,0:T(8,128)(2,1)S(1)}, u32[]{:S(2)}, u32[]{:S(2)}) collective-permute-start(bf16[8,2,48,128]{3,2,1,0:T(8,128)(2,1)S(1)} %get-tuple-element.44), channel_id=1, source_target_pairs={{0,1},{1,0},{2,3},{3,2},{4,5},{5,4},{6,7},{7,6},{8,9},{9,8},{10,11... | collective-permute-start | bytes 589832 | tf_op jit(solution)/shard_map/ppermute | solution.py:500
  29.5 6.8 %collective-permute-start.4 = (bf16[8,2,48,128]{3,2,1,0:T(8,128)(2,1)S(1)}, bf16[8,2,48,128]{3,2,1,0:T(8,128)(2,1)S(1)}, u32[]{:S(2)}, u32[]{:S(2)}) collective-permute-start(bf16[8,2,48,128]{3,2,1,0:T(8,128)(2,1)S(1)} %get-tuple-element.45), channel_id=1, source_target_pairs={{1,2},{2,1},{5,6},{6,5},{9,10},{10,9},{13,14},{14,13},{17,18},{18,... | collective-permute-start | bytes 589832 | tf_op jit(solution)/shard_map/ppermute | solution.py:574
  30.2 6.1 %collective-permute-start.8 = (bf16[512,128]{1,0:T(8,128)(2,1)S(1)}, bf16[512,128]{1,0:T(8,128)(2,1)S(1)}, u32[]{:S(2)}, u32[]{:S(2)}) collective-permute-start(bf16[512,128]{1,0:T(8,128)(2,1)S(1)} %get-tuple-element.63), channel_id=1, source_target_pairs={{0,1},{1,0},{2,3},{3,2},{4,5},{5,4},{6,7},{7,6},{8,9},{9,8},{10,11... | collective-permute-start | bytes 393224 | tf_op jit(solution)/shard_map/ppermute | solution.py:500
  33.1 3.2 %collective-permute-start.9 = (bf16[512,128]{1,0:T(8,128)(2,1)S(1)}, bf16[512,128]{1,0:T(8,128)(2,1)S(1)}, u32[]{:S(2)}, u32[]{:S(2)}) collective-permute-start(bf16[512,128]{1,0:T(8,128)(2,1)S(1)} %get-tuple-element.64), channel_id=1, source_target_pairs={{0,1},{1,0},{2,3},{3,2},{4,5},{5,4},{6,7},{7,6},{8,9},{9,8},{10,11... | collective-permute-start | bytes 393224 | tf_op jit(solution)/shard_map/ppermute | solution.py:500
  33.2 4.9 %copy-start.4 = (bf16[256,128]{1,0:T(8,128)(2,1)S(1)}, bf16[256,128]{1,0:T(8,128)(2,1)}, u32[]{:S(2)}) copy-start(bf16[256,128]{1,0:T(8,128)(2,1)} %get-tuple-element.54.i0) | copy-start | bytes 196612
  36.3 9.0 %collective-permute-start.10 = (bf16[1024,128]{1,0:T(8,128)(2,1)S(1)}, bf16[1024,128]{1,0:T(8,128)(2,1)S(1)}, u32[]{:S(2)}, u32[]{:S(2)}) collective-permute-start(bf16[1024,128]{1,0:T(8,128)(2,1)S(1)} %add_convert_fusion), channel_id=1, source_target_pairs={{0,2},{1,3},{2,0},{3,1},{4,6},{5,7},{6,4},{7,5},{8,10},{9,11},{10,... | collective-permute-start | bytes 786440 | tf_op jit(solution)/shard_map/ppermute | solution.py:500
  45.4 1.6 %collective-permute-start.11 = (bf16[896,128]{1,0:T(8,128)(2,1)S(1)}, bf16[896,128]{1,0:T(8,128)(2,1)S(1)}, u32[]{:S(2)}, u32[]{:S(2)}) collective-permute-start(bf16[896,128]{1,0:T(8,128)(2,1)S(1)} %get-tuple-element.65), channel_id=1, source_target_pairs={{0,1},{1,0},{2,3},{3,2},{4,5},{5,4},{6,7},{7,6},{8,9},{9,8},{10,11... | collective-permute-start | bytes 688136 | tf_op jit(solution)/shard_map/ppermute | solution.py:500
  45.4 3.8 %collective-permute-start.13 = (f32[1024,128]{1,0:T(8,128)S(1)}, f32[1024,128]{1,0:T(8,128)S(1)}, u32[]{:S(2)}, u32[]{:S(2)}) collective-permute-start(f32[1024,128]{1,0:T(8,128)S(1)} %convert_add_fusion.mine_ref), channel_id=1, source_target_pairs={{0,1},{1,0},{2,3},{3,2},{4,5},{5,4},{6,7},{7,6},{8,9},{9,8},{10,11... | collective-permute-start | bytes 1572872 | tf_op jit(solution)/shard_map/ppermute | solution.py:500
  47.0 7.7 %collective-permute-start.12 = (bf16[896,128]{1,0:T(8,128)(2,1)S(1)}, bf16[896,128]{1,0:T(8,128)(2,1)S(1)}, u32[]{:S(2)}, u32[]{:S(2)}) collective-permute-start(bf16[896,128]{1,0:T(8,128)(2,1)S(1)} %add_convert_fusion.2), channel_id=1, source_target_pairs={{0,2},{1,3},{2,0},{3,1},{4,6},{5,7},{6,4},{7,5},{8,10},{9,11},{10,... | collective-permute-start | bytes 688136 | tf_op jit(solution)/shard_map/ppermute | solution.py:500
  54.7 1.7 %collective-permute-start.14 = (bf16[896,128]{1,0:T(8,128)(2,1)S(1)}, bf16[896,128]{1,0:T(8,128)(2,1)S(1)}, u32[]{:S(2)}, u32[]{:S(2)}) collective-permute-start(bf16[896,128]{1,0:T(8,128)(2,1)S(1)} %add_convert_fusion.1.ref), channel_id=1, source_target_pairs={{0,1},{1,0},{2,3},{3,2},{4,5},{5,4},{6,7},{7,6},{8,9},{9,8},{10,11... | collective-permute-start | bytes 688136 | tf_op jit(solution)/shard_map/ppermute | solution.py:500

commit v11 on v9

--- a/solution.py
+++ b/solution.py
@@ -220,16 +220,16 @@
     return copies
 
 
-def pack_kernel(og, two, one, act, first_ref, second_ref, og_v, two_v, one_v, act_v, turn_ref, sems):
+def pack_kernel(og, two, one, act, first_ref, og_v, two_v, one_v, act_v, turn_ref, sems):
     copies = fetch(((og, og_v), (two, two_v), (one, one_v), (act, act_v)), sems)
     copies[0].wait()
     first_ref[0:256] = og_v[...].astype(F32).reshape(256, 128).astype(BF16)
-    for k, (ref, out, at) in enumerate(((two_v, first_ref, 256), (one_v, first_ref, 512), (act_v, second_ref, 0))):
+    for k, (ref, at) in enumerate(((two_v, 256), (one_v, 512), (act_v, 768))):
         copies[k + 1].wait()
         for x in range(4):
             for t in range(8):
                 turn_ref[k, pl.ds(64 * x + t, 8, stride=8), :] = ref[x, :, 128 * t : 128 * t + 128].astype(F32)
-        out[at : at + 256] = turn_ref[k].astype(BF16)
+        first_ref[at : at + 256] = turn_ref[k].astype(BF16)
 
 
 def weight_kernel(wt, keep, w2, w1, kept_ref, mask_ref, d2_ref, d1_ref, wt_v, keep_v, w2_v, w1_v, sems):
@@ -387,7 +387,7 @@
     parts = (i0, i1, i2, i3)
     n = len(parts)
     for s, part in enumerate(parts):
-        in_ref[pl.ds(lax.rem(me + n - s, n) * 4, 4)] = part[...].reshape(4, 64, 128)
+        in_ref[pl.ds(lax.rem(me + n - s, n) * 4, 4)] = part[768:1024].reshape(4, 64, 128)
 
     def put(side, ref):
         rim_ref[side] = ref[...]
@@ -514,9 +514,9 @@
     shape = jax.ShapeDtypeStruct
     vmem = pltpu.VMEM
     natural = vmem((4, 8, 1024), BF16)
-    first, second = call(
+    first = call(
         pack_kernel,
-        (shape((768, 128), BF16), shape((256, 128), BF16)),
+        shape((1024, 128), BF16),
         [
             vmem((8, 4, 8, 128), BF16), natural, natural, natural, vmem((3, 256, 128), F32),
             pltpu.SemaphoreType.DMA((4,)),
@@ -529,7 +529,6 @@
         (input_activation,),
     )
     firsts = [first] + [rotate(first, "gx", s) for s in (1, 2, 3)]
-    seconds = [second] + [rotate(second, "gx", s) for s in (1, 2, 3)]
     kept, mask, d2, d1 = call(
         weight_kernel,
         (
@@ -570,7 +569,6 @@
     pairs = [(i, i + 1) for i in range(1, n - 1, 2)]
     cross = lax.ppermute(cross, "gy", pairs + [(j, i) for i, j in pairs])
     chip = swap(chip, "gy", 1)
-    tsend, *seconds = lax.optimization_barrier((tsend, *seconds))
     tmine = on_chip(tmine, tsend)
     one, tmine = lax.optimization_barrier((one, tmine))
     acc, sums = call(
@@ -603,7 +601,7 @@
         chip.reshape(16, 48, 128),
         cross.reshape(16, 48, 128),
         d2,
-        *seconds,
+        *firsts,
     )
     send, tmine = lax.optimization_barrier((send, tmine))
     mine = on_chip(mine, send)

time: 55.9 us -> 56.9 us (1.018)
  the two profiles are of different devices: /device:TPU:0 before, /device:TPU:9 now
where the time goes in v11:
time: 56.9 us; the launch traced here: 56.6 us
  waiting for transfers between devices  22.4 us (39%)
  Pallas kernels  17.9 us (31%)
  starting transfers between devices  11.4 us (20%)
  local copies, waits for them, and re-layouts  3.76 us (7%)
  between operations  0.76 us (1%)
    pallas_call x9, Pallas kernels, call(): pl.pallas_call(kernel, out_shape=out_shape, in_specs=spec, out_specs=jax....  17.9 us
    ppermute x3, waiting for transfers between devices, rotate(): return lax.ppermute(value, axis, [(i, (i + step) % n) for i in range(n)])  17.2 us
    ppermute x7, starting transfers between devices, swap(): return lax.ppermute(value, axis, [(i, i ^ bit) for i in range(n)])  4.21 us
    ppermute x7, waiting for transfers between devices, swap(): return lax.ppermute(value, axis, [(i, i ^ bit) for i in range(n)])  3.88 us
    ppermute x3, starting transfers between devices, rotate(): return lax.ppermute(value, axis, [(i, (i + step) % n) for i in range(n)])  3.83 us
    unnamed x10, local copies, waits for them, and re-layouts  3.76 us
    ppermute x1, starting transfers between devices, slab_body(): cross = lax.ppermute(cross, 'gy', pairs + [(j, i) for i, j in pairs])  3.41 us
    ppermute x1, waiting for transfers between devices, slab_body(): cross = lax.ppermute(cross, 'gy', pairs + [(j, i) for i, j in pairs])  1.38 us
  transfers between devices with their start and end apart: 11, of which 6 were waited for; matrix products, arithmetic and copies ran while one was open for 0% of the time, Pallas kernels for 23%

profile of v11, /device:TPU:9, one launch (start us, length us, event | category | flops | bytes accessed | tf_op | source)
XLA Modules:
  0.0 56.6 jit_solution(15352927386049324767)
XLA Ops:
  0.6 1.7 %shard_map.111.a0.i0 = bf16[1024,128]{1,0:T(8,128)(2,1)} custom-call(bf16[8,4,8,128]{3,2,1,0:T(8,128)(2,1)} %og.1, bf16[4,8,1024]{2,1,0:T(8,128)(2,1)} %two.1, bf16[4,8,1024]{2,1,0:T(8,128)(2,1)} %one.1, bf16[4,8,1024]{2,1,0:T(8,128)(2,1)} %act.1), custom_call_target="tpu_custom_call" | custom-call | tf_op jit(solution)/shard_map/pallas_call | solution.py:200
  2.3 0.0 copy-start
  2.3 1.3 %collective-permute-start = (bf16[1024,128]{1,0:T(8,128)(2,1)}, bf16[1024,128]{1,0:T(8,128)(2,1)S(1)}, u32[]{:S(2)}, u32[]{:S(2)}) collective-permute-start(bf16[1024,128]{1,0:T(8,128)(2,1)} %shard_map.111.a0.i0), channel_id=1, source_target_pairs={{0,4},{4,8},{8,12},{12,0},{1,5},{5,9},{9,13},{13,1},{2,6},{6,10},{... | collective-permute-start | bytes 786440 | tf_op jit(solution)/shard_map/ppermute | solution.py:493
  3.7 1.1 %collective-permute-start.1 = (bf16[1024,128]{1,0:T(8,128)(2,1)}, bf16[1024,128]{1,0:T(8,128)(2,1)S(1)}, u32[]{:S(2)}, u32[]{:S(2)}) collective-permute-start(bf16[1024,128]{1,0:T(8,128)(2,1)} %shard_map.111.a0.i0), channel_id=1, source_target_pairs={{0,8},{4,12},{8,0},{12,4},{1,9},{5,13},{9,1},{13,5},{2,10},{6,14},... | collective-permute-start | bytes 786440 | tf_op jit(solution)/shard_map/ppermute | solution.py:493
  4.8 1.4 %collective-permute-start.2 = (bf16[1024,128]{1,0:T(8,128)(2,1)}, bf16[1024,128]{1,0:T(8,128)(2,1)S(1)}, u32[]{:S(2)}, u32[]{:S(2)}) collective-permute-start(bf16[1024,128]{1,0:T(8,128)(2,1)} %shard_map.111.a0.i0), channel_id=1, source_target_pairs={{0,12},{4,0},{8,4},{12,8},{1,13},{5,1},{9,5},{13,9},{2,14},{6,2},{... | collective-permute-start | bytes 786440 | tf_op jit(solution)/shard_map/ppermute | solution.py:493
  6.2 0.0 copy-start.1
  6.2 1.0 %copy-done.1 = bf16[512,512]{1,0:T(8,128)(2,1)S(1)} copy-done((bf16[512,512]{1,0:T(8,128)(2,1)S(1)}, bf16[512,512]{1,0:T(8,128)(2,1)}, u32[]{:S(2)}) %copy-start.1) | copy-done | bytes 524312
  7.2 0.0 copy-start.2
  7.2 1.0 %copy-done.2 = bf16[27,64,64]{2,1,0:T(8,128)(2,1)S(1)} copy-done((bf16[27,64,64]{2,1,0:T(8,128)(2,1)S(1)}, bf16[27,64,64]{2,1,0:T(8,128)(2,1)}, u32[]{:S(2)}) %copy-start.2) | copy-done | bytes 221208
  8.2 0.0 copy-start.3
  8.2 1.0 %copy-done.3 = bf16[27,64,64]{2,1,0:T(8,128)(2,1)S(1)} copy-done((bf16[27,64,64]{2,1,0:T(8,128)(2,1)S(1)}, bf16[27,64,64]{2,1,0:T(8,128)(2,1)}, u32[]{:S(2)}) %copy-start.3) | copy-done | bytes 221208
  9.2 0.0 copy-start.4
  9.2 0.7 %copy-done.4 = s32[8,8]{1,0:T(8,128)S(1)} copy-done((s32[8,8]{1,0:T(8,128)S(1)}, s32[8,8]{1,0:T(8,128)}, u32[]{:S(2)}) %copy-start.4) | copy-done | bytes 280
  9.9 1.4 %shard_map.112 = (bf16[512,512]{1,0:T(8,128)(2,1)S(1)}, bf16[512,512]{1,0:T(8,128)(2,1)S(1)}, bf16[9,128,384]{2,1,0:T(8,128)(2,1)S(1)}, bf16[9,128,384]{2,1,0:T(8,128)(2,1)S(1)}) custom-call(bf16[512,512]{1,0:T(8,128)(2,1)S(1)} %copy-done.1, s32[8,8]{1,0:T(8,128)S(1)} %copy-done.4, bf16[27,64,64]{2,1,0:T(8,128)(2,1)S(1)} %copy-done.2, ...), custom_call_target="tpu_custom_call" | custom-call | flops 10000000 | bytes 966912 | tf_op jit(solution)/shard_map/pallas_call | solution.py:200
  11.4 0.1 pad_add_fusion.at_ref
  11.4 0.0 collective-permute-done.a1.i1
  11.4 14.4 %collective-permute-done.1.a2.i2 = bf16[1024,128]{1,0:T(8,128)(2,1)S(1)} collective-permute-done((bf16[1024,128]{1,0:T(8,128)(2,1)}, bf16[1024,128]{1,0:T(8,128)(2,1)S(1)}, u32[]{:S(2)}, u32[]{:S(2)}) %collective-permute-start.1) | collective-permute-done | bytes 262176 | tf_op jit(solution)/shard_map/ppermute | solution.py:493
  25.8 2.8 %collective-permute-done.2.a3.i3 = bf16[1024,128]{1,0:T(8,128)(2,1)S(1)} collective-permute-done((bf16[1024,128]{1,0:T(8,128)(2,1)}, bf16[1024,128]{1,0:T(8,128)(2,1)S(1)}, u32[]{:S(2)}, u32[]{:S(2)}) %collective-permute-start.2) | collective-permute-done | bytes 262176 | tf_op jit(solution)/shard_map/ppermute | solution.py:493
  28.6 0.0 copy-done
  28.6 1.3 %shard_map.113 = (bf16[8,2,64,128]{3,2,1,0:T(8,128)(2,1)S(1)}, bf16[16,64,128]{2,1,0:T(8,128)(2,1)S(1)}, bf16[8,2,48,128]{3,2,1,0:T(8,128)(2,1)S(1)}, bf16[8,2,4...) custom-call(s32[2]{0:T(128)S(1)} %pad_add_fusion.at_ref, ...), custom_call_target="tpu_custom_call" | custom-call | flops 268435456 | bytes 2097160 | tf_op jit(solution)/shard_map/pallas_call | solution.py:200
  29.9 0.6 %collective-permute-start.3 = (bf16[1024,128]{1,0:T(8,128)(2,1)S(1)}, bf16[1024,128]{1,0:T(8,128)(2,1)S(1)}, u32[]{:S(2)}, u32[]{:S(2)}) collective-permute-start(bf16[1024,128]{1,0:T(8,128)(2,1)S(1)} %get-tuple-element.35), channel_id=1, source_target_pairs={{0,1},{1,0},{2,3},{3,2},{4,5},{5,4},{6,7},{7,6},{8,9},{9,8},{10,11... | collective-permute-start | bytes 786440 | tf_op jit(solution)/shard_map/ppermute | solution.py:498
  30.5 0.1 collective-permute-start.4
  30.6 3.4 %collective-permute-start.5 = (bf16[8,2,48,128]{3,2,1,0:T(8,128)(2,1)S(1)}, bf16[8,2,48,128]{3,2,1,0:T(8,128)(2,1)S(1)}, u32[]{:S(2)}, u32[]{:S(2)}) collective-permute-start(bf16[8,2,48,128]{3,2,1,0:T(8,128)(2,1)S(1)} %get-tuple-element.41), channel_id=1, source_target_pairs={{1,2},{2,1},{5,6},{6,5},{9,10},{10,9},{13,14},{14,13},{17,18},{18,... | collective-permute-start | bytes 589832 | tf_op jit(solution)/shard_map/ppermute | solution.py:570
  34.0 0.0 collective-permute-done.3
  34.0 0.1 add_convert_fusion
  34.1 0.1 collective-permute-start.6
  34.2 3.0 %shard_map.114 = (f32[16,96,128]{2,1,0:T(8,128)S(1)}, f32[896,128]{1,0:T(8,128)S(1)}) custom-call(bf16[16,64,128]{2,1,0:T(8,128)(2,1)S(1)} %bitcast.7, bf16[16,64,128]{2,1,0:T(8,128)(2,1)S(1)} %get-tuple-element.36.one_ref, bf16[9,128,384]{2,1,0:T(8,128)(2,1)S(1)} %get-tuple-element.37.w_ref), custom_call_target="tpu_custom_call" | custom-call | flops 1811939328 | bytes 1409024 | tf_op jit(solution)/shard_map/pallas_call | solution.py:200
  37.2 0.0 collective-permute-done.4
  37.2 1.4 %collective-permute-done.5 = bf16[8,2,48,128]{3,2,1,0:T(8,128)(2,1)S(1)} collective-permute-done((bf16[8,2,48,128]{3,2,1,0:T(8,128)(2,1)S(1)}, bf16[8,2,48,128]{3,2,1,0:T(8,128)(2,1)S(1)}, u32[]{:S(2)}, u32[]{:S(2)}) %collective-permute-start.5) | collective-permute-done | bytes 196640 | tf_op jit(solution)/shard_map/ppermute | solution.py:570
  38.6 3.8 %shard_map.115 = (f32[896,128]{1,0:T(8,128)S(1)}, bf16[896,128]{1,0:T(8,128)(2,1)S(1)}, bf16[20,96,384]{2,1,0:T(8,128)(2,1)S(1)}) custom-call(s32[2]{0:T(128)S(1)} %pad_add_fusion.at_ref, f32[16,96,128]{2,1,0:T(8,128)S(1)} %get-tuple-element.38.acc_ref, f32[896,128]{1,0:T(8,128)S(1)} %get-tuple-element.39.sums_ref, ...), custom_call_target="tpu_custom_call" | custom-call | flops 796262400 | bytes 3833864 | tf_op jit(solution)/shard_map/pallas_call | solution.py:200
  42.4 0.1 collective-permute-done.6
  42.5 0.1 convert_add_fusion.mine_ref
  42.5 1.5 %collective-permute-start.7 = (bf16[896,128]{1,0:T(8,128)(2,1)S(1)}, bf16[896,128]{1,0:T(8,128)(2,1)S(1)}, u32[]{:S(2)}, u32[]{:S(2)}) collective-permute-start(bf16[896,128]{1,0:T(8,128)(2,1)S(1)} %get-tuple-element.45), channel_id=1, source_target_pairs={{0,1},{1,0},{2,3},{3,2},{4,5},{5,4},{6,7},{7,6},{8,9},{9,8},{10,11... | collective-permute-start | bytes 688136 | tf_op jit(solution)/shard_map/ppermute | solution.py:498
  44.0 0.1 collective-permute-start.9
  44.1 1.0 %collective-permute-done.7 = bf16[896,128]{1,0:T(8,128)(2,1)S(1)} collective-permute-done((bf16[896,128]{1,0:T(8,128)(2,1)S(1)}, bf16[896,128]{1,0:T(8,128)(2,1)S(1)}, u32[]{:S(2)}, u32[]{:S(2)}) %collective-permute-start.7) | collective-permute-done | bytes 229408 | tf_op jit(solution)/shard_map/ppermute | solution.py:498
  45.2 0.7 %collective-permute-start.8 = (bf16[896,128]{1,0:T(8,128)(2,1)S(1)}, bf16[896,128]{1,0:T(8,128)(2,1)S(1)}, u32[]{:S(2)}, u32[]{:S(2)}) collective-permute-start(bf16[896,128]{1,0:T(8,128)(2,1)S(1)} %add_convert_fusion.2), channel_id=1, source_target_pairs={{0,2},{1,3},{2,0},{3,1},{4,6},{5,7},{6,4},{7,5},{8,10},{9,11},{10,... | collective-permute-start | bytes 688136 | tf_op jit(solution)/shard_map/ppermute | solution.py:498
  45.9 1.8 %shard_map.117 = bf16[4,8,1024]{2,1,0:T(8,128)(2,1)} custom-call(s32[2]{0:T(128)S(1)} %pad_add_fusion.at_ref, bf16[20,96,384]{2,1,0:T(8,128)(2,1)S(1)} %get-tuple-element.47.outer_ref, bf16[9,128,384]{2,1,0:T(8,128)(2,1)S(1)} %get-tuple-element.48.w_ref), custom_call_target="tpu_custom_call" | custom-call | flops 226492416 | bytes 2359304 | tf_op jit(solution)/shard_map/pallas_call | solution.py:200
  47.7 0.0 collective-permute-done.9.other_ref
  47.7 1.6 %shard_map.116 = f32[512,512]{1,0:T(8,128)} custom-call(s32[2]{0:T(128)S(1)} %pad_add_fusion.at_ref, f32[1024,128]{1,0:T(8,128)S(1)} %convert_add_fusion.mine_ref, f32[1024,128]{1,0:T(8,128)S(1)} %collective-permute-done.9.other_ref), custom_call_target="tpu_custom_call" | custom-call | flops 10000000 | bytes 1048584 | tf_op jit(solution)/shard_map/pallas_call | solution.py:200
  49.3 2.7 %collective-permute-done.8 = bf16[896,128]{1,0:T(8,128)(2,1)S(1)} collective-permute-done((bf16[896,128]{1,0:T(8,128)(2,1)S(1)}, bf16[896,128]{1,0:T(8,128)(2,1)S(1)}, u32[]{:S(2)}, u32[]{:S(2)}) %collective-permute-start.8) | collective-permute-done | bytes 229408 | tf_op jit(solution)/shard_map/ppermute | solution.py:498
  52.0 0.1 add_convert_fusion.1.ref
  52.1 1.3 %collective-permute-start.10 = (bf16[896,128]{1,0:T(8,128)(2,1)S(1)}, bf16[896,128]{1,0:T(8,128)(2,1)S(1)}, u32[]{:S(2)}, u32[]{:S(2)}) collective-permute-start(bf16[896,128]{1,0:T(8,128)(2,1)S(1)} %add_convert_fusion.1.ref), channel_id=1, source_target_pairs={{0,1},{1,0},{2,3},{3,2},{4,5},{5,4},{6,7},{7,6},{8,9},{9,8},{10,11... | collective-permute-start | bytes 688136 | tf_op jit(solution)/shard_map/ppermute | solution.py:498
  53.4 1.6 %shard_map.118 = (f32[27,64,64]{2,1,0:T(8,128)}, f32[27,64,64]{2,1,0:T(8,128)}) custom-call(s32[2]{0:T(128)S(1)} %pad_add_fusion.at_ref, bf16[896,128]{1,0:T(8,128)(2,1)S(1)} %add_convert_fusion.1.ref), custom_call_target="tpu_custom_call" | custom-call | flops 100000000 | bytes 229384 | tf_op jit(solution)/shard_map/pallas_call | solution.py:200
  55.0 0.0 collective-permute-done.10.ref
  55.0 1.6 %shard_map.119 = (f32[27,64,64]{2,1,0:T(8,128)}, f32[27,64,64]{2,1,0:T(8,128)}) custom-call(s32[2]{0:T(128)S(1)} %pad_add_fusion.at_ref, bf16[896,128]{1,0:T(8,128)(2,1)S(1)} %collective-permute-done.10.ref, f32[27,64,64]{2,1,0:T(8,128)} %get-tuple-element.51.one_in, ...), custom_call_target="tpu_custom_call", output_to_operand_aliasing={{0}: (2, {}), {1}: (3, {})} | custom-call | tf_op jit(solution)/shard_map/pallas_call | solution.py:200
  (1 shorter events, 0.0 us)
Async XLA Ops:
  2.3 26.3 %copy-start = (bf16[1024,128]{1,0:T(8,128)(2,1)S(1)}, bf16[1024,128]{1,0:T(8,128)(2,1)}, u32[]{:S(2)}) copy-start(bf16[1024,128]{1,0:T(8,128)(2,1)} %shard_map.111.a0.i0) | copy-start | bytes 786436
  2.3 9.1 %collective-permute-start = (bf16[1024,128]{1,0:T(8,128)(2,1)}, bf16[1024,128]{1,0:T(8,128)(2,1)S(1)}, u32[]{:S(2)}, u32[]{:S(2)}) collective-permute-start(bf16[1024,128]{1,0:T(8,128)(2,1)} %shard_map.111.a0.i0), channel_id=1, source_target_pairs={{0,4},{4,8},{8,12},{12,0},{1,5},{5,9},{9,13},{13,1},{2,6},{6,10},{... | collective-permute-start | bytes 786440 | tf_op jit(solution)/shard_map/ppermute | solution.py:493
  3.7 22.1 %collective-permute-start.1 = (bf16[1024,128]{1,0:T(8,128)(2,1)}, bf16[1024,128]{1,0:T(8,128)(2,1)S(1)}, u32[]{:S(2)}, u32[]{:S(2)}) collective-permute-start(bf16[1024,128]{1,0:T(8,128)(2,1)} %shard_map.111.a0.i0), channel_id=1, source_target_pairs={{0,8},{4,12},{8,0},{12,4},{1,9},{5,13},{9,1},{13,5},{2,10},{6,14},... | collective-permute-start | bytes 786440 | tf_op jit(solution)/shard_map/ppermute | solution.py:493
  4.8 23.8 %collective-permute-start.2 = (bf16[1024,128]{1,0:T(8,128)(2,1)}, bf16[1024,128]{1,0:T(8,128)(2,1)S(1)}, u32[]{:S(2)}, u32[]{:S(2)}) collective-permute-start(bf16[1024,128]{1,0:T(8,128)(2,1)} %shard_map.111.a0.i0), channel_id=1, source_target_pairs={{0,12},{4,0},{8,4},{12,8},{1,13},{5,1},{9,5},{13,9},{2,14},{6,2},{... | collective-permute-start | bytes 786440 | tf_op jit(solution)/shard_map/ppermute | solution.py:493
  6.2 1.0 %copy-start.1 = (bf16[512,512]{1,0:T(8,128)(2,1)S(1)}, bf16[512,512]{1,0:T(8,128)(2,1)}, u32[]{:S(2)}) copy-start(bf16[512,512]{1,0:T(8,128)(2,1)} %wt.1) | copy-start | bytes 1572868
  7.2 1.0 %copy-start.2 = (bf16[27,64,64]{2,1,0:T(8,128)(2,1)S(1)}, bf16[27,64,64]{2,1,0:T(8,128)(2,1)}, u32[]{:S(2)}) copy-start(bf16[27,64,64]{2,1,0:T(8,128)(2,1)} %w2.1) | copy-start | bytes 663556
  8.2 1.0 %copy-start.3 = (bf16[27,64,64]{2,1,0:T(8,128)(2,1)S(1)}, bf16[27,64,64]{2,1,0:T(8,128)(2,1)}, u32[]{:S(2)}) copy-start(bf16[27,64,64]{2,1,0:T(8,128)(2,1)} %w1.1) | copy-start | bytes 663556
  9.2 0.7 %copy-start.4 = (s32[8,8]{1,0:T(8,128)S(1)}, s32[8,8]{1,0:T(8,128)}, u32[]{:S(2)}) copy-start(s32[8,8]{1,0:T(8,128)} %keep.1) | copy-start | bytes 772
  29.9 4.1 %collective-permute-start.3 = (bf16[1024,128]{1,0:T(8,128)(2,1)S(1)}, bf16[1024,128]{1,0:T(8,128)(2,1)S(1)}, u32[]{:S(2)}, u32[]{:S(2)}) collective-permute-start(bf16[1024,128]{1,0:T(8,128)(2,1)S(1)} %get-tuple-element.35), channel_id=1, source_target_pairs={{0,1},{1,0},{2,3},{3,2},{4,5},{5,4},{6,7},{7,6},{8,9},{9,8},{10,11... | collective-permute-start | bytes 786440 | tf_op jit(solution)/shard_map/ppermute | solution.py:498
  30.5 6.7 %collective-permute-start.4 = (bf16[8,2,48,128]{3,2,1,0:T(8,128)(2,1)S(1)}, bf16[8,2,48,128]{3,2,1,0:T(8,128)(2,1)S(1)}, u32[]{:S(2)}, u32[]{:S(2)}) collective-permute-start(bf16[8,2,48,128]{3,2,1,0:T(8,128)(2,1)S(1)} %get-tuple-element.40), channel_id=1, source_target_pairs={{0,1},{1,0},{2,3},{3,2},{4,5},{5,4},{6,7},{7,6},{8,9},{9,8},{10,11... | collective-permute-start | bytes 589832 | tf_op jit(solution)/shard_map/ppermute | solution.py:498
  30.6 8.0 %collective-permute-start.5 = (bf16[8,2,48,128]{3,2,1,0:T(8,128)(2,1)S(1)}, bf16[8,2,48,128]{3,2,1,0:T(8,128)(2,1)S(1)}, u32[]{:S(2)}, u32[]{:S(2)}) collective-permute-start(bf16[8,2,48,128]{3,2,1,0:T(8,128)(2,1)S(1)} %get-tuple-element.41), channel_id=1, source_target_pairs={{1,2},{2,1},{5,6},{6,5},{9,10},{10,9},{13,14},{14,13},{17,18},{18,... | collective-permute-start | bytes 589832 | tf_op jit(solution)/shard_map/ppermute | solution.py:570
  34.1 8.4 %collective-permute-start.6 = (bf16[1024,128]{1,0:T(8,128)(2,1)S(1)}, bf16[1024,128]{1,0:T(8,128)(2,1)S(1)}, u32[]{:S(2)}, u32[]{:S(2)}) collective-permute-start(bf16[1024,128]{1,0:T(8,128)(2,1)S(1)} %add_convert_fusion), channel_id=1, source_target_pairs={{0,2},{1,3},{2,0},{3,1},{4,6},{5,7},{6,4},{7,5},{8,10},{9,11},{10,... | collective-permute-start | bytes 786440 | tf_op jit(solution)/shard_map/ppermute | solution.py:498
  42.5 2.6 %collective-permute-start.7 = (bf16[896,128]{1,0:T(8,128)(2,1)S(1)}, bf16[896,128]{1,0:T(8,128)(2,1)S(1)}, u32[]{:S(2)}, u32[]{:S(2)}) collective-permute-start(bf16[896,128]{1,0:T(8,128)(2,1)S(1)} %get-tuple-element.45), channel_id=1, source_target_pairs={{0,1},{1,0},{2,3},{3,2},{4,5},{5,4},{6,7},{7,6},{8,9},{9,8},{10,11... | collective-permute-start | bytes 688136 | tf_op jit(solution)/shard_map/ppermute | solution.py:498
  44.0 3.7 %collective-permute-start.9 = (f32[1024,128]{1,0:T(8,128)S(1)}, f32[1024,128]{1,0:T(8,128)S(1)}, u32[]{:S(2)}, u32[]{:S(2)}) collective-permute-start(f32[1024,128]{1,0:T(8,128)S(1)} %convert_add_fusion.mine_ref), channel_id=1, source_target_pairs={{0,1},{1,0},{2,3},{3,2},{4,5},{5,4},{6,7},{7,6},{8,9},{9,8},{10,11... | collective-permute-start | bytes 1572872 | tf_op jit(solution)/shard_map/ppermute | solution.py:498
  45.2 6.9 %collective-permute-start.8 = (bf16[896,128]{1,0:T(8,128)(2,1)S(1)}, bf16[896,128]{1,0:T(8,128)(2,1)S(1)}, u32[]{:S(2)}, u32[]{:S(2)}) collective-permute-start(bf16[896,128]{1,0:T(8,128)(2,1)S(1)} %add_convert_fusion.2), channel_id=1, source_target_pairs={{0,2},{1,3},{2,0},{3,1},{4,6},{5,7},{6,4},{7,5},{8,10},{9,11},{10,... | collective-permute-start | bytes 688136 | tf_op jit(solution)/shard_map/ppermute | solution.py:498
  52.1 2.8 %collective-permute-start.10 = (bf16[896,128]{1,0:T(8,128)(2,1)S(1)}, bf16[896,128]{1,0:T(8,128)(2,1)S(1)}, u32[]{:S(2)}, u32[]{:S(2)}) collective-permute-start(bf16[896,128]{1,0:T(8,128)(2,1)S(1)} %add_convert_fusion.1.ref), channel_id=1, source_target_pairs={{0,1},{1,0},{2,3},{3,2},{4,5},{5,4},{6,7},{7,6},{8,9},{9,8},{10,11... | collective-permute-start | bytes 688136 | tf_op jit(solution)/shard_map/ppermute | solution.py:498

commit v12 on v9

--- a/solution.py
+++ b/solution.py
@@ -346,12 +346,15 @@
     return lax.dot_general(rows, taps, (((1,), (1,)), ((), ())), preferred_element_type=F32)
 
 
-def weight_sums(act, wide_ref, act_ref):
+def stack(act, act_ref):
     act_ref[0:128] = jnp.zeros((128, 128), F32)
     act_ref[128:1152] = act.reshape(1024, 128)
     act_ref[1152:1280] = jnp.zeros((128, 128), F32)
     turned = act_ref[...].T.astype(BF16)
-    stacked = jnp.concatenate([turned[:, 128 * i : 128 * i + 1024] for i in range(3)], axis=0)
+    return jnp.concatenate([turned[:, 128 * i : 128 * i + 1024] for i in range(3)], axis=0)
+
+
+def weight_sums(stacked, wide_ref):
     sums = [None] * 9
     for j in range(3):
         rows = wide_ref[2:18, 32 - 16 * j : 96 - 16 * j].reshape(1024, 384)
@@ -361,7 +364,9 @@
     return sums
 
 
-def own_kernel(factor, back_ref, one_ref, w_ref, acc_ref, sums_ref, wide_ref, act_ref):
+def own_kernel(
+    factor, at_ref, back_ref, one_ref, w_ref, i0, i1, i2, i3, acc_ref, sums_ref, stack_ref, wide_ref, act_ref, in_ref
+):
     wide_ref[2:18, 0:16] = jnp.zeros((16, 16, 384), BF16)
     wide_ref[2:18, 80:96] = jnp.zeros((16, 16, 384), BF16)
     wide_ref[2:18, 16:80] = triple(back_ref[...].astype(F32))
@@ -374,20 +379,21 @@
         acc_ref[0:14, ys] += part[2:16, :, 0:128]
         acc_ref[:, ys] += part[:, :, 128:256]
         acc_ref[2:16, ys] += part[0:14, :, 256:384]
-    sums = weight_sums(jnp.maximum(one_ref[...].astype(F32), 0.0), wide_ref, act_ref)
+    sums = weight_sums(stack(jnp.maximum(one_ref[...].astype(F32), 0.0), act_ref), wide_ref)
     for m, block in enumerate(fold(sums, factor)):
         sums_ref[64 * m : 64 * m + 64] = block
-
-
-def conv_kernel(
-    factor, at_ref, acc_ref, sums_ref, one_ref, chip_ref, cross_ref, w_ref, i0, i1, i2, i3,
-    mine_ref, send_ref, outer_ref, rim_ref, wide_ref, in_ref, first_ref, act_ref,
-):
     me = at_ref[0]
     parts = (i0, i1, i2, i3)
     n = len(parts)
     for s, part in enumerate(parts):
         in_ref[pl.ds(lax.rem(me + n - s, n) * 4, 4)] = part[...].reshape(4, 64, 128)
+    stack_ref[...] = stack(in_ref[...].astype(F32), act_ref)
+
+
+def conv_kernel(
+    factor, at_ref, acc_ref, sums_ref, one_ref, chip_ref, cross_ref, w_ref, stack_ref,
+    mine_ref, send_ref, outer_ref, rim_ref, wide_ref, first_ref,
+):
 
     def put(side, ref):
         rim_ref[side] = ref[...]
@@ -420,7 +426,7 @@
     second = fold(sums, factor)
     pre = jnp.concatenate([rim_ref[0, :, 32:48], one_ref[...], rim_ref[1, :, 32:48]], axis=1).astype(F32)
     outer_ref[2:18] = triple(jnp.where(pre > 0, first_ref[...], 0.0))
-    first = fold(weight_sums(in_ref[...].astype(F32), outer_ref, act_ref), factor)
+    first = fold(weight_sums(stack_ref[...], outer_ref), factor)
 
     def emit(half, ref):
         for m in range(7):
@@ -573,15 +579,17 @@
     tsend, *seconds = lax.optimization_barrier((tsend, *seconds))
     tmine = on_chip(tmine, tsend)
     one, tmine = lax.optimization_barrier((one, tmine))
-    acc, sums = call(
+    acc, sums, stacked = call(
         functools.partial(own_kernel, factor),
-        (shape((16, 96, 128), F32), shape((896, 128), F32)),
-        [vmem((20, 96, 384), BF16), vmem((1280, 128), F32)],
+        (shape((16, 96, 128), F32), shape((896, 128), F32), shape((384, 1024), BF16)),
+        [vmem((20, 96, 384), BF16), vmem((1280, 128), F32), vmem((16, 64, 128), BF16)],
         2 * 128 * 3456 * 2048,
         16,
+        at,
         back.reshape(16, 64, 128),
         one,
         d2,
+        *seconds,
     )
     tmine = across(tmine)
     mine, send, outer = call(
@@ -590,9 +598,7 @@
         [
             vmem((2, 16, 48, 128), BF16),
             vmem((2, 20, 32, 384), BF16),
-            vmem((16, 64, 128), BF16),
             vmem((16, 96, 128), F32),
-            vmem((1280, 128), F32),
         ],
         2 * 128 * 3456 * 900,
         20,
@@ -603,7 +609,7 @@
         chip.reshape(16, 48, 128),
         cross.reshape(16, 48, 128),
         d2,
-        *seconds,
+        stacked,
     )
     send, tmine = lax.optimization_barrier((send, tmine))
     mine = on_chip(mine, send)

time: 55.9 us -> 55.9 us (level)
  Pallas kernels: 17.9 us -> 18.5 us
    pallas_call x9, Pallas kernels: 17.9 us -> 18.5 us  [call(): pl.pallas_call(kernel, out_shape=out_shape, in_specs=spec, out_specs=jax....]
    ppermute x7, waiting for transfers between devices: 6.9 us -> 6.33 us  [swap(): return lax.ppermute(value, axis, [(i, i ^ bit) for i in range(n)])]
  transfers between devices with their start and end apart: 14 -> 14, of which waited for: 7 -> 7; matrix products, arithmetic and copies ran while one was open for 0% -> 0% of each run, Pallas kernels for 27% -> 28%
where the time goes in v12:
time: 55.9 us; the launch traced here: 55.5 us
  Pallas kernels  18.5 us (33%)
  waiting for transfers between devices  16.9 us (30%)
  starting transfers between devices  15.3 us (27%)
  local copies, waits for them, and re-layouts  3.76 us (7%)
  between operations  0.77 us (1%)
    pallas_call x9, Pallas kernels, call(): pl.pallas_call(kernel, out_shape=out_shape, in_specs=spec, out_specs=jax....  18.5 us
    ppermute x6, waiting for transfers between devices, rotate(): return lax.ppermute(value, axis, [(i, (i + step) % n) for i in range(n)])  10.5 us
    ppermute x6, starting transfers between devices, rotate(): return lax.ppermute(value, axis, [(i, (i + step) % n) for i in range(n)])  10.1 us
    ppermute x7, waiting for transfers between devices, swap(): return lax.ppermute(value, axis, [(i, i ^ bit) for i in range(n)])  6.33 us
    ppermute x7, starting transfers between devices, swap(): return lax.ppermute(value, axis, [(i, i ^ bit) for i in range(n)])  4.55 us
    unnamed x12, local copies, waits for them, and re-layouts  3.76 us
  transfers between devices with their start and end apart: 14, of which 7 were waited for; matrix products, arithmetic and copies ran while one was open for 0% of the time, Pallas kernels for 28%

profile of v12, /device:TPU:0, one launch (start us, length us, event | category | flops | bytes accessed | tf_op | source)
XLA Modules:
  0.0 55.5 jit_solution(10519285851206484845)
XLA Ops:
  0.6 1.7 %shard_map.111 = (bf16[768,128]{1,0:T(8,128)(2,1)}, bf16[256,128]{1,0:T(8,128)(2,1)}) custom-call(bf16[8,4,8,128]{3,2,1,0:T(8,128)(2,1)} %og.1, bf16[4,8,1024]{2,1,0:T(8,128)(2,1)} %two.1, bf16[4,8,1024]{2,1,0:T(8,128)(2,1)} %one.1, bf16[4,8,1024]{2,1,0:T(8,128)(2,1)} %act.1), custom_call_target="tpu_custom_call" | custom-call | tf_op jit(solution)/shard_map/pallas_call | solution.py:200
  2.3 3.1 %collective-permute-start = (bf16[768,128]{1,0:T(8,128)(2,1)}, bf16[768,128]{1,0:T(8,128)(2,1)S(1)}, u32[]{:S(2)}, u32[]{:S(2)}) collective-permute-start(bf16[768,128]{1,0:T(8,128)(2,1)} %get-tuple-element.38.a0), channel_id=1, source_target_pairs={{0,4},{4,8},{8,12},{12,0},{1,5},{5,9},{9,13},{13,1},{2,6},{6,10},{... | collective-permute-start | bytes 589832 | tf_op jit(solution)/shard_map/ppermute | solution.py:499
  5.4 2.6 %collective-permute-start.1 = (bf16[768,128]{1,0:T(8,128)(2,1)}, bf16[768,128]{1,0:T(8,128)(2,1)S(1)}, u32[]{:S(2)}, u32[]{:S(2)}) collective-permute-start(bf16[768,128]{1,0:T(8,128)(2,1)} %get-tuple-element.38.a0), channel_id=1, source_target_pairs={{0,8},{4,12},{8,0},{12,4},{1,9},{5,13},{9,1},{13,5},{2,10},{6,14},... | collective-permute-start | bytes 589832 | tf_op jit(solution)/shard_map/ppermute | solution.py:499
  8.0 1.3 %collective-permute-start.2 = (bf16[768,128]{1,0:T(8,128)(2,1)}, bf16[768,128]{1,0:T(8,128)(2,1)S(1)}, u32[]{:S(2)}, u32[]{:S(2)}) collective-permute-start(bf16[768,128]{1,0:T(8,128)(2,1)} %get-tuple-element.38.a0), channel_id=1, source_target_pairs={{0,12},{4,0},{8,4},{12,8},{1,13},{5,1},{9,5},{13,9},{2,14},{6,2},{... | collective-permute-start | bytes 589832 | tf_op jit(solution)/shard_map/ppermute | solution.py:499
  9.3 0.7 %collective-permute-start.3 = (bf16[256,128]{1,0:T(8,128)(2,1)}, bf16[256,128]{1,0:T(8,128)(2,1)S(1)}, u32[]{:S(2)}, u32[]{:S(2)}) collective-permute-start(bf16[256,128]{1,0:T(8,128)(2,1)} %get-tuple-element.49.i0), channel_id=1, source_target_pairs={{0,4},{4,8},{8,12},{12,0},{1,5},{5,9},{9,13},{13,1},{2,6},{6,10},{... | collective-permute-start | bytes 196616 | tf_op jit(solution)/shard_map/ppermute | solution.py:499
  10.0 0.3 collective-permute-start.4
  10.3 3.1 %collective-permute-done.a1 = bf16[768,128]{1,0:T(8,128)(2,1)S(1)} collective-permute-done((bf16[768,128]{1,0:T(8,128)(2,1)}, bf16[768,128]{1,0:T(8,128)(2,1)S(1)}, u32[]{:S(2)}, u32[]{:S(2)}) %collective-permute-start) | collective-permute-done | bytes 196640 | tf_op jit(solution)/shard_map/ppermute | solution.py:499
  13.5 2.1 %collective-permute-start.5 = (bf16[256,128]{1,0:T(8,128)(2,1)}, bf16[256,128]{1,0:T(8,128)(2,1)S(1)}, u32[]{:S(2)}, u32[]{:S(2)}) collective-permute-start(bf16[256,128]{1,0:T(8,128)(2,1)} %get-tuple-element.49.i0), channel_id=1, source_target_pairs={{0,12},{4,0},{8,4},{12,8},{1,13},{5,1},{9,5},{13,9},{2,14},{6,2},{... | collective-permute-start | bytes 196616 | tf_op jit(solution)/shard_map/ppermute | solution.py:499
  15.5 0.1 pad_add_fusion.at_ref
  15.6 1.0 %copy-done = bf16[512,512]{1,0:T(8,128)(2,1)S(1)} copy-done((bf16[512,512]{1,0:T(8,128)(2,1)S(1)}, bf16[512,512]{1,0:T(8,128)(2,1)}, u32[]{:S(2)}) %copy-start) | copy-done | bytes 524312
  16.6 1.0 %copy-done.1 = bf16[27,64,64]{2,1,0:T(8,128)(2,1)S(1)} copy-done((bf16[27,64,64]{2,1,0:T(8,128)(2,1)S(1)}, bf16[27,64,64]{2,1,0:T(8,128)(2,1)}, u32[]{:S(2)}) %copy-start.1) | copy-done | bytes 221208
  17.7 1.0 %copy-done.2 = bf16[27,64,64]{2,1,0:T(8,128)(2,1)S(1)} copy-done((bf16[27,64,64]{2,1,0:T(8,128)(2,1)S(1)}, bf16[27,64,64]{2,1,0:T(8,128)(2,1)}, u32[]{:S(2)}) %copy-start.2) | copy-done | bytes 221208
  18.7 0.7 %copy-done.4 = s32[8,8]{1,0:T(8,128)S(1)} copy-done((s32[8,8]{1,0:T(8,128)S(1)}, s32[8,8]{1,0:T(8,128)}, u32[]{:S(2)}) %copy-start.4) | copy-done | bytes 280
  19.4 1.4 %shard_map.112 = (bf16[512,512]{1,0:T(8,128)(2,1)S(1)}, bf16[512,512]{1,0:T(8,128)(2,1)S(1)}, bf16[9,128,384]{2,1,0:T(8,128)(2,1)S(1)}, bf16[9,128,384]{2,1,0:T(8,128)(2,1)S(1)}) custom-call(bf16[512,512]{1,0:T(8,128)(2,1)S(1)} %copy-done, s32[8,8]{1,0:T(8,128)S(1)} %copy-done.4, bf16[27,64,64]{2,1,0:T(8,128)(2,1)S(1)} %copy-done.1, ...), custom_call_target="tpu_custom_call" | custom-call | flops 10000000 | bytes 966912 | tf_op jit(solution)/shard_map/pallas_call | solution.py:200
  20.8 0.0 copy-start.5
  20.8 1.1 %collective-permute-done.1.a2 = bf16[768,128]{1,0:T(8,128)(2,1)S(1)} collective-permute-done((bf16[768,128]{1,0:T(8,128)(2,1)}, bf16[768,128]{1,0:T(8,128)(2,1)S(1)}, u32[]{:S(2)}, u32[]{:S(2)}) %collective-permute-start.1) | collective-permute-done | bytes 196640 | tf_op jit(solution)/shard_map/ppermute | solution.py:499
  21.9 0.0 collective-permute-done.2.a3
  21.9 0.0 copy-done.3
  22.0 1.3 %shard_map.113 = (bf16[8,2,64,128]{3,2,1,0:T(8,128)(2,1)S(1)}, bf16[16,64,128]{2,1,0:T(8,128)(2,1)S(1)}, bf16[8,2,48,128]{3,2,1,0:T(8,128)(2,1)S(1)}, bf16[8,2,4...) custom-call(s32[2]{0:T(128)S(1)} %pad_add_fusion.at_ref, ...), custom_call_target="tpu_custom_call" | custom-call | flops 268435456 | bytes 1835016 | tf_op jit(solution)/shard_map/pallas_call | solution.py:200
  23.3 0.0 collective-permute-done.3.i1
  23.3 6.2 %collective-permute-done.4.i2 = bf16[256,128]{1,0:T(8,128)(2,1)S(1)} collective-permute-done((bf16[256,128]{1,0:T(8,128)(2,1)}, bf16[256,128]{1,0:T(8,128)(2,1)S(1)}, u32[]{:S(2)}, u32[]{:S(2)}) %collective-permute-start.4) | collective-permute-done | bytes 65568 | tf_op jit(solution)/shard_map/ppermute | solution.py:499
  29.5 0.0 collective-permute-done.5.i3
  29.5 0.0 collective-permute-start.6
  29.5 0.5 collective-permute-start.7
  30.0 0.7 %collective-permute-start.8 = (bf16[8,2,48,128]{3,2,1,0:T(8,128)(2,1)S(1)}, bf16[8,2,48,128]{3,2,1,0:T(8,128)(2,1)S(1)}, u32[]{:S(2)}, u32[]{:S(2)}) collective-permute-start(bf16[8,2,48,128]{3,2,1,0:T(8,128)(2,1)S(1)} %get-tuple-element.56), channel_id=1, source_target_pairs={{1,2},{2,1},{5,6},{6,5},{9,10},{10,9},{13,14},{14,13},{17,18},{18,... | collective-permute-start | bytes 589832 | tf_op jit(solution)/shard_map/ppermute | solution.py:577
  30.7 0.4 collective-permute-done.6
  31.1 0.1 add_convert_fusion
  31.1 2.6 %collective-permute-start.9 = (bf16[1024,128]{1,0:T(8,128)(2,1)S(1)}, bf16[1024,128]{1,0:T(8,128)(2,1)S(1)}, u32[]{:S(2)}, u32[]{:S(2)}) collective-permute-start(bf16[1024,128]{1,0:T(8,128)(2,1)S(1)} %add_convert_fusion), channel_id=1, source_target_pairs={{0,2},{1,3},{2,0},{3,1},{4,6},{5,7},{6,4},{7,5},{8,10},{9,11},{10,... | collective-permute-start | bytes 786440 | tf_op jit(solution)/shard_map/ppermute | solution.py:504
  33.7 0.0 copy-done.5
  33.7 3.7 %shard_map.114 = (f32[16,96,128]{2,1,0:T(8,128)S(1)}, f32[896,128]{1,0:T(8,128)S(1)}, bf16[384,1024]{1,0:T(8,128)(2,1)S(1)}) custom-call(s32[2]{0:T(128)S(1)} %pad_add_fusion.at_ref, bf16[16,64,128]{2,1,0:T(8,128)(2,1)S(1)} %bitcast.7, bf16[16,64,128]{2,1,0:T(8,128)(2,1)S(1)} %get-tuple-element.47.one_ref, bf16[9,128,384]{2,1,0:T(8,128)(2,1)S(1)} %get-tuple-element.48.w_ref, ...), custom_call_target="tpu_custom_call" | custom-call | flops 1811939328 | bytes 1671176 | tf_op jit(solution)/shard_map/pallas_call | solution.py:200
  37.4 0.0 collective-permute-done.7
  37.4 0.0 collective-permute-done.8
  37.4 3.8 %shard_map.115 = (f32[896,128]{1,0:T(8,128)S(1)}, bf16[896,128]{1,0:T(8,128)(2,1)S(1)}, bf16[20,96,384]{2,1,0:T(8,128)(2,1)S(1)}) custom-call(s32[2]{0:T(128)S(1)} %pad_add_fusion.at_ref, f32[16,96,128]{2,1,0:T(8,128)S(1)} %get-tuple-element.53.acc_ref, f32[896,128]{1,0:T(8,128)S(1)} %get-tuple-element.54.sums_ref, ...), custom_call_target="tpu_custom_call" | custom-call | flops 796262400 | bytes 3571720 | tf_op jit(solution)/shard_map/pallas_call | solution.py:200
  41.3 1.6 %collective-permute-done.9 = bf16[1024,128]{1,0:T(8,128)(2,1)S(1)} collective-permute-done((bf16[1024,128]{1,0:T(8,128)(2,1)S(1)}, bf16[1024,128]{1,0:T(8,128)(2,1)S(1)}, u32[]{:S(2)}, u32[]{:S(2)}) %collective-permute-start.9) | collective-permute-done | bytes 262176 | tf_op jit(solution)/shard_map/ppermute | solution.py:504
  42.8 0.1 convert_add_fusion.mine_ref
  42.9 0.1 collective-permute-start.10
  43.0 0.5 collective-permute-start.12
  43.5 1.0 %collective-permute-done.10 = bf16[896,128]{1,0:T(8,128)(2,1)S(1)} collective-permute-done((bf16[896,128]{1,0:T(8,128)(2,1)S(1)}, bf16[896,128]{1,0:T(8,128)(2,1)S(1)}, u32[]{:S(2)}, u32[]{:S(2)}) %collective-permute-start.10) | collective-permute-done | bytes 229408 | tf_op jit(solution)/shard_map/ppermute | solution.py:504
  44.5 0.8 %collective-permute-start.11 = (bf16[896,128]{1,0:T(8,128)(2,1)S(1)}, bf16[896,128]{1,0:T(8,128)(2,1)S(1)}, u32[]{:S(2)}, u32[]{:S(2)}) collective-permute-start(bf16[896,128]{1,0:T(8,128)(2,1)S(1)} %add_convert_fusion.2), channel_id=1, source_target_pairs={{0,2},{1,3},{2,0},{3,1},{4,6},{5,7},{6,4},{7,5},{8,10},{9,11},{10,... | collective-permute-start | bytes 688136 | tf_op jit(solution)/shard_map/ppermute | solution.py:504
  45.3 1.8 %shard_map.117 = bf16[4,8,1024]{2,1,0:T(8,128)(2,1)} custom-call(s32[2]{0:T(128)S(1)} %pad_add_fusion.at_ref, bf16[20,96,384]{2,1,0:T(8,128)(2,1)S(1)} %get-tuple-element.63.outer_ref, bf16[9,128,384]{2,1,0:T(8,128)(2,1)S(1)} %get-tuple-element.64.w_ref), custom_call_target="tpu_custom_call" | custom-call | flops 226492416 | bytes 2359304 | tf_op jit(solution)/shard_map/pallas_call | solution.py:200
  47.1 0.0 collective-permute-done.12.other_ref
  47.1 1.6 %shard_map.116 = f32[512,512]{1,0:T(8,128)} custom-call(s32[2]{0:T(128)S(1)} %pad_add_fusion.at_ref, f32[1024,128]{1,0:T(8,128)S(1)} %convert_add_fusion.mine_ref, f32[1024,128]{1,0:T(8,128)S(1)} %collective-permute-done.12.other_ref), custom_call_target="tpu_custom_call" | custom-call | flops 10000000 | bytes 1048584 | tf_op jit(solution)/shard_map/pallas_call | solution.py:200
  48.8 3.4 %collective-permute-done.11 = bf16[896,128]{1,0:T(8,128)(2,1)S(1)} collective-permute-done((bf16[896,128]{1,0:T(8,128)(2,1)S(1)}, bf16[896,128]{1,0:T(8,128)(2,1)S(1)}, u32[]{:S(2)}, u32[]{:S(2)}) %collective-permute-start.11) | collective-permute-done | bytes 229408 | tf_op jit(solution)/shard_map/ppermute | solution.py:504
  52.2 0.1 add_convert_fusion.1.ref
  52.3 0.1 collective-permute-start.13
  52.4 1.6 %shard_map.118 = (f32[27,64,64]{2,1,0:T(8,128)}, f32[27,64,64]{2,1,0:T(8,128)}) custom-call(s32[2]{0:T(128)S(1)} %pad_add_fusion.at_ref, bf16[896,128]{1,0:T(8,128)(2,1)S(1)} %add_convert_fusion.1.ref), custom_call_target="tpu_custom_call" | custom-call | flops 100000000 | bytes 229384 | tf_op jit(solution)/shard_map/pallas_call | solution.py:200
  54.0 0.0 collective-permute-done.13.ref
  54.0 1.6 %shard_map.119 = (f32[27,64,64]{2,1,0:T(8,128)}, f32[27,64,64]{2,1,0:T(8,128)}) custom-call(s32[2]{0:T(128)S(1)} %pad_add_fusion.at_ref, bf16[896,128]{1,0:T(8,128)(2,1)S(1)} %collective-permute-done.13.ref, f32[27,64,64]{2,1,0:T(8,128)} %get-tuple-element.67.one_in, ...), custom_call_target="tpu_custom_call", output_to_operand_aliasing={{0}: (2, {}), {1}: (3, {})} | custom-call | tf_op jit(solution)/shard_map/pallas_call | solution.py:200
  (6 shorter events, 0.1 us)
Async XLA Ops:
  2.3 11.2 %collective-permute-start = (bf16[768,128]{1,0:T(8,128)(2,1)}, bf16[768,128]{1,0:T(8,128)(2,1)S(1)}, u32[]{:S(2)}, u32[]{:S(2)}) collective-permute-start(bf16[768,128]{1,0:T(8,128)(2,1)} %get-tuple-element.38.a0), channel_id=1, source_target_pairs={{0,4},{4,8},{8,12},{12,0},{1,5},{5,9},{9,13},{13,1},{2,6},{6,10},{... | collective-permute-start | bytes 589832 | tf_op jit(solution)/shard_map/ppermute | solution.py:499
  5.4 16.6 %collective-permute-start.1 = (bf16[768,128]{1,0:T(8,128)(2,1)}, bf16[768,128]{1,0:T(8,128)(2,1)S(1)}, u32[]{:S(2)}, u32[]{:S(2)}) collective-permute-start(bf16[768,128]{1,0:T(8,128)(2,1)} %get-tuple-element.38.a0), channel_id=1, source_target_pairs={{0,8},{4,12},{8,0},{12,4},{1,9},{5,13},{9,1},{13,5},{2,10},{6,14},... | collective-permute-start | bytes 589832 | tf_op jit(solution)/shard_map/ppermute | solution.py:499
  8.0 14.0 %collective-permute-start.2 = (bf16[768,128]{1,0:T(8,128)(2,1)}, bf16[768,128]{1,0:T(8,128)(2,1)S(1)}, u32[]{:S(2)}, u32[]{:S(2)}) collective-permute-start(bf16[768,128]{1,0:T(8,128)(2,1)} %get-tuple-element.38.a0), channel_id=1, source_target_pairs={{0,12},{4,0},{8,4},{12,8},{1,13},{5,1},{9,5},{13,9},{2,14},{6,2},{... | collective-permute-start | bytes 589832 | tf_op jit(solution)/shard_map/ppermute | solution.py:499
  9.3 14.0 %collective-permute-start.3 = (bf16[256,128]{1,0:T(8,128)(2,1)}, bf16[256,128]{1,0:T(8,128)(2,1)S(1)}, u32[]{:S(2)}, u32[]{:S(2)}) collective-permute-start(bf16[256,128]{1,0:T(8,128)(2,1)} %get-tuple-element.49.i0), channel_id=1, source_target_pairs={{0,4},{4,8},{8,12},{12,0},{1,5},{5,9},{9,13},{13,1},{2,6},{6,10},{... | collective-permute-start | bytes 196616 | tf_op jit(solution)/shard_map/ppermute | solution.py:499
  10.0 19.5 %collective-permute-start.4 = (bf16[256,128]{1,0:T(8,128)(2,1)}, bf16[256,128]{1,0:T(8,128)(2,1)S(1)}, u32[]{:S(2)}, u32[]{:S(2)}) collective-permute-start(bf16[256,128]{1,0:T(8,128)(2,1)} %get-tuple-element.49.i0), channel_id=1, source_target_pairs={{0,8},{4,12},{8,0},{12,4},{1,9},{5,13},{9,1},{13,5},{2,10},{6,14},... | collective-permute-start | bytes 196616 | tf_op jit(solution)/shard_map/ppermute | solution.py:499
  13.5 16.1 %collective-permute-start.5 = (bf16[256,128]{1,0:T(8,128)(2,1)}, bf16[256,128]{1,0:T(8,128)(2,1)S(1)}, u32[]{:S(2)}, u32[]{:S(2)}) collective-permute-start(bf16[256,128]{1,0:T(8,128)(2,1)} %get-tuple-element.49.i0), channel_id=1, source_target_pairs={{0,12},{4,0},{8,4},{12,8},{1,13},{5,1},{9,5},{13,9},{2,14},{6,2},{... | collective-permute-start | bytes 196616 | tf_op jit(solution)/shard_map/ppermute | solution.py:499
  15.6 1.0 %copy-start = (bf16[512,512]{1,0:T(8,128)(2,1)S(1)}, bf16[512,512]{1,0:T(8,128)(2,1)}, u32[]{:S(2)}) copy-start(bf16[512,512]{1,0:T(8,128)(2,1)} %wt.1) | copy-start | bytes 1572868
  16.6 1.0 %copy-start.1 = (bf16[27,64,64]{2,1,0:T(8,128)(2,1)S(1)}, bf16[27,64,64]{2,1,0:T(8,128)(2,1)}, u32[]{:S(2)}) copy-start(bf16[27,64,64]{2,1,0:T(8,128)(2,1)} %w2.1) | copy-start | bytes 663556
  17.7 1.0 %copy-start.2 = (bf16[27,64,64]{2,1,0:T(8,128)(2,1)S(1)}, bf16[27,64,64]{2,1,0:T(8,128)(2,1)}, u32[]{:S(2)}) copy-start(bf16[27,64,64]{2,1,0:T(8,128)(2,1)} %w1.1) | copy-start | bytes 663556
  18.7 0.7 %copy-start.4 = (s32[8,8]{1,0:T(8,128)S(1)}, s32[8,8]{1,0:T(8,128)}, u32[]{:S(2)}) copy-start(s32[8,8]{1,0:T(8,128)} %keep.1) | copy-start | bytes 772
  19.4 2.6 %copy-start.3 = (bf16[768,128]{1,0:T(8,128)(2,1)S(1)}, bf16[768,128]{1,0:T(8,128)(2,1)}, u32[]{:S(2)}) copy-start(bf16[768,128]{1,0:T(8,128)(2,1)} %get-tuple-element.38.a0) | copy-start | bytes 589828
  20.8 12.9 %copy-start.5 = (bf16[256,128]{1,0:T(8,128)(2,1)S(1)}, bf16[256,128]{1,0:T(8,128)(2,1)}, u32[]{:S(2)}) copy-start(bf16[256,128]{1,0:T(8,128)(2,1)} %get-tuple-element.49.i0) | copy-start | bytes 196612
  29.5 1.5 %collective-permute-start.6 = (bf16[1024,128]{1,0:T(8,128)(2,1)S(1)}, bf16[1024,128]{1,0:T(8,128)(2,1)S(1)}, u32[]{:S(2)}, u32[]{:S(2)}) collective-permute-start(bf16[1024,128]{1,0:T(8,128)(2,1)S(1)} %get-tuple-element.46), channel_id=1, source_target_pairs={{0,1},{1,0},{2,3},{3,2},{4,5},{5,4},{6,7},{7,6},{8,9},{9,8},{10,11... | collective-permute-start | bytes 786440 | tf_op jit(solution)/shard_map/ppermute | solution.py:504
  29.5 7.9 %collective-permute-start.7 = (bf16[8,2,48,128]{3,2,1,0:T(8,128)(2,1)S(1)}, bf16[8,2,48,128]{3,2,1,0:T(8,128)(2,1)S(1)}, u32[]{:S(2)}, u32[]{:S(2)}) collective-permute-start(bf16[8,2,48,128]{3,2,1,0:T(8,128)(2,1)S(1)} %get-tuple-element.55), channel_id=1, source_target_pairs={{0,1},{1,0},{2,3},{3,2},{4,5},{5,4},{6,7},{7,6},{8,9},{9,8},{10,11... | collective-permute-start | bytes 589832 | tf_op jit(solution)/shard_map/ppermute | solution.py:504
  30.0 7.4 %collective-permute-start.8 = (bf16[8,2,48,128]{3,2,1,0:T(8,128)(2,1)S(1)}, bf16[8,2,48,128]{3,2,1,0:T(8,128)(2,1)S(1)}, u32[]{:S(2)}, u32[]{:S(2)}) collective-permute-start(bf16[8,2,48,128]{3,2,1,0:T(8,128)(2,1)S(1)} %get-tuple-element.56), channel_id=1, source_target_pairs={{1,2},{2,1},{5,6},{6,5},{9,10},{10,9},{13,14},{14,13},{17,18},{18,... | collective-permute-start | bytes 589832 | tf_op jit(solution)/shard_map/ppermute | solution.py:577
  31.1 11.7 %collective-permute-start.9 = (bf16[1024,128]{1,0:T(8,128)(2,1)S(1)}, bf16[1024,128]{1,0:T(8,128)(2,1)S(1)}, u32[]{:S(2)}, u32[]{:S(2)}) collective-permute-start(bf16[1024,128]{1,0:T(8,128)(2,1)S(1)} %add_convert_fusion), channel_id=1, source_target_pairs={{0,2},{1,3},{2,0},{3,1},{4,6},{5,7},{6,4},{7,5},{8,10},{9,11},{10,... | collective-permute-start | bytes 786440 | tf_op jit(solution)/shard_map/ppermute | solution.py:504
  42.9 1.6 %collective-permute-start.10 = (bf16[896,128]{1,0:T(8,128)(2,1)S(1)}, bf16[896,128]{1,0:T(8,128)(2,1)S(1)}, u32[]{:S(2)}, u32[]{:S(2)}) collective-permute-start(bf16[896,128]{1,0:T(8,128)(2,1)S(1)} %get-tuple-element.61), channel_id=1, source_target_pairs={{0,1},{1,0},{2,3},{3,2},{4,5},{5,4},{6,7},{7,6},{8,9},{9,8},{10,11... | collective-permute-start | bytes 688136 | tf_op jit(solution)/shard_map/ppermute | solution.py:504
  43.0 4.2 %collective-permute-start.12 = (f32[1024,128]{1,0:T(8,128)S(1)}, f32[1024,128]{1,0:T(8,128)S(1)}, u32[]{:S(2)}, u32[]{:S(2)}) collective-permute-start(f32[1024,128]{1,0:T(8,128)S(1)} %convert_add_fusion.mine_ref), channel_id=1, source_target_pairs={{0,1},{1,0},{2,3},{3,2},{4,5},{5,4},{6,7},{7,6},{8,9},{9,8},{10,11... | collective-permute-start | bytes 1572872 | tf_op jit(solution)/shard_map/ppermute | solution.py:504
  44.5 7.7 %collective-permute-start.11 = (bf16[896,128]{1,0:T(8,128)(2,1)S(1)}, bf16[896,128]{1,0:T(8,128)(2,1)S(1)}, u32[]{:S(2)}, u32[]{:S(2)}) collective-permute-start(bf16[896,128]{1,0:T(8,128)(2,1)S(1)} %add_convert_fusion.2), channel_id=1, source_target_pairs={{0,2},{1,3},{2,0},{3,1},{4,6},{5,7},{6,4},{7,5},{8,10},{9,11},{10,... | collective-permute-start | bytes 688136 | tf_op jit(solution)/shard_map/ppermute | solution.py:504
  52.3 1.7 %collective-permute-start.13 = (bf16[896,128]{1,0:T(8,128)(2,1)S(1)}, bf16[896,128]{1,0:T(8,128)(2,1)S(1)}, u32[]{:S(2)}, u32[]{:S(2)}) collective-permute-start(bf16[896,128]{1,0:T(8,128)(2,1)S(1)} %add_convert_fusion.1.ref), channel_id=1, source_target_pairs={{0,1},{1,0},{2,3},{3,2},{4,5},{5,4},{6,7},{7,6},{8,9},{9,8},{10,11... | collective-permute-start | bytes 688136 | tf_op jit(solution)/shard_map/ppermute | solution.py:504

commit v13 on v9

--- a/solution.py
+++ b/solution.py
@@ -220,16 +220,26 @@
     return copies
 
 
-def pack_kernel(og, two, one, act, first_ref, second_ref, og_v, two_v, one_v, act_v, turn_ref, sems):
+def pack_kernel(og, two, one, act, first_hbm, second_hbm, og_v, two_v, one_v, act_v, turn_ref, out_ref, sems, out_sems):
     copies = fetch(((og, og_v), (two, two_v), (one, one_v), (act, act_v)), sems)
+    sent = []
+
+    def send(k, hbm, at):
+        sent.append(pltpu.make_async_copy(out_ref.at[k], hbm.at[at : at + 256], out_sems.at[k]))
+        sent[-1].start()
+
     copies[0].wait()
-    first_ref[0:256] = og_v[...].astype(F32).reshape(256, 128).astype(BF16)
-    for k, (ref, out, at) in enumerate(((two_v, first_ref, 256), (one_v, first_ref, 512), (act_v, second_ref, 0))):
+    out_ref[0] = og_v[...].astype(F32).reshape(256, 128).astype(BF16)
+    send(0, first_hbm, 0)
+    for k, (ref, hbm, at) in enumerate(((two_v, first_hbm, 256), (one_v, first_hbm, 512), (act_v, second_hbm, 0))):
         copies[k + 1].wait()
         for x in range(4):
             for t in range(8):
                 turn_ref[k, pl.ds(64 * x + t, 8, stride=8), :] = ref[x, :, 128 * t : 128 * t + 128].astype(F32)
-        out[at : at + 256] = turn_ref[k].astype(BF16)
+        out_ref[k + 1] = turn_ref[k].astype(BF16)
+        send(k + 1, hbm, at)
+    for copy in sent:
+        copy.wait()
 
 
 def weight_kernel(wt, keep, w2, w1, kept_ref, mask_ref, d2_ref, d1_ref, wt_v, keep_v, w2_v, w1_v, sems):
@@ -519,7 +529,7 @@
         (shape((768, 128), BF16), shape((256, 128), BF16)),
         [
             vmem((8, 4, 8, 128), BF16), natural, natural, natural, vmem((3, 256, 128), F32),
-            pltpu.SemaphoreType.DMA((4,)),
+            vmem((4, 256, 128), BF16), pltpu.SemaphoreType.DMA((4,)), pltpu.SemaphoreType.DMA((4,)),
         ],
         0,
         56,
@@ -527,6 +537,7 @@
         (pre_two,),
         (pre_one,),
         (input_activation,),
+        out_space=pltpu.MemorySpace.HBM,
     )
     firsts = [first] + [rotate(first, "gx", s) for s in (1, 2, 3)]
     seconds = [second] + [rotate(second, "gx", s) for s in (1, 2, 3)]

time: 55.9 us -> 55.9 us (level)
  no operation moved by 1% of the time
where the time goes in v13:
time: 55.9 us; the launch traced here: 55.5 us
  Pallas kernels  17.9 us (32%)
  waiting for transfers between devices  17.4 us (31%)
  starting transfers between devices  15.3 us (27%)
  local copies, waits for them, and re-layouts  3.76 us (7%)
  between operations  0.77 us (1%)
    pallas_call x9, Pallas kernels, call(): pl.pallas_call(kernel, out_shape=out_shape, in_specs=spec, out_specs=jax....  17.9 us
    ppermute x6, waiting for transfers between devices, rotate(): return lax.ppermute(value, axis, [(i, (i + step) % n) for i in range(n)])  10.5 us
    ppermute x6, starting transfers between devices, rotate(): return lax.ppermute(value, axis, [(i, (i + step) % n) for i in range(n)])  10.1 us
    ppermute x7, waiting for transfers between devices, swap(): return lax.ppermute(value, axis, [(i, i ^ bit) for i in range(n)])  6.91 us
    ppermute x7, starting transfers between devices, swap(): return lax.ppermute(value, axis, [(i, i ^ bit) for i in range(n)])  4.56 us
    unnamed x12, local copies, waits for them, and re-layouts  3.76 us
  transfers between devices with their start and end apart: 14, of which 7 were waited for; matrix products, arithmetic and copies ran while one was open for 0% of the time, Pallas kernels for 27%

profile of v13, /device:TPU:0, one launch (start us, length us, event | category | flops | bytes accessed | tf_op | source)
XLA Modules:
  0.0 55.5 jit_solution(2742982585289549840)
XLA Ops:
  0.6 1.7 %shard_map.111 = (bf16[768,128]{1,0:T(8,128)(2,1)}, bf16[256,128]{1,0:T(8,128)(2,1)}) custom-call(bf16[8,4,8,128]{3,2,1,0:T(8,128)(2,1)} %og.1, bf16[4,8,1024]{2,1,0:T(8,128)(2,1)} %two.1, bf16[4,8,1024]{2,1,0:T(8,128)(2,1)} %one.1, bf16[4,8,1024]{2,1,0:T(8,128)(2,1)} %act.1), custom_call_target="tpu_custom_call" | custom-call | tf_op jit(solution)/shard_map/pallas_call | solution.py:200
  2.3 3.1 %collective-permute-start = (bf16[768,128]{1,0:T(8,128)(2,1)}, bf16[768,128]{1,0:T(8,128)(2,1)S(1)}, u32[]{:S(2)}, u32[]{:S(2)}) collective-permute-start(bf16[768,128]{1,0:T(8,128)(2,1)} %get-tuple-element.37.a0), channel_id=1, source_target_pairs={{0,4},{4,8},{8,12},{12,0},{1,5},{5,9},{9,13},{13,1},{2,6},{6,10},{... | collective-permute-start | bytes 589832 | tf_op jit(solution)/shard_map/ppermute | solution.py:503
  5.4 2.6 %collective-permute-start.1 = (bf16[768,128]{1,0:T(8,128)(2,1)}, bf16[768,128]{1,0:T(8,128)(2,1)S(1)}, u32[]{:S(2)}, u32[]{:S(2)}) collective-permute-start(bf16[768,128]{1,0:T(8,128)(2,1)} %get-tuple-element.37.a0), channel_id=1, source_target_pairs={{0,8},{4,12},{8,0},{12,4},{1,9},{5,13},{9,1},{13,5},{2,10},{6,14},... | collective-permute-start | bytes 589832 | tf_op jit(solution)/shard_map/ppermute | solution.py:503
  8.0 1.3 %collective-permute-start.2 = (bf16[768,128]{1,0:T(8,128)(2,1)}, bf16[768,128]{1,0:T(8,128)(2,1)S(1)}, u32[]{:S(2)}, u32[]{:S(2)}) collective-permute-start(bf16[768,128]{1,0:T(8,128)(2,1)} %get-tuple-element.37.a0), channel_id=1, source_target_pairs={{0,12},{4,0},{8,4},{12,8},{1,13},{5,1},{9,5},{13,9},{2,14},{6,2},{... | collective-permute-start | bytes 589832 | tf_op jit(solution)/shard_map/ppermute | solution.py:503
  9.3 0.7 %collective-permute-start.3 = (bf16[256,128]{1,0:T(8,128)(2,1)}, bf16[256,128]{1,0:T(8,128)(2,1)S(1)}, u32[]{:S(2)}, u32[]{:S(2)}) collective-permute-start(bf16[256,128]{1,0:T(8,128)(2,1)} %get-tuple-element.52.i0), channel_id=1, source_target_pairs={{0,4},{4,8},{8,12},{12,0},{1,5},{5,9},{9,13},{13,1},{2,6},{6,10},{... | collective-permute-start | bytes 196616 | tf_op jit(solution)/shard_map/ppermute | solution.py:503
  10.0 0.3 collective-permute-start.4
  10.3 3.1 %collective-permute-done.a1 = bf16[768,128]{1,0:T(8,128)(2,1)S(1)} collective-permute-done((bf16[768,128]{1,0:T(8,128)(2,1)}, bf16[768,128]{1,0:T(8,128)(2,1)S(1)}, u32[]{:S(2)}, u32[]{:S(2)}) %collective-permute-start) | collective-permute-done | bytes 196640 | tf_op jit(solution)/shard_map/ppermute | solution.py:503
  13.5 2.1 %collective-permute-start.5 = (bf16[256,128]{1,0:T(8,128)(2,1)}, bf16[256,128]{1,0:T(8,128)(2,1)S(1)}, u32[]{:S(2)}, u32[]{:S(2)}) collective-permute-start(bf16[256,128]{1,0:T(8,128)(2,1)} %get-tuple-element.52.i0), channel_id=1, source_target_pairs={{0,12},{4,0},{8,4},{12,8},{1,13},{5,1},{9,5},{13,9},{2,14},{6,2},{... | collective-permute-start | bytes 196616 | tf_op jit(solution)/shard_map/ppermute | solution.py:503
  15.5 0.1 pad_add_fusion.at_ref
  15.6 1.0 %copy-done = bf16[512,512]{1,0:T(8,128)(2,1)S(1)} copy-done((bf16[512,512]{1,0:T(8,128)(2,1)S(1)}, bf16[512,512]{1,0:T(8,128)(2,1)}, u32[]{:S(2)}) %copy-start) | copy-done | bytes 524312
  16.6 1.0 %copy-done.1 = bf16[27,64,64]{2,1,0:T(8,128)(2,1)S(1)} copy-done((bf16[27,64,64]{2,1,0:T(8,128)(2,1)S(1)}, bf16[27,64,64]{2,1,0:T(8,128)(2,1)}, u32[]{:S(2)}) %copy-start.1) | copy-done | bytes 221208
  17.7 1.0 %copy-done.2 = bf16[27,64,64]{2,1,0:T(8,128)(2,1)S(1)} copy-done((bf16[27,64,64]{2,1,0:T(8,128)(2,1)S(1)}, bf16[27,64,64]{2,1,0:T(8,128)(2,1)}, u32[]{:S(2)}) %copy-start.2) | copy-done | bytes 221208
  18.7 0.7 %copy-done.5 = s32[8,8]{1,0:T(8,128)S(1)} copy-done((s32[8,8]{1,0:T(8,128)S(1)}, s32[8,8]{1,0:T(8,128)}, u32[]{:S(2)}) %copy-start.5) | copy-done | bytes 280
  19.4 1.4 %shard_map.112 = (bf16[512,512]{1,0:T(8,128)(2,1)S(1)}, bf16[512,512]{1,0:T(8,128)(2,1)S(1)}, bf16[9,128,384]{2,1,0:T(8,128)(2,1)S(1)}, bf16[9,128,384]{2,1,0:T(8,128)(2,1)S(1)}) custom-call(bf16[512,512]{1,0:T(8,128)(2,1)S(1)} %copy-done, s32[8,8]{1,0:T(8,128)S(1)} %copy-done.5, bf16[27,64,64]{2,1,0:T(8,128)(2,1)S(1)} %copy-done.1, ...), custom_call_target="tpu_custom_call" | custom-call | flops 10000000 | bytes 966912 | tf_op jit(solution)/shard_map/pallas_call | solution.py:200
  20.8 1.2 %collective-permute-done.1.a2 = bf16[768,128]{1,0:T(8,128)(2,1)S(1)} collective-permute-done((bf16[768,128]{1,0:T(8,128)(2,1)}, bf16[768,128]{1,0:T(8,128)(2,1)S(1)}, u32[]{:S(2)}, u32[]{:S(2)}) %collective-permute-start.1) | collective-permute-done | bytes 196640 | tf_op jit(solution)/shard_map/ppermute | solution.py:503
  21.9 0.0 collective-permute-done.2.a3
  21.9 0.0 copy-done.3
  21.9 1.3 %shard_map.113 = (bf16[8,2,64,128]{3,2,1,0:T(8,128)(2,1)S(1)}, bf16[16,64,128]{2,1,0:T(8,128)(2,1)S(1)}, bf16[8,2,48,128]{3,2,1,0:T(8,128)(2,1)S(1)}, bf16[8,2,4...) custom-call(s32[2]{0:T(128)S(1)} %pad_add_fusion.at_ref, ...), custom_call_target="tpu_custom_call" | custom-call | flops 268435456 | bytes 1835016 | tf_op jit(solution)/shard_map/pallas_call | solution.py:200
  23.3 0.0 collective-permute-done.3.i1
  23.3 6.2 %collective-permute-done.4.i2 = bf16[256,128]{1,0:T(8,128)(2,1)S(1)} collective-permute-done((bf16[256,128]{1,0:T(8,128)(2,1)}, bf16[256,128]{1,0:T(8,128)(2,1)S(1)}, u32[]{:S(2)}, u32[]{:S(2)}) %collective-permute-start.4) | collective-permute-done | bytes 65568 | tf_op jit(solution)/shard_map/ppermute | solution.py:503
  29.5 0.0 collective-permute-done.5.i3
  29.5 0.0 collective-permute-start.6
  29.5 0.5 collective-permute-start.7
  30.0 0.7 %collective-permute-start.8 = (bf16[8,2,48,128]{3,2,1,0:T(8,128)(2,1)S(1)}, bf16[8,2,48,128]{3,2,1,0:T(8,128)(2,1)S(1)}, u32[]{:S(2)}, u32[]{:S(2)}) collective-permute-start(bf16[8,2,48,128]{3,2,1,0:T(8,128)(2,1)S(1)} %get-tuple-element.51), channel_id=1, source_target_pairs={{1,2},{2,1},{5,6},{6,5},{9,10},{10,9},{13,14},{14,13},{17,18},{18,... | collective-permute-start | bytes 589832 | tf_op jit(solution)/shard_map/ppermute | solution.py:582
  30.7 0.4 collective-permute-done.6
  31.1 0.1 add_convert_fusion
  31.1 2.6 %collective-permute-start.9 = (bf16[1024,128]{1,0:T(8,128)(2,1)S(1)}, bf16[1024,128]{1,0:T(8,128)(2,1)S(1)}, u32[]{:S(2)}, u32[]{:S(2)}) collective-permute-start(bf16[1024,128]{1,0:T(8,128)(2,1)S(1)} %add_convert_fusion), channel_id=1, source_target_pairs={{0,2},{1,3},{2,0},{3,1},{4,6},{5,7},{6,4},{7,5},{8,10},{9,11},{10,... | collective-permute-start | bytes 786440 | tf_op jit(solution)/shard_map/ppermute | solution.py:508
  33.7 3.0 %shard_map.114 = (f32[16,96,128]{2,1,0:T(8,128)S(1)}, f32[896,128]{1,0:T(8,128)S(1)}) custom-call(bf16[16,64,128]{2,1,0:T(8,128)(2,1)S(1)} %bitcast.7, bf16[16,64,128]{2,1,0:T(8,128)(2,1)S(1)} %get-tuple-element.46.one_ref, bf16[9,128,384]{2,1,0:T(8,128)(2,1)S(1)} %get-tuple-element.47.w_ref), custom_call_target="tpu_custom_call" | custom-call | flops 1811939328 | bytes 1409024 | tf_op jit(solution)/shard_map/pallas_call | solution.py:200
  36.8 0.0 collective-permute-done.7
  36.8 0.0 collective-permute-done.8
  36.8 0.0 copy-done.4
  36.8 3.9 %shard_map.115 = (f32[896,128]{1,0:T(8,128)S(1)}, bf16[896,128]{1,0:T(8,128)(2,1)S(1)}, bf16[20,96,384]{2,1,0:T(8,128)(2,1)S(1)}) custom-call(s32[2]{0:T(128)S(1)} %pad_add_fusion.at_ref, f32[16,96,128]{2,1,0:T(8,128)S(1)} %get-tuple-element.48.acc_ref, f32[896,128]{1,0:T(8,128)S(1)} %get-tuple-element.49.sums_ref, ...), custom_call_target="tpu_custom_call" | custom-call | flops 796262400 | bytes 3047432 | tf_op jit(solution)/shard_map/pallas_call | solution.py:200
  40.7 2.2 %collective-permute-done.9 = bf16[1024,128]{1,0:T(8,128)(2,1)S(1)} collective-permute-done((bf16[1024,128]{1,0:T(8,128)(2,1)S(1)}, bf16[1024,128]{1,0:T(8,128)(2,1)S(1)}, u32[]{:S(2)}, u32[]{:S(2)}) %collective-permute-start.9) | collective-permute-done | bytes 262176 | tf_op jit(solution)/shard_map/ppermute | solution.py:508
  42.8 0.1 convert_add_fusion.mine_ref
  42.9 0.1 collective-permute-start.10
  43.0 0.5 collective-permute-start.12
  43.5 1.0 %collective-permute-done.10 = bf16[896,128]{1,0:T(8,128)(2,1)S(1)} collective-permute-done((bf16[896,128]{1,0:T(8,128)(2,1)S(1)}, bf16[896,128]{1,0:T(8,128)(2,1)S(1)}, u32[]{:S(2)}, u32[]{:S(2)}) %collective-permute-start.10) | collective-permute-done | bytes 229408 | tf_op jit(solution)/shard_map/ppermute | solution.py:508
  44.4 0.1 add_convert_fusion.2
  44.5 0.8 %collective-permute-start.11 = (bf16[896,128]{1,0:T(8,128)(2,1)S(1)}, bf16[896,128]{1,0:T(8,128)(2,1)S(1)}, u32[]{:S(2)}, u32[]{:S(2)}) collective-permute-start(bf16[896,128]{1,0:T(8,128)(2,1)S(1)} %add_convert_fusion.2), channel_id=1, source_target_pairs={{0,2},{1,3},{2,0},{3,1},{4,6},{5,7},{6,4},{7,5},{8,10},{9,11},{10,... | collective-permute-start | bytes 688136 | tf_op jit(solution)/shard_map/ppermute | solution.py:508
  45.3 1.8 %shard_map.117 = bf16[4,8,1024]{2,1,0:T(8,128)(2,1)} custom-call(s32[2]{0:T(128)S(1)} %pad_add_fusion.at_ref, bf16[20,96,384]{2,1,0:T(8,128)(2,1)S(1)} %get-tuple-element.61.outer_ref, bf16[9,128,384]{2,1,0:T(8,128)(2,1)S(1)} %get-tuple-element.62.w_ref), custom_call_target="tpu_custom_call" | custom-call | flops 226492416 | bytes 2359304 | tf_op jit(solution)/shard_map/pallas_call | solution.py:200
  47.1 0.0 collective-permute-done.12.other_ref
  47.2 1.6 %shard_map.116 = f32[512,512]{1,0:T(8,128)} custom-call(s32[2]{0:T(128)S(1)} %pad_add_fusion.at_ref, f32[1024,128]{1,0:T(8,128)S(1)} %convert_add_fusion.mine_ref, f32[1024,128]{1,0:T(8,128)S(1)} %collective-permute-done.12.other_ref), custom_call_target="tpu_custom_call" | custom-call | flops 10000000 | bytes 1048584 | tf_op jit(solution)/shard_map/pallas_call | solution.py:200
  48.8 3.4 %collective-permute-done.11 = bf16[896,128]{1,0:T(8,128)(2,1)S(1)} collective-permute-done((bf16[896,128]{1,0:T(8,128)(2,1)S(1)}, bf16[896,128]{1,0:T(8,128)(2,1)S(1)}, u32[]{:S(2)}, u32[]{:S(2)}) %collective-permute-start.11) | collective-permute-done | bytes 229408 | tf_op jit(solution)/shard_map/ppermute | solution.py:508
  52.2 0.1 add_convert_fusion.1.ref
  52.3 0.1 collective-permute-start.13
  52.4 1.6 %shard_map.118 = (f32[27,64,64]{2,1,0:T(8,128)}, f32[27,64,64]{2,1,0:T(8,128)}) custom-call(s32[2]{0:T(128)S(1)} %pad_add_fusion.at_ref, bf16[896,128]{1,0:T(8,128)(2,1)S(1)} %add_convert_fusion.1.ref), custom_call_target="tpu_custom_call" | custom-call | flops 100000000 | bytes 229384 | tf_op jit(solution)/shard_map/pallas_call | solution.py:200
  53.9 0.0 collective-permute-done.13.ref
  54.0 1.6 %shard_map.119 = (f32[27,64,64]{2,1,0:T(8,128)}, f32[27,64,64]{2,1,0:T(8,128)}) custom-call(s32[2]{0:T(128)S(1)} %pad_add_fusion.at_ref, bf16[896,128]{1,0:T(8,128)(2,1)S(1)} %collective-permute-done.13.ref, f32[27,64,64]{2,1,0:T(8,128)} %get-tuple-element.65.one_in, ...), custom_call_target="tpu_custom_call", output_to_operand_aliasing={{0}: (2, {}), {1}: (3, {})} | custom-call | tf_op jit(solution)/shard_map/pallas_call | solution.py:200
  (6 shorter events, 0.0 us)
Async XLA Ops:
  2.3 11.2 %collective-permute-start = (bf16[768,128]{1,0:T(8,128)(2,1)}, bf16[768,128]{1,0:T(8,128)(2,1)S(1)}, u32[]{:S(2)}, u32[]{:S(2)}) collective-permute-start(bf16[768,128]{1,0:T(8,128)(2,1)} %get-tuple-element.37.a0), channel_id=1, source_target_pairs={{0,4},{4,8},{8,12},{12,0},{1,5},{5,9},{9,13},{13,1},{2,6},{6,10},{... | collective-permute-start | bytes 589832 | tf_op jit(solution)/shard_map/ppermute | solution.py:503
  5.4 16.6 %collective-permute-start.1 = (bf16[768,128]{1,0:T(8,128)(2,1)}, bf16[768,128]{1,0:T(8,128)(2,1)S(1)}, u32[]{:S(2)}, u32[]{:S(2)}) collective-permute-start(bf16[768,128]{1,0:T(8,128)(2,1)} %get-tuple-element.37.a0), channel_id=1, source_target_pairs={{0,8},{4,12},{8,0},{12,4},{1,9},{5,13},{9,1},{13,5},{2,10},{6,14},... | collective-permute-start | bytes 589832 | tf_op jit(solution)/shard_map/ppermute | solution.py:503
  8.0 14.0 %collective-permute-start.2 = (bf16[768,128]{1,0:T(8,128)(2,1)}, bf16[768,128]{1,0:T(8,128)(2,1)S(1)}, u32[]{:S(2)}, u32[]{:S(2)}) collective-permute-start(bf16[768,128]{1,0:T(8,128)(2,1)} %get-tuple-element.37.a0), channel_id=1, source_target_pairs={{0,12},{4,0},{8,4},{12,8},{1,13},{5,1},{9,5},{13,9},{2,14},{6,2},{... | collective-permute-start | bytes 589832 | tf_op jit(solution)/shard_map/ppermute | solution.py:503
  9.3 14.0 %collective-permute-start.3 = (bf16[256,128]{1,0:T(8,128)(2,1)}, bf16[256,128]{1,0:T(8,128)(2,1)S(1)}, u32[]{:S(2)}, u32[]{:S(2)}) collective-permute-start(bf16[256,128]{1,0:T(8,128)(2,1)} %get-tuple-element.52.i0), channel_id=1, source_target_pairs={{0,4},{4,8},{8,12},{12,0},{1,5},{5,9},{9,13},{13,1},{2,6},{6,10},{... | collective-permute-start | bytes 196616 | tf_op jit(solution)/shard_map/ppermute | solution.py:503
  10.0 19.5 %collective-permute-start.4 = (bf16[256,128]{1,0:T(8,128)(2,1)}, bf16[256,128]{1,0:T(8,128)(2,1)S(1)}, u32[]{:S(2)}, u32[]{:S(2)}) collective-permute-start(bf16[256,128]{1,0:T(8,128)(2,1)} %get-tuple-element.52.i0), channel_id=1, source_target_pairs={{0,8},{4,12},{8,0},{12,4},{1,9},{5,13},{9,1},{13,5},{2,10},{6,14},... | collective-permute-start | bytes 196616 | tf_op jit(solution)/shard_map/ppermute | solution.py:503
  13.5 16.1 %collective-permute-start.5 = (bf16[256,128]{1,0:T(8,128)(2,1)}, bf16[256,128]{1,0:T(8,128)(2,1)S(1)}, u32[]{:S(2)}, u32[]{:S(2)}) collective-permute-start(bf16[256,128]{1,0:T(8,128)(2,1)} %get-tuple-element.52.i0), channel_id=1, source_target_pairs={{0,12},{4,0},{8,4},{12,8},{1,13},{5,1},{9,5},{13,9},{2,14},{6,2},{... | collective-permute-start | bytes 196616 | tf_op jit(solution)/shard_map/ppermute | solution.py:503
  15.6 1.0 %copy-start = (bf16[512,512]{1,0:T(8,128)(2,1)S(1)}, bf16[512,512]{1,0:T(8,128)(2,1)}, u32[]{:S(2)}) copy-start(bf16[512,512]{1,0:T(8,128)(2,1)} %wt.1) | copy-start | bytes 1572868
  16.6 1.0 %copy-start.1 = (bf16[27,64,64]{2,1,0:T(8,128)(2,1)S(1)}, bf16[27,64,64]{2,1,0:T(8,128)(2,1)}, u32[]{:S(2)}) copy-start(bf16[27,64,64]{2,1,0:T(8,128)(2,1)} %w2.1) | copy-start | bytes 663556
  17.7 1.0 %copy-start.2 = (bf16[27,64,64]{2,1,0:T(8,128)(2,1)S(1)}, bf16[27,64,64]{2,1,0:T(8,128)(2,1)}, u32[]{:S(2)}) copy-start(bf16[27,64,64]{2,1,0:T(8,128)(2,1)} %w1.1) | copy-start | bytes 663556
  18.7 0.7 %copy-start.5 = (s32[8,8]{1,0:T(8,128)S(1)}, s32[8,8]{1,0:T(8,128)}, u32[]{:S(2)}) copy-start(s32[8,8]{1,0:T(8,128)} %keep.1) | copy-start | bytes 772
  19.4 2.6 %copy-start.3 = (bf16[768,128]{1,0:T(8,128)(2,1)S(1)}, bf16[768,128]{1,0:T(8,128)(2,1)}, u32[]{:S(2)}) copy-start(bf16[768,128]{1,0:T(8,128)(2,1)} %get-tuple-element.37.a0) | copy-start | bytes 589828
  29.5 1.5 %collective-permute-start.6 = (bf16[1024,128]{1,0:T(8,128)(2,1)S(1)}, bf16[1024,128]{1,0:T(8,128)(2,1)S(1)}, u32[]{:S(2)}, u32[]{:S(2)}) collective-permute-start(bf16[1024,128]{1,0:T(8,128)(2,1)S(1)} %get-tuple-element.45), channel_id=1, source_target_pairs={{0,1},{1,0},{2,3},{3,2},{4,5},{5,4},{6,7},{7,6},{8,9},{9,8},{10,11... | collective-permute-start | bytes 786440 | tf_op jit(solution)/shard_map/ppermute | solution.py:508
  29.5 7.2 %collective-permute-start.7 = (bf16[8,2,48,128]{3,2,1,0:T(8,128)(2,1)S(1)}, bf16[8,2,48,128]{3,2,1,0:T(8,128)(2,1)S(1)}, u32[]{:S(2)}, u32[]{:S(2)}) collective-permute-start(bf16[8,2,48,128]{3,2,1,0:T(8,128)(2,1)S(1)} %get-tuple-element.50), channel_id=1, source_target_pairs={{0,1},{1,0},{2,3},{3,2},{4,5},{5,4},{6,7},{7,6},{8,9},{9,8},{10,11... | collective-permute-start | bytes 589832 | tf_op jit(solution)/shard_map/ppermute | solution.py:508
  30.0 6.7 %collective-permute-start.8 = (bf16[8,2,48,128]{3,2,1,0:T(8,128)(2,1)S(1)}, bf16[8,2,48,128]{3,2,1,0:T(8,128)(2,1)S(1)}, u32[]{:S(2)}, u32[]{:S(2)}) collective-permute-start(bf16[8,2,48,128]{3,2,1,0:T(8,128)(2,1)S(1)} %get-tuple-element.51), channel_id=1, source_target_pairs={{1,2},{2,1},{5,6},{6,5},{9,10},{10,9},{13,14},{14,13},{17,18},{18,... | collective-permute-start | bytes 589832 | tf_op jit(solution)/shard_map/ppermute | solution.py:582
  31.1 11.7 %collective-permute-start.9 = (bf16[1024,128]{1,0:T(8,128)(2,1)S(1)}, bf16[1024,128]{1,0:T(8,128)(2,1)S(1)}, u32[]{:S(2)}, u32[]{:S(2)}) collective-permute-start(bf16[1024,128]{1,0:T(8,128)(2,1)S(1)} %add_convert_fusion), channel_id=1, source_target_pairs={{0,2},{1,3},{2,0},{3,1},{4,6},{5,7},{6,4},{7,5},{8,10},{9,11},{10,... | collective-permute-start | bytes 786440 | tf_op jit(solution)/shard_map/ppermute | solution.py:508
  33.7 3.1 %copy-start.4 = (bf16[256,128]{1,0:T(8,128)(2,1)S(1)}, bf16[256,128]{1,0:T(8,128)(2,1)}, u32[]{:S(2)}) copy-start(bf16[256,128]{1,0:T(8,128)(2,1)} %get-tuple-element.52.i0) | copy-start | bytes 196612
  42.9 1.6 %collective-permute-start.10 = (bf16[896,128]{1,0:T(8,128)(2,1)S(1)}, bf16[896,128]{1,0:T(8,128)(2,1)S(1)}, u32[]{:S(2)}, u32[]{:S(2)}) collective-permute-start(bf16[896,128]{1,0:T(8,128)(2,1)S(1)} %get-tuple-element.59), channel_id=1, source_target_pairs={{0,1},{1,0},{2,3},{3,2},{4,5},{5,4},{6,7},{7,6},{8,9},{9,8},{10,11... | collective-permute-start | bytes 688136 | tf_op jit(solution)/shard_map/ppermute | solution.py:508
  43.0 4.2 %collective-permute-start.12 = (f32[1024,128]{1,0:T(8,128)S(1)}, f32[1024,128]{1,0:T(8,128)S(1)}, u32[]{:S(2)}, u32[]{:S(2)}) collective-permute-start(f32[1024,128]{1,0:T(8,128)S(1)} %convert_add_fusion.mine_ref), channel_id=1, source_target_pairs={{0,1},{1,0},{2,3},{3,2},{4,5},{5,4},{6,7},{7,6},{8,9},{9,8},{10,11... | collective-permute-start | bytes 1572872 | tf_op jit(solution)/shard_map/ppermute | solution.py:508
  44.5 7.7 %collective-permute-start.11 = (bf16[896,128]{1,0:T(8,128)(2,1)S(1)}, bf16[896,128]{1,0:T(8,128)(2,1)S(1)}, u32[]{:S(2)}, u32[]{:S(2)}) collective-permute-start(bf16[896,128]{1,0:T(8,128)(2,1)S(1)} %add_convert_fusion.2), channel_id=1, source_target_pairs={{0,2},{1,3},{2,0},{3,1},{4,6},{5,7},{6,4},{7,5},{8,10},{9,11},{10,... | collective-permute-start | bytes 688136 | tf_op jit(solution)/shard_map/ppermute | solution.py:508
  52.3 1.7 %collective-permute-start.13 = (bf16[896,128]{1,0:T(8,128)(2,1)S(1)}, bf16[896,128]{1,0:T(8,128)(2,1)S(1)}, u32[]{:S(2)}, u32[]{:S(2)}) collective-permute-start(bf16[896,128]{1,0:T(8,128)(2,1)S(1)} %add_convert_fusion.1.ref), channel_id=1, source_target_pairs={{0,1},{1,0},{2,3},{3,2},{4,5},{5,4},{6,7},{7,6},{8,9},{9,8},{10,11... | collective-permute-start | bytes 688136 | tf_op jit(solution)/shard_map/ppermute | solution.py:508

commit v14 on v8

--- a/solution.py
+++ b/solution.py
@@ -445,7 +445,7 @@
 
 def unpack(ref, at, out_ref):
     for m in range(7):
-        block = ref[at + 64 * m : at + 64 * m + 64]
+        block = ref[at + 64 * m : at + 64 * m + 64].astype(F32)
         out_ref[2 * m] = block[:, 0:64]
         out_ref[2 * m + 1] = block[:, 64:128]
 
@@ -619,7 +619,7 @@
         grad_kernel, shape((4, 8, 1024), BF16), [vmem((256, 128), F32)], 2 * 128 * 3456 * 256, 12, at, outer, d1
     )
     away, grad_w_trans, grad_in = lax.optimization_barrier((away, grad_w_trans, grad_in))
-    mine = mine.astype(F32) + away.astype(F32)
+    mine = (mine.astype(F32) + away.astype(F32)).astype(BF16)
     other = swap(mine, "gy", 1)
     taps = shape((27, 64, 64), F32)
     half = shape((14, 64, 64), F32)

time: 56.3 us -> 56 us (level)
  no operation moved by 1% of the time
where the time goes in v14:
time: 56 us; the launch traced here: 55.6 us
  waiting for transfers between devices  18.8 us (34%)
  Pallas kernels  16.7 us (30%)
  starting transfers between devices  15.3 us (27%)
  local copies, waits for them, and re-layouts  3.76 us (7%)
  between operations  0.77 us (1%)
    pallas_call x9, Pallas kernels, call(): pl.pallas_call(kernel, out_shape=out_shape, in_specs=spec, out_specs=jax....  16.7 us
    ppermute x6, waiting for transfers between devices, rotate(): return lax.ppermute(value, axis, [(i, (i + step) % n) for i in range(n)])  10.5 us
    ppermute x6, starting transfers between devices, rotate(): return lax.ppermute(value, axis, [(i, (i + step) % n) for i in range(n)])  10.1 us
    ppermute x7, waiting for transfers between devices, swap(): return lax.ppermute(value, axis, [(i, i ^ bit) for i in range(n)])  8.24 us
    ppermute x7, starting transfers between devices, swap(): return lax.ppermute(value, axis, [(i, i ^ bit) for i in range(n)])  4.56 us
    unnamed x12, local copies, waits for them, and re-layouts  3.76 us
  transfers between devices with their start and end apart: 14, of which 8 were waited for; matrix products, arithmetic and copies ran while one was open for 0% of the time, Pallas kernels for 24%

profile of v14, /device:TPU:0, one launch (start us, length us, event | category | flops | bytes accessed | tf_op | source)
XLA Modules:
  0.0 55.6 jit_solution(12642573531463975538)
XLA Ops:
  0.6 1.7 %shard_map.111 = (bf16[768,128]{1,0:T(8,128)(2,1)}, bf16[256,128]{1,0:T(8,128)(2,1)}) custom-call(bf16[8,4,8,128]{3,2,1,0:T(8,128)(2,1)} %og.1, bf16[4,8,1024]{2,1,0:T(8,128)(2,1)} %two.1, bf16[4,8,1024]{2,1,0:T(8,128)(2,1)} %one.1, bf16[4,8,1024]{2,1,0:T(8,128)(2,1)} %act.1), custom_call_target="tpu_custom_call" | custom-call | tf_op jit(solution)/shard_map/pallas_call | solution.py:200
  2.3 3.1 %collective-permute-start = (bf16[768,128]{1,0:T(8,128)(2,1)}, bf16[768,128]{1,0:T(8,128)(2,1)S(1)}, u32[]{:S(2)}, u32[]{:S(2)}) collective-permute-start(bf16[768,128]{1,0:T(8,128)(2,1)} %get-tuple-element.37.a0), channel_id=1, source_target_pairs={{0,4},{4,8},{8,12},{12,0},{1,5},{5,9},{9,13},{13,1},{2,6},{6,10},{... | collective-permute-start | bytes 589832 | tf_op jit(solution)/shard_map/ppermute | solution.py:498
  5.4 2.6 %collective-permute-start.1 = (bf16[768,128]{1,0:T(8,128)(2,1)}, bf16[768,128]{1,0:T(8,128)(2,1)S(1)}, u32[]{:S(2)}, u32[]{:S(2)}) collective-permute-start(bf16[768,128]{1,0:T(8,128)(2,1)} %get-tuple-element.37.a0), channel_id=1, source_target_pairs={{0,8},{4,12},{8,0},{12,4},{1,9},{5,13},{9,1},{13,5},{2,10},{6,14},... | collective-permute-start | bytes 589832 | tf_op jit(solution)/shard_map/ppermute | solution.py:498
  8.0 1.3 %collective-permute-start.2 = (bf16[768,128]{1,0:T(8,128)(2,1)}, bf16[768,128]{1,0:T(8,128)(2,1)S(1)}, u32[]{:S(2)}, u32[]{:S(2)}) collective-permute-start(bf16[768,128]{1,0:T(8,128)(2,1)} %get-tuple-element.37.a0), channel_id=1, source_target_pairs={{0,12},{4,0},{8,4},{12,8},{1,13},{5,1},{9,5},{13,9},{2,14},{6,2},{... | collective-permute-start | bytes 589832 | tf_op jit(solution)/shard_map/ppermute | solution.py:498
  9.3 0.7 %collective-permute-start.3 = (bf16[256,128]{1,0:T(8,128)(2,1)}, bf16[256,128]{1,0:T(8,128)(2,1)S(1)}, u32[]{:S(2)}, u32[]{:S(2)}) collective-permute-start(bf16[256,128]{1,0:T(8,128)(2,1)} %get-tuple-element.52.i0), channel_id=1, source_target_pairs={{0,4},{4,8},{8,12},{12,0},{1,5},{5,9},{9,13},{13,1},{2,6},{6,10},{... | collective-permute-start | bytes 196616 | tf_op jit(solution)/shard_map/ppermute | solution.py:498
  10.0 0.3 collective-permute-start.4
  10.3 3.1 %collective-permute-done.a1 = bf16[768,128]{1,0:T(8,128)(2,1)S(1)} collective-permute-done((bf16[768,128]{1,0:T(8,128)(2,1)}, bf16[768,128]{1,0:T(8,128)(2,1)S(1)}, u32[]{:S(2)}, u32[]{:S(2)}) %collective-permute-start) | collective-permute-done | bytes 196640 | tf_op jit(solution)/shard_map/ppermute | solution.py:498
  13.5 2.1 %collective-permute-start.5 = (bf16[256,128]{1,0:T(8,128)(2,1)}, bf16[256,128]{1,0:T(8,128)(2,1)S(1)}, u32[]{:S(2)}, u32[]{:S(2)}) collective-permute-start(bf16[256,128]{1,0:T(8,128)(2,1)} %get-tuple-element.52.i0), channel_id=1, source_target_pairs={{0,12},{4,0},{8,4},{12,8},{1,13},{5,1},{9,5},{13,9},{2,14},{6,2},{... | collective-permute-start | bytes 196616 | tf_op jit(solution)/shard_map/ppermute | solution.py:498
  15.5 0.1 pad_add_fusion.at_ref
  15.6 1.0 %copy-done = bf16[512,512]{1,0:T(8,128)(2,1)S(1)} copy-done((bf16[512,512]{1,0:T(8,128)(2,1)S(1)}, bf16[512,512]{1,0:T(8,128)(2,1)}, u32[]{:S(2)}) %copy-start) | copy-done | bytes 524312
  16.6 1.0 %copy-done.1 = bf16[27,64,64]{2,1,0:T(8,128)(2,1)S(1)} copy-done((bf16[27,64,64]{2,1,0:T(8,128)(2,1)S(1)}, bf16[27,64,64]{2,1,0:T(8,128)(2,1)}, u32[]{:S(2)}) %copy-start.1) | copy-done | bytes 221208
  17.7 1.0 %copy-done.2 = bf16[27,64,64]{2,1,0:T(8,128)(2,1)S(1)} copy-done((bf16[27,64,64]{2,1,0:T(8,128)(2,1)S(1)}, bf16[27,64,64]{2,1,0:T(8,128)(2,1)}, u32[]{:S(2)}) %copy-start.2) | copy-done | bytes 221208
  18.7 0.7 %copy-done.5 = s32[8,8]{1,0:T(8,128)S(1)} copy-done((s32[8,8]{1,0:T(8,128)S(1)}, s32[8,8]{1,0:T(8,128)}, u32[]{:S(2)}) %copy-start.5) | copy-done | bytes 280
  19.4 1.4 %shard_map.112 = (bf16[512,512]{1,0:T(8,128)(2,1)S(1)}, bf16[512,512]{1,0:T(8,128)(2,1)S(1)}, bf16[9,128,384]{2,1,0:T(8,128)(2,1)S(1)}, bf16[9,128,384]{2,1,0:T(8,128)(2,1)S(1)}) custom-call(bf16[512,512]{1,0:T(8,128)(2,1)S(1)} %copy-done, s32[8,8]{1,0:T(8,128)S(1)} %copy-done.5, bf16[27,64,64]{2,1,0:T(8,128)(2,1)S(1)} %copy-done.1, ...), custom_call_target="tpu_custom_call" | custom-call | flops 10000000 | bytes 966912 | tf_op jit(solution)/shard_map/pallas_call | solution.py:200
  20.8 1.2 %collective-permute-done.1.a2 = bf16[768,128]{1,0:T(8,128)(2,1)S(1)} collective-permute-done((bf16[768,128]{1,0:T(8,128)(2,1)}, bf16[768,128]{1,0:T(8,128)(2,1)S(1)}, u32[]{:S(2)}, u32[]{:S(2)}) %collective-permute-start.1) | collective-permute-done | bytes 196640 | tf_op jit(solution)/shard_map/ppermute | solution.py:498
  21.9 0.0 collective-permute-done.2.a3
  21.9 0.0 copy-done.3
  22.0 1.3 %shard_map.113 = (bf16[8,2,64,128]{3,2,1,0:T(8,128)(2,1)S(1)}, bf16[16,64,128]{2,1,0:T(8,128)(2,1)S(1)}, bf16[8,2,48,128]{3,2,1,0:T(8,128)(2,1)S(1)}, bf16[8,2,4...) custom-call(s32[2]{0:T(128)S(1)} %pad_add_fusion.at_ref, ...), custom_call_target="tpu_custom_call" | custom-call | flops 268435456 | bytes 1835016 | tf_op jit(solution)/shard_map/pallas_call | solution.py:200
  23.3 0.0 collective-permute-done.3.i1
  23.3 6.2 %collective-permute-done.4.i2 = bf16[256,128]{1,0:T(8,128)(2,1)S(1)} collective-permute-done((bf16[256,128]{1,0:T(8,128)(2,1)}, bf16[256,128]{1,0:T(8,128)(2,1)S(1)}, u32[]{:S(2)}, u32[]{:S(2)}) %collective-permute-start.4) | collective-permute-done | bytes 65568 | tf_op jit(solution)/shard_map/ppermute | solution.py:498
  29.5 0.0 collective-permute-done.5.i3
  29.5 0.0 collective-permute-start.6
  29.5 0.5 collective-permute-start.7
  30.0 0.7 %collective-permute-start.8 = (bf16[8,2,48,128]{3,2,1,0:T(8,128)(2,1)S(1)}, bf16[8,2,48,128]{3,2,1,0:T(8,128)(2,1)S(1)}, u32[]{:S(2)}, u32[]{:S(2)}) collective-permute-start(bf16[8,2,48,128]{3,2,1,0:T(8,128)(2,1)S(1)} %get-tuple-element.51), channel_id=1, source_target_pairs={{1,2},{2,1},{5,6},{6,5},{9,10},{10,9},{13,14},{14,13},{17,18},{18,... | collective-permute-start | bytes 589832 | tf_op jit(solution)/shard_map/ppermute | solution.py:576
  30.7 0.4 collective-permute-done.6
  31.1 0.1 add_convert_fusion
  31.1 2.6 %collective-permute-start.9 = (bf16[1024,128]{1,0:T(8,128)(2,1)S(1)}, bf16[1024,128]{1,0:T(8,128)(2,1)S(1)}, u32[]{:S(2)}, u32[]{:S(2)}) collective-permute-start(bf16[1024,128]{1,0:T(8,128)(2,1)S(1)} %add_convert_fusion), channel_id=1, source_target_pairs={{0,2},{1,3},{2,0},{3,1},{4,6},{5,7},{6,4},{7,5},{8,10},{9,11},{10,... | collective-permute-start | bytes 786440 | tf_op jit(solution)/shard_map/ppermute | solution.py:503
  33.7 3.0 %shard_map.114 = (f32[16,96,128]{2,1,0:T(8,128)S(1)}, f32[896,128]{1,0:T(8,128)S(1)}) custom-call(bf16[16,64,128]{2,1,0:T(8,128)(2,1)S(1)} %bitcast.7, bf16[16,64,128]{2,1,0:T(8,128)(2,1)S(1)} %get-tuple-element.46.one_ref, bf16[9,128,384]{2,1,0:T(8,128)(2,1)S(1)} %get-tuple-element.47.w_ref), custom_call_target="tpu_custom_call" | custom-call | flops 1811939328 | bytes 1409024 | tf_op jit(solution)/shard_map/pallas_call | solution.py:200
  36.8 0.0 collective-permute-done.7
  36.8 0.0 collective-permute-done.8
  36.8 0.0 copy-done.4
  36.8 3.9 %shard_map.115 = (f32[896,128]{1,0:T(8,128)S(1)}, bf16[896,128]{1,0:T(8,128)(2,1)S(1)}, bf16[20,96,384]{2,1,0:T(8,128)(2,1)S(1)}) custom-call(s32[2]{0:T(128)S(1)} %pad_add_fusion.at_ref, f32[16,96,128]{2,1,0:T(8,128)S(1)} %get-tuple-element.48.acc_ref, f32[896,128]{1,0:T(8,128)S(1)} %get-tuple-element.49.sums_ref, ...), custom_call_target="tpu_custom_call" | custom-call | flops 796262400 | bytes 3047432 | tf_op jit(solution)/shard_map/pallas_call | solution.py:200
  40.7 2.2 %collective-permute-done.9 = bf16[1024,128]{1,0:T(8,128)(2,1)S(1)} collective-permute-done((bf16[1024,128]{1,0:T(8,128)(2,1)S(1)}, bf16[1024,128]{1,0:T(8,128)(2,1)S(1)}, u32[]{:S(2)}, u32[]{:S(2)}) %collective-permute-start.9) | collective-permute-done | bytes 262176 | tf_op jit(solution)/shard_map/ppermute | solution.py:503
  42.8 0.1 convert_add_fusion.mine_ref
  42.9 0.1 collective-permute-start.10
  43.0 0.5 collective-permute-start.12
  43.5 1.0 %collective-permute-done.10 = bf16[896,128]{1,0:T(8,128)(2,1)S(1)} collective-permute-done((bf16[896,128]{1,0:T(8,128)(2,1)S(1)}, bf16[896,128]{1,0:T(8,128)(2,1)S(1)}, u32[]{:S(2)}, u32[]{:S(2)}) %collective-permute-start.10) | collective-permute-done | bytes 229408 | tf_op jit(solution)/shard_map/ppermute | solution.py:503
  44.4 0.1 add_convert_fusion.2
  44.5 0.8 %collective-permute-start.11 = (bf16[896,128]{1,0:T(8,128)(2,1)S(1)}, bf16[896,128]{1,0:T(8,128)(2,1)S(1)}, u32[]{:S(2)}, u32[]{:S(2)}) collective-permute-start(bf16[896,128]{1,0:T(8,128)(2,1)S(1)} %add_convert_fusion.2), channel_id=1, source_target_pairs={{0,2},{1,3},{2,0},{3,1},{4,6},{5,7},{6,4},{7,5},{8,10},{9,11},{10,... | collective-permute-start | bytes 688136 | tf_op jit(solution)/shard_map/ppermute | solution.py:503
  45.3 1.8 %shard_map.117 = bf16[4,8,1024]{2,1,0:T(8,128)(2,1)} custom-call(s32[2]{0:T(128)S(1)} %pad_add_fusion.at_ref, bf16[20,96,384]{2,1,0:T(8,128)(2,1)S(1)} %get-tuple-element.61.outer_ref, bf16[9,128,384]{2,1,0:T(8,128)(2,1)S(1)} %get-tuple-element.62.w_ref), custom_call_target="tpu_custom_call" | custom-call | flops 226492416 | bytes 2359304 | tf_op jit(solution)/shard_map/pallas_call | solution.py:200
  47.2 0.0 collective-permute-done.12.other_ref
  47.2 1.6 %shard_map.116 = f32[512,512]{1,0:T(8,128)} custom-call(s32[2]{0:T(128)S(1)} %pad_add_fusion.at_ref, f32[1024,128]{1,0:T(8,128)S(1)} %convert_add_fusion.mine_ref, f32[1024,128]{1,0:T(8,128)S(1)} %collective-permute-done.12.other_ref), custom_call_target="tpu_custom_call" | custom-call | flops 10000000 | bytes 1048584 | tf_op jit(solution)/shard_map/pallas_call | solution.py:200
  48.8 3.4 %collective-permute-done.11 = bf16[896,128]{1,0:T(8,128)(2,1)S(1)} collective-permute-done((bf16[896,128]{1,0:T(8,128)(2,1)S(1)}, bf16[896,128]{1,0:T(8,128)(2,1)S(1)}, u32[]{:S(2)}, u32[]{:S(2)}) %collective-permute-start.11) | collective-permute-done | bytes 229408 | tf_op jit(solution)/shard_map/ppermute | solution.py:503
  52.2 0.1 add_convert_fusion.1.mine_ref
  52.3 0.1 collective-permute-start.13
  52.4 0.1 shard_map.118
  52.5 1.3 %collective-permute-done.13.other_ref = bf16[896,128]{1,0:T(8,128)(2,1)S(1)} collective-permute-done((bf16[896,128]{1,0:T(8,128)(2,1)S(1)}, bf16[896,128]{1,0:T(8,128)(2,1)S(1)}, u32[]{:S(2)}, u32[]{:S(2)}) %collective-permute-start.13) | collective-permute-done | bytes 229408 | tf_op jit(solution)/shard_map/ppermute | solution.py:503
  53.8 1.8 %shard_map.119 = (f32[27,64,64]{2,1,0:T(8,128)}, f32[27,64,64]{2,1,0:T(8,128)}) custom-call(s32[2]{0:T(128)S(1)} %pad_add_fusion.at_ref, f32[14,64,64]{2,1,0:T(8,128)S(1)} %get-tuple-element.65.mine_one, f32[14,64,64]{2,1,0:T(8,128)S(1)} %get-tuple-element.66.mine_two, bf16[896,128]{1,0:T(8,128)(2,1)S(1)} %collective-permute-done.13.other_ref), custom_call_target="tpu_custom_call" | custom-call | tf_op jit(solution)/shard_map/pallas_call | solution.py:200
  (6 shorter events, 0.0 us)
Async XLA Ops:
  2.3 11.2 %collective-permute-start = (bf16[768,128]{1,0:T(8,128)(2,1)}, bf16[768,128]{1,0:T(8,128)(2,1)S(1)}, u32[]{:S(2)}, u32[]{:S(2)}) collective-permute-start(bf16[768,128]{1,0:T(8,128)(2,1)} %get-tuple-element.37.a0), channel_id=1, source_target_pairs={{0,4},{4,8},{8,12},{12,0},{1,5},{5,9},{9,13},{13,1},{2,6},{6,10},{... | collective-permute-start | bytes 589832 | tf_op jit(solution)/shard_map/ppermute | solution.py:498
  5.4 16.6 %collective-permute-start.1 = (bf16[768,128]{1,0:T(8,128)(2,1)}, bf16[768,128]{1,0:T(8,128)(2,1)S(1)}, u32[]{:S(2)}, u32[]{:S(2)}) collective-permute-start(bf16[768,128]{1,0:T(8,128)(2,1)} %get-tuple-element.37.a0), channel_id=1, source_target_pairs={{0,8},{4,12},{8,0},{12,4},{1,9},{5,13},{9,1},{13,5},{2,10},{6,14},... | collective-permute-start | bytes 589832 | tf_op jit(solution)/shard_map/ppermute | solution.py:498
  8.0 14.0 %collective-permute-start.2 = (bf16[768,128]{1,0:T(8,128)(2,1)}, bf16[768,128]{1,0:T(8,128)(2,1)S(1)}, u32[]{:S(2)}, u32[]{:S(2)}) collective-permute-start(bf16[768,128]{1,0:T(8,128)(2,1)} %get-tuple-element.37.a0), channel_id=1, source_target_pairs={{0,12},{4,0},{8,4},{12,8},{1,13},{5,1},{9,5},{13,9},{2,14},{6,2},{... | collective-permute-start | bytes 589832 | tf_op jit(solution)/shard_map/ppermute | solution.py:498
  9.3 14.0 %collective-permute-start.3 = (bf16[256,128]{1,0:T(8,128)(2,1)}, bf16[256,128]{1,0:T(8,128)(2,1)S(1)}, u32[]{:S(2)}, u32[]{:S(2)}) collective-permute-start(bf16[256,128]{1,0:T(8,128)(2,1)} %get-tuple-element.52.i0), channel_id=1, source_target_pairs={{0,4},{4,8},{8,12},{12,0},{1,5},{5,9},{9,13},{13,1},{2,6},{6,10},{... | collective-permute-start | bytes 196616 | tf_op jit(solution)/shard_map/ppermute | solution.py:498
  10.0 19.5 %collective-permute-start.4 = (bf16[256,128]{1,0:T(8,128)(2,1)}, bf16[256,128]{1,0:T(8,128)(2,1)S(1)}, u32[]{:S(2)}, u32[]{:S(2)}) collective-permute-start(bf16[256,128]{1,0:T(8,128)(2,1)} %get-tuple-element.52.i0), channel_id=1, source_target_pairs={{0,8},{4,12},{8,0},{12,4},{1,9},{5,13},{9,1},{13,5},{2,10},{6,14},... | collective-permute-start | bytes 196616 | tf_op jit(solution)/shard_map/ppermute | solution.py:498
  13.5 16.1 %collective-permute-start.5 = (bf16[256,128]{1,0:T(8,128)(2,1)}, bf16[256,128]{1,0:T(8,128)(2,1)S(1)}, u32[]{:S(2)}, u32[]{:S(2)}) collective-permute-start(bf16[256,128]{1,0:T(8,128)(2,1)} %get-tuple-element.52.i0), channel_id=1, source_target_pairs={{0,12},{4,0},{8,4},{12,8},{1,13},{5,1},{9,5},{13,9},{2,14},{6,2},{... | collective-permute-start | bytes 196616 | tf_op jit(solution)/shard_map/ppermute | solution.py:498
  15.6 1.0 %copy-start = (bf16[512,512]{1,0:T(8,128)(2,1)S(1)}, bf16[512,512]{1,0:T(8,128)(2,1)}, u32[]{:S(2)}) copy-start(bf16[512,512]{1,0:T(8,128)(2,1)} %wt.1) | copy-start | bytes 1572868
  16.6 1.0 %copy-start.1 = (bf16[27,64,64]{2,1,0:T(8,128)(2,1)S(1)}, bf16[27,64,64]{2,1,0:T(8,128)(2,1)}, u32[]{:S(2)}) copy-start(bf16[27,64,64]{2,1,0:T(8,128)(2,1)} %w2.1) | copy-start | bytes 663556
  17.7 1.0 %copy-start.2 = (bf16[27,64,64]{2,1,0:T(8,128)(2,1)S(1)}, bf16[27,64,64]{2,1,0:T(8,128)(2,1)}, u32[]{:S(2)}) copy-start(bf16[27,64,64]{2,1,0:T(8,128)(2,1)} %w1.1) | copy-start | bytes 663556
  18.7 0.7 %copy-start.5 = (s32[8,8]{1,0:T(8,128)S(1)}, s32[8,8]{1,0:T(8,128)}, u32[]{:S(2)}) copy-start(s32[8,8]{1,0:T(8,128)} %keep.1) | copy-start | bytes 772
  19.4 2.6 %copy-start.3 = (bf16[768,128]{1,0:T(8,128)(2,1)S(1)}, bf16[768,128]{1,0:T(8,128)(2,1)}, u32[]{:S(2)}) copy-start(bf16[768,128]{1,0:T(8,128)(2,1)} %get-tuple-element.37.a0) | copy-start | bytes 589828
  29.5 1.5 %collective-permute-start.6 = (bf16[1024,128]{1,0:T(8,128)(2,1)S(1)}, bf16[1024,128]{1,0:T(8,128)(2,1)S(1)}, u32[]{:S(2)}, u32[]{:S(2)}) collective-permute-start(bf16[1024,128]{1,0:T(8,128)(2,1)S(1)} %get-tuple-element.45), channel_id=1, source_target_pairs={{0,1},{1,0},{2,3},{3,2},{4,5},{5,4},{6,7},{7,6},{8,9},{9,8},{10,11... | collective-permute-start | bytes 786440 | tf_op jit(solution)/shard_map/ppermute | solution.py:503
  29.5 7.2 %collective-permute-start.7 = (bf16[8,2,48,128]{3,2,1,0:T(8,128)(2,1)S(1)}, bf16[8,2,48,128]{3,2,1,0:T(8,128)(2,1)S(1)}, u32[]{:S(2)}, u32[]{:S(2)}) collective-permute-start(bf16[8,2,48,128]{3,2,1,0:T(8,128)(2,1)S(1)} %get-tuple-element.50), channel_id=1, source_target_pairs={{0,1},{1,0},{2,3},{3,2},{4,5},{5,4},{6,7},{7,6},{8,9},{9,8},{10,11... | collective-permute-start | bytes 589832 | tf_op jit(solution)/shard_map/ppermute | solution.py:503
  30.0 6.7 %collective-permute-start.8 = (bf16[8,2,48,128]{3,2,1,0:T(8,128)(2,1)S(1)}, bf16[8,2,48,128]{3,2,1,0:T(8,128)(2,1)S(1)}, u32[]{:S(2)}, u32[]{:S(2)}) collective-permute-start(bf16[8,2,48,128]{3,2,1,0:T(8,128)(2,1)S(1)} %get-tuple-element.51), channel_id=1, source_target_pairs={{1,2},{2,1},{5,6},{6,5},{9,10},{10,9},{13,14},{14,13},{17,18},{18,... | collective-permute-start | bytes 589832 | tf_op jit(solution)/shard_map/ppermute | solution.py:576
  31.1 11.7 %collective-permute-start.9 = (bf16[1024,128]{1,0:T(8,128)(2,1)S(1)}, bf16[1024,128]{1,0:T(8,128)(2,1)S(1)}, u32[]{:S(2)}, u32[]{:S(2)}) collective-permute-start(bf16[1024,128]{1,0:T(8,128)(2,1)S(1)} %add_convert_fusion), channel_id=1, source_target_pairs={{0,2},{1,3},{2,0},{3,1},{4,6},{5,7},{6,4},{7,5},{8,10},{9,11},{10,... | collective-permute-start | bytes 786440 | tf_op jit(solution)/shard_map/ppermute | solution.py:503
  33.7 3.1 %copy-start.4 = (bf16[256,128]{1,0:T(8,128)(2,1)S(1)}, bf16[256,128]{1,0:T(8,128)(2,1)}, u32[]{:S(2)}) copy-start(bf16[256,128]{1,0:T(8,128)(2,1)} %get-tuple-element.52.i0) | copy-start | bytes 196612
  42.9 1.6 %collective-permute-start.10 = (bf16[896,128]{1,0:T(8,128)(2,1)S(1)}, bf16[896,128]{1,0:T(8,128)(2,1)S(1)}, u32[]{:S(2)}, u32[]{:S(2)}) collective-permute-start(bf16[896,128]{1,0:T(8,128)(2,1)S(1)} %get-tuple-element.59), channel_id=1, source_target_pairs={{0,1},{1,0},{2,3},{3,2},{4,5},{5,4},{6,7},{7,6},{8,9},{9,8},{10,11... | collective-permute-start | bytes 688136 | tf_op jit(solution)/shard_map/ppermute | solution.py:503
  43.0 4.2 %collective-permute-start.12 = (f32[1024,128]{1,0:T(8,128)S(1)}, f32[1024,128]{1,0:T(8,128)S(1)}, u32[]{:S(2)}, u32[]{:S(2)}) collective-permute-start(f32[1024,128]{1,0:T(8,128)S(1)} %convert_add_fusion.mine_ref), channel_id=1, source_target_pairs={{0,1},{1,0},{2,3},{3,2},{4,5},{5,4},{6,7},{7,6},{8,9},{9,8},{10,11... | collective-permute-start | bytes 1572872 | tf_op jit(solution)/shard_map/ppermute | solution.py:503
  44.5 7.7 %collective-permute-start.11 = (bf16[896,128]{1,0:T(8,128)(2,1)S(1)}, bf16[896,128]{1,0:T(8,128)(2,1)S(1)}, u32[]{:S(2)}, u32[]{:S(2)}) collective-permute-start(bf16[896,128]{1,0:T(8,128)(2,1)S(1)} %add_convert_fusion.2), channel_id=1, source_target_pairs={{0,2},{1,3},{2,0},{3,1},{4,6},{5,7},{6,4},{7,5},{8,10},{9,11},{10,... | collective-permute-start | bytes 688136 | tf_op jit(solution)/shard_map/ppermute | solution.py:503
  52.3 1.6 %collective-permute-start.13 = (bf16[896,128]{1,0:T(8,128)(2,1)S(1)}, bf16[896,128]{1,0:T(8,128)(2,1)S(1)}, u32[]{:S(2)}, u32[]{:S(2)}) collective-permute-start(bf16[896,128]{1,0:T(8,128)(2,1)S(1)} %add_convert_fusion.1.mine_ref), channel_id=1, source_target_pairs={{0,1},{1,0},{2,3},{3,2},{4,5},{5,4},{6,7},{7,6},{8,9},{9,8},{10,11... | collective-permute-start | bytes 688136 | tf_op jit(solution)/shard_map/ppermute | solution.py:503
